TPU v7x, 32 devices: a whole 2x2x4 slice. The times are simulated.
32 devices in a mesh: fsdp: 8 (over y, x, core), seq: 4 (over z).
Axes of the slice: x: 2, y: 2, z: 4, core: 2. Of those that a mesh axis runs over, the one named last changes fastest.
Arguments:
- tokens: bfloat16 [16384, 512], P(('fsdp', 'seq')), may hold values from -6 to 6
- memory: bfloat16 [16384, 512], P(('fsdp', 'seq')), may hold values from -6 to 6
- targets: bfloat16 [16384, 512], P(('fsdp', 'seq')), may hold values from -21 to 21
- doc_lengths: int32 [8, 4], P('fsdp'), may hold values from 1 to 1024, 2048 in all within a row
- doc_order: int32 [8, 4], P('fsdp'), may hold values from 0 to 3, each once within a row
- memory_lengths: int32 [8, 4], P('fsdp'), may hold values from 1 to 512, 1536 in all within a row
- self_query: bfloat16 [512, 512], P('fsdp'), may hold values from -0.25 to 0.25
- self_query_bias: bfloat16 [512], P('fsdp'), may hold values from -1.75 to 1.75
- self_key: bfloat16 [512, 512], P('fsdp'), may hold values from -0.25 to 0.25
- self_value: bfloat16 [512, 512], P('fsdp'), may hold values from -0.25 to 0.25
- self_value_bias: bfloat16 [512], P('fsdp'), may hold values from -1.75 to 1.75
- self_output: bfloat16 [512, 512], P('fsdp'), may hold values from -2 to 2
- self_output_bias: bfloat16 [512], P('fsdp'), may hold values from -1.75 to 1.75
- first_gain: bfloat16 [512], P('fsdp'), may hold values from 0.5 to 1.5
- first_shift: bfloat16 [512], P('fsdp'), may hold values from -1.75 to 1.75
- cross_query: bfloat16 [512, 512], P('fsdp'), may hold values from -0.25 to 0.25
- cross_query_bias: bfloat16 [512], P('fsdp'), may hold values from -1.75 to 1.75
- cross_key: bfloat16 [512, 512], P('fsdp'), may hold values from -0.25 to 0.25
- cross_value: bfloat16 [512, 512], P('fsdp'), may hold values from -0.25 to 0.25
- cross_value_bias: bfloat16 [512], P('fsdp'), may hold values from -1.75 to 1.75
- cross_output: bfloat16 [512, 512], P('fsdp'), may hold values from -2 to 2
- cross_output_bias: bfloat16 [512], P('fsdp'), may hold values from -1.75 to 1.75
- second_gain: bfloat16 [512], P('fsdp'), may hold values from 0.5 to 1.5
- second_shift: bfloat16 [512], P('fsdp'), may hold values from -1.75 to 1.75
- expand_weight: bfloat16 [512, 2048], P('fsdp'), may hold values from -0.25 to 0.25
- expand_bias: bfloat16 [2048], P('fsdp'), may hold values from -1.75 to 1.75
- contract_weight: bfloat16 [2048, 512], P('fsdp'), may hold values from -0.25 to 0.25
- contract_bias: bfloat16 [512], P('fsdp'), may hold values from -1.75 to 1.75
- third_gain: bfloat16 [512], P('fsdp'), may hold values from 0.5 to 1.5
- third_shift: bfloat16 [512], P('fsdp'), may hold values from -1.75 to 1.75
Outputs:
- block_output: bfloat16 [16384, 512], P(('fsdp', 'seq'))
- loss_value: float32 [], replicated
- input_grad: float32 [16384, 512], P(('fsdp', 'seq'))
- memory_grad: float32 [16384, 512], P(('fsdp', 'seq'))
- self_query_grad: float32 [512, 512], P('fsdp')
- self_query_bias_grad: float32 [512], P('fsdp')
- self_key_grad: float32 [512, 512], P('fsdp')
- self_value_grad: float32 [512, 512], P('fsdp')
- self_value_bias_grad: float32 [512], P('fsdp')
- self_output_grad: float32 [512, 512], P('fsdp')
- self_output_bias_grad: float32 [512], P('fsdp')
- first_gain_grad: float32 [512], P('fsdp')
- first_shift_grad: float32 [512], P('fsdp')
- cross_query_grad: float32 [512, 512], P('fsdp')
- cross_query_bias_grad: float32 [512], P('fsdp')
- cross_key_grad: float32 [512, 512], P('fsdp')
- cross_value_grad: float32 [512, 512], P('fsdp')
- cross_value_bias_grad: float32 [512], P('fsdp')
- cross_output_grad: float32 [512, 512], P('fsdp')
- cross_output_bias_grad: float32 [512], P('fsdp')
- second_gain_grad: float32 [512], P('fsdp')
- second_shift_grad: float32 [512], P('fsdp')
- expand_weight_grad: float32 [512, 2048], P('fsdp')
- expand_bias_grad: float32 [2048], P('fsdp')
- contract_weight_grad: float32 [2048, 512], P('fsdp')
- contract_bias_grad: float32 [512], P('fsdp')
- third_gain_grad: float32 [512], P('fsdp')
- third_shift_grad: float32 [512], P('fsdp')
Inputs may be any that keep to these rules, and one draw needn't show every extreme that they name: `doc_lengths`: the 4 lengths of a group sum to 2048; in every group the largest is 1024. `doc_order`: each row holds every slot number once. `memory_lengths`: in every group the largest is 512.
All inputs are finite; a program needn't handle non-finite values.
Results may differ from a plain program's by a relative error of at most 0.025.
Values may be sent and summed in bfloat16 or wider, within the bound.
No kernel may reach another device: no remote copies, remote signals or barrier semaphores. Data moves between devices by JAX's collectives and lax.ppermute only.
A program may use at most 128 MiB of HBM per device.

v0:
```python
import jax
import jax.numpy as jnp
from jax import lax
from jax.sharding import PartitionSpec as P

D = 512
HDIM = 64
DOCS = 4
MEM = 512


def product(left_side, right_side):
    return jnp.dot(left_side, right_side, preferred_element_type=jnp.float32)


def product_left(left_side, right_side):
    return lax.dot_general(
        left_side, right_side, (((0,), (0,)), ((), ())), preferred_element_type=jnp.float32
    )


def product_right(left_side, right_side):
    return lax.dot_general(
        left_side, right_side, (((1,), (1,)), ((), ())), preferred_element_type=jnp.float32
    )


def column_sums(values):
    return jnp.sum(values.astype(jnp.float32), axis=0)


def layer_norm(values, norm_gain, norm_shift):
    centred = values - jnp.mean(values, axis=1, keepdims=True)
    inverse = lax.rsqrt(jnp.mean(centred * centred, axis=1, keepdims=True) + 1e-05)
    normal = centred * inverse
    return (normal * norm_gain + norm_shift, normal, inverse)


def norm_backward(grad_out, normal, inverse, norm_gain):
    scaled = grad_out * norm_gain
    grad_input = inverse * (
        scaled
        - jnp.mean(scaled, axis=1, keepdims=True)
        - normal * jnp.mean(scaled * normal, axis=1, keepdims=True)
    )
    return (grad_input, jnp.sum(grad_out * normal, axis=0), jnp.sum(grad_out, axis=0))


def document_slots(lengths, slot_order, group_rows):
    slot_range = jnp.arange(DOCS, dtype=jnp.int32)
    matches = (slot_order[:, None] == slot_range[None, :]).astype(jnp.int32)
    placed = jnp.sum(matches * lengths[None, :], axis=1)
    slot_ends = jnp.cumsum(placed)
    positions = jnp.arange(group_rows, dtype=jnp.int32)
    slot_index = jnp.sum((positions[:, None] >= slot_ends[None, :]).astype(jnp.int32), axis=1)
    pick_table = (slot_index[:, None] == slot_range[None, :]).astype(jnp.int32)
    return jnp.sum(pick_table * slot_order[None, :], axis=1)


def memory_slots(memory_limits):
    key_index = jnp.arange(DOCS * MEM, dtype=jnp.int32)
    key_document = key_index // MEM
    pick_table = (key_document[:, None] == jnp.arange(DOCS, dtype=jnp.int32)[None, :]).astype(
        jnp.int32
    )
    key_limit = jnp.sum(pick_table * memory_limits[None, :], axis=1)
    return (key_document, key_index % MEM < key_limit)


def attention_forward(queries, key_rows, value_rows, allowed_fn, score_scale):
    group_rows = queries.shape[0]
    block_rows = min(512, group_rows)
    blocks = group_rows // block_rows
    head_count = queries.shape[1] // HDIM
    key_heads = key_rows.reshape(key_rows.shape[0], head_count, HDIM)
    value_heads = value_rows.reshape(value_rows.shape[0], head_count, HDIM)
    query_blocks = queries.reshape(blocks, block_rows, head_count, HDIM)
    block_starts = jnp.arange(blocks, dtype=jnp.int32) * block_rows

    def one_block(inputs_pair):
        block_start, query_part = inputs_pair
        scores = (
            jnp.einsum("qhd,khd->hqk", query_part, key_heads, preferred_element_type=jnp.float32)
            * score_scale
        )
        scores = jnp.where(allowed_fn(block_start, block_rows)[None], scores, -1e30)
        largest = jnp.max(scores, axis=2, keepdims=True)
        expo = jnp.exp(scores - largest)
        denominator = jnp.sum(expo, axis=2, keepdims=True)
        softmax_weights = (expo / denominator).astype(jnp.bfloat16)
        result = jnp.einsum(
            "hqk,khd->qhd", softmax_weights, value_heads, preferred_element_type=jnp.float32
        )
        return (
            result.reshape(block_rows, head_count * HDIM),
            (largest + jnp.log(denominator))[:, :, 0],
        )

    outputs, log_totals = lax.map(one_block, (block_starts, query_blocks))
    return (outputs.reshape(group_rows, head_count * HDIM).astype(jnp.bfloat16), log_totals)


def attention_backward(
    queries, key_rows, value_rows, grad_context, log_totals, allowed_fn, score_scale
):
    group_rows = queries.shape[0]
    block_rows = min(512, group_rows)
    blocks = group_rows // block_rows
    head_count = queries.shape[1] // HDIM
    key_heads = key_rows.reshape(key_rows.shape[0], head_count, HDIM)
    value_heads = value_rows.reshape(value_rows.shape[0], head_count, HDIM)
    query_blocks = queries.reshape(blocks, block_rows, head_count, HDIM)
    grad_blocks = grad_context.reshape(blocks, block_rows, head_count, HDIM)
    block_starts = jnp.arange(blocks, dtype=jnp.int32) * block_rows

    def block_step(carried, block_item):
        grad_keys, grad_values = carried
        block_start, query_part, grad_part, log_part = block_item
        scores = (
            jnp.einsum("qhd,khd->hqk", query_part, key_heads, preferred_element_type=jnp.float32)
            * score_scale
        )
        allowed = allowed_fn(block_start, block_rows)[None]
        probs_full = jnp.where(allowed, jnp.exp(scores - log_part[:, :, None]), 0.0)
        probs_low = probs_full.astype(jnp.bfloat16)
        grad_probs = jnp.einsum(
            "qhd,khd->hqk", grad_part, value_heads, preferred_element_type=jnp.float32
        )
        inner_sum = jnp.sum(grad_probs * probs_full, axis=2, keepdims=True)
        grad_scores = (probs_full * (grad_probs - inner_sum)).astype(jnp.bfloat16)
        grad_query = jnp.einsum(
            "hqk,khd->qhd", grad_scores, key_heads, preferred_element_type=jnp.float32
        )
        grad_keys = grad_keys + jnp.einsum(
            "hqk,qhd->khd", grad_scores, query_part, preferred_element_type=jnp.float32
        )
        grad_values = grad_values + jnp.einsum(
            "hqk,qhd->khd", probs_low, grad_part, preferred_element_type=jnp.float32
        )
        grad_query = (grad_query * score_scale).astype(jnp.bfloat16)
        return ((grad_keys, grad_values), grad_query.reshape(block_rows, head_count * HDIM))

    zero_keys = jnp.zeros(key_heads.shape, jnp.float32)
    (grad_keys, grad_values), grad_queries = lax.scan(
        block_step, (zero_keys, zero_keys), (block_starts, query_blocks, grad_blocks, log_totals)
    )
    key_count = key_rows.shape[0]
    return (
        grad_queries.reshape(group_rows, head_count * HDIM),
        (grad_keys * score_scale).reshape(key_count, head_count * HDIM).astype(jnp.bfloat16),
        grad_values.reshape(key_count, head_count * HDIM).astype(jnp.bfloat16),
    )


def to_tokens(context):
    return lax.all_to_all(context, "seq", split_axis=0, concat_axis=1, tiled=True)


def to_heads(gradient_rows):
    return lax.all_to_all(gradient_rows, "seq", split_axis=1, concat_axis=0, tiled=True)


def shards(
    tokens,
    memory,
    targets,
    doc_lengths,
    doc_order,
    memory_lengths,
    self_query,
    self_query_bias,
    self_key,
    self_value,
    self_value_bias,
    self_output,
    self_output_bias,
    first_gain,
    first_shift,
    cross_query,
    cross_query_bias,
    cross_key,
    cross_value,
    cross_value_bias,
    cross_output,
    cross_output_bias,
    second_gain,
    second_shift,
    expand_weight,
    expand_bias,
    contract_weight,
    contract_bias,
    third_gain,
    third_shift,
):
    split_count = lax.axis_size("seq")
    split_index = lax.axis_index("seq")
    local_rows = tokens.shape[0]
    group_rows = local_rows * split_count
    score_scale = HDIM ** (-0.5)
    (
        full_self_query,
        full_self_query_bias,
        full_self_key,
        full_self_value,
        full_self_value_bias,
        full_self_output,
        full_self_output_bias,
        full_first_gain,
        full_first_shift,
        full_cross_query,
        full_cross_query_bias,
        full_cross_key,
        full_cross_value,
        full_cross_value_bias,
        full_cross_output,
        full_cross_output_bias,
        full_second_gain,
        full_second_shift,
        full_expand_weight,
        full_expand_bias,
        full_contract_weight,
        full_contract_bias,
        full_third_gain,
        full_third_shift,
    ) = (
        lax.all_gather(self_query, "fsdp", axis=0, tiled=True),
        lax.all_gather(self_query_bias, "fsdp", axis=0, tiled=True),
        lax.all_gather(self_key, "fsdp", axis=0, tiled=True),
        lax.all_gather(self_value, "fsdp", axis=0, tiled=True),
        lax.all_gather(self_value_bias, "fsdp", axis=0, tiled=True),
        lax.all_gather(self_output, "fsdp", axis=0, tiled=True),
        lax.all_gather(self_output_bias, "fsdp", axis=0, tiled=True),
        lax.all_gather(first_gain, "fsdp", axis=0, tiled=True),
        lax.all_gather(first_shift, "fsdp", axis=0, tiled=True),
        lax.all_gather(cross_query, "fsdp", axis=0, tiled=True),
        lax.all_gather(cross_query_bias, "fsdp", axis=0, tiled=True),
        lax.all_gather(cross_key, "fsdp", axis=0, tiled=True),
        lax.all_gather(cross_value, "fsdp", axis=0, tiled=True),
        lax.all_gather(cross_value_bias, "fsdp", axis=0, tiled=True),
        lax.all_gather(cross_output, "fsdp", axis=0, tiled=True),
        lax.all_gather(cross_output_bias, "fsdp", axis=0, tiled=True),
        lax.all_gather(second_gain, "fsdp", axis=0, tiled=True),
        lax.all_gather(second_shift, "fsdp", axis=0, tiled=True),
        lax.all_gather(expand_weight, "fsdp", axis=0, tiled=True),
        lax.all_gather(expand_bias, "fsdp", axis=0, tiled=True),
        lax.all_gather(contract_weight, "fsdp", axis=0, tiled=True),
        lax.all_gather(contract_bias, "fsdp", axis=0, tiled=True),
        lax.all_gather(third_gain, "fsdp", axis=0, tiled=True),
        lax.all_gather(third_shift, "fsdp", axis=0, tiled=True),
    )
    document_slot = document_slots(doc_lengths[0], doc_order[0], group_rows)
    local_slots = lax.dynamic_slice_in_dim(document_slot, split_index * local_rows, local_rows)
    live_rows = (local_slots != DOCS - 1).astype(jnp.float32)[:, None]
    key_document, key_valid = memory_slots(memory_lengths[0])
    positions = jnp.arange(group_rows, dtype=jnp.int32)

    def self_allowed(block_start, span_rows):
        query_docs = lax.dynamic_slice_in_dim(document_slot, block_start, span_rows)
        query_pos = block_start + jnp.arange(span_rows, dtype=jnp.int32)
        return (query_docs[:, None] == document_slot[None, :]) & (
            query_pos[:, None] >= positions[None, :]
        )

    def cross_allowed(block_start, span_rows):
        query_docs = lax.dynamic_slice_in_dim(document_slot, block_start, span_rows)
        return (query_docs[:, None] == key_document[None, :]) & key_valid[None, :]

    queries = (product(tokens, full_self_query) + full_self_query_bias.astype(jnp.float32)).astype(
        jnp.bfloat16
    )
    key_rows = product(tokens, full_self_key).astype(jnp.bfloat16)
    value_rows = (
        product(tokens, full_self_value) + full_self_value_bias.astype(jnp.float32)
    ).astype(jnp.bfloat16)
    head_queries, head_keys, head_values = (
        lax.all_to_all(queries, "seq", split_axis=1, concat_axis=0, tiled=True),
        lax.all_to_all(key_rows, "seq", split_axis=1, concat_axis=0, tiled=True),
        lax.all_to_all(value_rows, "seq", split_axis=1, concat_axis=0, tiled=True),
    )
    context_heads, self_log = attention_forward(
        head_queries, head_keys, head_values, self_allowed, score_scale
    )
    context_low = to_tokens(context_heads)
    self_branch = product(context_low, full_self_output) + full_self_output_bias.astype(jnp.float32)
    first_out, first_normal, first_inverse = layer_norm(
        tokens.astype(jnp.float32) + self_branch,
        full_first_gain.astype(jnp.float32),
        full_first_shift.astype(jnp.float32),
    )
    first_low = first_out.astype(jnp.bfloat16)
    cross_queries = (
        product(first_low, full_cross_query) + full_cross_query_bias.astype(jnp.float32)
    ).astype(jnp.bfloat16)
    memory_keys = product(memory, full_cross_key).astype(jnp.bfloat16)
    memory_values = (
        product(memory, full_cross_value) + full_cross_value_bias.astype(jnp.float32)
    ).astype(jnp.bfloat16)
    head_cross, head_memory_keys, head_memory_values = (
        lax.all_to_all(cross_queries, "seq", split_axis=1, concat_axis=0, tiled=True),
        lax.all_to_all(memory_keys, "seq", split_axis=1, concat_axis=0, tiled=True),
        lax.all_to_all(memory_values, "seq", split_axis=1, concat_axis=0, tiled=True),
    )
    cross_heads_out, cross_log = attention_forward(
        head_cross, head_memory_keys, head_memory_values, cross_allowed, score_scale
    )
    cross_low = to_tokens(cross_heads_out)
    cross_branch = product(cross_low, full_cross_output) + full_cross_output_bias.astype(
        jnp.float32
    )
    second, second_normal, second_inverse = layer_norm(
        first_out + cross_branch,
        full_second_gain.astype(jnp.float32),
        full_second_shift.astype(jnp.float32),
    )
    second_low = second.astype(jnp.bfloat16)
    expanded = product(second_low, full_expand_weight) + full_expand_bias.astype(jnp.float32)
    hidden_low = jax.nn.silu(expanded).astype(jnp.bfloat16)
    feed_out = product(hidden_low, full_contract_weight) + full_contract_bias.astype(jnp.float32)
    final_out, third_normal, third_inverse = layer_norm(
        second + feed_out, full_third_gain.astype(jnp.float32), full_third_shift.astype(jnp.float32)
    )
    difference = final_out - targets.astype(jnp.float32)
    error_sum, live_count = lax.psum(
        (jnp.sum(live_rows * difference * difference), jnp.sum(live_rows)), ("fsdp", "seq")
    )
    loss_value = error_sum / (live_count * D)
    (
        back_self_query,
        back_self_key,
        back_self_value,
        back_self_output,
        back_cross_query,
        back_cross_key,
        back_cross_value,
        back_cross_output,
        back_expand,
        back_contract,
        back_first_gain,
        back_second_gain,
        back_third_gain,
    ) = (
        lax.all_gather(self_query, "fsdp", axis=0, tiled=True),
        lax.all_gather(self_key, "fsdp", axis=0, tiled=True),
        lax.all_gather(self_value, "fsdp", axis=0, tiled=True),
        lax.all_gather(self_output, "fsdp", axis=0, tiled=True),
        lax.all_gather(cross_query, "fsdp", axis=0, tiled=True),
        lax.all_gather(cross_key, "fsdp", axis=0, tiled=True),
        lax.all_gather(cross_value, "fsdp", axis=0, tiled=True),
        lax.all_gather(cross_output, "fsdp", axis=0, tiled=True),
        lax.all_gather(expand_weight, "fsdp", axis=0, tiled=True),
        lax.all_gather(contract_weight, "fsdp", axis=0, tiled=True),
        lax.all_gather(first_gain, "fsdp", axis=0, tiled=True),
        lax.all_gather(second_gain, "fsdp", axis=0, tiled=True),
        lax.all_gather(third_gain, "fsdp", axis=0, tiled=True),
    )
    grad_final = live_rows * difference
    grad_third, third_gain_grad, third_shift_grad = norm_backward(
        grad_final, third_normal, third_inverse, back_third_gain.astype(jnp.float32)
    )
    feed_low = grad_third.astype(jnp.bfloat16)
    contract_grad = product_left(hidden_low, feed_low)
    contract_bias_grad = column_sums(feed_low)
    grad_hidden = product_right(feed_low, back_contract)
    sigmoid_value = jax.nn.sigmoid(expanded)
    grad_expanded = (grad_hidden * sigmoid_value * (1.0 + expanded * (1.0 - sigmoid_value))).astype(
        jnp.bfloat16
    )
    expand_grad = product_left(second_low, grad_expanded)
    expand_bias_grad = column_sums(grad_expanded)
    grad_second, second_gain_grad, second_shift_grad = norm_backward(
        grad_third + product_right(grad_expanded, back_expand),
        second_normal,
        second_inverse,
        back_second_gain.astype(jnp.float32),
    )
    cross_grad_low = grad_second.astype(jnp.bfloat16)
    cross_output_grad = product_left(cross_low, cross_grad_low)
    cross_output_bias_grad = column_sums(cross_grad_low)
    grad_cross_context = to_heads(
        product_right(cross_grad_low, back_cross_output).astype(jnp.bfloat16)
    )
    grad_cross_heads, grad_memory_key_heads, grad_memory_value_heads = attention_backward(
        head_cross,
        head_memory_keys,
        head_memory_values,
        grad_cross_context,
        cross_log,
        cross_allowed,
        score_scale,
    )
    grad_cross_queries, grad_memory_keys, grad_memory_values = (
        lax.all_to_all(grad_cross_heads, "seq", split_axis=0, concat_axis=1, tiled=True),
        lax.all_to_all(grad_memory_key_heads, "seq", split_axis=0, concat_axis=1, tiled=True),
        lax.all_to_all(grad_memory_value_heads, "seq", split_axis=0, concat_axis=1, tiled=True),
    )
    cross_query_grad = product_left(first_low, grad_cross_queries)
    cross_query_bias_grad = column_sums(grad_cross_queries)
    cross_key_grad = product_left(memory, grad_memory_keys)
    cross_value_grad = product_left(memory, grad_memory_values)
    cross_value_bias_grad = column_sums(grad_memory_values)
    memory_grad = product_right(grad_memory_keys, back_cross_key) + product_right(
        grad_memory_values, back_cross_value
    )
    grad_first, first_gain_grad, first_shift_grad = norm_backward(
        grad_second + product_right(grad_cross_queries, back_cross_query),
        first_normal,
        first_inverse,
        back_first_gain.astype(jnp.float32),
    )
    self_grad_low = grad_first.astype(jnp.bfloat16)
    self_output_grad = product_left(context_low, self_grad_low)
    self_output_bias_grad = column_sums(self_grad_low)
    grad_context = to_heads(product_right(self_grad_low, back_self_output).astype(jnp.bfloat16))
    grad_query_heads, grad_key_heads, grad_value_heads = attention_backward(
        head_queries, head_keys, head_values, grad_context, self_log, self_allowed, score_scale
    )
    grad_queries, grad_keys, grad_values = (
        lax.all_to_all(grad_query_heads, "seq", split_axis=0, concat_axis=1, tiled=True),
        lax.all_to_all(grad_key_heads, "seq", split_axis=0, concat_axis=1, tiled=True),
        lax.all_to_all(grad_value_heads, "seq", split_axis=0, concat_axis=1, tiled=True),
    )
    self_query_grad = product_left(tokens, grad_queries)
    self_query_bias_grad = column_sums(grad_queries)
    self_key_grad = product_left(tokens, grad_keys)
    self_value_grad = product_left(tokens, grad_values)
    self_value_bias_grad = column_sums(grad_values)
    input_grad = (
        grad_first
        + product_right(grad_queries, back_self_query)
        + product_right(grad_keys, back_self_key)
        + product_right(grad_values, back_self_value)
    )
    gradients = (
        self_query_grad,
        self_query_bias_grad,
        self_key_grad,
        self_value_grad,
        self_value_bias_grad,
        self_output_grad,
        self_output_bias_grad,
        first_gain_grad,
        first_shift_grad,
        cross_query_grad,
        cross_query_bias_grad,
        cross_key_grad,
        cross_value_grad,
        cross_value_bias_grad,
        cross_output_grad,
        cross_output_bias_grad,
        second_gain_grad,
        second_shift_grad,
        expand_grad,
        expand_bias_grad,
        contract_grad,
        contract_bias_grad,
        third_gain_grad,
        third_shift_grad,
    )
    summed = (
        lax.psum(gradients[0].astype(jnp.bfloat16), "seq").astype(jnp.float32),
        lax.psum(gradients[1].astype(jnp.bfloat16), "seq").astype(jnp.float32),
        lax.psum(gradients[2].astype(jnp.bfloat16), "seq").astype(jnp.float32),
        lax.psum(gradients[3].astype(jnp.bfloat16), "seq").astype(jnp.float32),
        lax.psum(gradients[4].astype(jnp.bfloat16), "seq").astype(jnp.float32),
        lax.psum(gradients[5].astype(jnp.bfloat16), "seq").astype(jnp.float32),
        lax.psum(gradients[6].astype(jnp.bfloat16), "seq").astype(jnp.float32),
        lax.psum(gradients[7].astype(jnp.bfloat16), "seq").astype(jnp.float32),
        lax.psum(gradients[8].astype(jnp.bfloat16), "seq").astype(jnp.float32),
        lax.psum(gradients[9].astype(jnp.bfloat16), "seq").astype(jnp.float32),
        lax.psum(gradients[10].astype(jnp.bfloat16), "seq").astype(jnp.float32),
        lax.psum(gradients[11].astype(jnp.bfloat16), "seq").astype(jnp.float32),
        lax.psum(gradients[12].astype(jnp.bfloat16), "seq").astype(jnp.float32),
        lax.psum(gradients[13].astype(jnp.bfloat16), "seq").astype(jnp.float32),
        lax.psum(gradients[14].astype(jnp.bfloat16), "seq").astype(jnp.float32),
        lax.psum(gradients[15].astype(jnp.bfloat16), "seq").astype(jnp.float32),
        lax.psum(gradients[16].astype(jnp.bfloat16), "seq").astype(jnp.float32),
        lax.psum(gradients[17].astype(jnp.bfloat16), "seq").astype(jnp.float32),
        lax.psum(gradients[18].astype(jnp.bfloat16), "seq").astype(jnp.float32),
        lax.psum(gradients[19].astype(jnp.bfloat16), "seq").astype(jnp.float32),
        lax.psum(gradients[20].astype(jnp.bfloat16), "seq").astype(jnp.float32),
        lax.psum(gradients[21].astype(jnp.bfloat16), "seq").astype(jnp.float32),
        lax.psum(gradients[22].astype(jnp.bfloat16), "seq").astype(jnp.float32),
        lax.psum(gradients[23].astype(jnp.bfloat16), "seq").astype(jnp.float32),
    )
    reduced = (
        lax.psum_scatter(
            summed[0].astype(jnp.bfloat16), "fsdp", scatter_dimension=0, tiled=True
        ).astype(jnp.float32),
        lax.psum_scatter(
            summed[1].astype(jnp.bfloat16), "fsdp", scatter_dimension=0, tiled=True
        ).astype(jnp.float32),
        lax.psum_scatter(
            summed[2].astype(jnp.bfloat16), "fsdp", scatter_dimension=0, tiled=True
        ).astype(jnp.float32),
        lax.psum_scatter(
            summed[3].astype(jnp.bfloat16), "fsdp", scatter_dimension=0, tiled=True
        ).astype(jnp.float32),
        lax.psum_scatter(
            summed[4].astype(jnp.bfloat16), "fsdp", scatter_dimension=0, tiled=True
        ).astype(jnp.float32),
        lax.psum_scatter(
            summed[5].astype(jnp.bfloat16), "fsdp", scatter_dimension=0, tiled=True
        ).astype(jnp.float32),
        lax.psum_scatter(
            summed[6].astype(jnp.bfloat16), "fsdp", scatter_dimension=0, tiled=True
        ).astype(jnp.float32),
        lax.psum_scatter(
            summed[7].astype(jnp.bfloat16), "fsdp", scatter_dimension=0, tiled=True
        ).astype(jnp.float32),
        lax.psum_scatter(
            summed[8].astype(jnp.bfloat16), "fsdp", scatter_dimension=0, tiled=True
        ).astype(jnp.float32),
        lax.psum_scatter(
            summed[9].astype(jnp.bfloat16), "fsdp", scatter_dimension=0, tiled=True
        ).astype(jnp.float32),
        lax.psum_scatter(
            summed[10].astype(jnp.bfloat16), "fsdp", scatter_dimension=0, tiled=True
        ).astype(jnp.float32),
        lax.psum_scatter(
            summed[11].astype(jnp.bfloat16), "fsdp", scatter_dimension=0, tiled=True
        ).astype(jnp.float32),
        lax.psum_scatter(
            summed[12].astype(jnp.bfloat16), "fsdp", scatter_dimension=0, tiled=True
        ).astype(jnp.float32),
        lax.psum_scatter(
            summed[13].astype(jnp.bfloat16), "fsdp", scatter_dimension=0, tiled=True
        ).astype(jnp.float32),
        lax.psum_scatter(
            summed[14].astype(jnp.bfloat16), "fsdp", scatter_dimension=0, tiled=True
        ).astype(jnp.float32),
        lax.psum_scatter(
            summed[15].astype(jnp.bfloat16), "fsdp", scatter_dimension=0, tiled=True
        ).astype(jnp.float32),
        lax.psum_scatter(
            summed[16].astype(jnp.bfloat16), "fsdp", scatter_dimension=0, tiled=True
        ).astype(jnp.float32),
        lax.psum_scatter(
            summed[17].astype(jnp.bfloat16), "fsdp", scatter_dimension=0, tiled=True
        ).astype(jnp.float32),
        lax.psum_scatter(
            summed[18].astype(jnp.bfloat16), "fsdp", scatter_dimension=0, tiled=True
        ).astype(jnp.float32),
        lax.psum_scatter(
            summed[19].astype(jnp.bfloat16), "fsdp", scatter_dimension=0, tiled=True
        ).astype(jnp.float32),
        lax.psum_scatter(
            summed[20].astype(jnp.bfloat16), "fsdp", scatter_dimension=0, tiled=True
        ).astype(jnp.float32),
        lax.psum_scatter(
            summed[21].astype(jnp.bfloat16), "fsdp", scatter_dimension=0, tiled=True
        ).astype(jnp.float32),
        lax.psum_scatter(
            summed[22].astype(jnp.bfloat16), "fsdp", scatter_dimension=0, tiled=True
        ).astype(jnp.float32),
        lax.psum_scatter(
            summed[23].astype(jnp.bfloat16), "fsdp", scatter_dimension=0, tiled=True
        ).astype(jnp.float32),
    )
    return (final_out.astype(jnp.bfloat16), loss_value, input_grad, memory_grad) + tuple(reduced)


def solution(mesh):
    placed = (
        P(("fsdp", "seq"), None),
        P(("fsdp", "seq"), None),
        P(("fsdp", "seq"), None),
        P("fsdp", None),
        P("fsdp", None),
        P("fsdp", None),
        P("fsdp", None),
        P("fsdp"),
        P("fsdp", None),
        P("fsdp", None),
        P("fsdp"),
        P("fsdp", None),
        P("fsdp"),
        P("fsdp"),
        P("fsdp"),
        P("fsdp", None),
        P("fsdp"),
        P("fsdp", None),
        P("fsdp", None),
        P("fsdp"),
        P("fsdp", None),
        P("fsdp"),
        P("fsdp"),
        P("fsdp"),
        P("fsdp", None),
        P("fsdp"),
        P("fsdp", None),
        P("fsdp"),
        P("fsdp"),
        P("fsdp"),
    )
    return jax.shard_map(
        shards,
        mesh=mesh,
        in_specs=placed,
        out_specs=(
            P(("fsdp", "seq"), None),
            P(),
            P(("fsdp", "seq"), None),
            P(("fsdp", "seq"), None),
            P("fsdp", None),
            P("fsdp"),
            P("fsdp", None),
            P("fsdp", None),
            P("fsdp"),
            P("fsdp", None),
            P("fsdp"),
            P("fsdp"),
            P("fsdp"),
            P("fsdp", None),
            P("fsdp"),
            P("fsdp", None),
            P("fsdp", None),
            P("fsdp"),
            P("fsdp", None),
            P("fsdp"),
            P("fsdp"),
            P("fsdp"),
            P("fsdp", None),
            P("fsdp"),
            P("fsdp", None),
            P("fsdp"),
            P("fsdp"),
            P("fsdp"),
        ),
        check_vma=False,
    )
```

profile of v0, /device:TPU:0, one launch (start us, length us, event | category | flops | bytes accessed | tf_op | source)
XLA Modules:
  0.0 1036.9 jit_solution(17829869689109831920)
XLA Ops:
  20.3 26.1 %all-reduce.29 = (bf16[512]{0:T(512)(128)(2,1)S(1)}, bf16[512]{0:T(512)(128)(2,1)S(1)}, bf16[512]{0:T(512)(128)(2,1)S(1)}, bf16[512]{0:T(512)(128)(2,1)S(1)}, bf...) all-reduce(bf16[512]{0:T(512)(128)(2,1)S(1)} %dynamic-update-slice,, ...), channel_id=1, replica_groups=mesh['fsdp'=8,'seq'=4] {'fsdp'}, use_global_device_ids=true, to_apply=%add | all-reduce | flops 6656 | bytes 26624
  82.0 9.6 all_gather.85
  102.7 12.1 %all-to-all-done = bf16[512,4,128]{0,2,1:T(8,128)(2,1)S(1)} async-done(((bf16[512,4,128]{0,2,1:T(8,128)(2,1)}), bf16[512,4,128]{0,2,1:T(8,128)(2,1)S(1)}, u32[]{:S(2)}, u32[]{:S(2)}) %all-to-all-start) | async-done | bytes 524320 | tf_op jit(solution)/shard_map/all_to_all | solution.py:276
  114.9 46.6 %while.56 = (s32[]{:T(128)}, bf16[4,512,128]{1,2,0:T(8,128)(2,1)S(1)}, f32[4,2,512]{2,1,0:T(2,128)S(1)}, s32[4]{0:T(128)S(1)}, s32[2048]{0:T(1024)S(1)}, /*index...) while((s32[]{:T(128)}, ...), condition=%wide.region_7.8_spmd.clone, body=%wide.region_4.7_spmd.clone.sunk | while | flops 565181952 | bytes 30984376 | solution.py:99
  184.0 10.0 all_gather.90
  195.1 10.7 %all_gather.94 = bf16[512,512]{1,0:T(8,128)(2,1)} all-gather(bf16[64,512]{1,0:T(8,128)(2,1)S(1)} %copy-done.42), channel_id=1, replica_groups=mesh['fsdp'=8,'seq'=4] {'fsdp'}, dimensions={0}, use_global_device_ids=true | all-gather | bytes 589824 | tf_op jit(solution)/shard_map/all_gather | solution.py:235
  225.7 12.4 %all-to-all-done.5 = bf16[512,4,128]{0,2,1:T(8,128)(2,1)S(1)} async-done(((bf16[512,4,128]{0,2,1:T(8,128)(2,1)}), bf16[512,4,128]{0,2,1:T(8,128)(2,1)S(1)}, u32[]{:S(2)}, u32[]{:S(2)}) %all-to-all-start.5) | async-done | bytes 524320 | tf_op jit(solution)/shard_map/all_to_all | solution.py:300
  257.3 44.7 %while.57 = (s32[]{:T(128)}, bf16[4,512,128]{1,2,0:T(8,128)(2,1)}, f32[4,2,512]{2,1,0:T(2,128)S(1)}, s32[4]{0:T(128)S(1)}, s32[2048]{0:T(1024)S(1)}, /*index=5*/...) while((s32[]{:T(128)}, bf16[4,512,128]{1,2,0:T(8,128)(2,1)}, ...), condition=%wide.region_14.15_spmd.clone, body=%wide.region_11.14_spmd.clone.sunk | while | flops 564149248 | bytes 30990524 | solution.py:99
  317.8 10.4 %all_gather.99 = bf16[512,512]{1,0:T(8,128)(2,1)} all-gather(bf16[64,512]{1,0:T(8,128)(2,1)S(1)} %copy-done.44), channel_id=1, replica_groups=mesh['fsdp'=8,'seq'=4] {'fsdp'}, dimensions={0}, use_global_device_ids=true | all-gather | bytes 589824 | tf_op jit(solution)/shard_map/all_gather | solution.py:240
  359.1 15.1 %all-to-all-done.8 = bf16[512,4,128]{0,2,1:T(8,128)(2,1)} async-done(((bf16[512,4,128]{0,2,1:T(8,128)(2,1)}), bf16[512,4,128]{0,2,1:T(8,128)(2,1)}, u32[]{:S(2)}, u32[]{:S(2)}) %all-to-all-start.8) | async-done | bytes 524320 | tf_op jit(solution)/shard_map/all_to_all | solution.py:160
  375.0 71.2 %while.58 = (s32[]{:T(128)}, f32[2048,2,64]{0,2,1:T(8,128)S(1)}, f32[2048,2,64]{0,2,1:T(8,128)}, bf16[4,512,128]{1,2,0:T(8,128)(2,1)}, bf16[4,512,2,64]{1,3,2,0:...) while((s32[]{:T(128)}, f32[2048,2,64]{0,2,1:T(8,128)S(1)}, ...), condition=%wide.region_29.30_spmd.clone, body=%wide.region_27.29_spmd.clone.sunk | while | flops 1376926720 | bytes 82235680 | solution.py:144
  453.0 10.9 %all-to-all-done.9 = bf16[4,512,128]{1,2,0:T(8,128)(2,1)S(1)} async-done(((bf16[4,512,128]{1,2,0:T(8,128)(2,1)}), bf16[4,512,128]{1,2,0:T(8,128)(2,1)S(1)}, u32[]{:S(2)}, u32[]{:S(2)}) %all-to-all-start.9) | async-done | bytes 524320 | tf_op jit(solution)/shard_map/all_to_all | solution.py:392
  505.3 78.7 %while.59 = (s32[]{:T(128)}, f32[2048,2,64]{0,2,1:T(8,128)S(1)}, f32[2048,2,64]{0,2,1:T(8,128)}, bf16[4,512,128]{1,2,0:T(8,128)(2,1)}, bf16[4,512,2,64]{1,3,2,0:...) while((s32[]{:T(128)}, f32[2048,2,64]{0,2,1:T(8,128)S(1)}, ...), condition=%wide.region_34.35_spmd.clone, body=%wide.region_32.34_spmd.clone.sunk | while | flops 1377959424 | bytes 82229544 | solution.py:144
  629.3 9.6 all-to-all-done.13
  661.4 37.3 %all-reduce.27 = (f32[]{:T(128)}, f32[]{:T(128)}) all-reduce(f32[]{:T(128)} %get-tuple-element.565, f32[]{:T(128)} %get-tuple-element.709), channel_id=1, replica_groups=mesh['fsdp'=8,'seq'=4] {'fsdp','seq'}, use_global_device_ids=true, to_apply=%region_20.21 | all-reduce | flops 2 | bytes 16 | tf_op jit(solution)/shard_map/psum | solution.py:323
  714.3 25.2 %reduce-scatter.35.cloned.1.call-done = bf16[64,512]{1,0:T(8,128)(2,1)} async-done(((bf16[512,512]{1,0:T(8,128)(2,1)}), bf16[64,512]{1,0:T(8,128)(2,1)}) %reduce-scatter.35.cloned.1.call-update) | async-done | bytes 65552
  741.0 36.0 %reduce-scatter.25.cloned.1.call-done = bf16[64,512]{1,0:T(8,128)(2,1)} async-done(((bf16[512,512]{1,0:T(8,128)(2,1)}), bf16[64,512]{1,0:T(8,128)(2,1)}) %reduce-scatter.25.cloned.1.call-update) | async-done | bytes 65552 | tf_op jit(solution)/shard_map/reduce_scatter | solution.py:528
  777.0 37.2 %reduce-scatter.21.cloned.1.call-done = bf16[64,512]{1,0:T(8,128)(2,1)} async-done(((bf16[512,512]{1,0:T(8,128)(2,1)}), bf16[64,512]{1,0:T(8,128)(2,1)}) %reduce-scatter.21.cloned.1.call-update) | async-done | bytes 65552 | tf_op jit(solution)/shard_map/reduce_scatter | solution.py:501
  814.2 38.0 %reduce-scatter.23.cloned.1.call-done = bf16[64,512]{1,0:T(8,128)(2,1)} async-done(((bf16[512,512]{1,0:T(8,128)(2,1)}), bf16[64,512]{1,0:T(8,128)(2,1)}) %reduce-scatter.23.cloned.1.call-update) | async-done | bytes 65552 | tf_op jit(solution)/shard_map/reduce_scatter | solution.py:513
  852.2 44.5 %reduce-scatter.29.cloned.1.call-done = bf16[256,512]{1,0:T(8,128)(2,1)} async-done(((bf16[2048,512]{1,0:T(8,128)(2,1)}), bf16[256,512]{1,0:T(8,128)(2,1)}) %reduce-scatter.29.cloned.1.call-update) | async-done | bytes 262160 | tf_op jit(solution)/shard_map/reduce_scatter | solution.py:546
  896.7 44.7 %reduce-scatter.27.cloned.1.call-done = bf16[64,2048]{1,0:T(8,128)(2,1)} async-done(((bf16[512,2048]{1,0:T(8,128)(2,1)}), bf16[64,2048]{1,0:T(8,128)(2,1)}) %reduce-scatter.27.cloned.1.call-update) | async-done | bytes 262160 | tf_op jit(solution)/shard_map/reduce_scatter | solution.py:540
  948.7 24.3 %all-reduce.28 = (bf16[512]{0:T(512)(128)(2,1)S(1)}, bf16[512]{0:T(512)(128)(2,1)S(1)}, bf16[512]{0:T(512)(128)(2,1)S(1)}, bf16[512]{0:T(512)(128)(2,1)S(1)}, bf...) all-reduce(bf16[512]{0:T(512)(128)(2,1)S(1)} %bitcast.343, ...), channel_id=3, replica_groups=mesh['fsdp'=8,'seq'=4] {'fsdp'}, use_global_device_ids=true, to_apply=%region_39.40.clone | all-reduce | flops 8704 | bytes 34816
  974.1 12.1 %all-reduce.30 = (bf16[64]{0:T(256)(128)(2,1)S(1)}, bf16[64]{0:T(256)(128)(2,1)S(1)}, bf16[64]{0:T(256)(128)(2,1)S(1)}, bf16[64]{0:T(256)(128)(2,1)S(1)}, bf16[6...) all-reduce(bf16[64]{0:T(256)(128)(2,1)S(1)} %dynamic-slice.14, ...), channel_id=1, replica_groups=mesh['fsdp'=8,'seq'=4] {'seq'}, use_global_device_ids=true, to_apply=%region_38.39 | all-reduce | flops 1088 | bytes 4352 | tf_op jit(solution)/shard_map/psum | solution.py:461
  993.4 19.1 %all-reduce.34.cloned.1.call-done = (bf16[64,512]{0,1:T(8,128)(2,1)}, bf16[64,512]{0,1:T(8,128)(2,1)}, bf16[64,512]{0,1:T(8,128)(2,1)}, bf16[64,512]{0,1:T(8,128...) async-done(((bf16[64,512]{0,1:T(8,128)(2,1)}, ...) | async-done | bytes 1048592 | tf_op jit(solution)/shard_map/psum | solution.py:460
  (593 shorter events, 539.7 us)
Async XLA Ops:
  58.6 19.9 %all-to-all-start.2 = ((bf16[512,4,128]{0,2,1:T(8,128)(2,1)}), bf16[512,4,128]{0,2,1:T(8,128)(2,1)S(1)}, u32[]{:S(2)}, u32[]{:S(2)}) async-start(bf16[512,4,128]{0,2,1:T(8,128)(2,1)} %bitcast.10), calls=%async_computation.2 | async-start | bytes 1048576 | tf_op jit(solution)/shard_map/all_to_all | solution.py:278
  96.3 18.5 %all-to-all-start = ((bf16[512,4,128]{0,2,1:T(8,128)(2,1)}), bf16[512,4,128]{0,2,1:T(8,128)(2,1)S(1)}, u32[]{:S(2)}, u32[]{:S(2)}) async-start(bf16[512,4,128]{0,2,1:T(8,128)(2,1)} %bitcast.5), calls=%async_computation | async-start | bytes 1048576 | tf_op jit(solution)/shard_map/all_to_all | solution.py:276
  99.7 231.5 %all-gather.4.cloned.1.call-start = ((), (), s32[]{:S(2)}) async-start(), calls=%async_computation.26 | async-start | bytes 2359296 | tf_op jit(solution)/shard_map/all_gather | solution.py:244
  179.9 38.1 %all-to-all-start.6 = ((bf16[512,4,128]{0,2,1:T(8,128)(2,1)}), bf16[512,4,128]{0,2,1:T(8,128)(2,1)}, u32[]{:S(2)}, u32[]{:S(2)}) async-start(bf16[512,4,128]{0,2,1:T(8,128)(2,1)} %bitcast.338), calls=%async_computation.6 | async-start | bytes 1048576 | tf_op jit(solution)/shard_map/all_to_all | solution.py:301
  218.0 20.0 %all-to-all-start.5 = ((bf16[512,4,128]{0,2,1:T(8,128)(2,1)}), bf16[512,4,128]{0,2,1:T(8,128)(2,1)S(1)}, u32[]{:S(2)}, u32[]{:S(2)}) async-start(bf16[512,4,128]{0,2,1:T(8,128)(2,1)} %bitcast.333), calls=%async_computation.5 | async-start | bytes 1048576 | tf_op jit(solution)/shard_map/all_to_all | solution.py:300
  242.3 95.5 %all-gather.6.cloned.1.call-start = ((), (), s32[]{:S(2)}) async-start(), calls=%async_computation.27 | async-start | bytes 2359296 | tf_op jit(solution)/shard_map/all_gather | solution.py:246
  302.0 26.2 %all-to-all-start.7 = ((bf16[4,512,128]{1,2,0:T(8,128)(2,1)}), bf16[4,512,128]{1,2,0:T(8,128)(2,1)}, u32[]{:S(2)}, u32[]{:S(2)}) async-start(bf16[4,512,128]{1,2,0:T(8,128)(2,1)} %get-tuple-element.263), calls=%async_computation.7 | async-start | bytes 1048576 | tf_op jit(solution)/shard_map/all_to_all | solution.py:156
  353.9 20.3 %all-to-all-start.8 = ((bf16[512,4,128]{0,2,1:T(8,128)(2,1)}), bf16[512,4,128]{0,2,1:T(8,128)(2,1)}, u32[]{:S(2)}, u32[]{:S(2)}) async-start(bf16[512,4,128]{0,2,1:T(8,128)(2,1)} %bitcast.26), calls=%async_computation.8 | async-start | bytes 1048576 | tf_op jit(solution)/shard_map/all_to_all | solution.py:160
  463.9 18.2 %all-to-all-start.14 = ((bf16[4,512,128]{1,2,0:T(8,128)(2,1)}), bf16[4,512,128]{1,2,0:T(8,128)(2,1)}, u32[]{:S(2)}, u32[]{:S(2)}) async-start(bf16[4,512,128]{1,2,0:T(8,128)(2,1)} %copy.185), calls=%async_computation.14 | async-start | bytes 1048576 | tf_op jit(solution)/shard_map/all_to_all | solution.py:393
  482.1 18.2 %all-to-all-start.10 = ((bf16[512,4,128]{0,2,1:T(8,128)(2,1)}), bf16[512,4,128]{0,2,1:T(8,128)(2,1)}, u32[]{:S(2)}, u32[]{:S(2)}) async-start(bf16[512,4,128]{0,2,1:T(8,128)(2,1)} %bitcast.32), calls=%async_computation.10 | async-start | bytes 1048576 | tf_op jit(solution)/shard_map/all_to_all | solution.py:160
  486.3 221.6 %reduce-scatter.37.cloned.1.call-start = ((), (), s32[]{:S(2)}) async-start(), calls=%async_computation.36 | async-start | bytes 589824
  500.3 83.7 %all-to-all-start.15 = ((bf16[4,512,128]{1,2,0:T(8,128)(2,1)}), bf16[4,512,128]{1,2,0:T(8,128)(2,1)}, u32[]{:S(2)}, u32[]{:S(2)}) async-start(bf16[4,512,128]{1,2,0:T(8,128)(2,1)} %copy.186), calls=%async_computation.15 | async-start | bytes 1048576 | tf_op jit(solution)/shard_map/all_to_all | solution.py:394
  584.0 18.6 %all-to-all-start.11 = ((bf16[4,512,128]{1,2,0:T(8,128)(2,1)}), bf16[4,512,128]{1,2,0:T(8,128)(2,1)S(1)}, u32[]{:S(2)}, u32[]{:S(2)}) async-start(bf16[4,512,128]{1,2,0:T(8,128)(2,1)} %get-tuple-element.267), calls=%async_computation.11 | async-start | bytes 1048576 | tf_op jit(solution)/shard_map/all_to_all | solution.py:418
  589.2 120.3 %reduce-scatter.39.cloned.1.call-start = ((), (), s32[]{:S(2)}) async-start(), calls=%async_computation.37 | async-start | bytes 589824
  606.8 104.3 %reduce-scatter.31.cloned.1.call-start = ((), (), s32[]{:S(2)}) async-start(), calls=%async_computation.33 | async-start | bytes 589824
  620.7 18.2 %all-to-all-start.13 = ((bf16[4,512,128]{1,2,0:T(8,128)(2,1)}), bf16[4,512,128]{1,2,0:T(8,128)(2,1)}, u32[]{:S(2)}, u32[]{:S(2)}) async-start(bf16[4,512,128]{1,2,0:T(8,128)(2,1)} %copy.183), calls=%async_computation.13 | async-start | bytes 1048576 | tf_op jit(solution)/shard_map/all_to_all | solution.py:420
  624.9 87.8 %reduce-scatter.33.cloned.1.call-start = ((), (), s32[]{:S(2)}) async-start(), calls=%async_computation.34 | async-start | bytes 589824
  629.3 110.1 %reduce-scatter.35.cloned.1.call-start = ((), (), s32[]{:S(2)}) async-start(), calls=%async_computation.35 | async-start | bytes 589824
  643.3 133.7 %reduce-scatter.25.cloned.1.call-start = ((), (), s32[]{:S(2)}) async-start(), calls=%async_computation.30 | async-start | bytes 589824 | tf_op jit(solution)/shard_map/reduce_scatter | solution.py:528
  646.1 168.1 %reduce-scatter.21.cloned.1.call-start = ((), (), s32[]{:S(2)}) async-start(), calls=%async_computation.28 | async-start | bytes 589824 | tf_op jit(solution)/shard_map/reduce_scatter | solution.py:501
  648.5 203.7 %reduce-scatter.23.cloned.1.call-start = ((), (), s32[]{:S(2)}) async-start(), calls=%async_computation.29 | async-start | bytes 589824 | tf_op jit(solution)/shard_map/reduce_scatter | solution.py:513
  650.9 245.8 %reduce-scatter.29.cloned.1.call-start = ((), (), s32[]{:S(2)}) async-start(), calls=%async_computation.32 | async-start | bytes 2359296 | tf_op jit(solution)/shard_map/reduce_scatter | solution.py:546
  655.5 285.9 %reduce-scatter.27.cloned.1.call-start = ((), (), s32[]{:S(2)}) async-start(), calls=%async_computation.31 | async-start | bytes 2359296 | tf_op jit(solution)/shard_map/reduce_scatter | solution.py:540
  659.9 352.5 %all-reduce.34.cloned.1.call-start = ((), (), s32[]{:S(2)}) async-start(), calls=%async_computation.38 | async-start | bytes 2752512 | tf_op jit(solution)/shard_map/psum | solution.py:460
  (93 other events, 4912.7 us)
Sparse Core Ops, SparseCore 0:
  102.5 28.3 all-gather.3
  245.0 28.3 all-gather.5
  497.4 34.5 reduce-scatter.36
  593.1 34.6 reduce-scatter.38
  630.7 34.1 reduce-scatter.30
  668.0 34.1 reduce-scatter.32
  705.3 34.0 reduce-scatter.34
  742.8 34.1 reduce-scatter.24
  780.1 34.0 reduce-scatter.20
  818.0 34.1 reduce-scatter.22
  855.5 41.1 reduce-scatter.28
  900.2 41.2 reduce-scatter.26
  945.8 66.6 all-reduce.33
where the time goes:
time: 1050 us; the launch traced here: 1040 us
  waiting for transfers between devices  347 us (33%)
  matrix products  197 us (19%)
  blocking collectives  186 us (18%)
  local copies, waits for them, and re-layouts  95.4 us (9%)
  other arithmetic  91.2 us (9%)
  starting transfers between devices  67.9 us (6%)
  loops' own time  32.1 us (3%)
  between operations  20 us (2%)
    unnamed x205, local copies, waits for them, and re-layouts  52.3 us
    unnamed x2, blocking collectives  50.4 us
    reduce_scatter x1, waiting for transfers between devices, shards(): lax.psum_scatter(summed[18].astype(jnp.bfloat16), 'fsdp', scatter_dimensi...  44.7 us
    reduce_scatter x1, waiting for transfers between devices, shards(): lax.psum_scatter(summed[20].astype(jnp.bfloat16), 'fsdp', scatter_dimensi...  44.5 us
    reduce_scatter x1, waiting for transfers between devices, shards(): lax.psum_scatter(summed[9].astype(jnp.bfloat16), 'fsdp', scatter_dimensio...  38 us
    psum x1, blocking collectives, shards(): lax.psum((jnp.sum(live_rows * difference * difference), jnp.sum(live_rows...  37.3 us
    reduce_scatter x1, waiting for transfers between devices, shards(): lax.psum_scatter(summed[5].astype(jnp.bfloat16), 'fsdp', scatter_dimensio...  37.2 us
    reduce_scatter x1, waiting for transfers between devices, shards(): lax.psum_scatter(summed[14].astype(jnp.bfloat16), 'fsdp', scatter_dimensi...  36 us
  transfers between devices with their start and end apart: 29, of which 20 were waited for; matrix products, arithmetic and copies ran while one was open for 26% of the time, Pallas kernels for 0%

commit v1 on v0

v1 whole, which is shorter than its diff:
```python
import jax
import jax.numpy as jnp
from jax import lax
from jax.experimental import pallas as pl
from jax.experimental.pallas import tpu as pltpu
from jax.sharding import PartitionSpec as P

D = 512
HDIM = 64
HEADS = D // HDIM
DOCS = 4
MEM = 512
FFB = 4
TILE = 256
VROWS = 32
NEG = -1e30
BF = jnp.bfloat16
F32 = jnp.float32
VMEM_BYTES = 60 * 1024 * 1024

(
    V_SQB,
    V_SVB,
    V_SOB,
    V_G1,
    V_S1,
    V_CQB,
    V_CVB,
    V_COB,
    V_G2,
    V_S2,
    V_CB,
    V_G3,
    V_S3,
    V_EB,
) = range(14)


def mm(a, b):
    return jnp.dot(a, b, preferred_element_type=F32)


def mm_nt(a, b):
    return lax.dot_general(a, b, (((1,), (1,)), ((), ())), preferred_element_type=F32)


def mm_tn(a, b):
    return lax.dot_general(a, b, (((0,), (0,)), ((), ())), preferred_element_type=F32)


def col_sum(v):
    return jnp.sum(v.astype(F32), axis=0, keepdims=True)


def chip_steps(count):
    bits = []
    bit = 2
    while bit < count:
        bits.append(bit)
        bit *= 2
    return bits, bits[::-1]


def gather_masks(count):
    result = []
    for steps in chip_steps(count):
        masks = [0]
        for step in steps:
            masks = masks + [m ^ step for m in masks]
        result.append(masks)
    own0, own1 = result
    return [own0 + [m ^ 1 for m in own1], own1 + [m ^ 1 for m in own0]]


def reduce_masks(count):
    result = []
    for steps in chip_steps(count):
        masks = [0]
        for step in steps[::-1]:
            masks = masks + [m ^ step for m in masks]
        result.append(masks)
    return result


def step_pairs(count, index):
    orders = chip_steps(count)
    return [(i, i ^ orders[i & 1][index]) for i in range(count)]


def fsdp_gather(own, count):
    have = [own]
    for index in range(len(chip_steps(count)[0])):
        pairs = step_pairs(count, index)
        have = have + [lax.ppermute(a, "fsdp", pairs) for a in have]
    swap = [(i, i ^ 1) for i in range(count)]
    return have + [lax.ppermute(a, "fsdp", swap) for a in have]


def add_low(a, b):
    return (a.astype(F32) + b.astype(F32)).astype(BF)


def fsdp_reduce(send, own, count):
    swap = [(i, i ^ 1) for i in range(count)]
    got = lax.ppermute(send, "fsdp", swap)
    half = own.shape[0]
    for index in range(len(chip_steps(count)[0])):
        half = half // 2
        upper = add_low(own[half:], got[half:])
        lower = add_low(own[:half], got[:half])
        own, got = lower, lax.ppermute(upper, "fsdp", step_pairs(count, index))
    return add_low(own[0], got[0])


def seq_sum(part, count):
    z = lax.axis_index("seq")
    odd = (z % 2) == 1
    half = part.shape[0] // 2
    low, high = part[:half], part[half:]
    pairs = [(i, i ^ 1) for i in range(count)]
    got = lax.ppermute(jnp.where(odd, low, high), "seq", pairs)
    mine = add_low(jnp.where(odd, high, low), got)
    bit = 2
    while bit < count:
        mine = add_low(mine, lax.ppermute(mine, "seq", [(i, i ^ bit) for i in range(count)]))
        bit *= 2
    other = lax.ppermute(mine, "seq", pairs)
    return jnp.where(odd, jnp.concatenate([other, mine]), jnp.concatenate([mine, other]))


def seq_up(a, count):
    return lax.ppermute(a, "seq", [(i, i + 1) for i in range(count - 1)])


def seq_down(a, count):
    return lax.ppermute(a, "seq", [(i + 1, i) for i in range(count - 1)])


def slot_place(index, masks, slot):
    return jnp.where(index % 2 == 0, index ^ masks[0][slot], index ^ masks[1][slot])


class Shard:
    def __init__(self, rows, mem_rows, count, split, piece, wide_piece):
        self.rows = rows
        self.mem_rows = mem_rows
        self.count = count
        self.split = split
        self.piece = piece
        self.wide_piece = wide_piece
        self.group_rows = rows * split
        self.group_mem = mem_rows * split
        self.halo = min(-(-(self.group_rows // 2 - 1) // rows), split - 1)
        self.window = rows * (self.halo + 1)
        self.q_blocks = rows // TILE
        self.k_blocks = self.window // TILE
        self.m_blocks = self.group_mem // TILE
        self.gather = gather_masks(count)
        self.reduce = reduce_masks(count)


def start_weight(sh, slots, row, n, target, sem):
    index = lax.axis_index("fsdp")
    for s, slot in enumerate(slots):
        place = pl.multiple_of(slot_place(index, sh.gather, s) * n, n)
        pltpu.make_async_copy(slot.at[pl.ds(row, n)], target.at[pl.ds(place, n)], sem).start()


def wait_all(target, sem):
    pltpu.make_async_copy(target, target, sem).wait()


def put_grad(sh, full, n, row, send_ref, own_ref):
    index = lax.axis_index("fsdp")
    partner = index ^ 1
    for s in range(sh.count // 2):
        mine = pl.multiple_of(slot_place(index, sh.reduce, s) * n, n)
        theirs = pl.multiple_of(slot_place(partner, sh.reduce, s) * n, n)
        own_ref[s, pl.ds(row, n), :] = full[pl.ds(mine, n), :]
        send_ref[s, pl.ds(row, n), :] = full[pl.ds(theirs, n), :]


def doc_bounds(lens, order):
    starts, ends = [], []
    total = jnp.int32(0)
    for p in range(DOCS):
        starts.append(total)
        total = total + lens[0, order[0, p]]
        ends.append(total)
    return starts, ends


def pick(starts, ends, pos, values):
    out = jnp.zeros_like(pos)
    for p in range(DOCS):
        out = jnp.where((pos >= starts[p]) & (pos < ends[p]), values[p], out)
    return out


def lane_pos(base):
    return base + lax.broadcasted_iota(jnp.int32, (1, TILE), 1)


def norm_stats(v):
    mean = jnp.mean(v, axis=1, keepdims=True)
    c = v - mean
    inv = lax.rsqrt(jnp.mean(c * c, axis=1, keepdims=True) + 1e-05)
    return c * inv, inv


def norm_back(dy, n, inv, gain):
    e = dy * gain
    return inv * (
        e - jnp.mean(e, axis=1, keepdims=True) - n * jnp.mean(e * n, axis=1, keepdims=True)
    )


def head_rows(h):
    return slice(h * HDIM, (h + 1) * HDIM)


def pair_lanes(h):
    j = h // 2
    return slice(j * 2 * HDIM, (j + 1) * 2 * HDIM)


def spread_rows(source, target):
    for h in range(HEADS):
        o = (h % 2) * HDIM
        target[h, pl.ds(o, HDIM), :] = source[head_rows(h), :]


def spread_zero(target):
    for h in range(HEADS):
        o = (1 - h % 2) * HDIM
        target[h, pl.ds(o, HDIM), :] = jnp.zeros((HDIM, TILE), BF)


def spread_lanes(source, target):
    lane = lax.broadcasted_iota(jnp.int32, (TILE, 2 * HDIM), 1)
    for h in range(HEADS):
        part = source[:, pair_lanes(h)]
        keep = (lane >= HDIM) if h % 2 else (lane < HDIM)
        target[h] = jnp.where(keep, part, jnp.zeros_like(part))


def forward_tile(keys, vals_t, bias, q_t, m_ref, l_ref, acc_ref):
    for h in range(HEADS):
        s = mm(keys[:, pair_lanes(h)], q_t[h]) + bias[...]
        m_old = m_ref[h : h + 1, :]
        m_new = jnp.maximum(m_old, jnp.max(s, axis=0, keepdims=True))
        p = jnp.exp(s - m_new)
        alpha = jnp.exp(m_old - m_new)
        m_ref[h : h + 1, :] = m_new
        l_ref[h : h + 1, :] = alpha * l_ref[h : h + 1, :] + jnp.sum(p, axis=0, keepdims=True)
        acc_ref[head_rows(h), :] = acc_ref[head_rows(h), :] * alpha + mm(
            vals_t[head_rows(h), :], p.astype(BF)
        )


def forward_start(m_ref, l_ref, acc_ref):
    m_ref[...] = jnp.full(m_ref.shape, NEG, F32)
    l_ref[...] = jnp.zeros(l_ref.shape, F32)
    acc_ref[...] = jnp.zeros(acc_ref.shape, F32)


def forward_end(b, m_ref, l_ref, acc_ref, ctx_ref, ctx_t_ref, lse_ref):
    lse_ref[b] = m_ref[...] + jnp.log(l_ref[...])
    for h in range(HEADS):
        acc_ref[head_rows(h), :] = acc_ref[head_rows(h), :] / l_ref[h : h + 1, :]
    ctx_t_ref[b] = acc_ref[...]
    ctx_ref[pl.ds(pl.multiple_of(b * TILE, TILE), TILE), :] = acc_ref[...].T.astype(BF)


def backward_tile(keys, vals, keys_t, bias, q_t, g_t, q_m, g_m, lse, delta, dk, dv, dq_t):
    for h in range(0, HEADS, 2):
        dk_sum = dk[:, pair_lanes(h)]
        dv_sum = dv[:, pair_lanes(h)]
        for i in (h, h + 1):
            s = mm(keys[:, pair_lanes(i)], q_t[i]) + bias[...]
            p = jnp.exp(s - lse[i : i + 1, :])
            dp = mm(vals[:, pair_lanes(i)], g_t[i])
            ds = (p * (dp - delta[i : i + 1, :])).astype(BF)
            dv_sum = dv_sum + mm(p.astype(BF), g_m[i])
            dk_sum = dk_sum + mm(ds, q_m[i])
            dq_t[head_rows(i), :] = dq_t[head_rows(i), :] + mm(keys_t[head_rows(i), :], ds)
        dk[:, pair_lanes(h)] = dk_sum
        dv[:, pair_lanes(h)] = dv_sum


def backward_start(b, q_t3, g_t3, q, g, ctx_t3, q_t, g_t, q_m, g_m, delta, dq_t):
    rows = pl.ds(pl.multiple_of(b * TILE, TILE), TILE)
    spread_rows(q_t3.at[b], q_t)
    spread_rows(g_t3.at[b], g_t)
    spread_lanes(q[rows, :], q_m)
    spread_lanes(g[rows, :], g_m)
    prod = g_t3[b].astype(F32) * ctx_t3[b]
    for h in range(HEADS):
        delta[h : h + 1, :] = jnp.sum(prod[head_rows(h), :], axis=0, keepdims=True)
    dq_t[...] = jnp.zeros(dq_t.shape, F32)


def self_tiles(sh, lens, order, b, bias, body):
    z = lax.axis_index("seq")
    starts, ends = doc_bounds(lens, order)
    shift = (z - sh.halo) * sh.rows
    q_base = sh.halo * sh.rows + b * TILE
    first = pick(starts, ends, q_base + shift, starts) - shift
    q_pos = lane_pos(q_base)
    q_start = pick(starts, ends, q_pos + shift, starts) - shift
    last = q_base // TILE
    number = last - first // TILE + 1

    def step(i, carry):
        t = last - i
        k_pos = t * TILE + lax.broadcasted_iota(jnp.int32, (TILE, TILE), 0)
        bias[...] = jnp.where((k_pos >= q_start) & (k_pos <= q_pos), 0.0, NEG)
        body(t)
        return carry

    lax.fori_loop(0, number, step, 0)


def self_forward_kernel(sh, lens, order, *refs):
    halo, count, rows, n = sh.halo, sh.count, sh.rows, sh.piece
    toks = refs[: halo + 1]
    slots = refs[halo + 1 : halo + 1 + count]
    (q_ref, q_t3, k3, v3, k_t3, ctx, ctx_t3, lse, vec) = refs[halo + 1 + count : halo + 10 + count]
    (wq, wk, wv, vec_slots, v_t3, q_t, bias, m_ref, l_ref, acc, sems) = refs[halo + 10 + count :]
    z = lax.axis_index("seq")
    for s, slot in enumerate(slots):
        pltpu.make_async_copy(slot.at[pl.ds(3 * n, VROWS)], vec_slots.at[s], sems.at[3]).start()
    for i, w in enumerate((wq, wk, wv)):
        start_weight(sh, slots, i * n, n, w, sems.at[i])
    spread_zero(q_t)
    wait_all(vec_slots, sems.at[3])
    vec[...] = jnp.sum(vec_slots[...].astype(F32), axis=0)
    wait_all(wq, sems.at[0])
    wait_all(wk, sems.at[1])
    wait_all(wv, sems.at[2])
    tiles = rows // TILE

    def own_rows(i, carry):
        r = pl.ds(pl.multiple_of(i * TILE, TILE), TILE)
        q = (mm(toks[0][r, :], wq[...]) + vec[V_SQB : V_SQB + 1, :]).astype(BF)
        q = q * BF(HDIM**-0.5)
        q_ref[r, :] = q
        q_t3[i] = q.T
        return carry

    lax.fori_loop(0, tiles, own_rows, 0)
    for k in range(halo + 1):

        def window_rows(i, carry, k=k):
            r = pl.ds(pl.multiple_of(i * TILE, TILE), TILE)
            t = (halo - k) * tiles + i
            x = toks[k][r, :]
            key = mm(x, wk[...]).astype(BF)
            val = (mm(x, wv[...]) + vec[V_SVB : V_SVB + 1, :]).astype(BF)
            k3[t] = key
            v3[t] = val
            k_t3[t] = key.T
            v_t3[t] = val.T
            return carry

        @pl.when(z >= k)
        def _(window_rows=window_rows):
            lax.fori_loop(0, tiles, window_rows, 0)

    def block(b, carry):
        spread_rows(q_t3.at[b], q_t)
        forward_start(m_ref, l_ref, acc)
        self_tiles(
            sh,
            lens,
            order,
            b,
            bias,
            lambda t: forward_tile(k3.at[t], v_t3.at[t], bias, q_t, m_ref, l_ref, acc),
        )
        forward_end(b, m_ref, l_ref, acc, ctx, ctx_t3, lse)
        return carry

    lax.fori_loop(0, sh.q_blocks, block, 0)


SMEM_SPEC = pl.BlockSpec(memory_space=pltpu.SMEM)
VMEM_SPEC = pl.BlockSpec(memory_space=pltpu.VMEM)
ANY_SPEC = pl.BlockSpec(memory_space=pl.ANY)


def shape(dims, dtype):
    return jax.ShapeDtypeStruct(dims, dtype)


def call(body, name, inputs, specs, outs, scratch):
    return pl.pallas_call(
        body,
        name=name,
        in_specs=specs,
        out_specs=[VMEM_SPEC] * len(outs),
        out_shape=outs,
        scratch_shapes=scratch,
        compiler_params=pltpu.CompilerParams(vmem_limit_bytes=VMEM_BYTES),
    )(*inputs)


def self_forward(sh, lens, order, toks, slots):
    nb, nq = sh.k_blocks, sh.q_blocks
    outs = [
        shape((sh.rows, D), BF),
        shape((nq, D, TILE), BF),
        shape((nb, TILE, D), BF),
        shape((nb, TILE, D), BF),
        shape((nb, D, TILE), BF),
        shape((sh.rows, D), BF),
        shape((nq, D, TILE), F32),
        shape((nq, HEADS, TILE), F32),
        shape((VROWS, D), F32),
    ]
    scratch = [
        pltpu.VMEM((D, D), BF),
        pltpu.VMEM((D, D), BF),
        pltpu.VMEM((D, D), BF),
        pltpu.VMEM((sh.count, VROWS, D), BF),
        pltpu.VMEM((nb, D, TILE), BF),
        pltpu.VMEM((HEADS, 2 * HDIM, TILE), BF),
        pltpu.VMEM((TILE, TILE), F32),
        pltpu.VMEM((HEADS, TILE), F32),
        pltpu.VMEM((HEADS, TILE), F32),
        pltpu.VMEM((D, TILE), F32),
        pltpu.SemaphoreType.DMA((4,)),
    ]
    specs = [SMEM_SPEC] * 2 + [VMEM_SPEC] * len(toks) + [ANY_SPEC] * len(slots)
    return call(
        lambda *refs: self_forward_kernel(sh, *refs),
        "self_forward",
        (lens, order, *toks, *slots),
        specs,
        outs,
        scratch,
    )


def cross_tiles(sh, lens, order, mlens, b, bias, bounds, skip_pad, body):
    z = lax.axis_index("seq")
    starts, ends = doc_bounds(lens, order)
    for p in range(DOCS):
        bounds[0, p] = starts[p]
        bounds[1, p] = ends[p]
    base = z * sh.rows + b * TILE
    slots = [order[0, p] for p in range(DOCS)]
    pos = lane_pos(base)
    low = pick(starts, ends, pos, [s * MEM for s in slots])
    high = pick(starts, ends, pos, [s * MEM + mlens[0, s] for s in slots])

    def doc(p, carry):
        slot = order[0, p]
        seen = (bounds[0, p] < base + TILE) & (bounds[1, p] > base)
        if skip_pad:
            seen = seen & (slot != DOCS - 1)
        number = jnp.where(seen, (mlens[0, slot] + TILE - 1) // TILE, 0)

        def step(i, inner):
            t = slot * (MEM // TILE) + i
            k_pos = t * TILE + lax.broadcasted_iota(jnp.int32, (TILE, TILE), 0)
            bias[...] = jnp.where((k_pos >= low) & (k_pos < high), 0.0, NEG)
            body(t)
            return inner

        return lax.fori_loop(0, number, step, carry)

    lax.fori_loop(0, DOCS, doc, 0)


def touched_tile(sh, lens, order, mlens, t, bounds, skip_pad):
    z = lax.axis_index("seq")
    slot = t // (MEM // TILE)
    base = z * sh.rows
    seen = (bounds[2, slot] < base + sh.rows) & (bounds[3, slot] > base)
    seen = seen & (t % (MEM // TILE) * TILE < mlens[0, slot])
    if skip_pad:
        seen = seen & (slot != DOCS - 1)
    return seen


def slot_bounds(lens, order, bounds):
    starts, ends = doc_bounds(lens, order)
    for p in range(DOCS):
        bounds[2, order[0, p]] = starts[p]
        bounds[3, order[0, p]] = ends[p]


def cross_forward_kernel(sh, lens, order, mlens, *refs):
    count, rows, n, split = sh.count, sh.rows, sh.piece, sh.split
    tok, ctx, vec = refs[:3]
    mems = refs[3 : 3 + 2 * split - 1]
    slots = refs[2 + 2 * split : 2 + 2 * split + count]
    outs = refs[2 + 2 * split + count :]
    (n1, inv1, first_low, q_ref, q_t3, mk3, mv3, mk_t3, cctx, cctx_t3, lse, mem) = outs[:12]
    (wo, wcq, wck, wcv, mv_t3, q_t, bias, m_ref, l_ref, acc, bounds, sems) = outs[12:]
    z = lax.axis_index("seq")
    for i, w in enumerate((wo, wcq, wck, wcv)):
        start_weight(sh, slots, i * n, n, w, sems.at[i])
    own = mems[0]
    tiles_per = sh.mem_rows // TILE

    def place(source, shard):
        for i in range(tiles_per):
            pltpu.make_async_copy(
                source.at[pl.ds(i * TILE, TILE)], mem.at[shard * tiles_per + i], sems.at[4]
            ).start()

    place(own, z)
    for k in range(1, split):
        up, down = mems[2 * k - 1], mems[2 * k]

        @pl.when(z >= k)
        def _(up=up, k=k):
            place(up, z - k)

        @pl.when(z + k < split)
        def _(down=down, k=k):
            place(down, z + k)

    slot_bounds(lens, order, bounds)
    spread_zero(q_t)
    wait_all(wo, sems.at[0])
    wait_all(wcq, sems.at[1])

    def own_rows(i, carry):
        r = pl.ds(pl.multiple_of(i * TILE, TILE), TILE)
        v = tok[r, :].astype(F32) + (mm(ctx[r, :], wo[...]) + vec[V_SOB : V_SOB + 1, :])
        normal, inv = norm_stats(v)
        n1[r, :] = normal
        inv1[r, :] = inv
        low = (normal * vec[V_G1 : V_G1 + 1, :] + vec[V_S1 : V_S1 + 1, :]).astype(BF)
        first_low[r, :] = low
        q = (mm(low, wcq[...]) + vec[V_CQB : V_CQB + 1, :]).astype(BF)
        q = q * BF(HDIM**-0.5)
        q_ref[r, :] = q
        q_t3[i] = q.T
        return carry

    lax.fori_loop(0, rows // TILE, own_rows, 0)
    wait_all(wck, sems.at[2])
    wait_all(wcv, sems.at[3])
    wait_all(mem, sems.at[4])

    def mem_tile(t, carry):
        @pl.when(touched_tile(sh, lens, order, mlens, t, bounds, False))
        def _():
            x = mem[t]
            key = mm(x, wck[...]).astype(BF)
            val = (mm(x, wcv[...]) + vec[V_CVB : V_CVB + 1, :]).astype(BF)
            mk3[t] = key
            mv3[t] = val
            mk_t3[t] = key.T
            mv_t3[t] = val.T

        return carry

    lax.fori_loop(0, sh.m_blocks, mem_tile, 0)

    def block(b, carry):
        spread_rows(q_t3.at[b], q_t)
        forward_start(m_ref, l_ref, acc)
        cross_tiles(
            sh,
            lens,
            order,
            mlens,
            b,
            bias,
            bounds,
            False,
            lambda t: forward_tile(mk3.at[t], mv_t3.at[t], bias, q_t, m_ref, l_ref, acc),
        )
        forward_end(b, m_ref, l_ref, acc, cctx, cctx_t3, lse)
        return carry

    lax.fori_loop(0, sh.q_blocks, block, 0)


def cross_forward(sh, lens, order, mlens, tok, ctx, vec, mems, slots):
    nm, nq = sh.m_blocks, sh.q_blocks
    outs = [
        shape((sh.rows, D), F32),
        shape((sh.rows, 1), F32),
        shape((sh.rows, D), BF),
        shape((sh.rows, D), BF),
        shape((nq, D, TILE), BF),
        shape((nm, TILE, D), BF),
        shape((nm, TILE, D), BF),
        shape((nm, D, TILE), BF),
        shape((sh.rows, D), BF),
        shape((nq, D, TILE), F32),
        shape((nq, HEADS, TILE), F32),
        shape((nm, TILE, D), BF),
    ]
    scratch = [
        pltpu.VMEM((D, D), BF),
        pltpu.VMEM((D, D), BF),
        pltpu.VMEM((D, D), BF),
        pltpu.VMEM((D, D), BF),
        pltpu.VMEM((nm, D, TILE), BF),
        pltpu.VMEM((HEADS, 2 * HDIM, TILE), BF),
        pltpu.VMEM((TILE, TILE), F32),
        pltpu.VMEM((HEADS, TILE), F32),
        pltpu.VMEM((HEADS, TILE), F32),
        pltpu.VMEM((D, TILE), F32),
        pltpu.SMEM((4, DOCS), jnp.int32),
        pltpu.SemaphoreType.DMA((5,)),
    ]
    specs = [SMEM_SPEC] * 3 + [VMEM_SPEC] * 3 + [ANY_SPEC] * (len(mems) + len(slots))
    return call(
        lambda *refs: cross_forward_kernel(sh, *refs),
        "cross_forward",
        (lens, order, mlens, tok, ctx, vec, *mems, *slots),
        specs,
        outs,
        scratch,
    )


def feed_kernel(sh, lens, order, *refs):
    count, rows, n, wide = sh.count, sh.rows, sh.piece, sh.wide_piece
    n1, cctx, targets, vec = refs[:4]
    slots = refs[4 : 4 + count]
    outs = refs[4 + count :]
    (final_ref, g_second, g_cc, g_cc_t3, g_send, g_own, vec_grad, loss) = outs[:8]
    (wco, w1, w2, n2, sec_low, hid, dact, feed_low, g_exp, g_cross, stage, stage2, sems) = outs[8:]
    z = lax.axis_index("seq")
    start_weight(sh, slots, 4 * n, n, wco, sems.at[0])
    for c in range(FFB):
        start_weight(sh, slots, (5 + c) * n, n, w1.at[c], sems.at[1 + c])
    start_weight(sh, slots, 9 * n, wide, w2, sems.at[5])
    vec_grad[...] = jnp.zeros(vec_grad.shape, F32)
    loss[...] = jnp.zeros(loss.shape, F32)
    starts, ends = doc_bounds(lens, order)
    pad_start, pad_end = jnp.int32(0), jnp.int32(0)
    for p in range(DOCS):
        is_pad = order[0, p] == DOCS - 1
        pad_start = jnp.where(is_pad, starts[p], pad_start)
        pad_end = jnp.where(is_pad, ends[p], pad_end)
    wait_all(wco, sems.at[0])
    for c in range(FFB):
        wait_all(w1.at[c], sems.at[1 + c])
    wait_all(w2, sems.at[5])

    def add_vec(row, value):
        vec_grad[row : row + 1, :] = vec_grad[row : row + 1, :] + value

    def chunk(i, carry):
        r = pl.ds(pl.multiple_of(i * TILE, TILE), TILE)
        first = n1[r, :] * vec[V_G1 : V_G1 + 1, :] + vec[V_S1 : V_S1 + 1, :]
        v = first + (mm(cctx[r, :], wco[...]) + vec[V_COB : V_COB + 1, :])
        normal2, inv2 = norm_stats(v)
        n2[...] = normal2
        second = normal2 * vec[V_G2 : V_G2 + 1, :] + vec[V_S2 : V_S2 + 1, :]
        low = second.astype(BF)
        sec_low[r, :] = low
        feed = second + vec[V_CB : V_CB + 1, :]
        for c in range(FFB):
            e = mm(low, w1[c]) + vec[V_EB + c : V_EB + c + 1, :]
            sg = jax.nn.sigmoid(e)
            h = (e * sg).astype(BF)
            hid[c, r, :] = h
            dact[c] = sg * (1.0 + e * (1.0 - sg))
            feed = feed + mm(h, w2[pl.ds(c * D, D), :])
        normal3, inv3 = norm_stats(feed)
        final = normal3 * vec[V_G3 : V_G3 + 1, :] + vec[V_S3 : V_S3 + 1, :]
        final_ref[r, :] = final.astype(BF)
        diff = final - targets[r, :].astype(F32)
        pos = z * rows + i * TILE + lax.broadcasted_iota(jnp.int32, (TILE, 1), 0)
        live = jnp.where((pos >= pad_start) & (pos < pad_end), 0.0, 1.0)
        g = live * diff
        loss[0:1, :] = loss[0:1, :] + col_sum(g * diff)
        add_vec(V_G3, col_sum(g * normal3))
        add_vec(V_S3, col_sum(g))
        g_third = norm_back(g, normal3, inv3, vec[V_G3 : V_G3 + 1, :])
        g_low = g_third.astype(BF)
        feed_low[r, :] = g_low
        add_vec(V_CB, col_sum(g_low))
        total = g_third
        for c in range(FFB):
            ge = (mm_nt(g_low, w2[pl.ds(c * D, D), :]) * dact[c]).astype(BF)
            g_exp[c, r, :] = ge
            add_vec(V_EB + c, col_sum(ge))
            total = total + mm_nt(ge, w1[c])
        normal2 = n2[...]
        add_vec(V_G2, col_sum(total * normal2))
        add_vec(V_S2, col_sum(total))
        gs = norm_back(total, normal2, inv2, vec[V_G2 : V_G2 + 1, :])
        g_second[r, :] = gs
        gc = gs.astype(BF)
        g_cross[r, :] = gc
        add_vec(V_COB, col_sum(gc))
        gcc = mm_nt(gc, wco[...]).astype(BF)
        g_cc[r, :] = gcc
        g_cc_t3[i] = gcc.T
        return carry

    lax.fori_loop(0, rows // TILE, chunk, 0)
    live_count = jnp.int32(rows) - jnp.maximum(
        jnp.minimum(pad_end, (z + 1) * rows) - jnp.maximum(pad_start, z * rows), 0
    )
    loss[1:2, :] = jnp.full((1, D), live_count.astype(F32))
    stage[...] = mm_tn(cctx[...], g_cross[...]).astype(BF)
    put_grad(sh, stage, n, 0, g_send, g_own)
    for c in range(FFB):
        stage[...] = mm_tn(sec_low[...], g_exp[c]).astype(BF)
        put_grad(sh, stage, n, (1 + c) * n, g_send, g_own)
    for c in range(FFB):
        stage2[pl.ds(c * D, D), :] = mm_tn(hid[c], feed_low[...]).astype(BF)
    put_grad(sh, stage2, wide, 5 * n, g_send, g_own)


def feed(sh, lens, order, n1, cctx, targets, vec, slots):
    rows, nq, n = sh.rows, sh.q_blocks, sh.piece
    block = 5 * n + sh.wide_piece
    outs = [
        shape((rows, D), BF),
        shape((rows, D), F32),
        shape((rows, D), BF),
        shape((nq, D, TILE), BF),
        shape((sh.count // 2, block, D), BF),
        shape((sh.count // 2, block, D), BF),
        shape((VROWS, D), F32),
        shape((8, D), F32),
    ]
    scratch = [
        pltpu.VMEM((D, D), BF),
        pltpu.VMEM((FFB, D, D), BF),
        pltpu.VMEM((FFB * D, D), BF),
        pltpu.VMEM((TILE, D), F32),
        pltpu.VMEM((rows, D), BF),
        pltpu.VMEM((FFB, rows, D), BF),
        pltpu.VMEM((FFB, TILE, D), F32),
        pltpu.VMEM((rows, D), BF),
        pltpu.VMEM((FFB, rows, D), BF),
        pltpu.VMEM((rows, D), BF),
        pltpu.VMEM((D, D), BF),
        pltpu.VMEM((FFB * D, D), BF),
        pltpu.SemaphoreType.DMA((6,)),
    ]
    specs = [SMEM_SPEC] * 2 + [VMEM_SPEC] * 4 + [ANY_SPEC] * len(slots)
    return call(
        lambda *refs: feed_kernel(sh, *refs),
        "feed",
        (lens, order, n1, cctx, targets, vec, *slots),
        specs,
        outs,
        scratch,
    )


def cross_backward_kernel(sh, lens, order, mlens, *refs):
    count, rows, n = sh.count, sh.rows, sh.piece
    (q_ref, q_t3, mk3, mv3, mk_t3, cctx_t3, lse, g_cc, g_cc_t3, g_second, n1, inv1) = refs[:12]
    (first_low, mem, ctx, vec, vec_in) = refs[12:17]
    slots = refs[17 : 17 + count]
    outs = refs[17 + count :]
    (g_send, g_own, mem_grad, g_first, g_ctx, g_ctx_t3, vec_grad) = outs[:7]
    (wo, wcq, wck, wcv, q_t, g_t, q_m, g_m, delta, bias, dk, dv, dq_t, dq, g_self) = outs[7:22]
    (acc_k, acc_v, stage, bounds, sems) = outs[22:]
    for i, w in enumerate((wo, wcq, wck, wcv)):
        start_weight(sh, slots, i * n, n, w, sems.at[i])
    vec_grad[...] = vec_in[...]
    slot_bounds(lens, order, bounds)
    spread_zero(q_t)
    spread_zero(g_t)

    def clear(t, carry):
        @pl.when(touched_tile(sh, lens, order, mlens, t, bounds, True))
        def _():
            dk[t] = jnp.zeros((TILE, D), F32)
            dv[t] = jnp.zeros((TILE, D), F32)

        return carry

    lax.fori_loop(0, sh.m_blocks, clear, 0)

    def block(b, carry):
        backward_start(b, q_t3, g_cc_t3, q_ref, g_cc, cctx_t3, q_t, g_t, q_m, g_m, delta, dq_t)
        cross_tiles(
            sh,
            lens,
            order,
            mlens,
            b,
            bias,
            bounds,
            True,
            lambda t: backward_tile(
                mk3.at[t],
                mv3.at[t],
                mk_t3.at[t],
                bias,
                q_t,
                g_t,
                q_m,
                g_m,
                lse.at[b],
                delta,
                dk.at[t],
                dv.at[t],
                dq_t,
            ),
        )
        r = pl.ds(pl.multiple_of(b * TILE, TILE), TILE)
        dq[r, :] = (dq_t[...] * HDIM**-0.5).T.astype(BF)
        return carry

    lax.fori_loop(0, sh.q_blocks, block, 0)
    for i, w in enumerate((wo, wcq, wck, wcv)):
        wait_all(w, sems.at[i])

    def add_vec(row, value):
        vec_grad[row : row + 1, :] = vec_grad[row : row + 1, :] + value

    acc_k[...] = jnp.zeros(acc_k.shape, F32)
    acc_v[...] = jnp.zeros(acc_v.shape, F32)

    def mem_tile(t, carry):
        seen = touched_tile(sh, lens, order, mlens, t, bounds, True)

        @pl.when(seen)
        def _():
            k_low = dk[t].astype(BF)
            v_low = dv[t].astype(BF)
            x = mem[t]
            acc_k[...] = acc_k[...] + mm_tn(x, k_low)
            acc_v[...] = acc_v[...] + mm_tn(x, v_low)
            add_vec(V_CVB, col_sum(v_low))
            mem_grad[t] = (mm_nt(k_low, wck[...]) + mm_nt(v_low, wcv[...])).astype(BF)

        @pl.when(jnp.logical_not(seen))
        def _():
            mem_grad[t] = jnp.zeros((TILE, D), BF)

        return carry

    lax.fori_loop(0, sh.m_blocks, mem_tile, 0)

    def own_rows(i, carry):
        r = pl.ds(pl.multiple_of(i * TILE, TILE), TILE)
        total = g_second[r, :] + mm_nt(dq[r, :], wcq[...])
        normal = n1[r, :]
        add_vec(V_G1, col_sum(total * normal))
        add_vec(V_S1, col_sum(total))
        gf = norm_back(total, normal, inv1[r, :], vec[V_G1 : V_G1 + 1, :])
        g_first[r, :] = gf
        low = gf.astype(BF)
        g_self[r, :] = low
        add_vec(V_SOB, col_sum(low))
        gc = mm_nt(low, wo[...]).astype(BF)
        g_ctx[r, :] = gc
        g_ctx_t3[i] = gc.T
        return carry

    lax.fori_loop(0, rows // TILE, own_rows, 0)
    add_vec(V_CQB, col_sum(dq[...]))
    stage[...] = mm_tn(ctx[...], g_self[...]).astype(BF)
    put_grad(sh, stage, n, 0, g_send, g_own)
    stage[...] = mm_tn(first_low[...], dq[...]).astype(BF)
    put_grad(sh, stage, n, n, g_send, g_own)
    stage[...] = acc_k[...].astype(BF)
    put_grad(sh, stage, n, 2 * n, g_send, g_own)
    stage[...] = acc_v[...].astype(BF)
    put_grad(sh, stage, n, 3 * n, g_send, g_own)


def cross_backward(sh, lens, order, mlens, arrays, slots):
    rows, nq, nm, n = sh.rows, sh.q_blocks, sh.m_blocks, sh.piece
    outs = [
        shape((sh.count // 2, 4 * n, D), BF),
        shape((sh.count // 2, 4 * n, D), BF),
        shape((nm, TILE, D), BF),
        shape((rows, D), F32),
        shape((rows, D), BF),
        shape((nq, D, TILE), BF),
        shape((VROWS, D), F32),
    ]
    scratch = [
        pltpu.VMEM((D, D), BF),
        pltpu.VMEM((D, D), BF),
        pltpu.VMEM((D, D), BF),
        pltpu.VMEM((D, D), BF),
        pltpu.VMEM((HEADS, 2 * HDIM, TILE), BF),
        pltpu.VMEM((HEADS, 2 * HDIM, TILE), BF),
        pltpu.VMEM((HEADS, TILE, 2 * HDIM), BF),
        pltpu.VMEM((HEADS, TILE, 2 * HDIM), BF),
        pltpu.VMEM((HEADS, TILE), F32),
        pltpu.VMEM((TILE, TILE), F32),
        pltpu.VMEM((nm, TILE, D), F32),
        pltpu.VMEM((nm, TILE, D), F32),
        pltpu.VMEM((D, TILE), F32),
        pltpu.VMEM((rows, D), BF),
        pltpu.VMEM((rows, D), BF),
        pltpu.VMEM((D, D), F32),
        pltpu.VMEM((D, D), F32),
        pltpu.VMEM((D, D), BF),
        pltpu.SMEM((4, DOCS), jnp.int32),
        pltpu.SemaphoreType.DMA((4,)),
    ]
    specs = [SMEM_SPEC] * 3 + [VMEM_SPEC] * len(arrays) + [ANY_SPEC] * len(slots)
    return call(
        lambda *refs: cross_backward_kernel(sh, *refs),
        "cross_backward",
        (lens, order, mlens, *arrays, *slots),
        specs,
        outs,
        scratch,
    )


def self_backward_kernel(sh, lens, order, *refs):
    count, rows, n, halo = sh.count, sh.rows, sh.piece, sh.halo
    (q_ref, q_t3, k3, v3, k_t3, ctx_t3, lse, g_ctx, g_ctx_t3, g_first, vec_in) = refs[:11]
    toks = refs[11 : 12 + halo]
    slots = refs[12 + halo : 12 + halo + count]
    outs = refs[12 + halo + count :]
    (g_send, g_own, grad_own, grad_halo) = outs[:4]
    (wq, wk, wv, q_t, g_t, q_m, g_m, delta, bias, dk, dv, dq_t, dq) = outs[4:17]
    (acc_k, acc_v, vec_grad, stage, sems) = outs[17:]
    z = lax.axis_index("seq")
    for i, w in enumerate((wq, wk, wv)):
        start_weight(sh, slots, i * n, n, w, sems.at[i])
    vec_grad[...] = vec_in[...]
    spread_zero(q_t)
    spread_zero(g_t)

    def clear(t, carry):
        dk[t] = jnp.zeros((TILE, D), F32)
        dv[t] = jnp.zeros((TILE, D), F32)
        return carry

    lax.fori_loop(0, sh.k_blocks, clear, 0)

    def block(b, carry):
        backward_start(b, q_t3, g_ctx_t3, q_ref, g_ctx, ctx_t3, q_t, g_t, q_m, g_m, delta, dq_t)
        self_tiles(
            sh,
            lens,
            order,
            b,
            bias,
            lambda t: backward_tile(
                k3.at[t],
                v3.at[t],
                k_t3.at[t],
                bias,
                q_t,
                g_t,
                q_m,
                g_m,
                lse.at[b],
                delta,
                dk.at[t],
                dv.at[t],
                dq_t,
            ),
        )
        r = pl.ds(pl.multiple_of(b * TILE, TILE), TILE)
        dq[r, :] = (dq_t[...] * HDIM**-0.5).T.astype(BF)
        return carry

    lax.fori_loop(0, sh.q_blocks, block, 0)
    for i, w in enumerate((wq, wk, wv)):
        wait_all(w, sems.at[i])

    def add_vec(row, value):
        vec_grad[row : row + 1, :] = vec_grad[row : row + 1, :] + value

    acc_k[...] = jnp.zeros(acc_k.shape, F32)
    acc_v[...] = jnp.zeros(acc_v.shape, F32)
    tiles = rows // TILE
    for k in range(halo, -1, -1):

        def window_rows(i, carry, k=k):
            r = pl.ds(pl.multiple_of(i * TILE, TILE), TILE)
            t = (halo - k) * tiles + i
            k_low = dk[t].astype(BF)
            v_low = dv[t].astype(BF)
            x = toks[k][r, :]
            acc_k[...] = acc_k[...] + mm_tn(x, k_low)
            acc_v[...] = acc_v[...] + mm_tn(x, v_low)
            add_vec(V_SVB, col_sum(v_low))
            part = mm_nt(k_low, wk[...]) + mm_nt(v_low, wv[...])
            if k == 0:
                grad_own[r, :] = g_first[r, :] + part + mm_nt(dq[r, :], wq[...])
            else:
                grad_halo[k - 1, r, :] = part.astype(BF)
            return carry

        @pl.when(z >= k)
        def _(window_rows=window_rows):
            lax.fori_loop(0, tiles, window_rows, 0)

        if k > 0:

            @pl.when(z < k)
            def _(k=k):
                grad_halo[k - 1] = jnp.zeros((rows, D), BF)

    add_vec(V_SQB, col_sum(dq[...]))
    stage[...] = mm_tn(toks[0][...], dq[...]).astype(BF)
    put_grad(sh, stage, n, 0, g_send, g_own)
    stage[...] = acc_k[...].astype(BF)
    put_grad(sh, stage, n, n, g_send, g_own)
    stage[...] = acc_v[...].astype(BF)
    put_grad(sh, stage, n, 2 * n, g_send, g_own)
    vec_low = vec_grad[...].astype(BF)
    for s in range(count // 2):
        g_send[s, pl.ds(3 * n, VROWS), :] = vec_low
        g_own[s, pl.ds(3 * n, VROWS), :] = vec_low


def self_backward(sh, lens, order, arrays, toks, slots):
    rows, nb, n = sh.rows, sh.k_blocks, sh.piece
    outs = [
        shape((sh.count // 2, 3 * n + VROWS, D), BF),
        shape((sh.count // 2, 3 * n + VROWS, D), BF),
        shape((rows, D), F32),
        shape((sh.halo, rows, D), BF),
    ]
    scratch = [
        pltpu.VMEM((D, D), BF),
        pltpu.VMEM((D, D), BF),
        pltpu.VMEM((D, D), BF),
        pltpu.VMEM((HEADS, 2 * HDIM, TILE), BF),
        pltpu.VMEM((HEADS, 2 * HDIM, TILE), BF),
        pltpu.VMEM((HEADS, TILE, 2 * HDIM), BF),
        pltpu.VMEM((HEADS, TILE, 2 * HDIM), BF),
        pltpu.VMEM((HEADS, TILE), F32),
        pltpu.VMEM((TILE, TILE), F32),
        pltpu.VMEM((nb, TILE, D), F32),
        pltpu.VMEM((nb, TILE, D), F32),
        pltpu.VMEM((D, TILE), F32),
        pltpu.VMEM((rows, D), BF),
        pltpu.VMEM((D, D), F32),
        pltpu.VMEM((D, D), F32),
        pltpu.VMEM((VROWS, D), F32),
        pltpu.VMEM((D, D), BF),
        pltpu.SemaphoreType.DMA((3,)),
    ]
    specs = [SMEM_SPEC] * 2 + [VMEM_SPEC] * (len(arrays) + len(toks)) + [ANY_SPEC] * len(slots)
    return call(
        lambda *refs: self_backward_kernel(sh, *refs),
        "self_backward",
        (lens, order, *arrays, *toks, *slots),
        specs,
        outs,
        scratch,
    )


def shards(
    tokens,
    memory,
    targets,
    doc_lengths,
    doc_order,
    memory_lengths,
    self_query,
    self_query_bias,
    self_key,
    self_value,
    self_value_bias,
    self_output,
    self_output_bias,
    first_gain,
    first_shift,
    cross_query,
    cross_query_bias,
    cross_key,
    cross_value,
    cross_value_bias,
    cross_output,
    cross_output_bias,
    second_gain,
    second_shift,
    expand_weight,
    expand_bias,
    contract_weight,
    contract_bias,
    third_gain,
    third_shift,
):
    split = lax.axis_size("seq")
    count = lax.axis_size("fsdp")
    fsdp = lax.axis_index("fsdp")
    n = self_query.shape[0]
    wide = contract_weight.shape[0]
    sh = Shard(tokens.shape[0], memory.shape[0], count, split, n, wide)

    toks = [tokens]
    for _ in range(sh.halo):
        toks.append(seq_up(toks[-1], split))

    small = jnp.stack(
        [
            self_query_bias,
            self_value_bias,
            self_output_bias,
            first_gain,
            first_shift,
            cross_query_bias,
            cross_value_bias,
            cross_output_bias,
            second_gain,
            second_shift,
            contract_bias,
            third_gain,
            third_shift,
        ]
    )
    block = jnp.zeros((V_EB, D), BF)
    block = lax.dynamic_update_slice(block, small, (jnp.int32(0), fsdp * n))
    wide_bias = jnp.zeros((FFB * D,), BF)
    wide_bias = lax.dynamic_update_slice(wide_bias, expand_bias, (fsdp * expand_bias.shape[0],))
    vec_own = jnp.concatenate(
        [block, wide_bias.reshape(FFB, D), jnp.zeros((VROWS - V_EB - FFB, D), BF)]
    )
    own_a = jnp.concatenate([self_query, self_key, self_value, vec_own])
    own_b = jnp.concatenate(
        [self_output, cross_query, cross_key, cross_value, cross_output]
        + [expand_weight[:, c * D : (c + 1) * D] for c in range(FFB)]
        + [contract_weight]
    )
    slots_a = fsdp_gather(own_a, count)
    slots_b = fsdp_gather(own_b, count)

    mems = [memory]
    up, down = memory, memory
    for _ in range(split - 1):
        up, down = seq_up(up, split), seq_down(down, split)
        mems += [up, down]

    (q, q_t3, k3, v3, k_t3, ctx, ctx_t3, lse, vec) = self_forward(
        sh, doc_lengths, doc_order, toks, slots_a
    )
    (n1, inv1, first_low, cq, cq_t3, mk3, mv3, mk_t3, cctx, cctx_t3, clse, mem) = cross_forward(
        sh, doc_lengths, doc_order, memory_lengths, tokens, ctx, vec, mems, slots_b
    )
    (final_low, g_second, g_cc, g_cc_t3, send_c, own_c, vec_grad, loss) = feed(
        sh, doc_lengths, doc_order, n1, cctx, targets, vec, slots_b
    )
    error_sum, live_count = lax.psum((jnp.sum(loss[0]), loss[1, 0]), ("fsdp", "seq"))
    loss_value = error_sum / (live_count * D)
    red_c = seq_sum(fsdp_reduce(send_c, own_c, count), split)
    (send_b, own_b2, mem_part, g_first, g_ctx, g_ctx_t3, vec_grad) = cross_backward(
        sh,
        doc_lengths,
        doc_order,
        memory_lengths,
        (
            cq,
            cq_t3,
            mk3,
            mv3,
            mk_t3,
            cctx_t3,
            clse,
            g_cc,
            g_cc_t3,
            g_second,
            n1,
            inv1,
            first_low,
            mem,
            ctx,
            vec,
            vec_grad,
        ),
        slots_b,
    )
    red_b = seq_sum(fsdp_reduce(send_b, own_b2, count), split)
    z = lax.axis_index("seq")
    parts = mem_part.reshape(split, sh.mem_rows, D)

    def mem_shard(k):
        index = jnp.clip(z + k, 0, split - 1)
        return lax.dynamic_index_in_dim(parts, index, 0, keepdims=False)

    memory_grad = mem_shard(0).astype(F32)
    up = down = None
    for k in range(split - 1, 0, -1):
        mine_up, mine_down = mem_shard(k), mem_shard(-k)
        up = seq_up(mine_up if up is None else add_low(mine_up, up), split)
        down = seq_down(mine_down if down is None else add_low(mine_down, down), split)
    memory_grad = memory_grad + up.astype(F32) + down.astype(F32)

    (send_a, own_a2, grad_own, grad_halo) = self_backward(
        sh,
        doc_lengths,
        doc_order,
        (q, q_t3, k3, v3, k_t3, ctx_t3, lse, g_ctx, g_ctx_t3, g_first, vec_grad),
        toks,
        slots_a,
    )
    red_a = seq_sum(fsdp_reduce(send_a, own_a2, count), split)
    back = None
    for k in range(sh.halo, 0, -1):
        mine = grad_halo[k - 1]
        back = seq_down(mine if back is None else add_low(mine, back), split)
    input_grad = grad_own + back.astype(F32)

    def rows_of(array, start, size):
        return array[start : start + size].astype(F32)

    vec_rows = red_a[3 * n : 3 * n + VROWS].astype(F32)
    small_grad = lax.dynamic_slice(vec_rows, (jnp.int32(0), fsdp * n), (V_EB, n))
    flat = vec_rows[V_EB : V_EB + FFB].reshape(FFB * D)
    expand_bias_grad = lax.dynamic_slice(
        flat, (fsdp * expand_bias.shape[0],), (expand_bias.shape[0],)
    )
    expand_grad = jnp.concatenate(
        [rows_of(red_c, (1 + c) * n, n) for c in range(FFB)], axis=1
    )
    return (
        final_low,
        loss_value,
        input_grad,
        memory_grad,
        rows_of(red_a, 0, n),
        small_grad[V_SQB],
        rows_of(red_a, n, n),
        rows_of(red_a, 2 * n, n),
        small_grad[V_SVB],
        rows_of(red_b, 0, n),
        small_grad[V_SOB],
        small_grad[V_G1],
        small_grad[V_S1],
        rows_of(red_b, n, n),
        small_grad[V_CQB],
        rows_of(red_b, 2 * n, n),
        rows_of(red_b, 3 * n, n),
        small_grad[V_CVB],
        rows_of(red_c, 0, n),
        small_grad[V_COB],
        small_grad[V_G2],
        small_grad[V_S2],
        expand_grad,
        expand_bias_grad,
        rows_of(red_c, 5 * n, wide),
        small_grad[V_CB],
        small_grad[V_G3],
        small_grad[V_S3],
    )


def solution(mesh):
    rows = P(("fsdp", "seq"), None)
    matrix = P("fsdp", None)
    vector = P("fsdp")
    kinds = (
        "mvmmvmvvvmvmmvmvvvmvmvvv"
    )
    weights = tuple(matrix if kind == "m" else vector for kind in kinds)
    return jax.shard_map(
        shards,
        mesh=mesh,
        in_specs=(rows, rows, rows, matrix, matrix, matrix) + weights,
        out_specs=(rows, P(), rows, rows) + weights,
        check_vma=False,
    )
```

time: 1050 us -> 368 us (0.35); the launches traced: 1040 us -> 370 us
  waiting for transfers between devices: 347 us -> 90.1 us
  matrix products: 197 us -> 0 us
  blocking collectives: 186 us -> 55.9 us
  Pallas kernels: 0 us -> 101 us
  local copies, waits for them, and re-layouts: 95.4 us -> 15.8 us
  other arithmetic: 91.2 us -> 15.9 us
  loops' own time: 32.1 us -> 0 us
  starting transfers between devices: 67.9 us -> 87.7 us
  between operations: 20 us -> 4.15 us
    reduce_scatter x5 -> x0, waiting for transfers between devices: 200 us -> none  [the longest x1 44.7 us: shards(): lax.psum_scatter(summed[18].astype(jnp.bfloat16), 'fsdp', scatter_dimensi...]
    dot_general x86 -> x0, matrix products: 197 us -> none  [the longest x8 33.9 us: block_step(): jnp.einsum('qhd,khd->hqk', grad_part, value_heads, preferred_element_type...]
    pallas_call x0 -> x5, Pallas kernels: none -> 101 us  [call(): pl.pallas_call(body, name=name, in_specs=specs, out_specs=[VMEM_SPEC] * l...]
    all_to_all x16 -> x0, waiting for transfers between devices: 101 us -> none  [the longest x2 18.2 us: to_heads(): lax.all_to_all(gradient_rows, 'seq', split_axis=1, concat_axis=0, tiled=T...]
    ppermute x0 -> x48, waiting for transfers between devices: none -> 90.1 us  [the longest x8 18.8 us: seq_up(): return lax.ppermute(a, 'seq', [(i, i + 1) for i in range(count - 1)])]
    ppermute x0 -> x48, starting transfers between devices: none -> 87.7 us  [the longest x8 31.7 us: seq_up(): return lax.ppermute(a, 'seq', [(i, i + 1) for i in range(count - 1)])]
    all_gather x9 -> x0, blocking collectives: 86.2 us -> none  [the longest x1 10.7 us: shards(): lax.all_gather(cross_query, 'fsdp', axis=0, tiled=True)]
    all_to_all x16 -> x0, starting transfers between devices: 66.8 us -> none  [the longest x2 9.35 us: to_heads(): lax.all_to_all(gradient_rows, 'seq', split_axis=1, concat_axis=0, tiled=T...]
  transfers between devices with their start and end apart: 29 -> 48, of which waited for: 20 -> 16; matrix products, arithmetic and copies ran while one was open for 26% -> 5% of each run, Pallas kernels for 0% -> 8%
where the time goes in v1:
time: 368 us; the launch traced here: 370 us
  Pallas kernels  101 us (27%)
  waiting for transfers between devices  90.1 us (24%)
  starting transfers between devices  87.7 us (24%)
  blocking collectives  55.9 us (15%)
  other arithmetic  15.9 us (4%)
  local copies, waits for them, and re-layouts  15.8 us (4%)
  between operations  4.15 us (1%)
    pallas_call x5, Pallas kernels, call(): pl.pallas_call(body, name=name, in_specs=specs, out_specs=[VMEM_SPEC] * l...  101 us
    psum x1, blocking collectives, shards(): lax.psum((jnp.sum(loss[0]), loss[1, 0]), ('fsdp', 'seq'))  55.9 us
    ppermute x8, starting transfers between devices, seq_up(): return lax.ppermute(a, 'seq', [(i, i + 1) for i in range(count - 1)])  31.7 us
    ppermute x8, waiting for transfers between devices, seq_up(): return lax.ppermute(a, 'seq', [(i, i + 1) for i in range(count - 1)])  18.8 us
    ppermute x3, starting transfers between devices, fsdp_reduce(): got = lax.ppermute(send, 'fsdp', swap)  16.6 us
    ppermute x3, waiting for transfers between devices, seq_sum(): lax.ppermute(mine, 'seq', [(i, i ^ bit) for i in range(count)])  14.7 us
    ppermute x6, waiting for transfers between devices, fsdp_gather(): have = have + [lax.ppermute(a, 'fsdp', pairs) for a in have]  12.3 us
    ppermute x3, waiting for transfers between devices, seq_sum(): other = lax.ppermute(mine, 'seq', pairs)  11.7 us
  transfers between devices with their start and end apart: 48, of which 16 were waited for; matrix products, arithmetic and copies ran while one was open for 5% of the time, Pallas kernels for 8%

profile of v1, /device:TPU:0, one launch (start us, length us, event | category | flops | bytes accessed | tf_op | source)
XLA Modules:
  0.0 370.4 jit_solution(10671631942068539745)
XLA Ops:
  18.2 9.0 %collective-permute-done.2.refs_6_.refs_17_ = bf16[224,512]{1,0:T(8,128)(2,1)S(1)} collective-permute-done((bf16[224,512]{1,0:T(8,128)(2,1)S(1)}, bf16[224,512]{1,0:T(8,128)(2,1)S(1)}, u32[]{:S(2)}, u32[]{:S(2)}) %collective-permute-start.2) | collective-permute-done | bytes 229408 | tf_op jit(solution)/shard_map/ppermute | solution.py:94
  40.8 7.4 %collective-permute-done.9.refs_7_ = bf16[512,512]{1,0:T(8,128)(2,1)S(1)} collective-permute-done((bf16[512,512]{1,0:T(8,128)(2,1)}, bf16[512,512]{1,0:T(8,128)(2,1)S(1)}, u32[]{:S(2)}, u32[]{:S(2)}) %collective-permute-start.9) | collective-permute-done | bytes 524320 | tf_op jit(solution)/shard_map/ppermute | solution.py:132
  48.3 4.3 %collective-permute-start.1 = (bf16[512,512]{1,0:T(8,128)(2,1)S(1)}, bf16[512,512]{1,0:T(8,128)(2,1)S(1)}, u32[]{:S(2)}, u32[]{:S(2)}) collective-permute-start(bf16[512,512]{1,0:T(8,128)(2,1)S(1)} %collective-permute-done.refs_3_.refs_14_), channel_id=1, source_target_pairs={{0,1},{1,2},{2,3},{4,5},{5,6},{6,7},{8,9},{9,10},{10,11},{12,13},{... | collective-permute-start | bytes 1572872 | tf_op jit(solution)/shard_map/ppermute | solution.py:132
  54.1 4.2 %collective-permute-start.11 = (bf16[512,512]{1,0:T(8,128)(2,1)S(1)}, bf16[512,512]{1,0:T(8,128)(2,1)}, u32[]{:S(2)}, u32[]{:S(2)}) collective-permute-start(bf16[512,512]{1,0:T(8,128)(2,1)S(1)} %collective-permute-done.9.refs_7_), channel_id=1, source_target_pairs={{0,1},{1,2},{2,3},{4,5},{5,6},{6,7},{8,9},{9,10},{10,11},{12,13},{... | collective-permute-start | bytes 1572872 | tf_op jit(solution)/shard_map/ppermute | solution.py:132
  59.8 3.8 %collective-permute-done.1.refs_4_.refs_15_ = bf16[512,512]{1,0:T(8,128)(2,1)S(1)} collective-permute-done((bf16[512,512]{1,0:T(8,128)(2,1)S(1)}, bf16[512,512]{1,0:T(8,128)(2,1)S(1)}, u32[]{:S(2)}, u32[]{:S(2)}) %collective-permute-start.1) | collective-permute-done | bytes 524320 | tf_op jit(solution)/shard_map/ppermute | solution.py:132
  64.4 7.6 %collective-permute-done.11.refs_9_ = bf16[512,512]{1,0:T(8,128)(2,1)} collective-permute-done((bf16[512,512]{1,0:T(8,128)(2,1)S(1)}, bf16[512,512]{1,0:T(8,128)(2,1)}, u32[]{:S(2)}, u32[]{:S(2)}) %collective-permute-start.11) | collective-permute-done | bytes 524320 | tf_op jit(solution)/shard_map/ppermute | solution.py:132
  72.0 5.3 %collective-permute-start.13 = (bf16[512,512]{1,0:T(8,128)(2,1)}, bf16[512,512]{1,0:T(8,128)(2,1)}, u32[]{:S(2)}, u32[]{:S(2)}) collective-permute-start(bf16[512,512]{1,0:T(8,128)(2,1)} %collective-permute-done.11.refs_9_), channel_id=1, source_target_pairs={{0,1},{1,2},{2,3},{4,5},{5,6},{6,7},{8,9},{9,10},{10,11},{12,13},{... | collective-permute-start | bytes 1572872 | tf_op jit(solution)/shard_map/ppermute | solution.py:132
  78.6 14.8 %self_forward.1 = (bf16[512,512]{1,0:T(8,128)(2,1)}, bf16[2,512,256]{2,1,0:T(8,128)(2,1)}, bf16[6,256,512]{2,1,0:T(8,128)(2,1)}, bf16[6,256,512]{2,1,0:T(8,128)(...) custom-call(s32[1,4]{1,0:T(1,128)} %refs_0_.9, ...), custom_call_target="tpu_custom_call" | custom-call | tf_op jit(solution)/shard_map/self_forward/pallas_call | solution.py:397
  93.5 24.7 %cross_forward.1 = (f32[512,512]{1,0:T(8,128)}, f32[512,1]{1,0:T(8,128)}, bf16[512,512]{1,0:T(8,128)(2,1)}, bf16[512,512]{1,0:T(8,128)(2,1)}, bf16[2,512,256]{2,...) custom-call(s32[1,4]{1,0:T(1,128)} %refs_0_.9, ...), custom_call_target="tpu_custom_call" | custom-call | tf_op jit(solution)/shard_map/cross_forward/pallas_call | solution.py:397
  118.2 18.4 %feed.1 = (bf16[512,512]{1,0:T(8,128)(2,1)}, f32[512,512]{1,0:T(8,128)}, bf16[512,512]{1,0:T(8,128)(2,1)}, bf16[2,512,256]{2,1,0:T(8,128)(2,1)}, bf16[4,576,512]...) custom-call(s32[1,4]{1,0:T(1,128)} %refs_0_.9, s32[1,4]{1,0:T(1,128)} %refs_1_.9, ...), custom_call_target="tpu_custom_call" | custom-call | tf_op jit(solution)/shard_map/feed/pallas_call | solution.py:397
  136.7 27.2 %cross_backward.1 = (bf16[4,256,512]{2,1,0:T(8,128)(2,1)}, bf16[4,256,512]{2,1,0:T(8,128)(2,1)}, bf16[8,256,512]{2,1,0:T(8,128)(2,1)}, f32[512,512]{1,0:T(8,128)...) custom-call(s32[1,4]{1,0:T(1,128)} %refs_0_.9, s32[1,4]{1,0:T(1,128)} %refs_1_.9, ...), custom_call_target="tpu_custom_call" | custom-call | tf_op jit(solution)/shard_map/cross_backward/pallas_call | solution.py:397
  168.3 15.7 %self_backward.1 = (bf16[4,224,512]{2,1,0:T(8,128)(2,1)}, bf16[4,224,512]{2,1,0:T(8,128)(2,1)}, f32[512,512]{1,0:T(8,128)}, bf16[2,512,512]{2,1,0:T(8,128)(2,1)}) custom-call(s32[1,4]{1,0:T(1,128)} %refs_0_.9, s32[1,4]{1,0:T(1,128)} %refs_1_.9, bf16[512,512]{1,0:T(8,128)(2,1)} %get-tuple-element.74.refs_2_, bf16[2,512,256]{2,1,0:T(8,128)(2,1)} %get-tuple-element.75.refs_3_, ...), custom_call_target="tpu_custom_call" | custom-call | tf_op jit(solution)/shard_map/self_backward/pallas_call | solution.py:397
  184.0 16.0 %collective-permute-start.30 = (bf16[4,224,512]{2,1,0:T(8,128)(2,1)}, bf16[4,224,512]{2,1,0:T(8,128)(2,1)}, u32[]{:S(2)}, u32[]{:S(2)}) collective-permute-start(bf16[4,224,512]{2,1,0:T(8,128)(2,1)} %get-tuple-element.103), channel_id=1, source_target_pairs={{0,4},{4,0},{8,12},{12,8},{16,20},{20,16},{24,28},{28,24},{1,5},{5... | collective-permute-start | bytes 2752520 | tf_op jit(solution)/shard_map/ppermute | solution.py:105
  206.3 55.9 %all-reduce = (f32[]{:T(128)}, f32[]{:T(128)}) all-reduce(f32[]{:T(128)} %slice_reduce_fusion, f32[]{:T(128)} %bitcast.13), channel_id=1, replica_groups=mesh['fsdp'=8,'seq'=4] {'fsdp','seq'}, use_global_device_ids=true, to_apply=%region_1.0 | all-reduce | flops 2 | bytes 16 | tf_op jit(solution)/shard_map/psum | solution.py:1150
  266.2 4.8 %collective-permute-start.25 = (bf16[512,512]{1,0:T(8,128)(2,1)S(1)}, bf16[512,512]{1,0:T(8,128)(2,1)S(1)}, u32[]{:S(2)}, u32[]{:S(2)}) collective-permute-start(bf16[512,512]{1,0:T(8,128)(2,1)S(1)} %fusion.2), channel_id=1, source_target_pairs={{0,1},{1,2},{2,3},{4,5},{5,6},{6,7},{8,9},{9,10},{10,11},{12,13},{... | collective-permute-start | bytes 1572872 | tf_op jit(solution)/shard_map/ppermute | solution.py:132
  284.6 7.4 %collective-permute-done.23 = bf16[512,512]{1,0:T(8,128)(2,1)S(1)} collective-permute-done((bf16[512,512]{1,0:T(8,128)(2,1)S(1)}, bf16[512,512]{1,0:T(8,128)(2,1)S(1)}, u32[]{:S(2)}, u32[]{:S(2)}) %collective-permute-start.23) | collective-permute-done | bytes 524320 | tf_op jit(solution)/shard_map/ppermute | solution.py:136
  292.0 3.9 %collective-permute-start.26 = (bf16[512,512]{1,0:T(8,128)(2,1)S(1)}, bf16[512,512]{1,0:T(8,128)(2,1)S(1)}, u32[]{:S(2)}, u32[]{:S(2)}) collective-permute-start(bf16[512,512]{1,0:T(8,128)(2,1)S(1)} %get-tuple-element.114), channel_id=1, source_target_pairs={{0,1},{1,2},{2,3},{4,5},{5,6},{6,7},{8,9},{9,10},{10,11},{12,13},{... | collective-permute-start | bytes 1572872 | tf_op jit(solution)/shard_map/ppermute | solution.py:132
  299.9 3.8 %collective-permute-done.32 = bf16[1,224,512]{2,1,0:T(8,128)(2,1)S(1)} collective-permute-done((bf16[1,224,512]{2,1,0:T(8,128)(2,1)S(1)}, bf16[1,224,512]{2,1,0:T(8,128)(2,1)S(1)}, u32[]{:S(2)}, u32[]{:S(2)}) %collective-permute-start.32) | collective-permute-done | bytes 229408 | tf_op jit(solution)/shard_map/ppermute | solution.py:111
  311.5 6.7 %collective-permute-done.34 = bf16[112,512]{1,0:T(8,128)(2,1)S(1)} collective-permute-done((bf16[112,512]{1,0:T(8,128)(2,1)S(1)}, bf16[112,512]{1,0:T(8,128)(2,1)S(1)}, u32[]{:S(2)}, u32[]{:S(2)}) %collective-permute-start.34) | collective-permute-done | bytes 114720 | tf_op jit(solution)/shard_map/ppermute | solution.py:125
  320.6 5.8 %collective-permute-done.35 = bf16[112,512]{1,0:T(8,128)(2,1)S(1)} collective-permute-done((bf16[112,512]{1,0:T(8,128)(2,1)S(1)}, bf16[112,512]{1,0:T(8,128)(2,1)S(1)}, u32[]{:S(2)}, u32[]{:S(2)}) %collective-permute-start.35) | collective-permute-done | bytes 114720 | tf_op jit(solution)/shard_map/ppermute | solution.py:127
  329.7 7.1 %collective-permute-done.44 = bf16[1,576,512]{2,1,0:T(8,128)(2,1)S(1)} collective-permute-done((bf16[1,576,512]{2,1,0:T(8,128)(2,1)S(1)}, bf16[1,576,512]{2,1,0:T(8,128)(2,1)S(1)}, u32[]{:S(2)}, u32[]{:S(2)}) %collective-permute-start.44) | collective-permute-done | bytes 589856 | tf_op jit(solution)/shard_map/ppermute | solution.py:111
  340.4 9.5 %collective-permute-done.45 = bf16[288,512]{1,0:T(8,128)(2,1)S(1)} collective-permute-done((bf16[288,512]{1,0:T(8,128)(2,1)S(1)}, bf16[288,512]{1,0:T(8,128)(2,1)S(1)}, u32[]{:S(2)}, u32[]{:S(2)}) %collective-permute-start.45) | collective-permute-done | bytes 294944 | tf_op jit(solution)/shard_map/ppermute | solution.py:121
  351.9 7.9 %collective-permute-done.46 = bf16[288,512]{1,0:T(8,128)(2,1)S(1)} collective-permute-done((bf16[288,512]{1,0:T(8,128)(2,1)S(1)}, bf16[288,512]{1,0:T(8,128)(2,1)S(1)}, u32[]{:S(2)}, u32[]{:S(2)}) %collective-permute-start.46) | collective-permute-done | bytes 294944 | tf_op jit(solution)/shard_map/ppermute | solution.py:125
  360.9 5.8 %collective-permute-done.47 = bf16[288,512]{1,0:T(8,128)(2,1)S(1)} collective-permute-done((bf16[288,512]{1,0:T(8,128)(2,1)S(1)}, bf16[288,512]{1,0:T(8,128)(2,1)S(1)}, u32[]{:S(2)}, u32[]{:S(2)}) %collective-permute-start.47) | collective-permute-done | bytes 294944 | tf_op jit(solution)/shard_map/ppermute | solution.py:127
  (219 shorter events, 88.9 us)
Async XLA Ops:
  8.6 31.6 %collective-permute-start.15 = (bf16[832,512]{1,0:T(8,128)(2,1)S(1)}, bf16[832,512]{1,0:T(8,128)(2,1)S(1)}, u32[]{:S(2)}, u32[]{:S(2)}) collective-permute-start(bf16[832,512]{1,0:T(8,128)(2,1)S(1)} %constant_dynamic-update-slice_fusion.refs_13_.refs_6_.refs_20_), channel_id=1, source_target_pairs={{0,8},{4,20},{8,0},{12,28},{16,24},{20,4},{24,16},{28,12},{1,9},{5... | collective-permute-start | bytes 2555912 | tf_op jit(solution)/shard_map/ppermute | solution.py:94
  14.7 25.5 %collective-permute-start = (bf16[512,512]{1,0:T(8,128)(2,1)S(1)}, bf16[512,512]{1,0:T(8,128)(2,1)S(1)}, u32[]{:S(2)}, u32[]{:S(2)}) collective-permute-start(bf16[512,512]{1,0:T(8,128)(2,1)S(1)} %copy-done.5), channel_id=1, source_target_pairs={{0,1},{1,2},{2,3},{4,5},{5,6},{6,7},{8,9},{9,10},{10,11},{12,13},{... | collective-permute-start | bytes 1572872 | tf_op jit(solution)/shard_map/ppermute | solution.py:132
  33.3 25.1 %collective-permute-start.16 = (bf16[832,512]{1,0:T(8,128)(2,1)S(1)}, bf16[832,512]{1,0:T(8,128)(2,1)S(1)}, u32[]{:S(2)}, u32[]{:S(2)}) collective-permute-start(bf16[832,512]{1,0:T(8,128)(2,1)S(1)} %constant_dynamic-update-slice_fusion.refs_13_.refs_6_.refs_20_), channel_id=1, source_target_pairs={{0,16},{4,12},{8,24},{12,4},{16,0},{20,28},{24,8},{28,20},{1,17},{... | collective-permute-start | bytes 2555912 | tf_op jit(solution)/shard_map/ppermute | solution.py:94
  40.2 19.5 %collective-permute-start.18 = (bf16[832,512]{1,0:T(8,128)(2,1)S(1)}, bf16[832,512]{1,0:T(8,128)(2,1)S(1)}, u32[]{:S(2)}, u32[]{:S(2)}) collective-permute-start(bf16[832,512]{1,0:T(8,128)(2,1)S(1)} %constant_dynamic-update-slice_fusion.refs_13_.refs_6_.refs_20_), channel_id=1, source_target_pairs={{0,4},{4,0},{8,12},{12,8},{16,20},{20,16},{24,28},{28,24},{1,5},{5... | collective-permute-start | bytes 2555912 | tf_op jit(solution)/shard_map/ppermute | solution.py:96
  40.3 23.4 %collective-permute-start.17 = (bf16[832,512]{1,0:T(8,128)(2,1)S(1)}, bf16[832,512]{1,0:T(8,128)(2,1)}, u32[]{:S(2)}, u32[]{:S(2)}) collective-permute-start(bf16[832,512]{1,0:T(8,128)(2,1)S(1)} %collective-permute-done.15.refs_14_.refs_7_.refs_21_), channel_id=1, source_target_pairs={{0,16},{4,12},{8,24},{12,4},{16,0},{20,28},{24,8},{28,20},{1,17},{... | collective-permute-start | bytes 2555912 | tf_op jit(solution)/shard_map/ppermute | solution.py:94
  58.4 18.9 %collective-permute-start.12 = (bf16[512,512]{1,0:T(8,128)(2,1)S(1)}, bf16[512,512]{1,0:T(8,128)(2,1)}, u32[]{:S(2)}, u32[]{:S(2)}) collective-permute-start(bf16[512,512]{1,0:T(8,128)(2,1)S(1)} %collective-permute-done.10.refs_8_), channel_id=1, source_target_pairs={{1,0},{2,1},{3,2},{5,4},{6,5},{7,6},{9,8},{10,9},{11,10},{13,12},{... | collective-permute-start | bytes 1572872 | tf_op jit(solution)/shard_map/ppermute | solution.py:136
  59.7 33.8 %collective-permute-start.19 = (bf16[832,512]{1,0:T(8,128)(2,1)S(1)}, bf16[832,512]{1,0:T(8,128)(2,1)}, u32[]{:S(2)}, u32[]{:S(2)}) collective-permute-start(bf16[832,512]{1,0:T(8,128)(2,1)S(1)} %collective-permute-done.15.refs_14_.refs_7_.refs_21_), channel_id=1, source_target_pairs={{0,4},{4,0},{8,12},{12,8},{16,20},{20,16},{24,28},{28,24},{1,5},{5... | collective-permute-start | bytes 2555912 | tf_op jit(solution)/shard_map/ppermute | solution.py:96
  63.6 29.9 %collective-permute-start.20 = (bf16[832,512]{1,0:T(8,128)(2,1)S(1)}, bf16[832,512]{1,0:T(8,128)(2,1)}, u32[]{:S(2)}, u32[]{:S(2)}) collective-permute-start(bf16[832,512]{1,0:T(8,128)(2,1)S(1)} %collective-permute-done.16.refs_15_.refs_8_.refs_22_), channel_id=1, source_target_pairs={{0,4},{4,0},{8,12},{12,8},{16,20},{20,16},{24,28},{28,24},{1,5},{5... | collective-permute-start | bytes 2555912 | tf_op jit(solution)/shard_map/ppermute | solution.py:96
  63.6 29.9 %collective-permute-start.21 = (bf16[832,512]{1,0:T(8,128)(2,1)}, bf16[832,512]{1,0:T(8,128)(2,1)}, u32[]{:S(2)}, u32[]{:S(2)}) collective-permute-start(bf16[832,512]{1,0:T(8,128)(2,1)} %collective-permute-done.17.refs_16_.refs_9_.refs_23_), channel_id=1, source_target_pairs={{0,4},{4,0},{8,12},{12,8},{16,20},{20,16},{24,28},{28,24},{1,5},{5... | collective-permute-start | bytes 2555912 | tf_op jit(solution)/shard_map/ppermute | solution.py:96
  72.0 21.5 %collective-permute-start.13 = (bf16[512,512]{1,0:T(8,128)(2,1)}, bf16[512,512]{1,0:T(8,128)(2,1)}, u32[]{:S(2)}, u32[]{:S(2)}) collective-permute-start(bf16[512,512]{1,0:T(8,128)(2,1)} %collective-permute-done.11.refs_9_), channel_id=1, source_target_pairs={{0,1},{1,2},{2,3},{4,5},{5,6},{6,7},{8,9},{9,10},{10,11},{12,13},{... | collective-permute-start | bytes 1572872 | tf_op jit(solution)/shard_map/ppermute | solution.py:132
  166.1 97.4 %collective-permute-start.24 = (bf16[512,512]{1,0:T(8,128)(2,1)}, bf16[512,512]{1,0:T(8,128)(2,1)}, u32[]{:S(2)}, u32[]{:S(2)}) collective-permute-start(bf16[512,512]{1,0:T(8,128)(2,1)} %get-tuple-element.116), channel_id=1, source_target_pairs={{0,1},{1,2},{2,3},{4,5},{5,6},{6,7},{8,9},{9,10},{10,11},{12,13},{... | collective-permute-start | bytes 1572872 | tf_op jit(solution)/shard_map/ppermute | solution.py:132
  184.0 88.2 %collective-permute-start.30 = (bf16[4,224,512]{2,1,0:T(8,128)(2,1)}, bf16[4,224,512]{2,1,0:T(8,128)(2,1)}, u32[]{:S(2)}, u32[]{:S(2)}) collective-permute-start(bf16[4,224,512]{2,1,0:T(8,128)(2,1)} %get-tuple-element.103), channel_id=1, source_target_pairs={{0,4},{4,0},{8,12},{12,8},{16,20},{20,16},{24,28},{28,24},{1,5},{5... | collective-permute-start | bytes 2752520 | tf_op jit(solution)/shard_map/ppermute | solution.py:105
  201.9 64.3 %collective-permute-start.22 = (bf16[512,512]{1,0:T(8,128)(2,1)}, bf16[512,512]{1,0:T(8,128)(2,1)}, u32[]{:S(2)}, u32[]{:S(2)}) collective-permute-start(bf16[512,512]{1,0:T(8,128)(2,1)} %slice_bitcast_fusion), channel_id=1, source_target_pairs={{1,0},{2,1},{3,2},{5,4},{6,5},{7,6},{9,8},{10,9},{11,10},{13,12},{... | collective-permute-start | bytes 1572872 | tf_op jit(solution)/shard_map/ppermute | solution.py:136
  203.2 72.1 %collective-permute-start.36 = (bf16[4,256,512]{2,1,0:T(8,128)(2,1)}, bf16[4,256,512]{2,1,0:T(8,128)(2,1)S(1)}, u32[]{:S(2)}, u32[]{:S(2)}) collective-permute-start(bf16[4,256,512]{2,1,0:T(8,128)(2,1)} %get-tuple-element.105), channel_id=1, source_target_pairs={{0,4},{4,0},{8,12},{12,8},{16,20},{20,16},{24,28},{28,24},{1,5},{5... | collective-permute-start | bytes 3145736 | tf_op jit(solution)/shard_map/ppermute | solution.py:105
  203.3 101.9 %collective-permute-start.42 = (bf16[4,576,512]{2,1,0:T(8,128)(2,1)}, bf16[4,576,512]{2,1,0:T(8,128)(2,1)}, u32[]{:S(2)}, u32[]{:S(2)}) collective-permute-start(bf16[4,576,512]{2,1,0:T(8,128)(2,1)} %get-tuple-element.107), channel_id=1, source_target_pairs={{0,4},{4,0},{8,12},{12,8},{16,20},{20,16},{24,28},{28,24},{1,5},{5... | collective-permute-start | bytes 7077896 | tf_op jit(solution)/shard_map/ppermute | solution.py:105
  272.3 19.8 %collective-permute-start.23 = (bf16[512,512]{1,0:T(8,128)(2,1)S(1)}, bf16[512,512]{1,0:T(8,128)(2,1)S(1)}, u32[]{:S(2)}, u32[]{:S(2)}) collective-permute-start(bf16[512,512]{1,0:T(8,128)(2,1)S(1)} %fusion.5), channel_id=1, source_target_pairs={{1,0},{2,1},{3,2},{5,4},{6,5},{7,6},{9,8},{10,9},{11,10},{13,12},{... | collective-permute-start | bytes 1572872 | tf_op jit(solution)/shard_map/ppermute | solution.py:136
  275.4 21.8 %collective-permute-start.31 = (bf16[2,224,512]{2,1,0:T(8,128)(2,1)S(1)}, bf16[2,224,512]{2,1,0:T(8,128)(2,1)S(1)}, u32[]{:S(2)}, u32[]{:S(2)}) collective-permute-start(bf16[2,224,512]{2,1,0:T(8,128)(2,1)S(1)} %get-tuple-element.119), channel_id=1, source_target_pairs={{0,8},{4,20},{8,0},{12,28},{16,24},{20,4},{24,16},{28,12},{1,9},{5... | collective-permute-start | bytes 1376264 | tf_op jit(solution)/shard_map/ppermute | solution.py:111
  280.8 18.9 %collective-permute-start.37 = (bf16[2,256,512]{2,1,0:T(8,128)(2,1)S(1)}, bf16[2,256,512]{2,1,0:T(8,128)(2,1)S(1)}, u32[]{:S(2)}, u32[]{:S(2)}) collective-permute-start(bf16[2,256,512]{2,1,0:T(8,128)(2,1)S(1)} %get-tuple-element.113), channel_id=1, source_target_pairs={{0,8},{4,20},{8,0},{12,28},{16,24},{20,4},{24,16},{28,12},{1,9},{5... | collective-permute-start | bytes 1572872 | tf_op jit(solution)/shard_map/ppermute | solution.py:111
  283.3 26.7 %collective-permute-start.28 = (bf16[512,512]{1,0:T(8,128)(2,1)S(1)}, bf16[512,512]{1,0:T(8,128)(2,1)S(1)}, u32[]{:S(2)}, u32[]{:S(2)}) collective-permute-start(bf16[512,512]{1,0:T(8,128)(2,1)S(1)} %get-tuple-element.115), channel_id=1, source_target_pairs={{1,0},{2,1},{3,2},{5,4},{6,5},{7,6},{9,8},{10,9},{11,10},{13,12},{... | collective-permute-start | bytes 1572872 | tf_op jit(solution)/shard_map/ppermute | solution.py:136
  292.0 58.0 %collective-permute-start.26 = (bf16[512,512]{1,0:T(8,128)(2,1)S(1)}, bf16[512,512]{1,0:T(8,128)(2,1)S(1)}, u32[]{:S(2)}, u32[]{:S(2)}) collective-permute-start(bf16[512,512]{1,0:T(8,128)(2,1)S(1)} %get-tuple-element.114), channel_id=1, source_target_pairs={{0,1},{1,2},{2,3},{4,5},{5,6},{6,7},{8,9},{9,10},{10,11},{12,13},{... | collective-permute-start | bytes 1572872 | tf_op jit(solution)/shard_map/ppermute | solution.py:132
  299.8 18.6 %collective-permute-start.38 = (bf16[1,256,512]{2,1,0:T(8,128)(2,1)S(1)}, bf16[1,256,512]{2,1,0:T(8,128)(2,1)S(1)}, u32[]{:S(2)}, u32[]{:S(2)}) collective-permute-start(bf16[1,256,512]{2,1,0:T(8,128)(2,1)S(1)} %add_convert_fusion.11), channel_id=1, source_target_pairs={{0,16},{4,12},{8,24},{12,4},{16,0},{20,28},{24,8},{28,20},{1,17},{... | collective-permute-start | bytes 786440 | tf_op jit(solution)/shard_map/ppermute | solution.py:111
  307.5 18.9 %collective-permute-start.43 = (bf16[2,576,512]{2,1,0:T(8,128)(2,1)S(1)}, bf16[2,576,512]{2,1,0:T(8,128)(2,1)S(1)}, u32[]{:S(2)}, u32[]{:S(2)}) collective-permute-start(bf16[2,576,512]{2,1,0:T(8,128)(2,1)S(1)} %get-tuple-element.111), channel_id=1, source_target_pairs={{0,8},{4,20},{8,0},{12,28},{16,24},{20,4},{24,16},{28,12},{1,9},{5... | collective-permute-start | bytes 3538952 | tf_op jit(solution)/shard_map/ppermute | solution.py:111
  310.2 39.9 %collective-permute-start.29 = (bf16[512,512]{1,0:T(8,128)(2,1)S(1)}, bf16[512,512]{1,0:T(8,128)(2,1)S(1)}, u32[]{:S(2)}, u32[]{:S(2)}) collective-permute-start(bf16[512,512]{1,0:T(8,128)(2,1)S(1)} %fusion.1), channel_id=1, source_target_pairs={{1,0},{2,1},{3,2},{5,4},{6,5},{7,6},{9,8},{10,9},{11,10},{13,12},{... | collective-permute-start | bytes 1572872 | tf_op jit(solution)/shard_map/ppermute | solution.py:136
  318.5 20.0 %collective-permute-start.39 = (bf16[128,512]{1,0:T(8,128)(2,1)S(1)}, bf16[128,512]{1,0:T(8,128)(2,1)S(1)}, u32[]{:S(2)}, u32[]{:S(2)}) collective-permute-start(bf16[128,512]{1,0:T(8,128)(2,1)S(1)} %select_bitcast_fusion.1), channel_id=1, source_target_pairs={{0,1},{1,0},{2,3},{3,2},{4,5},{5,4},{6,7},{7,6},{8,9},{9,8},{10,11... | collective-permute-start | bytes 393224 | tf_op jit(solution)/shard_map/ppermute | solution.py:121
  (65 other events, 1090.7 us)

commit v2 on v1

--- a/solution.py
+++ b/solution.py
@@ -12,11 +12,14 @@
 MEM = 512
 FFB = 4
 TILE = 256
+GROUP = 4
 VROWS = 32
 NEG = -1e30
 BF = jnp.bfloat16
 F32 = jnp.float32
 VMEM_BYTES = 60 * 1024 * 1024
+SHARED_BYTES = 36 * 1024 * 1024
+FLOPS_RATE = 3e13
 
 (
     V_SQB,
@@ -34,6 +37,10 @@
     V_S3,
     V_EB,
 ) = range(14)
+V_LOSS = V_EB + FFB
+V_LIVE = V_LOSS + 1
+LOW_BITS = 36
+HIGH_BITS = 36
 
 
 def mm(a, b):
@@ -100,32 +107,66 @@
     return (a.astype(F32) + b.astype(F32)).astype(BF)
 
 
-def fsdp_reduce(send, own, count):
-    swap = [(i, i ^ 1) for i in range(count)]
-    got = lax.ppermute(send, "fsdp", swap)
-    half = own.shape[0]
-    for index in range(len(chip_steps(count)[0])):
-        half = half // 2
-        upper = add_low(own[half:], got[half:])
-        lower = add_low(own[:half], got[:half])
-        own, got = lower, lax.ppermute(upper, "fsdp", step_pairs(count, index))
-    return add_low(own[0], got[0])
-
-
-def seq_sum(part, count):
+def after(value, *others):
+    return lax.optimization_barrier((value, *others))[0]
+
+
+class Reduction:
+    def __init__(self, send, own, count, split, halves):
+        self.count, self.split, self.halves = count, split, halves
+        self.send, self.own = send, own
+        self.odd = (lax.axis_index("seq") % 2) == 1
+        self.got = None
+        self.plan = [("fsdp", [(i, i ^ 1) for i in range(count)])]
+        for index in range(len(chip_steps(count)[0])):
+            self.plan.append(("fsdp", step_pairs(count, index)))
+        bits = [1 << k for k in range(split.bit_length() - 1)]
+        for bit in bits + [1] * halves:
+            self.plan.append(("seq", [(i, i ^ bit) for i in range(split)]))
+
+    def step(self, *others):
+        send = after(self.send, *others) if others else self.send
+        axis, pairs = self.plan.pop(0)
+        got = self.got = lax.ppermute(send, axis, pairs)
+        left = sum(1 for a, _ in self.plan if a == "fsdp")
+        if axis == "fsdp" and left > 0:
+            half = self.own.shape[0] // 2
+            self.send = add_low(self.own[half:], got[half:])
+            self.own = add_low(self.own[:half], got[:half])
+        elif axis == "fsdp":
+            total = add_low(self.own[0], got[0])
+            if self.halves:
+                half = total.shape[0] // 2
+                self.send = jnp.where(self.odd, total[:half], total[half:])
+                self.own = jnp.where(self.odd, total[half:], total[:half])
+            else:
+                self.send = self.own = total
+        elif self.halves and not self.plan:
+            self.send = jnp.where(
+                self.odd, jnp.concatenate([got, self.own]), jnp.concatenate([self.own, got])
+            )
+        else:
+            self.send = self.own = add_low(self.own, got)
+        return self
+
+    def finish(self):
+        while self.plan:
+            self.step()
+        return self.send
+
+
+def seq_rest(parts, split):
     z = lax.axis_index("seq")
-    odd = (z % 2) == 1
-    half = part.shape[0] // 2
-    low, high = part[:half], part[half:]
-    pairs = [(i, i ^ 1) for i in range(count)]
-    got = lax.ppermute(jnp.where(odd, low, high), "seq", pairs)
-    mine = add_low(jnp.where(odd, high, low), got)
-    bit = 2
-    while bit < count:
-        mine = add_low(mine, lax.ppermute(mine, "seq", [(i, i ^ bit) for i in range(count)]))
+    bit = 4
+    while bit < split:
+        pairs = parts.reshape(parts.shape[0] // 2, 2, *parts.shape[1:])
+        odd = (z // bit) % 2 == 1
+        got = lax.ppermute(
+            jnp.where(odd, pairs[:, 0], pairs[:, 1]), "seq", [(i, i ^ bit) for i in range(split)]
+        )
+        parts = jnp.where(odd, pairs[:, 1], pairs[:, 0]) + got
         bit *= 2
-    other = lax.ppermute(mine, "seq", pairs)
-    return jnp.where(odd, jnp.concatenate([other, mine]), jnp.concatenate([mine, other]))
+    return parts
 
 
 def seq_up(a, count):
@@ -245,17 +286,23 @@
 
 
 def forward_tile(keys, vals_t, bias, q_t, m_ref, l_ref, acc_ref):
-    for h in range(HEADS):
-        s = mm(keys[:, pair_lanes(h)], q_t[h]) + bias[...]
-        m_old = m_ref[h : h + 1, :]
-        m_new = jnp.maximum(m_old, jnp.max(s, axis=0, keepdims=True))
-        p = jnp.exp(s - m_new)
-        alpha = jnp.exp(m_old - m_new)
-        m_ref[h : h + 1, :] = m_new
-        l_ref[h : h + 1, :] = alpha * l_ref[h : h + 1, :] + jnp.sum(p, axis=0, keepdims=True)
-        acc_ref[head_rows(h), :] = acc_ref[head_rows(h), :] * alpha + mm(
-            vals_t[head_rows(h), :], p.astype(BF)
-        )
+    heads = range(HEADS)
+    mask = bias[...]
+    m_old, l_old = m_ref[...], l_ref[...]
+    scores = [mm(keys[:, pair_lanes(h)], q_t[h]) + mask for h in heads]
+    tops = [
+        jnp.maximum(m_old[h : h + 1], jnp.max(scores[h], axis=0, keepdims=True)) for h in heads
+    ]
+    probs = [jnp.exp(scores[h] - tops[h]) for h in heads]
+    alphas = [jnp.exp(m_old[h : h + 1] - tops[h]) for h in heads]
+    sums = [
+        alphas[h] * l_old[h : h + 1] + jnp.sum(probs[h], axis=0, keepdims=True) for h in heads
+    ]
+    outs = [mm(vals_t[head_rows(h), :], probs[h].astype(BF)) for h in heads]
+    for h in heads:
+        acc_ref[head_rows(h), :] = acc_ref[head_rows(h), :] * alphas[h] + outs[h]
+    m_ref[...] = jnp.concatenate(tops, axis=0)
+    l_ref[...] = jnp.concatenate(sums, axis=0)
 
 
 def forward_start(m_ref, l_ref, acc_ref):
@@ -273,19 +320,24 @@
 
 
 def backward_tile(keys, vals, keys_t, bias, q_t, g_t, q_m, g_m, lse, delta, dk, dv, dq_t):
-    for h in range(0, HEADS, 2):
-        dk_sum = dk[:, pair_lanes(h)]
-        dv_sum = dv[:, pair_lanes(h)]
-        for i in (h, h + 1):
-            s = mm(keys[:, pair_lanes(i)], q_t[i]) + bias[...]
-            p = jnp.exp(s - lse[i : i + 1, :])
-            dp = mm(vals[:, pair_lanes(i)], g_t[i])
-            ds = (p * (dp - delta[i : i + 1, :])).astype(BF)
-            dv_sum = dv_sum + mm(p.astype(BF), g_m[i])
-            dk_sum = dk_sum + mm(ds, q_m[i])
-            dq_t[head_rows(i), :] = dq_t[head_rows(i), :] + mm(keys_t[head_rows(i), :], ds)
-        dk[:, pair_lanes(h)] = dk_sum
-        dv[:, pair_lanes(h)] = dv_sum
+    mask = bias[...]
+    for first in range(0, HEADS, GROUP):
+        heads = range(first, first + GROUP)
+        scores = [mm(keys[:, pair_lanes(h)], q_t[h]) for h in heads]
+        probs = [jnp.exp(s + mask - lse[h : h + 1, :]) for h, s in zip(heads, scores)]
+        dvs = [mm(p.astype(BF), g_m[h]) for h, p in zip(heads, probs)]
+        dps = [mm(vals[:, pair_lanes(h)], g_t[h]) for h in heads]
+        dss = [
+            (p * (dp - delta[h : h + 1, :])).astype(BF) for h, p, dp in zip(heads, probs, dps)
+        ]
+        dks = [mm(ds, q_m[h]) for h, ds in zip(heads, dss)]
+        dqs = [mm(keys_t[head_rows(h), :], ds) for h, ds in zip(heads, dss)]
+        for i in range(0, GROUP, 2):
+            lanes = pair_lanes(first + i)
+            dv[:, lanes] = dv[:, lanes] + dvs[i] + dvs[i + 1]
+            dk[:, lanes] = dk[:, lanes] + dks[i] + dks[i + 1]
+        for h, dq in zip(heads, dqs):
+            dq_t[head_rows(h), :] = dq_t[head_rows(h), :] + dq
 
 
 def backward_start(b, q_t3, g_t3, q, g, ctx_t3, q_t, g_t, q_m, g_m, delta, dq_t):
@@ -393,7 +445,11 @@
     return jax.ShapeDtypeStruct(dims, dtype)
 
 
-def call(body, name, inputs, specs, outs, scratch):
+def call(body, name, inputs, specs, outs, scratch, micros, vmem=VMEM_BYTES):
+    moved = sum(a.size * a.dtype.itemsize for a in (*inputs, *outs))
+    cost = pl.CostEstimate(
+        flops=int(micros * 1e-6 * FLOPS_RATE), transcendentals=0, bytes_accessed=moved // 50
+    )
     return pl.pallas_call(
         body,
         name=name,
@@ -401,8 +457,121 @@
         out_specs=[VMEM_SPEC] * len(outs),
         out_shape=outs,
         scratch_shapes=scratch,
-        compiler_params=pltpu.CompilerParams(vmem_limit_bytes=VMEM_BYTES),
+        cost_estimate=cost,
+        compiler_params=pltpu.CompilerParams(vmem_limit_bytes=vmem),
     )(*inputs)
+
+
+def pack_kernel(sh, *refs):
+    small = refs[:V_EB]
+    wide_bias = refs[V_EB]
+    mats = refs[V_EB + 1 : V_EB + 11]
+    own_a, own_b = refs[V_EB + 11 :]
+    n, wide = sh.piece, sh.wide_piece
+    (sq, sk, sv, so, cq, ck, cv, co, w1, w2) = mats
+    for i, m in enumerate((sq, sk, sv)):
+        own_a[pl.ds(i * n, n), :] = m[...]
+    for i, m in enumerate((so, cq, ck, cv, co)):
+        own_b[pl.ds(i * n, n), :] = m[...]
+    for c in range(FFB):
+        own_b[pl.ds((5 + c) * n, n), :] = w1[:, c * D : (c + 1) * D]
+    own_b[pl.ds(9 * n, wide), :] = w2[...]
+    index = lax.axis_index("fsdp")
+
+    def spread(piece, size, offset):
+        hot = lax.broadcasted_iota(jnp.int32, (size, D), 1) == offset + lax.broadcasted_iota(
+            jnp.int32, (size, D), 0
+        )
+        return mm(piece, hot.astype(BF)).astype(BF)
+
+    rows = jnp.concatenate([r[...].reshape(1, n) for r in small], axis=0)
+    size = wide_bias.shape[0]
+    flat = index * size
+    line = spread(wide_bias[...].reshape(1, size), size, flat % D)
+    row = lax.broadcasted_iota(jnp.int32, (FFB, D), 0)
+    own_a[pl.ds(3 * n, VROWS), :] = jnp.concatenate(
+        [
+            spread(rows, n, index * n),
+            jnp.where(row == flat // D, line, jnp.zeros((FFB, D), BF)),
+            jnp.zeros((VROWS - V_EB - FFB, D), BF),
+        ],
+        axis=0,
+    )
+
+
+def pack(sh, small, wide_bias, mats):
+    n, wide = sh.piece, sh.wide_piece
+    outs = [shape((3 * n + VROWS, D), BF), shape((9 * n + wide, D), BF)]
+    return call(
+        lambda *refs: pack_kernel(sh, *refs),
+        "pack",
+        (*small, wide_bias, *mats),
+        [VMEM_SPEC] * (V_EB + 1 + len(mats)),
+        outs,
+        [],
+        2,
+    )
+
+
+def digit_bits(devices):
+    return 3 if 7 * devices <= 256 else 1
+
+
+def digits(value, bits):
+    lane = lax.broadcasted_iota(jnp.int32, (1, D), 1)
+    scale = jnp.full((1, D), 2.0**LOW_BITS, F32)
+    for i in range(9):
+        scale = scale * jnp.where((lane // 2**i) % 2 == 1, 2.0 ** -min(bits * 2**i, 140), 1.0)
+    whole = jnp.floor(value * scale)
+    return whole - 2.0**bits * jnp.floor(value * scale * 2.0**-bits)
+
+
+def undigits(row, bits):
+    lane = lax.broadcasted_iota(jnp.int32, (1, D), 1)
+    scale = jnp.full((1, D), 2.0**-LOW_BITS, F32)
+    for i in range(7):
+        scale = scale * jnp.where(
+            (lane // 2**i) % 2 == 1, 2.0 ** min(bits * 2**i, LOW_BITS + HIGH_BITS), 1.0
+        )
+    used = lane < (LOW_BITS + HIGH_BITS) // bits
+    return jnp.sum(jnp.where(used, row * jnp.where(used, scale, 0.0), 0.0), axis=1, keepdims=True)
+
+
+def finish_kernel(sh, red, *outs):
+    n = sh.piece
+    mats, small, wide_bias, loss = outs[:3], outs[3 : 3 + V_EB], outs[3 + V_EB], outs[4 + V_EB]
+    for i, m in enumerate(mats):
+        m[...] = red[pl.ds(i * n, n), :].astype(F32)
+    index = lax.axis_index("fsdp")
+    vec = red[pl.ds(3 * n, VROWS), :]
+
+    def cut(rows, size, offset):
+        hot = lax.broadcasted_iota(jnp.int32, (D, size), 0) == offset + lax.broadcasted_iota(
+            jnp.int32, (D, size), 1
+        )
+        return mm(rows, hot.astype(BF))
+
+    parts = cut(vec, n, index * n)
+    for i in range(V_EB):
+        small[i][...] = parts[i : i + 1, :].reshape(n)
+    size = wide_bias.shape[0]
+    flat = index * size
+    row = lax.broadcasted_iota(jnp.int32, (VROWS, D), 0)
+    lines = jnp.where(row == V_EB + flat // D, vec.astype(F32), 0.0).astype(BF)
+    wide_bias[...] = jnp.sum(cut(lines, size, flat % D), axis=0, keepdims=True).reshape(size)
+    bits = digit_bits(sh.count * sh.split)
+    error_sum = undigits(vec[V_LOSS : V_LOSS + 1, :].astype(F32), bits)
+    live = undigits(vec[V_LIVE : V_LIVE + 1, :].astype(F32), bits)
+    loss[...] = error_sum / (live * D)
+
+
+def finish(sh, red, bias_size):
+    n = sh.piece
+    outs = [shape((n, D), F32)] * 3 + [shape((n,), F32)] * V_EB
+    outs += [shape((bias_size,), F32), shape((1, 1), F32)]
+    return call(
+        lambda *refs: finish_kernel(sh, *refs), "finish", (red,), [VMEM_SPEC], outs, [], 2
+    )
 
 
 def self_forward(sh, lens, order, toks, slots):
@@ -439,6 +608,7 @@
         specs,
         outs,
         scratch,
+        16,
     )
 
 
@@ -620,6 +790,7 @@
         specs,
         outs,
         scratch,
+        21,
     )
 
 
@@ -628,8 +799,9 @@
     n1, cctx, targets, vec = refs[:4]
     slots = refs[4 : 4 + count]
     outs = refs[4 + count :]
-    (final_ref, g_second, g_cc, g_cc_t3, g_send, g_own, vec_grad, loss) = outs[:8]
-    (wco, w1, w2, n2, sec_low, hid, dact, feed_low, g_exp, g_cross, stage, stage2, sems) = outs[8:]
+    (final_ref, g_second, g_cc, g_cc_t3, vec_grad) = outs[:5]
+    (sec_low, hid, feed_low, g_exp, g_cross) = outs[5:10]
+    (wco, w1, w2, n2, dact, loss, sems) = outs[10:]
     z = lax.axis_index("seq")
     start_weight(sh, slots, 4 * n, n, wco, sems.at[0])
     for c in range(FFB):
@@ -705,7 +877,15 @@
     live_count = jnp.int32(rows) - jnp.maximum(
         jnp.minimum(pad_end, (z + 1) * rows) - jnp.maximum(pad_start, z * rows), 0
     )
-    loss[1:2, :] = jnp.full((1, D), live_count.astype(F32))
+    bits = digit_bits(count * sh.split)
+    error_sum = jnp.sum(loss[0:1, :], axis=1, keepdims=True)
+    vec_grad[V_LOSS : V_LOSS + 1, :] = digits(error_sum, bits)
+    vec_grad[V_LIVE : V_LIVE + 1, :] = digits(jnp.full((1, 1), live_count.astype(F32)), bits)
+
+
+def feed_weights_kernel(sh, cctx, sec_low, hid, feed_low, g_exp, g_cross, *outs):
+    n, wide = sh.piece, sh.wide_piece
+    (g_send, g_own, stage, stage2) = outs
     stage[...] = mm_tn(cctx[...], g_cross[...]).astype(BF)
     put_grad(sh, stage, n, 0, g_send, g_own)
     for c in range(FFB):
@@ -716,32 +896,45 @@
     put_grad(sh, stage2, wide, 5 * n, g_send, g_own)
 
 
+def feed_weights(sh, arrays):
+    block = 5 * sh.piece + sh.wide_piece
+    outs = [
+        shape((sh.count // 2, block, D), BF),
+        shape((sh.count // 2, block, D), BF),
+    ]
+    return call(
+        lambda *refs: feed_weights_kernel(sh, *refs),
+        "feed_weights",
+        arrays,
+        [VMEM_SPEC] * len(arrays),
+        outs,
+        [pltpu.VMEM((D, D), BF), pltpu.VMEM((FFB * D, D), BF)],
+        6,
+        SHARED_BYTES,
+    )
+
+
 def feed(sh, lens, order, n1, cctx, targets, vec, slots):
-    rows, nq, n = sh.rows, sh.q_blocks, sh.piece
-    block = 5 * n + sh.wide_piece
+    rows, nq = sh.rows, sh.q_blocks
     outs = [
         shape((rows, D), BF),
         shape((rows, D), F32),
         shape((rows, D), BF),
         shape((nq, D, TILE), BF),
-        shape((sh.count // 2, block, D), BF),
-        shape((sh.count // 2, block, D), BF),
         shape((VROWS, D), F32),
-        shape((8, D), F32),
+        shape((rows, D), BF),
+        shape((FFB, rows, D), BF),
+        shape((rows, D), BF),
+        shape((FFB, rows, D), BF),
+        shape((rows, D), BF),
     ]
     scratch = [
         pltpu.VMEM((D, D), BF),
         pltpu.VMEM((FFB, D, D), BF),
         pltpu.VMEM((FFB * D, D), BF),
         pltpu.VMEM((TILE, D), F32),
-        pltpu.VMEM((rows, D), BF),
-        pltpu.VMEM((FFB, rows, D), BF),
         pltpu.VMEM((FFB, TILE, D), F32),
-        pltpu.VMEM((rows, D), BF),
-        pltpu.VMEM((FFB, rows, D), BF),
-        pltpu.VMEM((rows, D), BF),
-        pltpu.VMEM((D, D), BF),
-        pltpu.VMEM((FFB * D, D), BF),
+        pltpu.VMEM((8, D), F32),
         pltpu.SemaphoreType.DMA((6,)),
     ]
     specs = [SMEM_SPEC] * 2 + [VMEM_SPEC] * 4 + [ANY_SPEC] * len(slots)
@@ -752,21 +945,28 @@
         specs,
         outs,
         scratch,
-    )
+        14,
+        SHARED_BYTES,
+    )
+
+
+def mem_shard(z, slot, high):
+    low, mid = z % 2, (z // 2) % 2
+    low = low if slot % 2 else 1 - low
+    mid = mid if slot >= 2 else 1 - mid
+    return 4 * high + 2 * mid + low
 
 
 def cross_backward_kernel(sh, lens, order, mlens, *refs):
-    count, rows, n = sh.count, sh.rows, sh.piece
-    (q_ref, q_t3, mk3, mv3, mk_t3, cctx_t3, lse, g_cc, g_cc_t3, g_second, n1, inv1) = refs[:12]
-    (first_low, mem, ctx, vec, vec_in) = refs[12:17]
-    slots = refs[17 : 17 + count]
-    outs = refs[17 + count :]
-    (g_send, g_own, mem_grad, g_first, g_ctx, g_ctx_t3, vec_grad) = outs[:7]
-    (wo, wcq, wck, wcv, q_t, g_t, q_m, g_m, delta, bias, dk, dv, dq_t, dq, g_self) = outs[7:22]
-    (acc_k, acc_v, stage, bounds, sems) = outs[22:]
-    for i, w in enumerate((wo, wcq, wck, wcv)):
-        start_weight(sh, slots, i * n, n, w, sems.at[i])
-    vec_grad[...] = vec_in[...]
+    count, n = sh.count, sh.piece
+    (q_ref, q_t3, mk3, mv3, mk_t3, cctx_t3, lse, g_cc, g_cc_t3) = refs[:9]
+    slots = refs[9 : 9 + count]
+    outs = refs[9 + count :]
+    mem_parts = outs[:4]
+    (dq, k_low3, v_low3) = outs[4:7]
+    (wck, wcv, q_t, g_t, q_m, g_m, delta, bias, dk, dv, dq_t, bounds, sems) = outs[7:]
+    for i, w in enumerate((wck, wcv)):
+        start_weight(sh, slots, (2 + i) * n, n, w, sems.at[i])
     slot_bounds(lens, order, bounds)
     spread_zero(q_t)
     spread_zero(g_t)
@@ -813,31 +1013,100 @@
         return carry
 
     lax.fori_loop(0, sh.q_blocks, block, 0)
-    for i, w in enumerate((wo, wcq, wck, wcv)):
-        wait_all(w, sems.at[i])
-
-    def add_vec(row, value):
-        vec_grad[row : row + 1, :] = vec_grad[row : row + 1, :] + value
-
-    acc_k[...] = jnp.zeros(acc_k.shape, F32)
-    acc_v[...] = jnp.zeros(acc_v.shape, F32)
-
-    def mem_tile(t, carry):
+    wait_all(wck, sems.at[0])
+    wait_all(wcv, sems.at[1])
+
+    z = lax.axis_index("seq")
+    tiles_per = sh.mem_rows // TILE
+
+    def mem_tile(i, carry, slot, out):
+        shard = mem_shard(z, slot, i // tiles_per)
+        t = shard * tiles_per + i % tiles_per
         seen = touched_tile(sh, lens, order, mlens, t, bounds, True)
 
         @pl.when(seen)
         def _():
             k_low = dk[t].astype(BF)
             v_low = dv[t].astype(BF)
+            k_low3[t] = k_low
+            v_low3[t] = v_low
+            out[i] = (mm_nt(k_low, wck[...]) + mm_nt(v_low, wcv[...])).astype(BF)
+
+        @pl.when(jnp.logical_not(seen))
+        def _():
+            out[i] = jnp.zeros((TILE, D), BF)
+
+        return carry
+
+    for slot, out in enumerate(mem_parts):
+        lax.fori_loop(
+            0, sh.m_blocks // 4, lambda i, c, slot=slot, out=out: mem_tile(i, c, slot, out), 0
+        )
+
+
+def cross_backward(sh, lens, order, mlens, arrays, slots):
+    rows, nm = sh.rows, sh.m_blocks
+    outs = [shape((nm // 4, TILE, D), BF)] * 4 + [
+        shape((rows, D), BF),
+        shape((nm, TILE, D), BF),
+        shape((nm, TILE, D), BF),
+    ]
+    scratch = [
+        pltpu.VMEM((D, D), BF),
+        pltpu.VMEM((D, D), BF),
+        pltpu.VMEM((HEADS, 2 * HDIM, TILE), BF),
+        pltpu.VMEM((HEADS, 2 * HDIM, TILE), BF),
+        pltpu.VMEM((HEADS, TILE, 2 * HDIM), BF),
+        pltpu.VMEM((HEADS, TILE, 2 * HDIM), BF),
+        pltpu.VMEM((HEADS, TILE), F32),
+        pltpu.VMEM((TILE, TILE), F32),
+        pltpu.VMEM((nm, TILE, D), F32),
+        pltpu.VMEM((nm, TILE, D), F32),
+        pltpu.VMEM((D, TILE), F32),
+        pltpu.SMEM((4, DOCS), jnp.int32),
+        pltpu.SemaphoreType.DMA((2,)),
+    ]
+    specs = [SMEM_SPEC] * 3 + [VMEM_SPEC] * len(arrays) + [ANY_SPEC] * len(slots)
+    return call(
+        lambda *refs: cross_backward_kernel(sh, *refs),
+        "cross_backward",
+        (lens, order, mlens, *arrays, *slots),
+        specs,
+        outs,
+        scratch,
+        15,
+    )
+
+
+def first_backward_kernel(sh, lens, order, mlens, *refs):
+    count, rows, n = sh.count, sh.rows, sh.piece
+    (dq, k_low3, v_low3, g_second, n1, inv1, first_low, mem, ctx, vec, vec_in) = refs[:11]
+    slots = refs[11 : 11 + count]
+    outs = refs[11 + count :]
+    (g_send, g_own, g_first, g_ctx, g_ctx_t3, vec_grad) = outs[:6]
+    (wo, wcq, g_self, acc_k, acc_v, stage, bounds, sems) = outs[6:]
+    for i, w in enumerate((wo, wcq)):
+        start_weight(sh, slots, i * n, n, w, sems.at[i])
+    vec_grad[...] = vec_in[...]
+    slot_bounds(lens, order, bounds)
+    wait_all(wo, sems.at[0])
+    wait_all(wcq, sems.at[1])
+
+    def add_vec(row, value):
+        vec_grad[row : row + 1, :] = vec_grad[row : row + 1, :] + value
+
+    acc_k[...] = jnp.zeros(acc_k.shape, F32)
+    acc_v[...] = jnp.zeros(acc_v.shape, F32)
+
+    def mem_tile(t, carry):
+        @pl.when(touched_tile(sh, lens, order, mlens, t, bounds, True))
+        def _():
+            k_low = k_low3[t]
+            v_low = v_low3[t]
             x = mem[t]
             acc_k[...] = acc_k[...] + mm_tn(x, k_low)
             acc_v[...] = acc_v[...] + mm_tn(x, v_low)
             add_vec(V_CVB, col_sum(v_low))
-            mem_grad[t] = (mm_nt(k_low, wck[...]) + mm_nt(v_low, wcv[...])).astype(BF)
-
-        @pl.when(jnp.logical_not(seen))
-        def _():
-            mem_grad[t] = jnp.zeros((TILE, D), BF)
 
         return carry
 
@@ -871,12 +1140,11 @@
     put_grad(sh, stage, n, 3 * n, g_send, g_own)
 
 
-def cross_backward(sh, lens, order, mlens, arrays, slots):
-    rows, nq, nm, n = sh.rows, sh.q_blocks, sh.m_blocks, sh.piece
+def first_backward(sh, lens, order, mlens, arrays, slots):
+    rows, nq, n = sh.rows, sh.q_blocks, sh.piece
     outs = [
         shape((sh.count // 2, 4 * n, D), BF),
         shape((sh.count // 2, 4 * n, D), BF),
-        shape((nm, TILE, D), BF),
         shape((rows, D), F32),
         shape((rows, D), BF),
         shape((nq, D, TILE), BF),
@@ -885,49 +1153,35 @@
     scratch = [
         pltpu.VMEM((D, D), BF),
         pltpu.VMEM((D, D), BF),
-        pltpu.VMEM((D, D), BF),
-        pltpu.VMEM((D, D), BF),
-        pltpu.VMEM((HEADS, 2 * HDIM, TILE), BF),
-        pltpu.VMEM((HEADS, 2 * HDIM, TILE), BF),
-        pltpu.VMEM((HEADS, TILE, 2 * HDIM), BF),
-        pltpu.VMEM((HEADS, TILE, 2 * HDIM), BF),
-        pltpu.VMEM((HEADS, TILE), F32),
-        pltpu.VMEM((TILE, TILE), F32),
-        pltpu.VMEM((nm, TILE, D), F32),
-        pltpu.VMEM((nm, TILE, D), F32),
-        pltpu.VMEM((D, TILE), F32),
-        pltpu.VMEM((rows, D), BF),
         pltpu.VMEM((rows, D), BF),
         pltpu.VMEM((D, D), F32),
         pltpu.VMEM((D, D), F32),
         pltpu.VMEM((D, D), BF),
         pltpu.SMEM((4, DOCS), jnp.int32),
-        pltpu.SemaphoreType.DMA((4,)),
+        pltpu.SemaphoreType.DMA((2,)),
     ]
     specs = [SMEM_SPEC] * 3 + [VMEM_SPEC] * len(arrays) + [ANY_SPEC] * len(slots)
     return call(
-        lambda *refs: cross_backward_kernel(sh, *refs),
-        "cross_backward",
+        lambda *refs: first_backward_kernel(sh, *refs),
+        "first_backward",
         (lens, order, mlens, *arrays, *slots),
         specs,
         outs,
         scratch,
+        6,
     )
 
 
 def self_backward_kernel(sh, lens, order, *refs):
     count, rows, n, halo = sh.count, sh.rows, sh.piece, sh.halo
-    (q_ref, q_t3, k3, v3, k_t3, ctx_t3, lse, g_ctx, g_ctx_t3, g_first, vec_in) = refs[:11]
-    toks = refs[11 : 12 + halo]
-    slots = refs[12 + halo : 12 + halo + count]
-    outs = refs[12 + halo + count :]
-    (g_send, g_own, grad_own, grad_halo) = outs[:4]
-    (wq, wk, wv, q_t, g_t, q_m, g_m, delta, bias, dk, dv, dq_t, dq) = outs[4:17]
-    (acc_k, acc_v, vec_grad, stage, sems) = outs[17:]
+    (q_ref, q_t3, k3, v3, k_t3, ctx_t3, lse, g_ctx, g_ctx_t3) = refs[:9]
+    slots = refs[9 : 9 + count]
+    outs = refs[9 + count :]
+    (grad_halo, dq, k_low3, v_low3) = outs[:4]
+    (wk, wv, q_t, g_t, q_m, g_m, delta, bias, dk, dv, dq_t, sems) = outs[4:]
     z = lax.axis_index("seq")
-    for i, w in enumerate((wq, wk, wv)):
-        start_weight(sh, slots, i * n, n, w, sems.at[i])
-    vec_grad[...] = vec_in[...]
+    for i, w in enumerate((wk, wv)):
+        start_weight(sh, slots, (1 + i) * n, n, w, sems.at[i])
     spread_zero(q_t)
     spread_zero(g_t)
 
@@ -967,42 +1221,101 @@
         return carry
 
     lax.fori_loop(0, sh.q_blocks, block, 0)
-    for i, w in enumerate((wq, wk, wv)):
-        wait_all(w, sems.at[i])
-
-    def add_vec(row, value):
-        vec_grad[row : row + 1, :] = vec_grad[row : row + 1, :] + value
-
-    acc_k[...] = jnp.zeros(acc_k.shape, F32)
-    acc_v[...] = jnp.zeros(acc_v.shape, F32)
+    wait_all(wk, sems.at[0])
+    wait_all(wv, sems.at[1])
     tiles = rows // TILE
-    for k in range(halo, -1, -1):
+
+    def lower(t, carry):
+        k_low3[t] = dk[t].astype(BF)
+        v_low3[t] = dv[t].astype(BF)
+        return carry
+
+    lax.fori_loop(0, sh.k_blocks, lower, 0)
+    for k in range(halo, 0, -1):
 
         def window_rows(i, carry, k=k):
             r = pl.ds(pl.multiple_of(i * TILE, TILE), TILE)
             t = (halo - k) * tiles + i
-            k_low = dk[t].astype(BF)
-            v_low = dv[t].astype(BF)
-            x = toks[k][r, :]
-            acc_k[...] = acc_k[...] + mm_tn(x, k_low)
-            acc_v[...] = acc_v[...] + mm_tn(x, v_low)
-            add_vec(V_SVB, col_sum(v_low))
-            part = mm_nt(k_low, wk[...]) + mm_nt(v_low, wv[...])
-            if k == 0:
-                grad_own[r, :] = g_first[r, :] + part + mm_nt(dq[r, :], wq[...])
-            else:
-                grad_halo[k - 1, r, :] = part.astype(BF)
+            part = mm_nt(k_low3[t], wk[...]) + mm_nt(v_low3[t], wv[...])
+            grad_halo[k - 1, r, :] = part.astype(BF)
             return carry
 
         @pl.when(z >= k)
         def _(window_rows=window_rows):
             lax.fori_loop(0, tiles, window_rows, 0)
 
-        if k > 0:
-
-            @pl.when(z < k)
-            def _(k=k):
-                grad_halo[k - 1] = jnp.zeros((rows, D), BF)
+        @pl.when(z < k)
+        def _(k=k):
+            grad_halo[k - 1] = jnp.zeros((rows, D), BF)
+
+
+def self_backward(sh, lens, order, arrays, slots):
+    rows, nb = sh.rows, sh.k_blocks
+    outs = [
+        shape((sh.halo, rows, D), BF),
+        shape((rows, D), BF),
+        shape((nb, TILE, D), BF),
+        shape((nb, TILE, D), BF),
+    ]
+    scratch = [
+        pltpu.VMEM((D, D), BF),
+        pltpu.VMEM((D, D), BF),
+        pltpu.VMEM((HEADS, 2 * HDIM, TILE), BF),
+        pltpu.VMEM((HEADS, 2 * HDIM, TILE), BF),
+        pltpu.VMEM((HEADS, TILE, 2 * HDIM), BF),
+        pltpu.VMEM((HEADS, TILE, 2 * HDIM), BF),
+        pltpu.VMEM((HEADS, TILE), F32),
+        pltpu.VMEM((TILE, TILE), F32),
+        pltpu.VMEM((nb, TILE, D), F32),
+        pltpu.VMEM((nb, TILE, D), F32),
+        pltpu.VMEM((D, TILE), F32),
+        pltpu.SemaphoreType.DMA((2,)),
+    ]
+    specs = [SMEM_SPEC] * 2 + [VMEM_SPEC] * len(arrays) + [ANY_SPEC] * len(slots)
+    return call(
+        lambda *refs: self_backward_kernel(sh, *refs),
+        "self_backward",
+        (lens, order, *arrays, *slots),
+        specs,
+        outs,
+        scratch,
+        14,
+    )
+
+
+def self_weights_kernel(sh, *refs):
+    count, rows, n, halo = sh.count, sh.rows, sh.piece, sh.halo
+    (dq, k_low3, v_low3, g_first, vec_in) = refs[:5]
+    toks = refs[5 : 6 + halo]
+    slots = refs[6 + halo : 6 + halo + count]
+    outs = refs[6 + halo + count :]
+    (g_send, g_own, grad_own) = outs[:3]
+    (wq, wk, wv, acc_k, acc_v, vec_grad, stage, sems) = outs[3:]
+    z = lax.axis_index("seq")
+    for i, w in enumerate((wq, wk, wv)):
+        start_weight(sh, slots, i * n, n, w, sems.at[i])
+    vec_grad[...] = vec_in[...]
+    tiles = rows // TILE
+
+    def add_vec(row, value):
+        vec_grad[row : row + 1, :] = vec_grad[row : row + 1, :] + value
+
+    acc_k[...] = jnp.zeros(acc_k.shape, F32)
+    acc_v[...] = jnp.zeros(acc_v.shape, F32)
+    for k in range(halo, -1, -1):
+
+        def window_rows(i, carry, k=k):
+            r = pl.ds(pl.multiple_of(i * TILE, TILE), TILE)
+            t = (halo - k) * tiles + i
+            x = toks[k][r, :]
+            acc_k[...] = acc_k[...] + mm_tn(x, k_low3[t])
+            acc_v[...] = acc_v[...] + mm_tn(x, v_low3[t])
+            add_vec(V_SVB, col_sum(v_low3[t]))
+            return carry
+
+        @pl.when(z >= k)
+        def _(window_rows=window_rows):
+            lax.fori_loop(0, tiles, window_rows, 0)
 
     add_vec(V_SQB, col_sum(dq[...]))
     stage[...] = mm_tn(toks[0][...], dq[...]).astype(BF)
@@ -1015,44 +1328,45 @@
     for s in range(count // 2):
         g_send[s, pl.ds(3 * n, VROWS), :] = vec_low
         g_own[s, pl.ds(3 * n, VROWS), :] = vec_low
-
-
-def self_backward(sh, lens, order, arrays, toks, slots):
-    rows, nb, n = sh.rows, sh.k_blocks, sh.piece
+    for i, w in enumerate((wq, wk, wv)):
+        wait_all(w, sems.at[i])
+
+    def own_rows(i, carry):
+        r = pl.ds(pl.multiple_of(i * TILE, TILE), TILE)
+        t = halo * tiles + i
+        part = mm_nt(k_low3[t], wk[...]) + mm_nt(v_low3[t], wv[...])
+        grad_own[r, :] = g_first[r, :] + part + mm_nt(dq[r, :], wq[...])
+        return carry
+
+    lax.fori_loop(0, tiles, own_rows, 0)
+
+
+def self_weights(sh, arrays, toks, slots):
+    rows, n = sh.rows, sh.piece
     outs = [
         shape((sh.count // 2, 3 * n + VROWS, D), BF),
         shape((sh.count // 2, 3 * n + VROWS, D), BF),
         shape((rows, D), F32),
-        shape((sh.halo, rows, D), BF),
     ]
     scratch = [
         pltpu.VMEM((D, D), BF),
         pltpu.VMEM((D, D), BF),
         pltpu.VMEM((D, D), BF),
-        pltpu.VMEM((HEADS, 2 * HDIM, TILE), BF),
-        pltpu.VMEM((HEADS, 2 * HDIM, TILE), BF),
-        pltpu.VMEM((HEADS, TILE, 2 * HDIM), BF),
-        pltpu.VMEM((HEADS, TILE, 2 * HDIM), BF),
-        pltpu.VMEM((HEADS, TILE), F32),
-        pltpu.VMEM((TILE, TILE), F32),
-        pltpu.VMEM((nb, TILE, D), F32),
-        pltpu.VMEM((nb, TILE, D), F32),
-        pltpu.VMEM((D, TILE), F32),
-        pltpu.VMEM((rows, D), BF),
         pltpu.VMEM((D, D), F32),
         pltpu.VMEM((D, D), F32),
         pltpu.VMEM((VROWS, D), F32),
         pltpu.VMEM((D, D), BF),
         pltpu.SemaphoreType.DMA((3,)),
     ]
-    specs = [SMEM_SPEC] * 2 + [VMEM_SPEC] * (len(arrays) + len(toks)) + [ANY_SPEC] * len(slots)
+    specs = [VMEM_SPEC] * (len(arrays) + len(toks)) + [ANY_SPEC] * len(slots)
     return call(
-        lambda *refs: self_backward_kernel(sh, *refs),
-        "self_backward",
-        (lens, order, *arrays, *toks, *slots),
+        lambda *refs: self_weights_kernel(sh, *refs),
+        "self_weights",
+        (*arrays, *toks, *slots),
         specs,
         outs,
         scratch,
+        7,
     )
 
 
@@ -1090,17 +1404,13 @@
 ):
     split = lax.axis_size("seq")
     count = lax.axis_size("fsdp")
-    fsdp = lax.axis_index("fsdp")
     n = self_query.shape[0]
     wide = contract_weight.shape[0]
     sh = Shard(tokens.shape[0], memory.shape[0], count, split, n, wide)
 
-    toks = [tokens]
-    for _ in range(sh.halo):
-        toks.append(seq_up(toks[-1], split))
-
-    small = jnp.stack(
-        [
+    own_a, own_b = pack(
+        sh,
+        (
             self_query_bias,
             self_value_bias,
             self_output_bias,
@@ -1114,108 +1424,129 @@
             contract_bias,
             third_gain,
             third_shift,
-        ]
-    )
-    block = jnp.zeros((V_EB, D), BF)
-    block = lax.dynamic_update_slice(block, small, (jnp.int32(0), fsdp * n))
-    wide_bias = jnp.zeros((FFB * D,), BF)
-    wide_bias = lax.dynamic_update_slice(wide_bias, expand_bias, (fsdp * expand_bias.shape[0],))
-    vec_own = jnp.concatenate(
-        [block, wide_bias.reshape(FFB, D), jnp.zeros((VROWS - V_EB - FFB, D), BF)]
-    )
-    own_a = jnp.concatenate([self_query, self_key, self_value, vec_own])
-    own_b = jnp.concatenate(
-        [self_output, cross_query, cross_key, cross_value, cross_output]
-        + [expand_weight[:, c * D : (c + 1) * D] for c in range(FFB)]
-        + [contract_weight]
-    )
+        ),
+        expand_bias,
+        (
+            self_query,
+            self_key,
+            self_value,
+            self_output,
+            cross_query,
+            cross_key,
+            cross_value,
+            cross_output,
+            expand_weight,
+            contract_weight,
+        ),
+    )
+    toks = [tokens]
+    for _ in range(sh.halo):
+        toks.append(seq_up(toks[-1], split))
     slots_a = fsdp_gather(own_a, count)
-    slots_b = fsdp_gather(own_b, count)
-
+    near = slots_a[count // 2 - 1]
+    slots_b = fsdp_gather(after(own_b, toks[1], near), count)
+    ups, downs = [seq_up(after(memory, toks[1]), split)], [seq_down(after(memory, toks[1]), split)]
+    for k in range(2, split):
+        if k == split - 1:
+            last = after(memory, ups[0])
+            ups.append(lax.ppermute(last, "seq", [(0, split - 1)]))
+            downs.append(lax.ppermute(last, "seq", [(split - 1, 0)]))
+        else:
+            ups.append(seq_up(ups[-1], split))
+            downs.append(seq_down(downs[-1], split))
     mems = [memory]
-    up, down = memory, memory
-    for _ in range(split - 1):
-        up, down = seq_up(up, split), seq_down(down, split)
+    for up, down in zip(ups, downs):
         mems += [up, down]
 
+    first_tok = after(tokens, ups[0], downs[0], slots_b[1], slots_b[2])
     (q, q_t3, k3, v3, k_t3, ctx, ctx_t3, lse, vec) = self_forward(
-        sh, doc_lengths, doc_order, toks, slots_a
+        sh, doc_lengths, doc_order, [first_tok] + toks[1:], slots_a
     )
     (n1, inv1, first_low, cq, cq_t3, mk3, mv3, mk_t3, cctx, cctx_t3, clse, mem) = cross_forward(
         sh, doc_lengths, doc_order, memory_lengths, tokens, ctx, vec, mems, slots_b
     )
-    (final_low, g_second, g_cc, g_cc_t3, send_c, own_c, vec_grad, loss) = feed(
-        sh, doc_lengths, doc_order, n1, cctx, targets, vec, slots_b
-    )
-    error_sum, live_count = lax.psum((jnp.sum(loss[0]), loss[1, 0]), ("fsdp", "seq"))
-    loss_value = error_sum / (live_count * D)
-    red_c = seq_sum(fsdp_reduce(send_c, own_c, count), split)
-    (send_b, own_b2, mem_part, g_first, g_ctx, g_ctx_t3, vec_grad) = cross_backward(
+    feed_out = feed(sh, doc_lengths, doc_order, n1, cctx, targets, vec, slots_b)
+    (final_low, g_second, g_cc, g_cc_t3, vec_grad, sec_low, hid, feed_low, g_exp, g_cross) = (
+        feed_out
+    )
+    (send_c, own_c) = feed_weights(sh, (cctx, sec_low, hid, feed_low, g_exp, g_cross))
+    sum_c = Reduction(send_c, own_c, count, split, True)
+    sum_c.step()
+    cq = after(cq, sum_c.send)
+    sum_c.step()
+    *mem_parts, dcq, k_low3, v_low3 = cross_backward(
         sh,
         doc_lengths,
         doc_order,
         memory_lengths,
-        (
-            cq,
-            cq_t3,
-            mk3,
-            mv3,
-            mk_t3,
-            cctx_t3,
-            clse,
-            g_cc,
-            g_cc_t3,
-            g_second,
-            n1,
-            inv1,
-            first_low,
-            mem,
-            ctx,
-            vec,
-            vec_grad,
-        ),
+        (cq, cq_t3, mk3, mv3, mk_t3, cctx_t3, clse, g_cc, g_cc_t3),
         slots_b,
     )
-    red_b = seq_sum(fsdp_reduce(send_b, own_b2, count), split)
-    z = lax.axis_index("seq")
-    parts = mem_part.reshape(split, sh.mem_rows, D)
-
-    def mem_shard(k):
-        index = jnp.clip(z + k, 0, split - 1)
-        return lax.dynamic_index_in_dim(parts, index, 0, keepdims=False)
-
-    memory_grad = mem_shard(0).astype(F32)
-    up = down = None
-    for k in range(split - 1, 0, -1):
-        mine_up, mine_down = mem_shard(k), mem_shard(-k)
-        up = seq_up(mine_up if up is None else add_low(mine_up, up), split)
-        down = seq_down(mine_down if down is None else add_low(mine_down, down), split)
-    memory_grad = memory_grad + up.astype(F32) + down.astype(F32)
-
-    (send_a, own_a2, grad_own, grad_halo) = self_backward(
+    dcq = after(dcq, sum_c.send)
+    sum_c.step(dcq)
+    swap = [(i, i ^ 1) for i in range(split)]
+    mem_got = lax.ppermute(mem_parts[0], "seq", swap)
+    (send_b, own_b, g_first, g_ctx, g_ctx_t3, vec_grad) = first_backward(
         sh,
         doc_lengths,
         doc_order,
-        (q, q_t3, k3, v3, k_t3, ctx_t3, lse, g_ctx, g_ctx_t3, g_first, vec_grad),
+        memory_lengths,
+        (dcq, k_low3, v_low3, g_second, n1, inv1, first_low, mem, ctx, vec, vec_grad),
+        slots_b,
+    )
+    mem_away = add_low(after(mem_parts[1], g_first), mem_got)
+    sum_b = Reduction(send_b, own_b, count, split, True)
+    g_ctx = after(g_ctx, sum_c.send, mem_away)
+    sum_c.step(g_ctx)
+    sum_b.step(g_ctx)
+    mem_got = lax.ppermute(after(mem_parts[2], g_ctx), "seq", swap)
+    mem_far = lax.ppermute(after(mem_away, g_ctx), "seq", [(i, i ^ 2) for i in range(split)])
+    mem_here = mem_parts[3].astype(F32) + mem_got.astype(F32) + mem_far.astype(F32)
+    (grad_halo, dq, sk_low3, sv_low3) = self_backward(
+        sh,
+        doc_lengths,
+        doc_order,
+        (q, q_t3, k3, v3, k_t3, ctx_t3, lse, g_ctx, g_ctx_t3),
+        slots_a,
+    )
+    dq = after(dq, mem_here, sum_c.send, sum_b.send)
+    back = seq_down(after(grad_halo[sh.halo - 1], dq), split)
+    sum_b.step(dq)
+    sum_c.step(dq)
+    (send_a, own_a, grad_own) = self_weights(
+        sh,
+        (dq, sk_low3, sv_low3, g_first, vec_grad),
         toks,
         slots_a,
     )
-    red_a = seq_sum(fsdp_reduce(send_a, own_a2, count), split)
-    back = None
-    for k in range(sh.halo, 0, -1):
-        mine = grad_halo[k - 1]
-        back = seq_down(mine if back is None else add_low(mine, back), split)
+    send_a = after(send_a, sum_b.send, sum_c.send)
+    sum_a = Reduction(send_a, own_a, count, split, True)
+    sum_a.step()
+    sum_b.step(send_a)
+    sum_c.step(send_a)
+    for k in range(sh.halo - 1, 0, -1):
+        back = seq_down(after(add_low(grad_halo[k - 1], back), send_a), split)
+    sum_a.step()
+    ready, held = sum_a.send, (sum_b.send, sum_c.send)
+    while [a for a, _ in sum_a.plan].count("fsdp"):
+        sum_a.step()
+    sum_b.step(ready)
+    ready = sum_a.send
+    sum_a.step(back, *held)
+    sum_b.step(ready)
+    red_a = sum_a.finish()
+    red_b = sum_b.finish()
+    red_c = sum_c.finish()
     input_grad = grad_own + back.astype(F32)
+    memory_grad = seq_rest(mem_here.reshape(split // 4, sh.mem_rows, D), split)[0]
 
     def rows_of(array, start, size):
         return array[start : start + size].astype(F32)
 
-    vec_rows = red_a[3 * n : 3 * n + VROWS].astype(F32)
-    small_grad = lax.dynamic_slice(vec_rows, (jnp.int32(0), fsdp * n), (V_EB, n))
-    flat = vec_rows[V_EB : V_EB + FFB].reshape(FFB * D)
-    expand_bias_grad = lax.dynamic_slice(
-        flat, (fsdp * expand_bias.shape[0],), (expand_bias.shape[0],)
-    )
+    done = finish(sh, red_a, expand_bias.shape[0])
+    small_grad = done[3 : 3 + V_EB]
+    expand_bias_grad = done[3 + V_EB]
+    loss_value = done[4 + V_EB].reshape(())
     expand_grad = jnp.concatenate(
         [rows_of(red_c, (1 + c) * n, n) for c in range(FFB)], axis=1
     )
@@ -1224,10 +1555,10 @@
         loss_value,
         input_grad,
         memory_grad,
-        rows_of(red_a, 0, n),
+        done[0],
         small_grad[V_SQB],
-        rows_of(red_a, n, n),
-        rows_of(red_a, 2 * n, n),
+        done[1],
+        done[2],
         small_grad[V_SVB],
         rows_of(red_b, 0, n),
         small_grad[V_SOB],

time: 368 us -> 279 us (0.76); the launches traced: 370 us -> 277 us
  blocking collectives: 55.9 us -> 0 us
  starting transfers between devices: 87.7 us -> 62.7 us
  local copies, waits for them, and re-layouts: 15.8 us -> 7.23 us
    psum x1 -> x0, blocking collectives: 55.9 us -> none  [shards(): lax.psum((jnp.sum(loss[0]), loss[1, 0]), ('fsdp', 'seq'))]
    ppermute x8 -> x4, waiting for transfers between devices: 18.8 us -> 0.01 us  [seq_up(): return lax.ppermute(a, 'seq', [(i, i + 1) for i in range(count - 1)])]
    ppermute x18 -> x23, waiting for transfers between devices: 47.2 us -> 65.2 us  [the longest x18 42.7 us: step(): got = self.got = lax.ppermute(send, axis, pairs)]
    ppermute x8 -> x4, starting transfers between devices: 31.7 us -> 15.9 us  [seq_up(): return lax.ppermute(a, 'seq', [(i, i + 1) for i in range(count - 1)])]
    ppermute x8 -> x4, starting transfers between devices: 10.7 us -> 5.15 us  [seq_down(): return lax.ppermute(a, 'seq', [(i + 1, i) for i in range(count - 1)])]
    squeeze x3 -> x1, local copies, waits for them, and re-layouts: 4.82 us -> 0.03 us  [shards(): back = seq_down(after(grad_halo[sh.halo - 1], dq), split)]
    ppermute x8 -> x4, waiting for transfers between devices: 10.2 us -> 14.4 us  [seq_down(): return lax.ppermute(a, 'seq', [(i + 1, i) for i in range(count - 1)])]
    ppermute x18 -> x23, starting transfers between devices: 34.3 us -> 31.3 us  [the longest x18 24 us: step(): got = self.got = lax.ppermute(send, axis, pairs)]
  transfers between devices with their start and end apart: 48 -> 45, of which waited for: 16 -> 23; matrix products, arithmetic and copies ran while one was open for 5% -> 4% of each run, Pallas kernels for 8% -> 23%
where the time goes in v2:
time: 279 us; the launch traced here: 277 us
  Pallas kernels  99.9 us (36%)
  waiting for transfers between devices  92.6 us (33%)
  starting transfers between devices  62.7 us (22%)
  other arithmetic  12.8 us (5%)
  local copies, waits for them, and re-layouts  7.23 us (3%)
    pallas_call x10, Pallas kernels, call(): pl.pallas_call(body, name=name, in_specs=specs, out_specs=[VMEM_SPEC] * l...  99.9 us
    ppermute x18, waiting for transfers between devices, step(): got = self.got = lax.ppermute(send, axis, pairs)  42.7 us
    ppermute x18, starting transfers between devices, step(): got = self.got = lax.ppermute(send, axis, pairs)  24 us
    ppermute x4, starting transfers between devices, seq_up(): return lax.ppermute(a, 'seq', [(i, i + 1) for i in range(count - 1)])  15.9 us
    ppermute x4, waiting for transfers between devices, seq_down(): return lax.ppermute(a, 'seq', [(i + 1, i) for i in range(count - 1)])  14.4 us
    ppermute x6, waiting for transfers between devices, fsdp_gather(): have = have + [lax.ppermute(a, 'fsdp', pairs) for a in have]  12.9 us
    ppermute x1, waiting for transfers between devices, shards(): mem_got = lax.ppermute(after(mem_parts[2], g_ctx), 'seq', swap)  10.2 us
    ppermute x6, starting transfers between devices, fsdp_gather(): have = have + [lax.ppermute(a, 'fsdp', pairs) for a in have]  8.61 us
  transfers between devices with their start and end apart: 45, of which 23 were waited for; matrix products, arithmetic and copies ran while one was open for 4% of the time, Pallas kernels for 23%

profile of v2, /device:TPU:0, one launch (start us, length us, event | category | flops | bytes accessed | tf_op | source)
XLA Modules:
  0.0 276.8 jit_solution(227850416089115088)
XLA Ops:
  0.7 5.0 %collective-permute-start = (bf16[512,512]{1,0:T(8,128)(2,1)}, bf16[512,512]{1,0:T(8,128)(2,1)S(1)}, u32[]{:S(2)}, u32[]{:S(2)}) collective-permute-start(bf16[512,512]{1,0:T(8,128)(2,1)} %refs_5_.3), channel_id=1, source_target_pairs={{0,1},{1,2},{2,3},{4,5},{5,6},{6,7},{8,9},{9,10},{10,11},{12,13},{... | collective-permute-start | bytes 1572872 | tf_op jit(solution)/shard_map/ppermute | solution.py:173
  9.8 4.7 %collective-permute-done.3.refs_6_.refs_12_.refs_9_ = bf16[224,512]{1,0:T(8,128)(2,1)S(1)} collective-permute-done((bf16[224,512]{1,0:T(8,128)(2,1)}, bf16[224,512]{1,0:T(8,128)(2,1)S(1)}, u32[]{:S(2)}, u32[]{:S(2)}) %collective-permute-start.3) | collective-permute-done | bytes 229408 | tf_op jit(solution)/shard_map/ppermute | solution.py:101
  16.0 4.5 %collective-permute-done.4.refs_8_.refs_14_.refs_11_ = bf16[224,512]{1,0:T(8,128)(2,1)S(1)} collective-permute-done((bf16[224,512]{1,0:T(8,128)(2,1)S(1)}, bf16[224,512]{1,0:T(8,128)(2,1)S(1)}, u32[]{:S(2)}, u32[]{:S(2)}) %collective-permute-start.4) | collective-permute-done | bytes 229408 | tf_op jit(solution)/shard_map/ppermute | solution.py:101
  23.6 4.2 %collective-permute-start.1 = (bf16[512,512]{1,0:T(8,128)(2,1)}, bf16[512,512]{1,0:T(8,128)(2,1)}, u32[]{:S(2)}, u32[]{:S(2)}) collective-permute-start(bf16[512,512]{1,0:T(8,128)(2,1)} %refs_6_.3), channel_id=1, source_target_pairs={{0,1},{1,2},{2,3},{4,5},{5,6},{6,7},{8,9},{9,10},{10,11},{12,13},{... | collective-permute-start | bytes 1572872 | tf_op jit(solution)/shard_map/ppermute | solution.py:173
  36.4 4.6 %collective-permute-start.7 = (bf16[512,512]{1,0:T(8,128)(2,1)S(1)}, bf16[512,512]{1,0:T(8,128)(2,1)S(1)}, u32[]{:S(2)}, u32[]{:S(2)}) collective-permute-start(bf16[512,512]{1,0:T(8,128)(2,1)S(1)} %collective-permute-done.refs_3_.refs_6_), channel_id=1, source_target_pairs={{0,1},{1,2},{2,3},{4,5},{5,6},{6,7},{8,9},{9,10},{10,11},{12,13},{... | collective-permute-start | bytes 1572872 | tf_op jit(solution)/shard_map/ppermute | solution.py:173
  41.0 9.3 %collective-permute-done.2.refs_8_ = bf16[512,512]{1,0:T(8,128)(2,1)} collective-permute-done((bf16[512,512]{1,0:T(8,128)(2,1)}, bf16[512,512]{1,0:T(8,128)(2,1)}, u32[]{:S(2)}, u32[]{:S(2)}) %collective-permute-start.2) | collective-permute-done | bytes 524320 | tf_op jit(solution)/shard_map/ppermute | solution.py:177
  55.9 8.4 %collective-permute-done.15.refs_11_ = bf16[512,512]{1,0:T(8,128)(2,1)S(1)} collective-permute-done((bf16[512,512]{1,0:T(8,128)(2,1)}, bf16[512,512]{1,0:T(8,128)(2,1)S(1)}, u32[]{:S(2)}, u32[]{:S(2)}) %collective-permute-start.15) | collective-permute-done | bytes 524320 | tf_op jit(solution)/shard_map/ppermute | solution.py:1452
  71.7 11.1 %self_forward.1 = (bf16[512,512]{1,0:T(8,128)(2,1)}, bf16[2,512,256]{2,1,0:T(8,128)(2,1)}, bf16[6,256,512]{2,1,0:T(8,128)(2,1)}, bf16[6,256,512]{2,1,0:T(8,128)(...) custom-call(s32[1,4]{1,0:T(1,128)} %refs_0_.13, ...), custom_call_target="tpu_custom_call" | custom-call | flops 480000000 | bytes 216597 | tf_op jit(solution)/shard_map/self_forward/pallas_call | solution.py:453
  83.6 17.6 %cross_forward.1 = (f32[512,512]{1,0:T(8,128)}, f32[512,1]{1,0:T(8,128)}, bf16[512,512]{1,0:T(8,128)(2,1)}, bf16[512,512]{1,0:T(8,128)(2,1)}, bf16[2,512,256]{2,...) custom-call(s32[1,4]{1,0:T(1,128)} %refs_0_.13, ...), custom_call_target="tpu_custom_call" | custom-call | flops 630000000 | bytes 484025 | tf_op jit(solution)/shard_map/cross_forward/pallas_call | solution.py:453
  104.7 14.5 %feed.1 = (bf16[512,512]{1,0:T(8,128)(2,1)}, f32[512,512]{1,0:T(8,128)S(1)}, bf16[512,512]{1,0:T(8,128)(2,1)S(1)}, bf16[2,512,256]{2,1,0:T(8,128)(2,1)S(1)}, f32...) custom-call(s32[1,4]{1,0:T(1,128)S(1)} %copy-done.18, ...), custom_call_target="tpu_custom_call" | custom-call | flops 420000000 | bytes 348652 | tf_op jit(solution)/shard_map/feed/pallas_call | solution.py:453
  124.7 4.5 %collective-permute-done.22 = bf16[4,576,512]{2,1,0:T(8,128)(2,1)S(1)} collective-permute-done((bf16[4,576,512]{2,1,0:T(8,128)(2,1)S(1)}, bf16[4,576,512]{2,1,0:T(8,128)(2,1)S(1)}, u32[]{:S(2)}, u32[]{:S(2)}) %collective-permute-start.22) | collective-permute-done | bytes 2359328 | tf_op jit(solution)/shard_map/ppermute | solution.py:130
  129.9 5.0 %collective-permute-start.23 = (bf16[2,576,512]{2,1,0:T(8,128)(2,1)S(1)}, bf16[2,576,512]{2,1,0:T(8,128)(2,1)S(1)}, u32[]{:S(2)}, u32[]{:S(2)}) collective-permute-start(bf16[2,576,512]{2,1,0:T(8,128)(2,1)S(1)} %get-tuple-element.223), channel_id=1, source_target_pairs={{0,8},{4,20},{8,0},{12,28},{16,24},{20,4},{24,16},{28,12},{1,9},{5... | collective-permute-start | bytes 3538952 | tf_op jit(solution)/shard_map/ppermute | solution.py:130
  134.9 19.2 %cross_backward.1 = (bf16[2,256,512]{2,1,0:T(8,128)(2,1)}, bf16[2,256,512]{2,1,0:T(8,128)(2,1)}, bf16[2,256,512]{2,1,0:T(8,128)(2,1)}, bf16[2,256,512]{2,1,0:T(8...) custom-call(s32[1,4]{1,0:T(1,128)} %refs_0_.13, ...), custom_call_target="tpu_custom_call" | custom-call | flops 450000000 | bytes 461702 | tf_op jit(solution)/shard_map/cross_backward/pallas_call | solution.py:453
  154.8 11.9 %first_backward.1 = (bf16[4,256,512]{2,1,0:T(8,128)(2,1)}, bf16[4,256,512]{2,1,0:T(8,128)(2,1)}, f32[512,512]{1,0:T(8,128)}, bf16[512,512]{1,0:T(8,128)(2,1)}, b...) custom-call(s32[1,4]{1,0:T(1,128)} %refs_0_.13, s32[1,4]{1,0:T(1,128)} %refs_1_.13, s32[1,4]{1,0:T(1,128)} %refs_2_.8, ...), custom_call_target="tpu_custom_call" | custom-call | flops 180000000 | bytes 423404 | tf_op jit(solution)/shard_map/first_backward/pallas_call | solution.py:453
  174.4 11.4 %self_backward.1 = (bf16[2,512,512]{2,1,0:T(8,128)(2,1)}, bf16[512,512]{1,0:T(8,128)(2,1)}, bf16[6,256,512]{2,1,0:T(8,128)(2,1)}, bf16[6,256,512]{2,1,0:T(8,128)(2,1)}) custom-call(s32[1,4]{1,0:T(1,128)} %refs_0_.13, s32[1,4]{1,0:T(1,128)} %refs_1_.13, bf16[512,512]{1,0:T(8,128)(2,1)} %get-tuple-element.136.refs_2_, ...), custom_call_target="tpu_custom_call" | custom-call | flops 420000000 | bytes 288686 | tf_op jit(solution)/shard_map/self_backward/pallas_call | solution.py:453
  185.8 7.6 %collective-permute-done.28 = bf16[288,512]{1,0:T(8,128)(2,1)S(1)} collective-permute-done((bf16[288,512]{1,0:T(8,128)(2,1)S(1)}, bf16[288,512]{1,0:T(8,128)(2,1)S(1)}, u32[]{:S(2)}, u32[]{:S(2)}) %collective-permute-start.28) | collective-permute-done | bytes 294944 | tf_op jit(solution)/shard_map/ppermute | solution.py:130
  193.5 10.2 %collective-permute-done.26 = bf16[2,256,512]{2,1,0:T(8,128)(2,1)S(1)} collective-permute-done((bf16[2,256,512]{2,1,0:T(8,128)(2,1)}, bf16[2,256,512]{2,1,0:T(8,128)(2,1)S(1)}, u32[]{:S(2)}, u32[]{:S(2)}) %collective-permute-start.26) | collective-permute-done | bytes 524320 | tf_op jit(solution)/shard_map/ppermute | solution.py:1502
  212.6 7.1 %self_weights.1 = (bf16[4,224,512]{2,1,0:T(8,128)(2,1)}, bf16[4,224,512]{2,1,0:T(8,128)(2,1)}, f32[512,512]{1,0:T(8,128)}) custom-call(bf16[512,512]{1,0:T(8,128)(2,1)} %get-tuple-element.186.refs_0_, bf16[6,256,512]{2,1,0:T(8,128)(2,1)} %get-tuple-element.187.refs_1_, bf16[6,256,512]{2,1,0:T(8,128)(2,1)} %get-tuple-element.188.refs_2_, ...), custom_call_target="tpu_custom_call" | custom-call | flops 210000000 | bytes 221511 | tf_op jit(solution)/shard_map/self_weights/pallas_call | solution.py:453
  225.9 4.5 %collective-permute-done.35 = bf16[512,512]{1,0:T(8,128)(2,1)S(1)} collective-permute-done((bf16[512,512]{1,0:T(8,128)(2,1)S(1)}, bf16[512,512]{1,0:T(8,128)(2,1)S(1)}, u32[]{:S(2)}, u32[]{:S(2)}) %collective-permute-start.35) | collective-permute-done | bytes 524320 | tf_op jit(solution)/shard_map/ppermute | solution.py:177
  236.1 5.6 %collective-permute-start.33 = (bf16[2,224,512]{2,1,0:T(8,128)(2,1)S(1)}, bf16[2,224,512]{2,1,0:T(8,128)(2,1)S(1)}, u32[]{:S(2)}, u32[]{:S(2)}) collective-permute-start(bf16[2,224,512]{2,1,0:T(8,128)(2,1)S(1)} %get-tuple-element.227), channel_id=1, source_target_pairs={{0,8},{4,20},{8,0},{12,28},{16,24},{20,4},{24,16},{28,12},{1,9},{5... | collective-permute-start | bytes 1376264 | tf_op jit(solution)/shard_map/ppermute | solution.py:130
  243.4 4.8 %collective-permute-done.33 = bf16[2,224,512]{2,1,0:T(8,128)(2,1)S(1)} collective-permute-done((bf16[2,224,512]{2,1,0:T(8,128)(2,1)S(1)}, bf16[2,224,512]{2,1,0:T(8,128)(2,1)S(1)}, u32[]{:S(2)}, u32[]{:S(2)}) %collective-permute-start.33) | collective-permute-done | bytes 458784 | tf_op jit(solution)/shard_map/ppermute | solution.py:130
  250.2 4.1 %collective-permute-done.34 = bf16[1,224,512]{2,1,0:T(8,128)(2,1)S(1)} collective-permute-done((bf16[1,224,512]{2,1,0:T(8,128)(2,1)S(1)}, bf16[1,224,512]{2,1,0:T(8,128)(2,1)S(1)}, u32[]{:S(2)}, u32[]{:S(2)}) %collective-permute-start.34) | collective-permute-done | bytes 229408 | tf_op jit(solution)/shard_map/ppermute | solution.py:130
  260.7 6.1 %collective-permute-done.43 = bf16[128,512]{1,0:T(8,128)(2,1)S(1)} collective-permute-done((bf16[128,512]{1,0:T(8,128)(2,1)S(1)}, bf16[128,512]{1,0:T(8,128)(2,1)S(1)}, u32[]{:S(2)}, u32[]{:S(2)}) %collective-permute-start.43) | collective-permute-done | bytes 131104 | tf_op jit(solution)/shard_map/ppermute | solution.py:130
  269.0 3.8 %collective-permute-done.44 = bf16[128,512]{1,0:T(8,128)(2,1)S(1)} collective-permute-done((bf16[128,512]{1,0:T(8,128)(2,1)S(1)}, bf16[128,512]{1,0:T(8,128)(2,1)S(1)}, u32[]{:S(2)}, u32[]{:S(2)}) %collective-permute-start.44) | collective-permute-done | bytes 131104 | tf_op jit(solution)/shard_map/ppermute | solution.py:130
  (182 shorter events, 85.5 us)
Async XLA Ops:
  0.7 19.9 %collective-permute-start = (bf16[512,512]{1,0:T(8,128)(2,1)}, bf16[512,512]{1,0:T(8,128)(2,1)S(1)}, u32[]{:S(2)}, u32[]{:S(2)}) collective-permute-start(bf16[512,512]{1,0:T(8,128)(2,1)} %refs_5_.3), channel_id=1, source_target_pairs={{0,1},{1,2},{2,3},{4,5},{5,6},{6,7},{8,9},{9,10},{10,11},{12,13},{... | collective-permute-start | bytes 1572872 | tf_op jit(solution)/shard_map/ppermute | solution.py:173
  20.5 13.5 %collective-permute-start.5 = (bf16[832,512]{1,0:T(8,128)(2,1)}, bf16[832,512]{1,0:T(8,128)(2,1)S(1)}, u32[]{:S(2)}, u32[]{:S(2)}) collective-permute-start(bf16[832,512]{1,0:T(8,128)(2,1)} %get-tuple-element.128.refs_13_.refs_6_.refs_12_.refs_14_), channel_id=1, source_target_pairs={{0,8},{4,20},{8,0},{12,28},{16,24},{20,4},{24,16},{28,12},{1,9},{5... | collective-permute-start | bytes 2555912 | tf_op jit(solution)/shard_map/ppermute | solution.py:101
  31.4 23.7 %collective-permute-start.6 = (bf16[832,512]{1,0:T(8,128)(2,1)}, bf16[832,512]{1,0:T(8,128)(2,1)S(1)}, u32[]{:S(2)}, u32[]{:S(2)}) collective-permute-start(bf16[832,512]{1,0:T(8,128)(2,1)} %get-tuple-element.128.refs_13_.refs_6_.refs_12_.refs_14_), channel_id=1, source_target_pairs={{0,16},{4,12},{8,24},{12,4},{16,0},{20,28},{24,8},{28,20},{1,17},{... | collective-permute-start | bytes 2555912 | tf_op jit(solution)/shard_map/ppermute | solution.py:101
  32.9 22.3 %collective-permute-start.18 = (bf16[832,512]{1,0:T(8,128)(2,1)}, bf16[832,512]{1,0:T(8,128)(2,1)S(1)}, u32[]{:S(2)}, u32[]{:S(2)}) collective-permute-start(bf16[832,512]{1,0:T(8,128)(2,1)} %get-tuple-element.128.refs_13_.refs_6_.refs_12_.refs_14_), channel_id=1, source_target_pairs={{0,4},{4,0},{8,12},{12,8},{16,20},{20,16},{24,28},{28,24},{1,5},{5... | collective-permute-start | bytes 2555912 | tf_op jit(solution)/shard_map/ppermute | solution.py:103
  34.1 21.6 %collective-permute-start.17 = (bf16[832,512]{1,0:T(8,128)(2,1)S(1)}, bf16[832,512]{1,0:T(8,128)(2,1)S(1)}, u32[]{:S(2)}, u32[]{:S(2)}) collective-permute-start(bf16[832,512]{1,0:T(8,128)(2,1)S(1)} %collective-permute-done.5.refs_14_.refs_7_.refs_13_.refs_15_), channel_id=1, source_target_pairs={{0,16},{4,12},{8,24},{12,4},{16,0},{20,28},{24,8},{28,20},{1,17},{... | collective-permute-start | bytes 2555912 | tf_op jit(solution)/shard_map/ppermute | solution.py:101
  35.0 15.2 %collective-permute-start.2 = (bf16[512,512]{1,0:T(8,128)(2,1)}, bf16[512,512]{1,0:T(8,128)(2,1)}, u32[]{:S(2)}, u32[]{:S(2)}) collective-permute-start(bf16[512,512]{1,0:T(8,128)(2,1)} %refs_6_.3), channel_id=1, source_target_pairs={{1,0},{2,1},{3,2},{5,4},{6,5},{7,6},{9,8},{10,9},{11,10},{13,12},{... | collective-permute-start | bytes 1572872 | tf_op jit(solution)/shard_map/ppermute | solution.py:177
  36.4 17.4 %collective-permute-start.7 = (bf16[512,512]{1,0:T(8,128)(2,1)S(1)}, bf16[512,512]{1,0:T(8,128)(2,1)S(1)}, u32[]{:S(2)}, u32[]{:S(2)}) collective-permute-start(bf16[512,512]{1,0:T(8,128)(2,1)S(1)} %collective-permute-done.refs_3_.refs_6_), channel_id=1, source_target_pairs={{0,1},{1,2},{2,3},{4,5},{5,6},{6,7},{8,9},{9,10},{10,11},{12,13},{... | collective-permute-start | bytes 1572872 | tf_op jit(solution)/shard_map/ppermute | solution.py:173
  50.2 14.1 %collective-permute-start.15 = (bf16[512,512]{1,0:T(8,128)(2,1)}, bf16[512,512]{1,0:T(8,128)(2,1)S(1)}, u32[]{:S(2)}, u32[]{:S(2)}) collective-permute-start(bf16[512,512]{1,0:T(8,128)(2,1)} %refs_6_.3), channel_id=1, source_target_pairs={{0,3},{4,7},{8,11},{12,15},{16,19},{20,23},{24,27},{28,31}} | collective-permute-start | bytes 1572872 | tf_op jit(solution)/shard_map/ppermute | solution.py:1452
  53.8 15.8 %collective-permute-start.16 = (bf16[512,512]{1,0:T(8,128)(2,1)}, bf16[512,512]{1,0:T(8,128)(2,1)S(1)}, u32[]{:S(2)}, u32[]{:S(2)}) collective-permute-start(bf16[512,512]{1,0:T(8,128)(2,1)} %refs_6_.3), channel_id=1, source_target_pairs={{3,0},{7,4},{11,8},{15,12},{19,16},{23,20},{27,24},{31,28}} | collective-permute-start | bytes 1572872 | tf_op jit(solution)/shard_map/ppermute | solution.py:1453
  55.1 28.4 %collective-permute-start.19 = (bf16[832,512]{1,0:T(8,128)(2,1)S(1)}, bf16[832,512]{1,0:T(8,128)(2,1)}, u32[]{:S(2)}, u32[]{:S(2)}) collective-permute-start(bf16[832,512]{1,0:T(8,128)(2,1)S(1)} %collective-permute-done.5.refs_14_.refs_7_.refs_13_.refs_15_), channel_id=1, source_target_pairs={{0,4},{4,0},{8,12},{12,8},{16,20},{20,16},{24,28},{28,24},{1,5},{5... | collective-permute-start | bytes 2555912 | tf_op jit(solution)/shard_map/ppermute | solution.py:103
  55.2 28.3 %collective-permute-start.20 = (bf16[832,512]{1,0:T(8,128)(2,1)S(1)}, bf16[832,512]{1,0:T(8,128)(2,1)}, u32[]{:S(2)}, u32[]{:S(2)}) collective-permute-start(bf16[832,512]{1,0:T(8,128)(2,1)S(1)} %collective-permute-done.6.refs_15_.refs_8_.refs_14_.refs_16_), channel_id=1, source_target_pairs={{0,4},{4,0},{8,12},{12,8},{16,20},{20,16},{24,28},{28,24},{1,5},{5... | collective-permute-start | bytes 2555912 | tf_op jit(solution)/shard_map/ppermute | solution.py:103
  55.7 27.8 %collective-permute-start.21 = (bf16[832,512]{1,0:T(8,128)(2,1)S(1)}, bf16[832,512]{1,0:T(8,128)(2,1)}, u32[]{:S(2)}, u32[]{:S(2)}) collective-permute-start(bf16[832,512]{1,0:T(8,128)(2,1)S(1)} %collective-permute-done.17.refs_16_.refs_9_.refs_15_.refs_17_), channel_id=1, source_target_pairs={{0,4},{4,0},{8,12},{12,8},{16,20},{20,16},{24,28},{28,24},{1,5},{5... | collective-permute-start | bytes 2555912 | tf_op jit(solution)/shard_map/ppermute | solution.py:103
  64.3 18.6 %collective-permute-start.13 = (bf16[512,512]{1,0:T(8,128)(2,1)}, bf16[512,512]{1,0:T(8,128)(2,1)}, u32[]{:S(2)}, u32[]{:S(2)}) collective-permute-start(bf16[512,512]{1,0:T(8,128)(2,1)} %collective-permute-done.1.refs_7_), channel_id=1, source_target_pairs={{0,1},{1,2},{2,3},{4,5},{5,6},{6,7},{8,9},{9,10},{10,11},{12,13},{... | collective-permute-start | bytes 1572872 | tf_op jit(solution)/shard_map/ppermute | solution.py:173
  129.9 24.6 %collective-permute-start.23 = (bf16[2,576,512]{2,1,0:T(8,128)(2,1)S(1)}, bf16[2,576,512]{2,1,0:T(8,128)(2,1)S(1)}, u32[]{:S(2)}, u32[]{:S(2)}) collective-permute-start(bf16[2,576,512]{2,1,0:T(8,128)(2,1)S(1)} %get-tuple-element.223), channel_id=1, source_target_pairs={{0,8},{4,20},{8,0},{12,28},{16,24},{20,4},{24,16},{28,12},{1,9},{5... | collective-permute-start | bytes 3538952 | tf_op jit(solution)/shard_map/ppermute | solution.py:130
  154.1 13.3 %collective-permute-start.25 = (bf16[2,256,512]{2,1,0:T(8,128)(2,1)}, bf16[2,256,512]{2,1,0:T(8,128)(2,1)}, u32[]{:S(2)}, u32[]{:S(2)}) collective-permute-start(bf16[2,256,512]{2,1,0:T(8,128)(2,1)} %get-tuple-element.174), channel_id=1, source_target_pairs={{0,1},{1,0},{2,3},{3,2},{4,5},{5,4},{6,7},{7,6},{8,9},{9,8},{10,11... | collective-permute-start | bytes 1572872 | tf_op jit(solution)/shard_map/ppermute | solution.py:1488
  154.7 14.7 %collective-permute-start.24 = (bf16[1,576,512]{2,1,0:T(8,128)(2,1)S(1)}, bf16[1,576,512]{2,1,0:T(8,128)(2,1)S(1)}, u32[]{:S(2)}, u32[]{:S(2)}) collective-permute-start(bf16[1,576,512]{2,1,0:T(8,128)(2,1)S(1)} %add_convert_fusion.4), channel_id=1, source_target_pairs={{0,16},{4,12},{8,24},{12,4},{16,0},{20,28},{24,8},{28,20},{1,17},{... | collective-permute-start | bytes 1769480 | tf_op jit(solution)/shard_map/ppermute | solution.py:130
  169.7 35.3 %collective-permute-start.29 = (bf16[4,256,512]{2,1,0:T(8,128)(2,1)}, bf16[4,256,512]{2,1,0:T(8,128)(2,1)S(1)}, u32[]{:S(2)}, u32[]{:S(2)}) collective-permute-start(bf16[4,256,512]{2,1,0:T(8,128)(2,1)} %get-tuple-element.185), channel_id=1, source_target_pairs={{0,4},{4,0},{8,12},{12,8},{16,20},{20,16},{24,28},{28,24},{1,5},{5... | collective-permute-start | bytes 3145736 | tf_op jit(solution)/shard_map/ppermute | solution.py:130
  172.3 21.1 %collective-permute-start.28 = (bf16[288,512]{1,0:T(8,128)(2,1)S(1)}, bf16[288,512]{1,0:T(8,128)(2,1)S(1)}, u32[]{:S(2)}, u32[]{:S(2)}) collective-permute-start(bf16[288,512]{1,0:T(8,128)(2,1)S(1)} %select_bitcast_fusion), channel_id=1, source_target_pairs={{0,1},{1,0},{2,3},{3,2},{4,5},{5,4},{6,7},{7,6},{8,9},{9,8},{10,11... | collective-permute-start | bytes 884744 | tf_op jit(solution)/shard_map/ppermute | solution.py:130
  172.3 31.5 %collective-permute-start.26 = (bf16[2,256,512]{2,1,0:T(8,128)(2,1)}, bf16[2,256,512]{2,1,0:T(8,128)(2,1)S(1)}, u32[]{:S(2)}, u32[]{:S(2)}) collective-permute-start(bf16[2,256,512]{2,1,0:T(8,128)(2,1)} %get-tuple-element.180), channel_id=1, source_target_pairs={{0,1},{1,0},{2,3},{3,2},{4,5},{5,4},{6,7},{7,6},{8,9},{9,8},{10,11... | collective-permute-start | bytes 1572872 | tf_op jit(solution)/shard_map/ppermute | solution.py:1502
  174.3 29.4 %collective-permute-start.27 = (bf16[2,256,512]{2,1,0:T(8,128)(2,1)}, bf16[2,256,512]{2,1,0:T(8,128)(2,1)S(1)}, u32[]{:S(2)}, u32[]{:S(2)}) collective-permute-start(bf16[2,256,512]{2,1,0:T(8,128)(2,1)} %add_convert_fusion.7), channel_id=1, source_target_pairs={{0,2},{1,3},{2,0},{3,1},{4,6},{5,7},{6,4},{7,5},{8,10},{9,11},{10,... | collective-permute-start | bytes 1572872 | tf_op jit(solution)/shard_map/ppermute | solution.py:1503
  206.3 15.9 %collective-permute-start.31 = (bf16[288,512]{1,0:T(8,128)(2,1)S(1)}, bf16[288,512]{1,0:T(8,128)(2,1)}, u32[]{:S(2)}, u32[]{:S(2)}) collective-permute-start(bf16[288,512]{1,0:T(8,128)(2,1)S(1)} %fusion.1), channel_id=1, source_target_pairs={{0,2},{1,3},{2,0},{3,1},{4,6},{5,7},{6,4},{7,5},{8,10},{9,11},{10,... | collective-permute-start | bytes 884744 | tf_op jit(solution)/shard_map/ppermute | solution.py:130
  207.5 15.8 %collective-permute-start.30 = (bf16[2,256,512]{2,1,0:T(8,128)(2,1)}, bf16[2,256,512]{2,1,0:T(8,128)(2,1)S(1)}, u32[]{:S(2)}, u32[]{:S(2)}) collective-permute-start(bf16[2,256,512]{2,1,0:T(8,128)(2,1)} %get-tuple-element.192), channel_id=1, source_target_pairs={{0,8},{4,20},{8,0},{12,28},{16,24},{20,4},{24,16},{28,12},{1,9},{5... | collective-permute-start | bytes 1572872 | tf_op jit(solution)/shard_map/ppermute | solution.py:130
  211.3 19.2 %collective-permute-start.35 = (bf16[512,512]{1,0:T(8,128)(2,1)S(1)}, bf16[512,512]{1,0:T(8,128)(2,1)S(1)}, u32[]{:S(2)}, u32[]{:S(2)}) collective-permute-start(bf16[512,512]{1,0:T(8,128)(2,1)S(1)} %slice_bitcast_fusion), channel_id=1, source_target_pairs={{1,0},{2,1},{3,2},{5,4},{6,5},{7,6},{9,8},{10,9},{11,10},{13,12},{... | collective-permute-start | bytes 1572872 | tf_op jit(solution)/shard_map/ppermute | solution.py:177
  230.6 18.0 %collective-permute-start.36 = (bf16[512,512]{1,0:T(8,128)(2,1)S(1)}, bf16[512,512]{1,0:T(8,128)(2,1)S(1)}, u32[]{:S(2)}, u32[]{:S(2)}) collective-permute-start(bf16[512,512]{1,0:T(8,128)(2,1)S(1)} %fusion), channel_id=1, source_target_pairs={{1,0},{2,1},{3,2},{5,4},{6,5},{7,6},{9,8},{10,9},{11,10},{13,12},{... | collective-permute-start | bytes 1572872 | tf_op jit(solution)/shard_map/ppermute | solution.py:177
  (59 other events, 740.9 us)

commit v3 on v2

--- a/solution.py
+++ b/solution.py
@@ -18,7 +18,6 @@
 BF = jnp.bfloat16
 F32 = jnp.float32
 VMEM_BYTES = 60 * 1024 * 1024
-SHARED_BYTES = 36 * 1024 * 1024
 FLOPS_RATE = 3e13
 
 (
@@ -94,12 +93,16 @@
     return [(i, i ^ orders[i & 1][index]) for i in range(count)]
 
 
-def fsdp_gather(own, count):
+def fsdp_gather_parts(own, count):
     have = [own]
     for index in range(len(chip_steps(count)[0])):
         pairs = step_pairs(count, index)
         have = have + [lax.ppermute(a, "fsdp", pairs) for a in have]
-    swap = [(i, i ^ 1) for i in range(count)]
+    return have, [(i, i ^ 1) for i in range(count)]
+
+
+def fsdp_gather(own, count):
+    have, swap = fsdp_gather_parts(own, count)
     return have + [lax.ppermute(a, "fsdp", swap) for a in have]
 
 
@@ -111,43 +114,57 @@
     return lax.optimization_barrier((value, *others))[0]
 
 
+def sum_low(parts):
+    total = parts[0].astype(F32)
+    for part in parts[1:]:
+        total = total + part.astype(F32)
+    return total.astype(BF)
+
+
 class Reduction:
-    def __init__(self, send, own, count, split, halves):
-        self.count, self.split, self.halves = count, split, halves
-        self.send, self.own = send, own
+    def __init__(self, send, own, count, split):
+        self.send, self.parts = send, [own]
         self.odd = (lax.axis_index("seq") % 2) == 1
         self.got = None
         self.plan = [("fsdp", [(i, i ^ 1) for i in range(count)])]
         for index in range(len(chip_steps(count)[0])):
             self.plan.append(("fsdp", step_pairs(count, index)))
         bits = [1 << k for k in range(split.bit_length() - 1)]
-        for bit in bits + [1] * halves:
+        for bit in bits + [1]:
             self.plan.append(("seq", [(i, i ^ bit) for i in range(split)]))
 
-    def step(self, *others):
+    def start(self, *others):
         send = after(self.send, *others) if others else self.send
-        axis, pairs = self.plan.pop(0)
-        got = self.got = lax.ppermute(send, axis, pairs)
-        left = sum(1 for a, _ in self.plan if a == "fsdp")
-        if axis == "fsdp" and left > 0:
-            half = self.own.shape[0] // 2
-            self.send = add_low(self.own[half:], got[half:])
-            self.own = add_low(self.own[:half], got[:half])
-        elif axis == "fsdp":
-            total = add_low(self.own[0], got[0])
-            if self.halves:
+        self.axis, pairs = self.plan.pop(0)
+        self.got = lax.ppermute(send, self.axis, pairs)
+
+    def end(self, *others):
+        if others:
+            self.parts[0] = after(self.parts[0], *others)
+        left = sum(1 for axis, _ in self.plan if axis == "fsdp")
+        if self.axis == "fsdp":
+            self.parts.append(self.got)
+            if left > 0:
+                half = self.got.shape[0] // 2
+                self.send = sum_low([part[half:] for part in self.parts])
+                self.parts = [part[:half] for part in self.parts]
+            else:
+                total = sum_low([part[0] for part in self.parts])
                 half = total.shape[0] // 2
                 self.send = jnp.where(self.odd, total[:half], total[half:])
-                self.own = jnp.where(self.odd, total[half:], total[:half])
-            else:
-                self.send = self.own = total
-        elif self.halves and not self.plan:
+                self.parts = [jnp.where(self.odd, total[half:], total[:half])]
+        elif self.plan:
+            self.send = sum_low([self.parts[0], self.got])
+            self.parts = [self.send]
+        else:
+            mine, got = self.parts[0], self.got
             self.send = jnp.where(
-                self.odd, jnp.concatenate([got, self.own]), jnp.concatenate([self.own, got])
+                self.odd, jnp.concatenate([got, mine]), jnp.concatenate([mine, got])
             )
-        else:
-            self.send = self.own = add_low(self.own, got)
-        return self
+
+    def step(self, *others):
+        self.start(*others)
+        self.end()
 
     def finish(self):
         while self.plan:
@@ -209,6 +226,44 @@
 
 def wait_all(target, sem):
     pltpu.make_async_copy(target, target, sem).wait()
+
+
+def tile_copies(t, sources, targets, sems):
+    return [
+        pltpu.make_async_copy(source.at[t], target.at[t], sems.at[i, t])
+        for i, (source, target) in enumerate(zip(sources, targets))
+    ]
+
+
+def start_mems(sh, mems, target, sems, wanted):
+    z = lax.axis_index("seq")
+    tiles_per = sh.mem_rows // TILE
+
+    def place(source, shard):
+        for i in range(tiles_per):
+            t = shard * tiles_per + i
+
+            @pl.when(wanted(t))
+            def _(i=i, t=t):
+                pltpu.make_async_copy(
+                    source.at[pl.ds(i * TILE, TILE)], target.at[t], sems.at[t]
+                ).start()
+
+    place(mems[0], z)
+    for k in range(1, sh.split):
+        up, down = mems[2 * k - 1], mems[2 * k]
+
+        @pl.when(z >= k)
+        def _(up=up, k=k):
+            place(up, z - k)
+
+        @pl.when(z + k < sh.split)
+        def _(down=down, k=k):
+            place(down, z + k)
+
+
+def wait_mem(target, t, sems):
+    pltpu.make_async_copy(target.at[t], target.at[t], sems.at[t]).wait()
 
 
 def put_grad(sh, full, n, row, send_ref, own_ref):
@@ -445,7 +500,7 @@
     return jax.ShapeDtypeStruct(dims, dtype)
 
 
-def call(body, name, inputs, specs, outs, scratch, micros, vmem=VMEM_BYTES):
+def call(body, name, inputs, specs, outs, scratch, micros, vmem=VMEM_BYTES, out_specs=None):
     moved = sum(a.size * a.dtype.itemsize for a in (*inputs, *outs))
     cost = pl.CostEstimate(
         flops=int(micros * 1e-6 * FLOPS_RATE), transcendentals=0, bytes_accessed=moved // 50
@@ -454,7 +509,7 @@
         body,
         name=name,
         in_specs=specs,
-        out_specs=[VMEM_SPEC] * len(outs),
+        out_specs=out_specs or [VMEM_SPEC] * len(outs),
         out_shape=outs,
         scratch_shapes=scratch,
         cost_estimate=cost,
@@ -667,33 +722,17 @@
     mems = refs[3 : 3 + 2 * split - 1]
     slots = refs[2 + 2 * split : 2 + 2 * split + count]
     outs = refs[2 + 2 * split + count :]
-    (n1, inv1, first_low, q_ref, q_t3, mk3, mv3, mk_t3, cctx, cctx_t3, lse, mem) = outs[:12]
-    (wo, wcq, wck, wcv, mv_t3, q_t, bias, m_ref, l_ref, acc, bounds, sems) = outs[12:]
-    z = lax.axis_index("seq")
+    (n1, inv1, first_low, q_ref, q_t3, *kept, cctx, cctx_t3, lse) = outs[:11]
+    (wo, wcq, wck, wcv, mem, mk3, mv3, mk_t3, mv_t3, q_t, bias, m_ref, l_ref, acc) = outs[11:25]
+    (bounds, sems, mem_sems, tile_sems) = outs[25:]
     for i, w in enumerate((wo, wcq, wck, wcv)):
         start_weight(sh, slots, i * n, n, w, sems.at[i])
-    own = mems[0]
-    tiles_per = sh.mem_rows // TILE
-
-    def place(source, shard):
-        for i in range(tiles_per):
-            pltpu.make_async_copy(
-                source.at[pl.ds(i * TILE, TILE)], mem.at[shard * tiles_per + i], sems.at[4]
-            ).start()
-
-    place(own, z)
-    for k in range(1, split):
-        up, down = mems[2 * k - 1], mems[2 * k]
-
-        @pl.when(z >= k)
-        def _(up=up, k=k):
-            place(up, z - k)
-
-        @pl.when(z + k < split)
-        def _(down=down, k=k):
-            place(down, z + k)
+
+    def wanted(t):
+        return touched_tile(sh, lens, order, mlens, t, bounds, False)
 
     slot_bounds(lens, order, bounds)
+    start_mems(sh, mems, mem, mem_sems, wanted)
     spread_zero(q_t)
     wait_all(wo, sems.at[0])
     wait_all(wcq, sems.at[1])
@@ -715,11 +754,11 @@
     lax.fori_loop(0, rows // TILE, own_rows, 0)
     wait_all(wck, sems.at[2])
     wait_all(wcv, sems.at[3])
-    wait_all(mem, sems.at[4])
 
     def mem_tile(t, carry):
-        @pl.when(touched_tile(sh, lens, order, mlens, t, bounds, False))
+        @pl.when(wanted(t))
         def _():
+            wait_mem(mem, t, mem_sems)
             x = mem[t]
             key = mm(x, wck[...]).astype(BF)
             val = (mm(x, wcv[...]) + vec[V_CVB : V_CVB + 1, :]).astype(BF)
@@ -727,6 +766,8 @@
             mv3[t] = val
             mk_t3[t] = key.T
             mv_t3[t] = val.T
+            for copy in tile_copies(t, (mk3, mv3, mk_t3), kept, tile_sems):
+                copy.start()
 
         return carry
 
@@ -751,6 +792,16 @@
 
     lax.fori_loop(0, sh.q_blocks, block, 0)
 
+    def settle(t, carry):
+        @pl.when(wanted(t))
+        def _():
+            for copy in tile_copies(t, (mk3, mv3, mk_t3), kept, tile_sems):
+                copy.wait()
+
+        return carry
+
+    lax.fori_loop(0, sh.m_blocks, settle, 0)
+
 
 def cross_forward(sh, lens, order, mlens, tok, ctx, vec, mems, slots):
     nm, nq = sh.m_blocks, sh.q_blocks
@@ -766,13 +817,16 @@
         shape((sh.rows, D), BF),
         shape((nq, D, TILE), F32),
         shape((nq, HEADS, TILE), F32),
-        shape((nm, TILE, D), BF),
     ]
     scratch = [
         pltpu.VMEM((D, D), BF),
         pltpu.VMEM((D, D), BF),
         pltpu.VMEM((D, D), BF),
         pltpu.VMEM((D, D), BF),
+        pltpu.VMEM((nm, TILE, D), BF),
+        pltpu.VMEM((nm, TILE, D), BF),
+        pltpu.VMEM((nm, TILE, D), BF),
+        pltpu.VMEM((nm, D, TILE), BF),
         pltpu.VMEM((nm, D, TILE), BF),
         pltpu.VMEM((HEADS, 2 * HDIM, TILE), BF),
         pltpu.VMEM((TILE, TILE), F32),
@@ -780,7 +834,9 @@
         pltpu.VMEM((HEADS, TILE), F32),
         pltpu.VMEM((D, TILE), F32),
         pltpu.SMEM((4, DOCS), jnp.int32),
-        pltpu.SemaphoreType.DMA((5,)),
+        pltpu.SemaphoreType.DMA((4,)),
+        pltpu.SemaphoreType.DMA((nm,)),
+        pltpu.SemaphoreType.DMA((3, nm)),
     ]
     specs = [SMEM_SPEC] * 3 + [VMEM_SPEC] * 3 + [ANY_SPEC] * (len(mems) + len(slots))
     return call(
@@ -791,6 +847,7 @@
         outs,
         scratch,
         21,
+        out_specs=[VMEM_SPEC] * 5 + [ANY_SPEC] * 3 + [VMEM_SPEC] * 3,
     )
 
 
@@ -799,9 +856,9 @@
     n1, cctx, targets, vec = refs[:4]
     slots = refs[4 : 4 + count]
     outs = refs[4 + count :]
-    (final_ref, g_second, g_cc, g_cc_t3, vec_grad) = outs[:5]
-    (sec_low, hid, feed_low, g_exp, g_cross) = outs[5:10]
-    (wco, w1, w2, n2, dact, loss, sems) = outs[10:]
+    (final_ref, g_second, g_cc, g_cc_t3, vec_grad, g_send, g_own) = outs[:7]
+    (sec_low, hid, feed_low, g_exp, g_cross) = outs[7:12]
+    (wco, w1, w2, n2, dact, loss, stage, stage2, sems) = outs[12:]
     z = lax.axis_index("seq")
     start_weight(sh, slots, 4 * n, n, wco, sems.at[0])
     for c in range(FFB):
@@ -833,13 +890,15 @@
         low = second.astype(BF)
         sec_low[r, :] = low
         feed = second + vec[V_CB : V_CB + 1, :]
-        for c in range(FFB):
-            e = mm(low, w1[c]) + vec[V_EB + c : V_EB + c + 1, :]
-            sg = jax.nn.sigmoid(e)
-            h = (e * sg).astype(BF)
-            hid[c, r, :] = h
-            dact[c] = sg * (1.0 + e * (1.0 - sg))
-            feed = feed + mm(h, w2[pl.ds(c * D, D), :])
+        wide = range(FFB)
+        es = [mm(low, w1[c]) + vec[V_EB + c : V_EB + c + 1, :] for c in wide]
+        sgs = [jax.nn.sigmoid(e) for e in es]
+        hs = [(e * sg).astype(BF) for e, sg in zip(es, sgs)]
+        for c in wide:
+            hid[c, r, :] = hs[c]
+            dact[c] = sgs[c] * (1.0 + es[c] * (1.0 - sgs[c]))
+        for c in wide:
+            feed = feed + mm(hs[c], w2[pl.ds(c * D, D), :])
         normal3, inv3 = norm_stats(feed)
         final = normal3 * vec[V_G3 : V_G3 + 1, :] + vec[V_S3 : V_S3 + 1, :]
         final_ref[r, :] = final.astype(BF)
@@ -855,11 +914,12 @@
         feed_low[r, :] = g_low
         add_vec(V_CB, col_sum(g_low))
         total = g_third
-        for c in range(FFB):
-            ge = (mm_nt(g_low, w2[pl.ds(c * D, D), :]) * dact[c]).astype(BF)
-            g_exp[c, r, :] = ge
-            add_vec(V_EB + c, col_sum(ge))
-            total = total + mm_nt(ge, w1[c])
+        ges = [(mm_nt(g_low, w2[pl.ds(c * D, D), :]) * dact[c]).astype(BF) for c in wide]
+        for c in wide:
+            total = total + mm_nt(ges[c], w1[c])
+        for c in wide:
+            g_exp[c, r, :] = ges[c]
+            add_vec(V_EB + c, col_sum(ges[c]))
         normal2 = n2[...]
         add_vec(V_G2, col_sum(total * normal2))
         add_vec(V_S2, col_sum(total))
@@ -881,11 +941,6 @@
     error_sum = jnp.sum(loss[0:1, :], axis=1, keepdims=True)
     vec_grad[V_LOSS : V_LOSS + 1, :] = digits(error_sum, bits)
     vec_grad[V_LIVE : V_LIVE + 1, :] = digits(jnp.full((1, 1), live_count.astype(F32)), bits)
-
-
-def feed_weights_kernel(sh, cctx, sec_low, hid, feed_low, g_exp, g_cross, *outs):
-    n, wide = sh.piece, sh.wide_piece
-    (g_send, g_own, stage, stage2) = outs
     stage[...] = mm_tn(cctx[...], g_cross[...]).astype(BF)
     put_grad(sh, stage, n, 0, g_send, g_own)
     for c in range(FFB):
@@ -896,45 +951,32 @@
     put_grad(sh, stage2, wide, 5 * n, g_send, g_own)
 
 
-def feed_weights(sh, arrays):
-    block = 5 * sh.piece + sh.wide_piece
-    outs = [
-        shape((sh.count // 2, block, D), BF),
-        shape((sh.count // 2, block, D), BF),
-    ]
-    return call(
-        lambda *refs: feed_weights_kernel(sh, *refs),
-        "feed_weights",
-        arrays,
-        [VMEM_SPEC] * len(arrays),
-        outs,
-        [pltpu.VMEM((D, D), BF), pltpu.VMEM((FFB * D, D), BF)],
-        6,
-        SHARED_BYTES,
-    )
-
-
 def feed(sh, lens, order, n1, cctx, targets, vec, slots):
     rows, nq = sh.rows, sh.q_blocks
+    block = 5 * sh.piece + sh.wide_piece
     outs = [
         shape((rows, D), BF),
         shape((rows, D), F32),
         shape((rows, D), BF),
         shape((nq, D, TILE), BF),
         shape((VROWS, D), F32),
-        shape((rows, D), BF),
-        shape((FFB, rows, D), BF),
-        shape((rows, D), BF),
-        shape((FFB, rows, D), BF),
-        shape((rows, D), BF),
+        shape((sh.count // 2, block, D), BF),
+        shape((sh.count // 2, block, D), BF),
     ]
     scratch = [
+        pltpu.VMEM((rows, D), BF),
+        pltpu.VMEM((FFB, rows, D), BF),
+        pltpu.VMEM((rows, D), BF),
+        pltpu.VMEM((FFB, rows, D), BF),
+        pltpu.VMEM((rows, D), BF),
         pltpu.VMEM((D, D), BF),
         pltpu.VMEM((FFB, D, D), BF),
         pltpu.VMEM((FFB * D, D), BF),
         pltpu.VMEM((TILE, D), F32),
         pltpu.VMEM((FFB, TILE, D), F32),
         pltpu.VMEM((8, D), F32),
+        pltpu.VMEM((D, D), BF),
+        pltpu.VMEM((FFB * D, D), BF),
         pltpu.SemaphoreType.DMA((6,)),
     ]
     specs = [SMEM_SPEC] * 2 + [VMEM_SPEC] * 4 + [ANY_SPEC] * len(slots)
@@ -945,8 +987,7 @@
         specs,
         outs,
         scratch,
-        14,
-        SHARED_BYTES,
+        17,
     )
 
 
@@ -959,27 +1000,44 @@
 
 def cross_backward_kernel(sh, lens, order, mlens, *refs):
     count, n = sh.count, sh.piece
-    (q_ref, q_t3, mk3, mv3, mk_t3, cctx_t3, lse, g_cc, g_cc_t3) = refs[:9]
+    (q_ref, q_t3, *kept, cctx_t3, lse, g_cc, g_cc_t3) = refs[:9]
     slots = refs[9 : 9 + count]
     outs = refs[9 + count :]
     mem_parts = outs[:4]
-    (dq, k_low3, v_low3) = outs[4:7]
-    (wck, wcv, q_t, g_t, q_m, g_m, delta, bias, dk, dv, dq_t, bounds, sems) = outs[7:]
+    (dq, *low_out) = outs[4:7]
+    (wck, wcv, q_t, g_t, q_m, g_m, delta, bias, dk, dv, dq_t) = outs[7:18]
+    (mk3, mv3, mk_t3, k_low3, v_low3, bounds, sems, tile_sems, low_sems) = outs[18:]
     for i, w in enumerate((wck, wcv)):
         start_weight(sh, slots, (2 + i) * n, n, w, sems.at[i])
     slot_bounds(lens, order, bounds)
     spread_zero(q_t)
     spread_zero(g_t)
 
-    def clear(t, carry):
-        @pl.when(touched_tile(sh, lens, order, mlens, t, bounds, True))
-        def _():
-            dk[t] = jnp.zeros((TILE, D), F32)
-            dv[t] = jnp.zeros((TILE, D), F32)
-
-        return carry
-
-    lax.fori_loop(0, sh.m_blocks, clear, 0)
+    def each_wanted(body):
+        def one(t, carry):
+            @pl.when(touched_tile(sh, lens, order, mlens, t, bounds, True))
+            def _():
+                body(t)
+
+            return carry
+
+        lax.fori_loop(0, sh.m_blocks, one, 0)
+
+    def fetch(t):
+        for copy in tile_copies(t, kept, (mk3, mv3, mk_t3), tile_sems):
+            copy.start()
+
+    def clear(t):
+        dk[t] = jnp.zeros((TILE, D), F32)
+        dv[t] = jnp.zeros((TILE, D), F32)
+        for copy in tile_copies(t, kept, (mk3, mv3, mk_t3), tile_sems):
+            copy.wait()
+
+    def low_copies(t):
+        return tile_copies(t, (k_low3, v_low3), low_out, low_sems)
+
+    each_wanted(fetch)
+    each_wanted(clear)
 
     def block(b, carry):
         backward_start(b, q_t3, g_cc_t3, q_ref, g_cc, cctx_t3, q_t, g_t, q_m, g_m, delta, dq_t)
@@ -1030,6 +1088,8 @@
             v_low = dv[t].astype(BF)
             k_low3[t] = k_low
             v_low3[t] = v_low
+            for copy in low_copies(t):
+                copy.start()
             out[i] = (mm_nt(k_low, wck[...]) + mm_nt(v_low, wcv[...])).astype(BF)
 
         @pl.when(jnp.logical_not(seen))
@@ -1042,6 +1102,12 @@
         lax.fori_loop(
             0, sh.m_blocks // 4, lambda i, c, slot=slot, out=out: mem_tile(i, c, slot, out), 0
         )
+
+    def settle(t):
+        for copy in low_copies(t):
+            copy.wait()
+
+    each_wanted(settle)
 
 
 def cross_backward(sh, lens, order, mlens, arrays, slots):
@@ -1063,10 +1129,18 @@
         pltpu.VMEM((nm, TILE, D), F32),
         pltpu.VMEM((nm, TILE, D), F32),
         pltpu.VMEM((D, TILE), F32),
+        pltpu.VMEM((nm, TILE, D), BF),
+        pltpu.VMEM((nm, TILE, D), BF),
+        pltpu.VMEM((nm, D, TILE), BF),
+        pltpu.VMEM((nm, TILE, D), BF),
+        pltpu.VMEM((nm, TILE, D), BF),
         pltpu.SMEM((4, DOCS), jnp.int32),
         pltpu.SemaphoreType.DMA((2,)),
+        pltpu.SemaphoreType.DMA((3, nm)),
+        pltpu.SemaphoreType.DMA((2, nm)),
     ]
-    specs = [SMEM_SPEC] * 3 + [VMEM_SPEC] * len(arrays) + [ANY_SPEC] * len(slots)
+    specs = [SMEM_SPEC] * 3 + [VMEM_SPEC] * 2 + [ANY_SPEC] * 3 + [VMEM_SPEC] * 4
+    specs += [ANY_SPEC] * len(slots)
     return call(
         lambda *refs: cross_backward_kernel(sh, *refs),
         "cross_backward",
@@ -1075,42 +1149,42 @@
         outs,
         scratch,
         15,
+        out_specs=[VMEM_SPEC] * 5 + [ANY_SPEC] * 2,
     )
 
 
 def first_backward_kernel(sh, lens, order, mlens, *refs):
     count, rows, n = sh.count, sh.rows, sh.piece
-    (dq, k_low3, v_low3, g_second, n1, inv1, first_low, mem, ctx, vec, vec_in) = refs[:11]
-    slots = refs[11 : 11 + count]
-    outs = refs[11 + count :]
+    (dq, *low_in, g_second, n1, inv1, first_low, ctx, vec, vec_in) = refs[:10]
+    mems = refs[10 : 9 + 2 * sh.split]
+    slots = refs[9 + 2 * sh.split : 9 + 2 * sh.split + count]
+    outs = refs[9 + 2 * sh.split + count :]
     (g_send, g_own, g_first, g_ctx, g_ctx_t3, vec_grad) = outs[:6]
-    (wo, wcq, g_self, acc_k, acc_v, stage, bounds, sems) = outs[6:]
+    (wo, wcq, g_self, acc_k, acc_v, stage, mem, k_low3, v_low3, bounds) = outs[6:16]
+    (sems, mem_sems, low_sems) = outs[16:]
     for i, w in enumerate((wo, wcq)):
         start_weight(sh, slots, i * n, n, w, sems.at[i])
     vec_grad[...] = vec_in[...]
     slot_bounds(lens, order, bounds)
+
+    def wanted(t):
+        return touched_tile(sh, lens, order, mlens, t, bounds, True)
+
+    def fetch(t, carry):
+        @pl.when(wanted(t))
+        def _():
+            for copy in tile_copies(t, low_in, (k_low3, v_low3), low_sems):
+                copy.start()
+
+        return carry
+
+    lax.fori_loop(0, sh.m_blocks, fetch, 0)
+    start_mems(sh, mems, mem, mem_sems, wanted)
     wait_all(wo, sems.at[0])
     wait_all(wcq, sems.at[1])
 
     def add_vec(row, value):
         vec_grad[row : row + 1, :] = vec_grad[row : row + 1, :] + value
-
-    acc_k[...] = jnp.zeros(acc_k.shape, F32)
-    acc_v[...] = jnp.zeros(acc_v.shape, F32)
-
-    def mem_tile(t, carry):
-        @pl.when(touched_tile(sh, lens, order, mlens, t, bounds, True))
-        def _():
-            k_low = k_low3[t]
-            v_low = v_low3[t]
-            x = mem[t]
-            acc_k[...] = acc_k[...] + mm_tn(x, k_low)
-            acc_v[...] = acc_v[...] + mm_tn(x, v_low)
-            add_vec(V_CVB, col_sum(v_low))
-
-        return carry
-
-    lax.fori_loop(0, sh.m_blocks, mem_tile, 0)
 
     def own_rows(i, carry):
         r = pl.ds(pl.multiple_of(i * TILE, TILE), TILE)
@@ -1129,6 +1203,26 @@
         return carry
 
     lax.fori_loop(0, rows // TILE, own_rows, 0)
+    acc_k[...] = jnp.zeros(acc_k.shape, F32)
+    acc_v[...] = jnp.zeros(acc_v.shape, F32)
+
+    def mem_tile(t, carry):
+        @pl.when(wanted(t))
+        def _():
+            wait_mem(mem, t, mem_sems)
+            for copy in tile_copies(t, low_in, (k_low3, v_low3), low_sems):
+                copy.wait()
+            k_low = k_low3[t]
+            v_low = v_low3[t]
+            x = mem[t]
+            acc_k[...] = acc_k[...] + mm_tn(x, k_low)
+            acc_v[...] = acc_v[...] + mm_tn(x, v_low)
+            add_vec(V_CVB, col_sum(v_low))
+
+        return carry
+
+    lax.fori_loop(0, sh.m_blocks, mem_tile, 0)
+
     add_vec(V_CQB, col_sum(dq[...]))
     stage[...] = mm_tn(ctx[...], g_self[...]).astype(BF)
     put_grad(sh, stage, n, 0, g_send, g_own)
@@ -1140,8 +1234,8 @@
     put_grad(sh, stage, n, 3 * n, g_send, g_own)
 
 
-def first_backward(sh, lens, order, mlens, arrays, slots):
-    rows, nq, n = sh.rows, sh.q_blocks, sh.piece
+def first_backward(sh, lens, order, mlens, arrays, mems, slots):
+    rows, nq, n, nm = sh.rows, sh.q_blocks, sh.piece, sh.m_blocks
     outs = [
         shape((sh.count // 2, 4 * n, D), BF),
         shape((sh.count // 2, 4 * n, D), BF),
@@ -1157,14 +1251,20 @@
         pltpu.VMEM((D, D), F32),
         pltpu.VMEM((D, D), F32),
         pltpu.VMEM((D, D), BF),
+        pltpu.VMEM((nm, TILE, D), BF),
+        pltpu.VMEM((nm, TILE, D), BF),
+        pltpu.VMEM((nm, TILE, D), BF),
         pltpu.SMEM((4, DOCS), jnp.int32),
         pltpu.SemaphoreType.DMA((2,)),
+        pltpu.SemaphoreType.DMA((nm,)),
+        pltpu.SemaphoreType.DMA((2, nm)),
     ]
-    specs = [SMEM_SPEC] * 3 + [VMEM_SPEC] * len(arrays) + [ANY_SPEC] * len(slots)
+    specs = [SMEM_SPEC] * 3 + [VMEM_SPEC] + [ANY_SPEC] * 2 + [VMEM_SPEC] * 7
+    specs += [ANY_SPEC] * (len(mems) + len(slots))
     return call(
         lambda *refs: first_backward_kernel(sh, *refs),
         "first_backward",
-        (lens, order, mlens, *arrays, *slots),
+        (lens, order, mlens, *arrays, *mems, *slots),
         specs,
         outs,
         scratch,
@@ -1439,38 +1539,54 @@
             contract_weight,
         ),
     )
-    toks = [tokens]
-    for _ in range(sh.halo):
-        toks.append(seq_up(toks[-1], split))
-    slots_a = fsdp_gather(own_a, count)
-    near = slots_a[count // 2 - 1]
-    slots_b = fsdp_gather(after(own_b, toks[1], near), count)
-    ups, downs = [seq_up(after(memory, toks[1]), split)], [seq_down(after(memory, toks[1]), split)]
+    toks, downs = [tokens, seq_up(tokens, split)], [seq_down(memory, split)]
+    swaps = [(i, i ^ 1) for i in range(count)]
+    pairs = [step_pairs(count, index) for index in range(len(chip_steps(count)[0]))]
+    slots_a, slots_b = [own_a], [own_b]
+    own_b_first = [own_b]
+    other_b = [lax.ppermute(own_b, "fsdp", swaps)]
+    first = [lax.ppermute(own_a, "fsdp", p) for p in pairs]
+    hold = (toks[1], downs[0], *first, *other_b)
+    for _ in range(1, sh.halo):
+        toks.append(seq_up(after(toks[-1], *hold), split))
+    ups = [seq_up(after(memory, *hold), split)]
+    held_b = after(own_b, *hold)
+    second = [lax.ppermute(held_b, "fsdp", p) for p in pairs]
+    for index, p in enumerate(pairs):
+        slots_a += [first[index]] + [lax.ppermute(after(a, *hold), "fsdp", p) for a in slots_a[1:]]
+    hold = (toks[-1], ups[0], *second, *slots_a[3:])
+    for index, p in enumerate(pairs):
+        slots_b += [second[index]] + [lax.ppermute(after(a, *hold), "fsdp", p) for a in slots_b[1:]]
+    slots_a = slots_a + [lax.ppermute(after(a, *hold), "fsdp", swaps) for a in slots_a]
     for k in range(2, split):
         if k == split - 1:
-            last = after(memory, ups[0])
+            last = after(memory, *hold)
             ups.append(lax.ppermute(last, "seq", [(0, split - 1)]))
             downs.append(lax.ppermute(last, "seq", [(split - 1, 0)]))
         else:
-            ups.append(seq_up(ups[-1], split))
-            downs.append(seq_down(downs[-1], split))
+            ups.append(seq_up(after(ups[-1], *hold), split))
+            downs.append(seq_down(after(downs[-1], *hold), split))
     mems = [memory]
     for up, down in zip(ups, downs):
         mems += [up, down]
 
-    first_tok = after(tokens, ups[0], downs[0], slots_b[1], slots_b[2])
+    near = [lax.ppermute(after(a, *hold), "fsdp", swaps) for a in second]
+    first_tok = after(tokens, *hold, *near)
     (q, q_t3, k3, v3, k_t3, ctx, ctx_t3, lse, vec) = self_forward(
         sh, doc_lengths, doc_order, [first_tok] + toks[1:], slots_a
     )
-    (n1, inv1, first_low, cq, cq_t3, mk3, mv3, mk_t3, cctx, cctx_t3, clse, mem) = cross_forward(
+    swapped = {id(a): b for a, b in zip(own_b_first + second, other_b + near)}
+    late = (ctx, *ups, *downs)
+    slots_b = slots_b + [
+        swapped[id(a)] if id(a) in swapped else lax.ppermute(after(a, *late), "fsdp", swaps)
+        for a in slots_b
+    ]
+    (n1, inv1, first_low, cq, cq_t3, mk3, mv3, mk_t3, cctx, cctx_t3, clse) = cross_forward(
         sh, doc_lengths, doc_order, memory_lengths, tokens, ctx, vec, mems, slots_b
     )
     feed_out = feed(sh, doc_lengths, doc_order, n1, cctx, targets, vec, slots_b)
-    (final_low, g_second, g_cc, g_cc_t3, vec_grad, sec_low, hid, feed_low, g_exp, g_cross) = (
-        feed_out
-    )
-    (send_c, own_c) = feed_weights(sh, (cctx, sec_low, hid, feed_low, g_exp, g_cross))
-    sum_c = Reduction(send_c, own_c, count, split, True)
+    (final_low, g_second, g_cc, g_cc_t3, vec_grad, send_c, own_c) = feed_out
+    sum_c = Reduction(send_c, own_c, count, split)
     sum_c.step()
     cq = after(cq, sum_c.send)
     sum_c.step()
@@ -1491,17 +1607,17 @@
         doc_lengths,
         doc_order,
         memory_lengths,
-        (dcq, k_low3, v_low3, g_second, n1, inv1, first_low, mem, ctx, vec, vec_grad),
+        (dcq, k_low3, v_low3, g_second, n1, inv1, first_low, ctx, vec, vec_grad),
+        mems,
         slots_b,
     )
     mem_away = add_low(after(mem_parts[1], g_first), mem_got)
-    sum_b = Reduction(send_b, own_b, count, split, True)
+    sum_b = Reduction(send_b, own_b, count, split)
     g_ctx = after(g_ctx, sum_c.send, mem_away)
     sum_c.step(g_ctx)
     sum_b.step(g_ctx)
     mem_got = lax.ppermute(after(mem_parts[2], g_ctx), "seq", swap)
     mem_far = lax.ppermute(after(mem_away, g_ctx), "seq", [(i, i ^ 2) for i in range(split)])
-    mem_here = mem_parts[3].astype(F32) + mem_got.astype(F32) + mem_far.astype(F32)
     (grad_halo, dq, sk_low3, sv_low3) = self_backward(
         sh,
         doc_lengths,
@@ -1509,7 +1625,7 @@
         (q, q_t3, k3, v3, k_t3, ctx_t3, lse, g_ctx, g_ctx_t3),
         slots_a,
     )
-    dq = after(dq, mem_here, sum_c.send, sum_b.send)
+    dq = after(dq, mem_got, mem_far, sum_c.send, sum_b.send)
     back = seq_down(after(grad_halo[sh.halo - 1], dq), split)
     sum_b.step(dq)
     sum_c.step(dq)
@@ -1520,7 +1636,7 @@
         slots_a,
     )
     send_a = after(send_a, sum_b.send, sum_c.send)
-    sum_a = Reduction(send_a, own_a, count, split, True)
+    sum_a = Reduction(send_a, own_a, count, split)
     sum_a.step()
     sum_b.step(send_a)
     sum_c.step(send_a)
@@ -1534,11 +1650,11 @@
     ready = sum_a.send
     sum_a.step(back, *held)
     sum_b.step(ready)
-    red_a = sum_a.finish()
-    red_b = sum_b.finish()
-    red_c = sum_c.finish()
     input_grad = grad_own + back.astype(F32)
+    mem_last = after(mem_parts[3], sum_a.send)
+    mem_here = mem_last.astype(F32) + mem_got.astype(F32) + mem_far.astype(F32)
     memory_grad = seq_rest(mem_here.reshape(split // 4, sh.mem_rows, D), split)[0]
+    red_a, red_b, red_c = sum_a.finish(), sum_b.finish(), sum_c.finish()
 
     def rows_of(array, start, size):
         return array[start : start + size].astype(F32)

time: 279 us -> 276 us (0.989); the launches traced: 277 us -> 277 us
  Pallas kernels: 99.9 us -> 80.7 us
  starting transfers between devices: 62.7 us -> 72.3 us
  other arithmetic: 12.8 us -> 19.8 us
  waiting for transfers between devices: 92.6 us -> 99.6 us
  local copies, waits for them, and re-layouts: 7.23 us -> 2.84 us
    pallas_call x10 -> x9, Pallas kernels: 99.9 us -> 80.7 us  [call(): pl.pallas_call(body, name=name, in_specs=specs, out_specs=out_specs or [V...]
    ppermute x1, starting transfers between devices: 0.48 us -> 13.7 us  [shards(): mem_got = lax.ppermute(mem_parts[0], 'seq', swap)]
    ppermute x32, waiting for transfers between devices: 55.6 us -> 68.7 us  [the longest x18 45 us: start(): self.got = lax.ppermute(send, self.axis, pairs)]
    ppermute x1, waiting for transfers between devices: 8.44 us -> 0.01 us  [shards(): ups.append(lax.ppermute(last, 'seq', [(0, split - 1)]))]
    convert_element_type x0 -> x12, other arithmetic: none -> 8.39 us  [sum_low(): return total.astype(BF)]
    ppermute x32, starting transfers between devices: 34.3 us -> 26.6 us  [the longest x18 17.7 us: start(): self.got = lax.ppermute(send, self.axis, pairs)]
    ppermute x4, waiting for transfers between devices: 0.01 us -> 6.24 us  [seq_up(): return lax.ppermute(a, 'seq', [(i, i + 1) for i in range(count - 1)])]
    unnamed x76 -> x48, local copies, waits for them, and re-layouts: 7.2 us -> 1.98 us
  transfers between devices with their start and end apart: 45 -> 45, of which waited for: 23 -> 25; matrix products, arithmetic and copies ran while one was open for 4% -> 6% of each run, Pallas kernels for 23% -> 18%
where the time goes in v3:
time: 276 us; the launch traced here: 277 us
  waiting for transfers between devices  99.6 us (36%)
  Pallas kernels  80.7 us (29%)
  starting transfers between devices  72.3 us (26%)
  other arithmetic  19.8 us (7%)
  local copies, waits for them, and re-layouts  2.84 us (1%)
    pallas_call x9, Pallas kernels, call(): pl.pallas_call(body, name=name, in_specs=specs, out_specs=out_specs or [V...  80.7 us
    ppermute x18, waiting for transfers between devices, start(): self.got = lax.ppermute(send, self.axis, pairs)  45 us
    ppermute x18, starting transfers between devices, start(): self.got = lax.ppermute(send, self.axis, pairs)  17.7 us
    ppermute x4, starting transfers between devices, seq_up(): return lax.ppermute(a, 'seq', [(i, i + 1) for i in range(count - 1)])  17.4 us
    ppermute x1, starting transfers between devices, shards(): mem_got = lax.ppermute(mem_parts[0], 'seq', swap)  13.7 us
    ppermute x2, waiting for transfers between devices, shards(): lax.ppermute(after(a, *hold), 'fsdp', p)  12.8 us
    ppermute x4, waiting for transfers between devices, seq_down(): return lax.ppermute(a, 'seq', [(i + 1, i) for i in range(count - 1)])  10.3 us
    ppermute x1, waiting for transfers between devices, shards(): mem_got = lax.ppermute(after(mem_parts[2], g_ctx), 'seq', swap)  9.9 us
  transfers between devices with their start and end apart: 45, of which 25 were waited for; matrix products, arithmetic and copies ran while one was open for 6% of the time, Pallas kernels for 18%

profile of v3, /device:TPU:0, one launch (start us, length us, event | category | flops | bytes accessed | tf_op | source)
XLA Modules:
  0.0 276.7 jit_solution(3781657856029560162)
XLA Ops:
  3.8 4.5 %collective-permute-start = (bf16[512,512]{1,0:T(8,128)(2,1)}, bf16[512,512]{1,0:T(8,128)(2,1)S(1)}, u32[]{:S(2)}, u32[]{:S(2)}) collective-permute-start(bf16[512,512]{1,0:T(8,128)(2,1)} %refs_5_.3), channel_id=1, source_target_pairs={{0,1},{1,2},{2,3},{4,5},{5,6},{6,7},{8,9},{9,10},{10,11},{12,13},{... | collective-permute-start | bytes 1572872 | tf_op jit(solution)/shard_map/ppermute | solution.py:190
  12.7 5.3 %collective-permute-done.3.refs_7_.refs_13_.refs_10_ = bf16[224,512]{1,0:T(8,128)(2,1)S(1)} collective-permute-done((bf16[224,512]{1,0:T(8,128)(2,1)}, bf16[224,512]{1,0:T(8,128)(2,1)S(1)}, u32[]{:S(2)}, u32[]{:S(2)}) %collective-permute-start.3) | collective-permute-done | bytes 229408 | tf_op jit(solution)/shard_map/ppermute | solution.py:1548
  20.4 4.1 %collective-permute-done.1.refs_8_.refs_15_ = bf16[512,512]{1,0:T(8,128)(2,1)} collective-permute-done((bf16[512,512]{1,0:T(8,128)(2,1)}, bf16[512,512]{1,0:T(8,128)(2,1)}, u32[]{:S(2)}, u32[]{:S(2)}) %collective-permute-start.1) | collective-permute-done | bytes 524320 | tf_op jit(solution)/shard_map/ppermute | solution.py:194
  31.1 4.3 %collective-permute-start.6 = (bf16[512,512]{1,0:T(8,128)(2,1)}, bf16[512,512]{1,0:T(8,128)(2,1)}, u32[]{:S(2)}, u32[]{:S(2)}) collective-permute-start(bf16[512,512]{1,0:T(8,128)(2,1)} %refs_13_.3), channel_id=1, source_target_pairs={{0,1},{1,2},{2,3},{4,5},{5,6},{6,7},{8,9},{9,10},{10,11},{12,13},{... | collective-permute-start | bytes 1572872 | tf_op jit(solution)/shard_map/ppermute | solution.py:190
  35.8 12.8 %collective-permute-done.9.refs_8_.refs_14_.refs_11_ = bf16[224,512]{1,0:T(8,128)(2,1)S(1)} collective-permute-done((bf16[224,512]{1,0:T(8,128)(2,1)S(1)}, bf16[224,512]{1,0:T(8,128)(2,1)S(1)}, u32[]{:S(2)}, u32[]{:S(2)}) %collective-permute-start.9) | collective-permute-done | bytes 229408 | tf_op jit(solution)/shard_map/ppermute | solution.py:1556
  48.7 3.8 %collective-permute-done.6.refs_7_.refs_14_ = bf16[512,512]{1,0:T(8,128)(2,1)} collective-permute-done((bf16[512,512]{1,0:T(8,128)(2,1)}, bf16[512,512]{1,0:T(8,128)(2,1)}, u32[]{:S(2)}, u32[]{:S(2)}) %collective-permute-start.6) | collective-permute-done | bytes 524320 | tf_op jit(solution)/shard_map/ppermute | solution.py:190
  57.3 5.2 %collective-permute-start.16 = (bf16[512,512]{1,0:T(8,128)(2,1)}, bf16[512,512]{1,0:T(8,128)(2,1)}, u32[]{:S(2)}, u32[]{:S(2)}) collective-permute-start(bf16[512,512]{1,0:T(8,128)(2,1)} %collective-permute-done.6.refs_7_.refs_14_), channel_id=1, source_target_pairs={{0,1},{1,2},{2,3},{4,5},{5,6},{6,7},{8,9},{9,10},{10,11},{12,13},{... | collective-permute-start | bytes 1572872 | tf_op jit(solution)/shard_map/ppermute | solution.py:190
  66.2 7.9 %collective-permute-start.18 = (bf16[512,512]{1,0:T(8,128)(2,1)}, bf16[512,512]{1,0:T(8,128)(2,1)}, u32[]{:S(2)}, u32[]{:S(2)}) collective-permute-start(bf16[512,512]{1,0:T(8,128)(2,1)} %refs_13_.3), channel_id=1, source_target_pairs={{0,3},{4,7},{8,11},{12,15},{16,19},{20,23},{24,27},{28,31}} | collective-permute-start | bytes 1572872 | tf_op jit(solution)/shard_map/ppermute | solution.py:1564
  74.1 11.1 %self_forward.1 = (bf16[512,512]{1,0:T(8,128)(2,1)}, bf16[2,512,256]{2,1,0:T(8,128)(2,1)}, bf16[6,256,512]{2,1,0:T(8,128)(2,1)}, bf16[6,256,512]{2,1,0:T(8,128)(...) custom-call(s32[1,4]{1,0:T(1,128)} %refs_0_.13, ...), custom_call_target="tpu_custom_call" | custom-call | flops 480000000 | bytes 216597 | tf_op jit(solution)/shard_map/self_forward/pallas_call | solution.py:508
  85.3 4.4 %collective-permute-done.19.refs_12_.refs_19_ = bf16[512,512]{1,0:T(8,128)(2,1)} collective-permute-done((bf16[512,512]{1,0:T(8,128)(2,1)}, bf16[512,512]{1,0:T(8,128)(2,1)}, u32[]{:S(2)}, u32[]{:S(2)}) %collective-permute-start.19) | collective-permute-done | bytes 524320 | tf_op jit(solution)/shard_map/ppermute | solution.py:1565
  93.2 9.9 %cross_forward.1 = (f32[512,512]{1,0:T(8,128)}, f32[512,1]{1,0:T(8,128)}, bf16[512,512]{1,0:T(8,128)(2,1)}, bf16[512,512]{1,0:T(8,128)(2,1)}, bf16[2,512,256]{2,...) custom-call(s32[1,4]{1,0:T(1,128)} %refs_0_.13, ...), custom_call_target="tpu_custom_call" | custom-call | flops 630000000 | bytes 442082 | tf_op jit(solution)/shard_map/cross_forward/pallas_call | solution.py:508
  103.2 17.3 %feed.1 = (bf16[512,512]{1,0:T(8,128)(2,1)}, f32[512,512]{1,0:T(8,128)}, bf16[512,512]{1,0:T(8,128)(2,1)}, bf16[2,512,256]{2,1,0:T(8,128)(2,1)}, f32[32,512]{1,0...) custom-call(s32[1,4]{1,0:T(1,128)} %refs_0_.13, s32[1,4]{1,0:T(1,128)} %refs_1_.13, ...), custom_call_target="tpu_custom_call" | custom-call | flops 510000000 | bytes 327680 | tf_op jit(solution)/shard_map/feed/pallas_call | solution.py:508
  123.7 4.4 %collective-permute-done.22 = bf16[4,576,512]{2,1,0:T(8,128)(2,1)S(1)} collective-permute-done((bf16[4,576,512]{2,1,0:T(8,128)(2,1)}, bf16[4,576,512]{2,1,0:T(8,128)(2,1)S(1)}, u32[]{:S(2)}, u32[]{:S(2)}) %collective-permute-start.22) | collective-permute-done | bytes 2359328 | tf_op jit(solution)/shard_map/ppermute | solution.py:139
  134.1 10.7 %cross_backward.1 = (bf16[2,256,512]{2,1,0:T(8,128)(2,1)}, bf16[2,256,512]{2,1,0:T(8,128)(2,1)}, bf16[2,256,512]{2,1,0:T(8,128)(2,1)}, bf16[2,256,512]{2,1,0:T(8...) custom-call(s32[1,4]{1,0:T(1,128)} %refs_0_.13, ...), custom_call_target="tpu_custom_call" | custom-call | flops 450000000 | bytes 461702 | tf_op jit(solution)/shard_map/cross_backward/pallas_call | solution.py:508
  144.8 13.7 %collective-permute-start.25 = (bf16[2,256,512]{2,1,0:T(8,128)(2,1)}, bf16[2,256,512]{2,1,0:T(8,128)(2,1)}, u32[]{:S(2)}, u32[]{:S(2)}) collective-permute-start(bf16[2,256,512]{2,1,0:T(8,128)(2,1)} %get-tuple-element.185), channel_id=1, source_target_pairs={{0,1},{1,0},{2,3},{3,2},{4,5},{5,4},{6,7},{7,6},{8,9},{9,8},{10,11... | collective-permute-start | bytes 1572872 | tf_op jit(solution)/shard_map/ppermute | solution.py:1604
  160.0 8.8 %first_backward.1 = (bf16[4,256,512]{2,1,0:T(8,128)(2,1)}, bf16[4,256,512]{2,1,0:T(8,128)(2,1)}, f32[512,512]{1,0:T(8,128)}, bf16[512,512]{1,0:T(8,128)(2,1)}, b...) custom-call(s32[1,4]{1,0:T(1,128)} %refs_0_.13, s32[1,4]{1,0:T(1,128)} %refs_1_.13, s32[1,4]{1,0:T(1,128)} %refs_2_.8, ...), custom_call_target="tpu_custom_call" | custom-call | flops 180000000 | bytes 454861 | tf_op jit(solution)/shard_map/first_backward/pallas_call | solution.py:508
  174.6 11.5 %self_backward.1 = (bf16[2,512,512]{2,1,0:T(8,128)(2,1)}, bf16[512,512]{1,0:T(8,128)(2,1)}, bf16[6,256,512]{2,1,0:T(8,128)(2,1)}, bf16[6,256,512]{2,1,0:T(8,128)(2,1)}) custom-call(s32[1,4]{1,0:T(1,128)} %refs_0_.13, s32[1,4]{1,0:T(1,128)} %refs_1_.13, bf16[512,512]{1,0:T(8,128)(2,1)} %get-tuple-element.153.refs_2_, ...), custom_call_target="tpu_custom_call" | custom-call | flops 420000000 | bytes 288686 | tf_op jit(solution)/shard_map/self_backward/pallas_call | solution.py:508
  186.1 6.5 %collective-permute-done.28 = bf16[288,512]{1,0:T(8,128)(2,1)} collective-permute-done((bf16[288,512]{1,0:T(8,128)(2,1)S(1)}, bf16[288,512]{1,0:T(8,128)(2,1)}, u32[]{:S(2)}, u32[]{:S(2)}) %collective-permute-start.28) | collective-permute-done | bytes 294944 | tf_op jit(solution)/shard_map/ppermute | solution.py:139
  194.7 9.9 %collective-permute-done.26 = bf16[2,256,512]{2,1,0:T(8,128)(2,1)S(1)} collective-permute-done((bf16[2,256,512]{2,1,0:T(8,128)(2,1)}, bf16[2,256,512]{2,1,0:T(8,128)(2,1)S(1)}, u32[]{:S(2)}, u32[]{:S(2)}) %collective-permute-start.26) | collective-permute-done | bytes 524320 | tf_op jit(solution)/shard_map/ppermute | solution.py:1619
  209.5 7.1 %self_weights.1 = (bf16[4,224,512]{2,1,0:T(8,128)(2,1)}, bf16[4,224,512]{2,1,0:T(8,128)(2,1)}, f32[512,512]{1,0:T(8,128)}) custom-call(bf16[512,512]{1,0:T(8,128)(2,1)} %get-tuple-element.196.refs_0_, bf16[6,256,512]{2,1,0:T(8,128)(2,1)} %get-tuple-element.197.refs_1_, bf16[6,256,512]{2,1,0:T(8,128)(2,1)} %get-tuple-element.198.refs_2_, ...), custom_call_target="tpu_custom_call" | custom-call | flops 210000000 | bytes 221511 | tf_op jit(solution)/shard_map/self_weights/pallas_call | solution.py:508
  225.1 5.7 %collective-permute-done.35 = bf16[512,512]{1,0:T(8,128)(2,1)S(1)} collective-permute-done((bf16[512,512]{1,0:T(8,128)(2,1)}, bf16[512,512]{1,0:T(8,128)(2,1)S(1)}, u32[]{:S(2)}, u32[]{:S(2)}) %collective-permute-start.35) | collective-permute-done | bytes 524320 | tf_op jit(solution)/shard_map/ppermute | solution.py:194
  233.4 3.7 %collective-permute-done.38 = bf16[288,512]{1,0:T(8,128)(2,1)S(1)} collective-permute-done((bf16[288,512]{1,0:T(8,128)(2,1)S(1)}, bf16[288,512]{1,0:T(8,128)(2,1)S(1)}, u32[]{:S(2)}, u32[]{:S(2)}) %collective-permute-start.38) | collective-permute-done | bytes 294944 | tf_op jit(solution)/shard_map/ppermute | solution.py:139
  240.0 6.8 %collective-permute-done.33 = bf16[2,224,512]{2,1,0:T(8,128)(2,1)S(1)} collective-permute-done((bf16[2,224,512]{2,1,0:T(8,128)(2,1)S(1)}, bf16[2,224,512]{2,1,0:T(8,128)(2,1)S(1)}, u32[]{:S(2)}, u32[]{:S(2)}) %collective-permute-start.33) | collective-permute-done | bytes 458784 | tf_op jit(solution)/shard_map/ppermute | solution.py:139
  260.2 5.9 %collective-permute-done.43 = bf16[128,512]{1,0:T(8,128)(2,1)S(1)} collective-permute-done((bf16[128,512]{1,0:T(8,128)(2,1)S(1)}, bf16[128,512]{1,0:T(8,128)(2,1)S(1)}, u32[]{:S(2)}, u32[]{:S(2)}) %collective-permute-start.43) | collective-permute-done | bytes 131104 | tf_op jit(solution)/shard_map/ppermute | solution.py:139
  (153 shorter events, 89.8 us)
Async XLA Ops:
  3.3 21.3 %collective-permute-start.4 = (bf16[832,512]{1,0:T(8,128)(2,1)}, bf16[832,512]{1,0:T(8,128)(2,1)S(1)}, u32[]{:S(2)}, u32[]{:S(2)}) collective-permute-start(bf16[832,512]{1,0:T(8,128)(2,1)} %get-tuple-element.135.refs_13_.refs_6_.refs_12_.refs_20_), channel_id=1, source_target_pairs={{0,4},{4,0},{8,12},{12,8},{16,20},{20,16},{24,28},{28,24},{1,5},{5... | collective-permute-start | bytes 2555912 | tf_op jit(solution)/shard_map/ppermute | solution.py:1547
  3.8 16.6 %collective-permute-start = (bf16[512,512]{1,0:T(8,128)(2,1)}, bf16[512,512]{1,0:T(8,128)(2,1)S(1)}, u32[]{:S(2)}, u32[]{:S(2)}) collective-permute-start(bf16[512,512]{1,0:T(8,128)(2,1)} %refs_5_.3), channel_id=1, source_target_pairs={{0,1},{1,2},{2,3},{4,5},{5,6},{6,7},{8,9},{9,10},{10,11},{12,13},{... | collective-permute-start | bytes 1572872 | tf_op jit(solution)/shard_map/ppermute | solution.py:190
  8.3 16.2 %collective-permute-start.1 = (bf16[512,512]{1,0:T(8,128)(2,1)}, bf16[512,512]{1,0:T(8,128)(2,1)}, u32[]{:S(2)}, u32[]{:S(2)}) collective-permute-start(bf16[512,512]{1,0:T(8,128)(2,1)} %refs_13_.3), channel_id=1, source_target_pairs={{1,0},{2,1},{3,2},{5,4},{6,5},{7,6},{9,8},{10,9},{11,10},{13,12},{... | collective-permute-start | bytes 1572872 | tf_op jit(solution)/shard_map/ppermute | solution.py:194
  24.6 28.0 %collective-permute-start.8 = (bf16[832,512]{1,0:T(8,128)(2,1)}, bf16[832,512]{1,0:T(8,128)(2,1)S(1)}, u32[]{:S(2)}, u32[]{:S(2)}) collective-permute-start(bf16[832,512]{1,0:T(8,128)(2,1)} %get-tuple-element.135.refs_13_.refs_6_.refs_12_.refs_20_), channel_id=1, source_target_pairs={{0,16},{4,12},{8,24},{12,4},{16,0},{20,28},{24,8},{28,20},{1,17},{... | collective-permute-start | bytes 2555912 | tf_op jit(solution)/shard_map/ppermute | solution.py:1554
  26.1 26.4 %collective-permute-start.7 = (bf16[832,512]{1,0:T(8,128)(2,1)}, bf16[832,512]{1,0:T(8,128)(2,1)S(1)}, u32[]{:S(2)}, u32[]{:S(2)}) collective-permute-start(bf16[832,512]{1,0:T(8,128)(2,1)} %get-tuple-element.135.refs_13_.refs_6_.refs_12_.refs_20_), channel_id=1, source_target_pairs={{0,8},{4,20},{8,0},{12,28},{16,24},{20,4},{24,16},{28,12},{1,9},{5... | collective-permute-start | bytes 2555912 | tf_op jit(solution)/shard_map/ppermute | solution.py:1554
  27.6 21.1 %collective-permute-start.5 = (bf16[512,512]{1,0:T(8,128)(2,1)S(1)}, bf16[512,512]{1,0:T(8,128)(2,1)S(1)}, u32[]{:S(2)}, u32[]{:S(2)}) collective-permute-start(bf16[512,512]{1,0:T(8,128)(2,1)S(1)} %collective-permute-done.refs_3_.refs_6_), channel_id=1, source_target_pairs={{0,1},{1,2},{2,3},{4,5},{5,6},{6,7},{8,9},{9,10},{10,11},{12,13},{... | collective-permute-start | bytes 1572872 | tf_op jit(solution)/shard_map/ppermute | solution.py:190
  31.1 21.5 %collective-permute-start.6 = (bf16[512,512]{1,0:T(8,128)(2,1)}, bf16[512,512]{1,0:T(8,128)(2,1)}, u32[]{:S(2)}, u32[]{:S(2)}) collective-permute-start(bf16[512,512]{1,0:T(8,128)(2,1)} %refs_13_.3), channel_id=1, source_target_pairs={{0,1},{1,2},{2,3},{4,5},{5,6},{6,7},{8,9},{9,10},{10,11},{12,13},{... | collective-permute-start | bytes 1572872 | tf_op jit(solution)/shard_map/ppermute | solution.py:190
  35.3 13.3 %collective-permute-start.9 = (bf16[224,512]{1,0:T(8,128)(2,1)S(1)}, bf16[224,512]{1,0:T(8,128)(2,1)S(1)}, u32[]{:S(2)}, u32[]{:S(2)}) collective-permute-start(bf16[224,512]{1,0:T(8,128)(2,1)S(1)} %collective-permute-done.2.refs_6_.refs_12_.refs_9_), channel_id=1, source_target_pairs={{0,16},{4,12},{8,24},{12,4},{16,0},{20,28},{24,8},{28,20},{1,17},{... | collective-permute-start | bytes 688136 | tf_op jit(solution)/shard_map/ppermute | solution.py:1556
  53.6 36.1 %collective-permute-start.20 = (bf16[832,512]{1,0:T(8,128)(2,1)S(1)}, bf16[832,512]{1,0:T(8,128)(2,1)}, u32[]{:S(2)}, u32[]{:S(2)}) collective-permute-start(bf16[832,512]{1,0:T(8,128)(2,1)S(1)} %collective-permute-done.7.refs_14_.refs_7_.refs_13_.refs_21_), channel_id=1, source_target_pairs={{0,16},{4,12},{8,24},{12,4},{16,0},{20,28},{24,8},{28,20},{1,17},{... | collective-permute-start | bytes 2555912 | tf_op jit(solution)/shard_map/ppermute | solution.py:1559
  57.3 28.0 %collective-permute-start.16 = (bf16[512,512]{1,0:T(8,128)(2,1)}, bf16[512,512]{1,0:T(8,128)(2,1)}, u32[]{:S(2)}, u32[]{:S(2)}) collective-permute-start(bf16[512,512]{1,0:T(8,128)(2,1)} %collective-permute-done.6.refs_7_.refs_14_), channel_id=1, source_target_pairs={{0,1},{1,2},{2,3},{4,5},{5,6},{6,7},{8,9},{9,10},{10,11},{12,13},{... | collective-permute-start | bytes 1572872 | tf_op jit(solution)/shard_map/ppermute | solution.py:190
  62.5 22.8 %collective-permute-start.17 = (bf16[512,512]{1,0:T(8,128)(2,1)}, bf16[512,512]{1,0:T(8,128)(2,1)}, u32[]{:S(2)}, u32[]{:S(2)}) collective-permute-start(bf16[512,512]{1,0:T(8,128)(2,1)} %collective-permute-done.1.refs_8_.refs_15_), channel_id=1, source_target_pairs={{1,0},{2,1},{3,2},{5,4},{6,5},{7,6},{9,8},{10,9},{11,10},{13,12},{... | collective-permute-start | bytes 1572872 | tf_op jit(solution)/shard_map/ppermute | solution.py:194
  63.8 25.9 %collective-permute-start.19 = (bf16[512,512]{1,0:T(8,128)(2,1)}, bf16[512,512]{1,0:T(8,128)(2,1)}, u32[]{:S(2)}, u32[]{:S(2)}) collective-permute-start(bf16[512,512]{1,0:T(8,128)(2,1)} %refs_13_.3), channel_id=1, source_target_pairs={{3,0},{7,4},{11,8},{15,12},{19,16},{23,20},{27,24},{31,28}} | collective-permute-start | bytes 1572872 | tf_op jit(solution)/shard_map/ppermute | solution.py:1565
  66.2 23.5 %collective-permute-start.18 = (bf16[512,512]{1,0:T(8,128)(2,1)}, bf16[512,512]{1,0:T(8,128)(2,1)}, u32[]{:S(2)}, u32[]{:S(2)}) collective-permute-start(bf16[512,512]{1,0:T(8,128)(2,1)} %refs_13_.3), channel_id=1, source_target_pairs={{0,3},{4,7},{8,11},{12,15},{16,19},{20,23},{24,27},{28,31}} | collective-permute-start | bytes 1572872 | tf_op jit(solution)/shard_map/ppermute | solution.py:1564
  130.5 27.9 %collective-permute-start.23 = (bf16[2,576,512]{2,1,0:T(8,128)(2,1)S(1)}, bf16[2,576,512]{2,1,0:T(8,128)(2,1)}, u32[]{:S(2)}, u32[]{:S(2)}) collective-permute-start(bf16[2,576,512]{2,1,0:T(8,128)(2,1)S(1)} %add_convert_fusion), channel_id=1, source_target_pairs={{0,8},{4,20},{8,0},{12,28},{16,24},{20,4},{24,16},{28,12},{1,9},{5... | collective-permute-start | bytes 3538952 | tf_op jit(solution)/shard_map/ppermute | solution.py:139
  144.8 24.1 %collective-permute-start.25 = (bf16[2,256,512]{2,1,0:T(8,128)(2,1)}, bf16[2,256,512]{2,1,0:T(8,128)(2,1)}, u32[]{:S(2)}, u32[]{:S(2)}) collective-permute-start(bf16[2,256,512]{2,1,0:T(8,128)(2,1)} %get-tuple-element.185), channel_id=1, source_target_pairs={{0,1},{1,0},{2,3},{3,2},{4,5},{5,4},{6,7},{7,6},{8,9},{9,8},{10,11... | collective-permute-start | bytes 1572872 | tf_op jit(solution)/shard_map/ppermute | solution.py:1604
  172.4 21.3 %collective-permute-start.29 = (bf16[4,256,512]{2,1,0:T(8,128)(2,1)}, bf16[4,256,512]{2,1,0:T(8,128)(2,1)S(1)}, u32[]{:S(2)}, u32[]{:S(2)}) collective-permute-start(bf16[4,256,512]{2,1,0:T(8,128)(2,1)} %get-tuple-element.195), channel_id=1, source_target_pairs={{0,4},{4,0},{8,12},{12,8},{16,20},{20,16},{24,28},{28,24},{1,5},{5... | collective-permute-start | bytes 3145736 | tf_op jit(solution)/shard_map/ppermute | solution.py:139
  172.5 20.1 %collective-permute-start.28 = (bf16[288,512]{1,0:T(8,128)(2,1)S(1)}, bf16[288,512]{1,0:T(8,128)(2,1)}, u32[]{:S(2)}, u32[]{:S(2)}) collective-permute-start(bf16[288,512]{1,0:T(8,128)(2,1)S(1)} %select_bitcast_fusion), channel_id=1, source_target_pairs={{0,1},{1,0},{2,3},{3,2},{4,5},{5,4},{6,7},{7,6},{8,9},{9,8},{10,11... | collective-permute-start | bytes 884744 | tf_op jit(solution)/shard_map/ppermute | solution.py:139
  174.5 30.1 %collective-permute-start.26 = (bf16[2,256,512]{2,1,0:T(8,128)(2,1)}, bf16[2,256,512]{2,1,0:T(8,128)(2,1)S(1)}, u32[]{:S(2)}, u32[]{:S(2)}) collective-permute-start(bf16[2,256,512]{2,1,0:T(8,128)(2,1)} %get-tuple-element.190), channel_id=1, source_target_pairs={{0,1},{1,0},{2,3},{3,2},{4,5},{5,4},{6,7},{7,6},{8,9},{9,8},{10,11... | collective-permute-start | bytes 1572872 | tf_op jit(solution)/shard_map/ppermute | solution.py:1619
  174.6 29.9 %collective-permute-start.27 = (bf16[2,256,512]{2,1,0:T(8,128)(2,1)}, bf16[2,256,512]{2,1,0:T(8,128)(2,1)S(1)}, u32[]{:S(2)}, u32[]{:S(2)}) collective-permute-start(bf16[2,256,512]{2,1,0:T(8,128)(2,1)} %add_convert_fusion.4), channel_id=1, source_target_pairs={{0,2},{1,3},{2,0},{3,1},{4,6},{5,7},{6,4},{7,5},{8,10},{9,11},{10,... | collective-permute-start | bytes 1572872 | tf_op jit(solution)/shard_map/ppermute | solution.py:1620
  204.6 15.3 %collective-permute-start.31 = (bf16[288,512]{1,0:T(8,128)(2,1)S(1)}, bf16[288,512]{1,0:T(8,128)(2,1)}, u32[]{:S(2)}, u32[]{:S(2)}) collective-permute-start(bf16[288,512]{1,0:T(8,128)(2,1)S(1)} %fusion.1), channel_id=1, source_target_pairs={{0,2},{1,3},{2,0},{3,1},{4,6},{5,7},{6,4},{7,5},{8,10},{9,11},{10,... | collective-permute-start | bytes 884744 | tf_op jit(solution)/shard_map/ppermute | solution.py:139
  207.3 13.6 %collective-permute-start.30 = (bf16[2,256,512]{2,1,0:T(8,128)(2,1)}, bf16[2,256,512]{2,1,0:T(8,128)(2,1)}, u32[]{:S(2)}, u32[]{:S(2)}) collective-permute-start(bf16[2,256,512]{2,1,0:T(8,128)(2,1)} %add_convert_fusion.3), channel_id=1, source_target_pairs={{0,8},{4,20},{8,0},{12,28},{16,24},{20,4},{24,16},{28,12},{1,9},{5... | collective-permute-start | bytes 1572872 | tf_op jit(solution)/shard_map/ppermute | solution.py:139
  208.2 22.7 %collective-permute-start.35 = (bf16[512,512]{1,0:T(8,128)(2,1)}, bf16[512,512]{1,0:T(8,128)(2,1)S(1)}, u32[]{:S(2)}, u32[]{:S(2)}) collective-permute-start(bf16[512,512]{1,0:T(8,128)(2,1)} %slice_bitcast_fusion), channel_id=1, source_target_pairs={{1,0},{2,1},{3,2},{5,4},{6,5},{7,6},{9,8},{10,9},{11,10},{13,12},{... | collective-permute-start | bytes 1572872 | tf_op jit(solution)/shard_map/ppermute | solution.py:194
  221.9 16.1 %collective-permute-start.32 = (bf16[4,224,512]{2,1,0:T(8,128)(2,1)}, bf16[4,224,512]{2,1,0:T(8,128)(2,1)S(1)}, u32[]{:S(2)}, u32[]{:S(2)}) collective-permute-start(bf16[4,224,512]{2,1,0:T(8,128)(2,1)} %get-tuple-element.204), channel_id=1, source_target_pairs={{0,4},{4,0},{8,12},{12,8},{16,20},{20,16},{24,28},{28,24},{1,5},{5... | collective-permute-start | bytes 2752520 | tf_op jit(solution)/shard_map/ppermute | solution.py:139
  231.0 17.4 %collective-permute-start.36 = (bf16[512,512]{1,0:T(8,128)(2,1)S(1)}, bf16[512,512]{1,0:T(8,128)(2,1)S(1)}, u32[]{:S(2)}, u32[]{:S(2)}) collective-permute-start(bf16[512,512]{1,0:T(8,128)(2,1)S(1)} %fusion), channel_id=1, source_target_pairs={{1,0},{2,1},{3,2},{5,4},{6,5},{7,6},{9,8},{10,9},{11,10},{13,12},{... | collective-permute-start | bytes 1572872 | tf_op jit(solution)/shard_map/ppermute | solution.py:194
  (45 other events, 602.8 us)

commit v4 on v3

--- a/solution.py
+++ b/solution.py
@@ -228,6 +228,16 @@
     pltpu.make_async_copy(target, target, sem).wait()
 
 
+def send_all(sources, targets, sems, first=0):
+    copies = [
+        pltpu.make_async_copy(source, target, sems.at[first + i])
+        for i, (source, target) in enumerate(zip(sources, targets))
+    ]
+    for copy in copies:
+        copy.start()
+    return copies
+
+
 def tile_copies(t, sources, targets, sems):
     return [
         pltpu.make_async_copy(source.at[t], target.at[t], sems.at[i, t])
@@ -432,8 +442,10 @@
     halo, count, rows, n = sh.halo, sh.count, sh.rows, sh.piece
     toks = refs[: halo + 1]
     slots = refs[halo + 1 : halo + 1 + count]
-    (q_ref, q_t3, k3, v3, k_t3, ctx, ctx_t3, lse, vec) = refs[halo + 1 + count : halo + 10 + count]
-    (wq, wk, wv, vec_slots, v_t3, q_t, bias, m_ref, l_ref, acc, sems) = refs[halo + 10 + count :]
+    (*kept, ctx, ctx_t3, lse, vec) = refs[halo + 1 + count : halo + 10 + count]
+    outs = refs[halo + 10 + count :]
+    (q_ref, q_t3, k3, v3, k_t3, wq, wk, wv, vec_slots, v_t3, q_t, bias) = outs[:12]
+    (m_ref, l_ref, acc, sems, q_sems, tile_sems) = outs[12:]
     z = lax.axis_index("seq")
     for s, slot in enumerate(slots):
         pltpu.make_async_copy(slot.at[pl.ds(3 * n, VROWS)], vec_slots.at[s], sems.at[3]).start()
@@ -443,8 +455,6 @@
     wait_all(vec_slots, sems.at[3])
     vec[...] = jnp.sum(vec_slots[...].astype(F32), axis=0)
     wait_all(wq, sems.at[0])
-    wait_all(wk, sems.at[1])
-    wait_all(wv, sems.at[2])
     tiles = rows // TILE
 
     def own_rows(i, carry):
@@ -456,6 +466,13 @@
         return carry
 
     lax.fori_loop(0, tiles, own_rows, 0)
+    q_copies = send_all((q_ref, q_t3), kept[:2], q_sems)
+    wait_all(wk, sems.at[1])
+    wait_all(wv, sems.at[2])
+
+    def window_copies(t):
+        return tile_copies(t, (k3, v3, k_t3), kept[2:], tile_sems)
+
     for k in range(halo + 1):
 
         def window_rows(i, carry, k=k):
@@ -468,6 +485,8 @@
             v3[t] = val
             k_t3[t] = key.T
             v_t3[t] = val.T
+            for copy in window_copies(t):
+                copy.start()
             return carry
 
         @pl.when(z >= k)
@@ -489,6 +508,15 @@
         return carry
 
     lax.fori_loop(0, sh.q_blocks, block, 0)
+    for copy in q_copies:
+        copy.wait()
+    for k in range(halo + 1):
+
+        @pl.when(z >= k)
+        def _(k=k):
+            for i in range(tiles):
+                for copy in window_copies((halo - k) * tiles + i):
+                    copy.wait()
 
 
 SMEM_SPEC = pl.BlockSpec(memory_space=pltpu.SMEM)
@@ -592,9 +620,14 @@
     return jnp.sum(jnp.where(used, row * jnp.where(used, scale, 0.0), 0.0), axis=1, keepdims=True)
 
 
-def finish_kernel(sh, red, *outs):
+def finish_kernel(sh, mine, got, *outs):
     n = sh.piece
     mats, small, wide_bias, loss = outs[:3], outs[3 : 3 + V_EB], outs[3 + V_EB], outs[4 + V_EB]
+    red = outs[5 + V_EB]
+    odd = lax.axis_index("seq") % 2 == 1
+    half = mine.shape[0]
+    red[pl.ds(0, half), :] = jnp.where(odd, got[...], mine[...])
+    red[pl.ds(half, half), :] = jnp.where(odd, mine[...], got[...])
     for i, m in enumerate(mats):
         m[...] = red[pl.ds(i * n, n), :].astype(F32)
     index = lax.axis_index("fsdp")
@@ -620,12 +653,18 @@
     loss[...] = error_sum / (live * D)
 
 
-def finish(sh, red, bias_size):
+def finish(sh, mine, got, bias_size):
     n = sh.piece
     outs = [shape((n, D), F32)] * 3 + [shape((n,), F32)] * V_EB
     outs += [shape((bias_size,), F32), shape((1, 1), F32)]
     return call(
-        lambda *refs: finish_kernel(sh, *refs), "finish", (red,), [VMEM_SPEC], outs, [], 2
+        lambda *refs: finish_kernel(sh, *refs),
+        "finish",
+        (mine, got),
+        [VMEM_SPEC] * 2,
+        outs,
+        [pltpu.VMEM((3 * n + VROWS, D), BF)],
+        2,
     )
 
 
@@ -643,6 +682,11 @@
         shape((VROWS, D), F32),
     ]
     scratch = [
+        pltpu.VMEM((sh.rows, D), BF),
+        pltpu.VMEM((nq, D, TILE), BF),
+        pltpu.VMEM((nb, TILE, D), BF),
+        pltpu.VMEM((nb, TILE, D), BF),
+        pltpu.VMEM((nb, D, TILE), BF),
         pltpu.VMEM((D, D), BF),
         pltpu.VMEM((D, D), BF),
         pltpu.VMEM((D, D), BF),
@@ -654,6 +698,8 @@
         pltpu.VMEM((HEADS, TILE), F32),
         pltpu.VMEM((D, TILE), F32),
         pltpu.SemaphoreType.DMA((4,)),
+        pltpu.SemaphoreType.DMA((2,)),
+        pltpu.SemaphoreType.DMA((3, nb)),
     ]
     specs = [SMEM_SPEC] * 2 + [VMEM_SPEC] * len(toks) + [ANY_SPEC] * len(slots)
     return call(
@@ -664,6 +710,7 @@
         outs,
         scratch,
         16,
+        out_specs=[ANY_SPEC] * 5 + [VMEM_SPEC] * 4,
     )
 
 
@@ -722,9 +769,12 @@
     mems = refs[3 : 3 + 2 * split - 1]
     slots = refs[2 + 2 * split : 2 + 2 * split + count]
     outs = refs[2 + 2 * split + count :]
-    (n1, inv1, first_low, q_ref, q_t3, *kept, cctx, cctx_t3, lse) = outs[:11]
+    (n1_out, inv1, *early, mk_out, mv_out, mk_t_out, cctx, cctx_t3, lse) = outs[:11]
+    kept = (mk_out, mv_out, mk_t_out)
+    (n1, first_low, q_ref, q_t3) = outs[11:15]
+    outs = outs[4:]
     (wo, wcq, wck, wcv, mem, mk3, mv3, mk_t3, mv_t3, q_t, bias, m_ref, l_ref, acc) = outs[11:25]
-    (bounds, sems, mem_sems, tile_sems) = outs[25:]
+    (bounds, sems, mem_sems, tile_sems, row_sems) = outs[25:]
     for i, w in enumerate((wo, wcq, wck, wcv)):
         start_weight(sh, slots, i * n, n, w, sems.at[i])
 
@@ -752,6 +802,7 @@
         return carry
 
     lax.fori_loop(0, rows // TILE, own_rows, 0)
+    row_copies = send_all((n1, first_low, q_ref, q_t3), (n1_out, *early), row_sems)
     wait_all(wck, sems.at[2])
     wait_all(wcv, sems.at[3])
 
@@ -801,6 +852,8 @@
         return carry
 
     lax.fori_loop(0, sh.m_blocks, settle, 0)
+    for copy in row_copies:
+        copy.wait()
 
 
 def cross_forward(sh, lens, order, mlens, tok, ctx, vec, mems, slots):
@@ -819,6 +872,10 @@
         shape((nq, HEADS, TILE), F32),
     ]
     scratch = [
+        pltpu.VMEM((sh.rows, D), F32),
+        pltpu.VMEM((sh.rows, D), BF),
+        pltpu.VMEM((sh.rows, D), BF),
+        pltpu.VMEM((nq, D, TILE), BF),
         pltpu.VMEM((D, D), BF),
         pltpu.VMEM((D, D), BF),
         pltpu.VMEM((D, D), BF),
@@ -837,6 +894,7 @@
         pltpu.SemaphoreType.DMA((4,)),
         pltpu.SemaphoreType.DMA((nm,)),
         pltpu.SemaphoreType.DMA((3, nm)),
+        pltpu.SemaphoreType.DMA((4,)),
     ]
     specs = [SMEM_SPEC] * 3 + [VMEM_SPEC] * 3 + [ANY_SPEC] * (len(mems) + len(slots))
     return call(
@@ -847,7 +905,7 @@
         outs,
         scratch,
         21,
-        out_specs=[VMEM_SPEC] * 5 + [ANY_SPEC] * 3 + [VMEM_SPEC] * 3,
+        out_specs=[ANY_SPEC, VMEM_SPEC] + [ANY_SPEC] * 6 + [VMEM_SPEC] * 3,
     )
 
 
@@ -856,9 +914,10 @@
     n1, cctx, targets, vec = refs[:4]
     slots = refs[4 : 4 + count]
     outs = refs[4 + count :]
-    (final_ref, g_second, g_cc, g_cc_t3, vec_grad, g_send, g_own) = outs[:7]
-    (sec_low, hid, feed_low, g_exp, g_cross) = outs[7:12]
-    (wco, w1, w2, n2, dact, loss, stage, stage2, sems) = outs[12:]
+    row_outs, vec_grad, grad_outs = outs[:4], outs[4], outs[5:7]
+    (final_ref, g_second, g_cc, g_cc_t3, g_send, g_own) = outs[7:13]
+    (sec_low, hid, feed_low, g_exp, g_cross) = outs[13:18]
+    (wco, w1, w2, n2, dact, loss, stage, stage2, sems, out_sems) = outs[18:]
     z = lax.axis_index("seq")
     start_weight(sh, slots, 4 * n, n, wco, sems.at[0])
     for c in range(FFB):
@@ -873,9 +932,6 @@
         pad_start = jnp.where(is_pad, starts[p], pad_start)
         pad_end = jnp.where(is_pad, ends[p], pad_end)
     wait_all(wco, sems.at[0])
-    for c in range(FFB):
-        wait_all(w1.at[c], sems.at[1 + c])
-    wait_all(w2, sems.at[5])
 
     def add_vec(row, value):
         vec_grad[row : row + 1, :] = vec_grad[row : row + 1, :] + value
@@ -891,6 +947,13 @@
         sec_low[r, :] = low
         feed = second + vec[V_CB : V_CB + 1, :]
         wide = range(FFB)
+
+        @pl.when(i == 0)
+        def _():
+            for c in wide:
+                wait_all(w1.at[c], sems.at[1 + c])
+            wait_all(w2, sems.at[5])
+
         es = [mm(low, w1[c]) + vec[V_EB + c : V_EB + c + 1, :] for c in wide]
         sgs = [jax.nn.sigmoid(e) for e in es]
         hs = [(e * sg).astype(BF) for e, sg in zip(es, sgs)]
@@ -941,14 +1004,29 @@
     error_sum = jnp.sum(loss[0:1, :], axis=1, keepdims=True)
     vec_grad[V_LOSS : V_LOSS + 1, :] = digits(error_sum, bits)
     vec_grad[V_LIVE : V_LIVE + 1, :] = digits(jnp.full((1, 1), live_count.astype(F32)), bits)
-    stage[...] = mm_tn(cctx[...], g_cross[...]).astype(BF)
-    put_grad(sh, stage, n, 0, g_send, g_own)
+    copies = send_all((final_ref, g_second, g_cc, g_cc_t3), row_outs, out_sems)
+
+    def send_grad(full, size, row):
+        put_grad(sh, full, size, row, g_send, g_own)
+        copies.extend(
+            send_all(
+                [ref.at[:, pl.ds(row, size)] for ref in (g_send, g_own)],
+                [ref.at[:, pl.ds(row, size)] for ref in grad_outs],
+                out_sems,
+                len(copies),
+            )
+        )
+
+    for c in range(FFB):
+        stage2[pl.ds(c * D, D), :] = mm_tn(hid[c], feed_low[...]).astype(BF)
+    send_grad(stage2, wide, 5 * n)
     for c in range(FFB):
         stage[...] = mm_tn(sec_low[...], g_exp[c]).astype(BF)
-        put_grad(sh, stage, n, (1 + c) * n, g_send, g_own)
-    for c in range(FFB):
-        stage2[pl.ds(c * D, D), :] = mm_tn(hid[c], feed_low[...]).astype(BF)
-    put_grad(sh, stage2, wide, 5 * n, g_send, g_own)
+        send_grad(stage, n, (1 + c) * n)
+    stage[...] = mm_tn(cctx[...], g_cross[...]).astype(BF)
+    send_grad(stage, n, 0)
+    for copy in copies:
+        copy.wait()
 
 
 def feed(sh, lens, order, n1, cctx, targets, vec, slots):
@@ -965,6 +1043,12 @@
     ]
     scratch = [
         pltpu.VMEM((rows, D), BF),
+        pltpu.VMEM((rows, D), F32),
+        pltpu.VMEM((rows, D), BF),
+        pltpu.VMEM((nq, D, TILE), BF),
+        pltpu.VMEM((sh.count // 2, block, D), BF),
+        pltpu.VMEM((sh.count // 2, block, D), BF),
+        pltpu.VMEM((rows, D), BF),
         pltpu.VMEM((FFB, rows, D), BF),
         pltpu.VMEM((rows, D), BF),
         pltpu.VMEM((FFB, rows, D), BF),
@@ -978,6 +1062,7 @@
         pltpu.VMEM((D, D), BF),
         pltpu.VMEM((FFB * D, D), BF),
         pltpu.SemaphoreType.DMA((6,)),
+        pltpu.SemaphoreType.DMA((4 + 2 * (FFB + 2),)),
     ]
     specs = [SMEM_SPEC] * 2 + [VMEM_SPEC] * 4 + [ANY_SPEC] * len(slots)
     return call(
@@ -988,6 +1073,7 @@
         outs,
         scratch,
         17,
+        out_specs=[ANY_SPEC] * 4 + [VMEM_SPEC] + [ANY_SPEC] * 2,
     )
 
 
@@ -1561,8 +1647,9 @@
     for k in range(2, split):
         if k == split - 1:
             last = after(memory, *hold)
-            ups.append(lax.ppermute(last, "seq", [(0, split - 1)]))
-            downs.append(lax.ppermute(last, "seq", [(split - 1, 0)]))
+            ends = lax.ppermute(last, "seq", [(0, split - 1), (split - 1, 0)])
+            ups.append(ends)
+            downs.append(ends)
         else:
             ups.append(seq_up(after(ups[-1], *hold), split))
             downs.append(seq_down(after(downs[-1], *hold), split))
@@ -1654,12 +1741,13 @@
     mem_last = after(mem_parts[3], sum_a.send)
     mem_here = mem_last.astype(F32) + mem_got.astype(F32) + mem_far.astype(F32)
     memory_grad = seq_rest(mem_here.reshape(split // 4, sh.mem_rows, D), split)[0]
-    red_a, red_b, red_c = sum_a.finish(), sum_b.finish(), sum_c.finish()
+    sum_a.finish()
+    red_b, red_c = sum_b.finish(), sum_c.finish()
 
     def rows_of(array, start, size):
         return array[start : start + size].astype(F32)
 
-    done = finish(sh, red_a, expand_bias.shape[0])
+    done = finish(sh, sum_a.parts[0], sum_a.got, expand_bias.shape[0])
     small_grad = done[3 : 3 + V_EB]
     expand_bias_grad = done[3 + V_EB]
     loss_value = done[4 + V_EB].reshape(())

time: 276 us -> 268 us (0.971)
  starting transfers between devices: 72.3 us -> 60 us
  Pallas kernels: 80.7 us -> 86.2 us
  waiting for transfers between devices: 99.6 us -> 96.4 us
    ppermute x1, starting transfers between devices: 13.7 us -> 0.19 us  [shards(): mem_got = lax.ppermute(mem_parts[0], 'seq', swap)]
    ppermute x18, waiting for transfers between devices: 45 us -> 38.3 us  [start(): self.got = lax.ppermute(send, self.axis, pairs)]
    pallas_call x9, Pallas kernels: 80.7 us -> 86.2 us  [call(): pl.pallas_call(body, name=name, in_specs=specs, out_specs=out_specs or [V...]
    ppermute x2 -> x1, waiting for transfers between devices: 4.41 us -> 8.47 us  [shards(): ends = lax.ppermute(last, 'seq', [(0, split - 1), (split - 1, 0)])]
    ppermute x18, starting transfers between devices: 17.7 us -> 21.6 us  [start(): self.got = lax.ppermute(send, self.axis, pairs)]
    ppermute x2 -> x1, starting transfers between devices: 9.22 us -> 5.32 us  [shards(): ends = lax.ppermute(last, 'seq', [(0, split - 1), (split - 1, 0)])]
  transfers between devices with their start and end apart: 45 -> 44, of which waited for: 25 -> 25; matrix products, arithmetic and copies ran while one was open for 6% -> 6% of each run, Pallas kernels for 18% -> 20%
where the time goes in v4:
time: 268 us; the launch traced here: 267 us
  waiting for transfers between devices  96.4 us (36%)
  Pallas kernels  86.2 us (32%)
  starting transfers between devices  60 us (22%)
  other arithmetic  19.1 us (7%)
  local copies, waits for them, and re-layouts  3.47 us (1%)
    pallas_call x9, Pallas kernels, call(): pl.pallas_call(body, name=name, in_specs=specs, out_specs=out_specs or [V...  86.2 us
    ppermute x18, waiting for transfers between devices, start(): self.got = lax.ppermute(send, self.axis, pairs)  38.3 us
    ppermute x18, starting transfers between devices, start(): self.got = lax.ppermute(send, self.axis, pairs)  21.6 us
    ppermute x4, starting transfers between devices, seq_up(): return lax.ppermute(a, 'seq', [(i, i + 1) for i in range(count - 1)])  17.5 us
    ppermute x2, waiting for transfers between devices, shards(): lax.ppermute(after(a, *hold), 'fsdp', p)  12.8 us
    ppermute x4, waiting for transfers between devices, seq_down(): return lax.ppermute(a, 'seq', [(i + 1, i) for i in range(count - 1)])  9.97 us
    ppermute x1, waiting for transfers between devices, shards(): ends = lax.ppermute(last, 'seq', [(0, split - 1), (split - 1, 0)])  8.47 us
    convert_element_type x12, other arithmetic, sum_low(): return total.astype(BF)  8.39 us
  transfers between devices with their start and end apart: 44, of which 25 were waited for; matrix products, arithmetic and copies ran while one was open for 6% of the time, Pallas kernels for 20%

profile of v4, /device:TPU:0, one launch (start us, length us, event | category | flops | bytes accessed | tf_op | source)
XLA Modules:
  0.0 266.6 jit_solution(13209038824792214817)
XLA Ops:
  3.8 4.5 %collective-permute-start = (bf16[512,512]{1,0:T(8,128)(2,1)}, bf16[512,512]{1,0:T(8,128)(2,1)S(1)}, u32[]{:S(2)}, u32[]{:S(2)}) collective-permute-start(bf16[512,512]{1,0:T(8,128)(2,1)} %refs_5_.3), channel_id=1, source_target_pairs={{0,1},{1,2},{2,3},{4,5},{5,6},{6,7},{8,9},{9,10},{10,11},{12,13},{... | collective-permute-start | bytes 1572872 | tf_op jit(solution)/shard_map/ppermute | solution.py:190
  12.7 5.3 %collective-permute-done.3.refs_7_.refs_13_.refs_10_ = bf16[224,512]{1,0:T(8,128)(2,1)S(1)} collective-permute-done((bf16[224,512]{1,0:T(8,128)(2,1)}, bf16[224,512]{1,0:T(8,128)(2,1)S(1)}, u32[]{:S(2)}, u32[]{:S(2)}) %collective-permute-start.3) | collective-permute-done | bytes 229408 | tf_op jit(solution)/shard_map/ppermute | solution.py:1634
  20.4 4.1 %collective-permute-done.1.refs_8_.refs_15_ = bf16[512,512]{1,0:T(8,128)(2,1)} collective-permute-done((bf16[512,512]{1,0:T(8,128)(2,1)}, bf16[512,512]{1,0:T(8,128)(2,1)}, u32[]{:S(2)}, u32[]{:S(2)}) %collective-permute-start.1) | collective-permute-done | bytes 524320 | tf_op jit(solution)/shard_map/ppermute | solution.py:194
  31.0 4.3 %collective-permute-start.6 = (bf16[512,512]{1,0:T(8,128)(2,1)}, bf16[512,512]{1,0:T(8,128)(2,1)}, u32[]{:S(2)}, u32[]{:S(2)}) collective-permute-start(bf16[512,512]{1,0:T(8,128)(2,1)} %refs_13_.3), channel_id=1, source_target_pairs={{0,1},{1,2},{2,3},{4,5},{5,6},{6,7},{8,9},{9,10},{10,11},{12,13},{... | collective-permute-start | bytes 1572872 | tf_op jit(solution)/shard_map/ppermute | solution.py:190
  35.8 12.8 %collective-permute-done.9.refs_8_.refs_14_.refs_11_ = bf16[224,512]{1,0:T(8,128)(2,1)S(1)} collective-permute-done((bf16[224,512]{1,0:T(8,128)(2,1)S(1)}, bf16[224,512]{1,0:T(8,128)(2,1)S(1)}, u32[]{:S(2)}, u32[]{:S(2)}) %collective-permute-start.9) | collective-permute-done | bytes 229408 | tf_op jit(solution)/shard_map/ppermute | solution.py:1642
  48.7 3.8 %collective-permute-done.6.refs_7_.refs_14_ = bf16[512,512]{1,0:T(8,128)(2,1)} collective-permute-done((bf16[512,512]{1,0:T(8,128)(2,1)}, bf16[512,512]{1,0:T(8,128)(2,1)}, u32[]{:S(2)}, u32[]{:S(2)}) %collective-permute-start.6) | collective-permute-done | bytes 524320 | tf_op jit(solution)/shard_map/ppermute | solution.py:190
  56.9 5.2 %collective-permute-start.16 = (bf16[512,512]{1,0:T(8,128)(2,1)}, bf16[512,512]{1,0:T(8,128)(2,1)}, u32[]{:S(2)}, u32[]{:S(2)}) collective-permute-start(bf16[512,512]{1,0:T(8,128)(2,1)} %collective-permute-done.6.refs_7_.refs_14_), channel_id=1, source_target_pairs={{0,1},{1,2},{2,3},{4,5},{5,6},{6,7},{8,9},{9,10},{10,11},{12,13},{... | collective-permute-start | bytes 1572872 | tf_op jit(solution)/shard_map/ppermute | solution.py:190
  63.3 5.3 %collective-permute-start.18 = (bf16[512,512]{1,0:T(8,128)(2,1)}, bf16[512,512]{1,0:T(8,128)(2,1)S(1)}, u32[]{:S(2)}, u32[]{:S(2)}) collective-permute-start(bf16[512,512]{1,0:T(8,128)(2,1)} %refs_13_.3), channel_id=1, source_target_pairs={{0,3},{3,0},{4,7},{7,4},{8,11},{11,8},{12,15},{15,12},{16,19},{19,... | collective-permute-start | bytes 1572872 | tf_op jit(solution)/shard_map/ppermute | solution.py:1650
  71.3 9.3 %self_forward.1 = (bf16[512,512]{1,0:T(8,128)(2,1)}, bf16[2,512,256]{2,1,0:T(8,128)(2,1)}, bf16[6,256,512]{2,1,0:T(8,128)(2,1)}, bf16[6,256,512]{2,1,0:T(8,128)(...) custom-call(s32[1,4]{1,0:T(1,128)} %refs_0_.13, ...), custom_call_target="tpu_custom_call" | custom-call | flops 480000000 | bytes 216597 | tf_op jit(solution)/shard_map/self_forward/pallas_call | solution.py:536
  80.7 8.5 %collective-permute-done.18.refs_11_.refs_12_.refs_18_.refs_19_ = bf16[512,512]{1,0:T(8,128)(2,1)S(1)} collective-permute-done((bf16[512,512]{1,0:T(8,128)(2,1)}, bf16[512,512]{1,0:T(8,128)(2,1)S(1)}, u32[]{:S(2)}, u32[]{:S(2)}) %collective-permute-start.18) | collective-permute-done | bytes 524320 | tf_op jit(solution)/shard_map/ppermute | solution.py:1650
  92.7 12.1 %cross_forward.1 = (f32[512,512]{1,0:T(8,128)}, f32[512,1]{1,0:T(8,128)}, bf16[512,512]{1,0:T(8,128)(2,1)}, bf16[512,512]{1,0:T(8,128)(2,1)}, bf16[2,512,256]{2,...) custom-call(s32[1,4]{1,0:T(1,128)} %refs_0_.13, ...), custom_call_target="tpu_custom_call" | custom-call | flops 630000000 | bytes 442082 | tf_op jit(solution)/shard_map/cross_forward/pallas_call | solution.py:536
  104.8 16.9 %feed.1 = (bf16[512,512]{1,0:T(8,128)(2,1)}, f32[512,512]{1,0:T(8,128)}, bf16[512,512]{1,0:T(8,128)(2,1)}, bf16[2,512,256]{2,1,0:T(8,128)(2,1)}, f32[32,512]{1,0...) custom-call(s32[1,4]{1,0:T(1,128)} %refs_0_.13, s32[1,4]{1,0:T(1,128)} %refs_1_.13, ...), custom_call_target="tpu_custom_call" | custom-call | flops 510000000 | bytes 327680 | tf_op jit(solution)/shard_map/feed/pallas_call | solution.py:536
  124.8 4.4 %collective-permute-done.21 = bf16[4,576,512]{2,1,0:T(8,128)(2,1)S(1)} collective-permute-done((bf16[4,576,512]{2,1,0:T(8,128)(2,1)}, bf16[4,576,512]{2,1,0:T(8,128)(2,1)S(1)}, u32[]{:S(2)}, u32[]{:S(2)}) %collective-permute-start.21) | collective-permute-done | bytes 2359328 | tf_op jit(solution)/shard_map/ppermute | solution.py:139
  131.8 15.3 %cross_backward.1 = (bf16[2,256,512]{2,1,0:T(8,128)(2,1)}, bf16[2,256,512]{2,1,0:T(8,128)(2,1)}, bf16[2,256,512]{2,1,0:T(8,128)(2,1)}, bf16[2,256,512]{2,1,0:T(8...) custom-call(s32[1,4]{1,0:T(1,128)} %refs_0_.13, ...), custom_call_target="tpu_custom_call" | custom-call | flops 450000000 | bytes 461702 | tf_op jit(solution)/shard_map/cross_backward/pallas_call | solution.py:536
  149.8 9.7 %first_backward.1 = (bf16[4,256,512]{2,1,0:T(8,128)(2,1)}, bf16[4,256,512]{2,1,0:T(8,128)(2,1)}, f32[512,512]{1,0:T(8,128)}, bf16[512,512]{1,0:T(8,128)(2,1)}, b...) custom-call(s32[1,4]{1,0:T(1,128)} %refs_0_.13, s32[1,4]{1,0:T(1,128)} %refs_1_.13, s32[1,4]{1,0:T(1,128)} %refs_2_.8, ...), custom_call_target="tpu_custom_call" | custom-call | flops 180000000 | bytes 454861 | tf_op jit(solution)/shard_map/first_backward/pallas_call | solution.py:536
  163.2 4.4 %collective-permute-start.28 = (bf16[4,256,512]{2,1,0:T(8,128)(2,1)}, bf16[4,256,512]{2,1,0:T(8,128)(2,1)S(1)}, u32[]{:S(2)}, u32[]{:S(2)}) collective-permute-start(bf16[4,256,512]{2,1,0:T(8,128)(2,1)} %get-tuple-element.195), channel_id=1, source_target_pairs={{0,4},{4,0},{8,12},{12,8},{16,20},{20,16},{24,28},{28,24},{1,5},{5... | collective-permute-start | bytes 3145736 | tf_op jit(solution)/shard_map/ppermute | solution.py:139
  169.6 11.5 %self_backward.1 = (bf16[2,512,512]{2,1,0:T(8,128)(2,1)}, bf16[512,512]{1,0:T(8,128)(2,1)}, bf16[6,256,512]{2,1,0:T(8,128)(2,1)}, bf16[6,256,512]{2,1,0:T(8,128)(2,1)}) custom-call(s32[1,4]{1,0:T(1,128)} %refs_0_.13, s32[1,4]{1,0:T(1,128)} %refs_1_.13, bf16[512,512]{1,0:T(8,128)(2,1)} %get-tuple-element.153.refs_2_, ...), custom_call_target="tpu_custom_call" | custom-call | flops 420000000 | bytes 288686 | tf_op jit(solution)/shard_map/self_backward/pallas_call | solution.py:536
  181.1 7.7 %collective-permute-done.27 = bf16[288,512]{1,0:T(8,128)(2,1)} collective-permute-done((bf16[288,512]{1,0:T(8,128)(2,1)S(1)}, bf16[288,512]{1,0:T(8,128)(2,1)}, u32[]{:S(2)}, u32[]{:S(2)}) %collective-permute-start.27) | collective-permute-done | bytes 294944 | tf_op jit(solution)/shard_map/ppermute | solution.py:139
  190.8 8.2 %collective-permute-done.25 = bf16[2,256,512]{2,1,0:T(8,128)(2,1)S(1)} collective-permute-done((bf16[2,256,512]{2,1,0:T(8,128)(2,1)}, bf16[2,256,512]{2,1,0:T(8,128)(2,1)S(1)}, u32[]{:S(2)}, u32[]{:S(2)}) %collective-permute-start.25) | collective-permute-done | bytes 524320 | tf_op jit(solution)/shard_map/ppermute | solution.py:1706
  205.1 7.1 %self_weights.1 = (bf16[4,224,512]{2,1,0:T(8,128)(2,1)}, bf16[4,224,512]{2,1,0:T(8,128)(2,1)}, f32[512,512]{1,0:T(8,128)}) custom-call(bf16[512,512]{1,0:T(8,128)(2,1)} %get-tuple-element.196.refs_0_, bf16[6,256,512]{2,1,0:T(8,128)(2,1)} %get-tuple-element.197.refs_1_, bf16[6,256,512]{2,1,0:T(8,128)(2,1)} %get-tuple-element.198.refs_2_, ...), custom_call_target="tpu_custom_call" | custom-call | flops 210000000 | bytes 221511 | tf_op jit(solution)/shard_map/self_weights/pallas_call | solution.py:536
  218.2 5.8 %collective-permute-done.34 = bf16[512,512]{1,0:T(8,128)(2,1)S(1)} collective-permute-done((bf16[512,512]{1,0:T(8,128)(2,1)}, bf16[512,512]{1,0:T(8,128)(2,1)S(1)}, u32[]{:S(2)}, u32[]{:S(2)}) %collective-permute-start.34) | collective-permute-done | bytes 524320 | tf_op jit(solution)/shard_map/ppermute | solution.py:194
  235.1 4.8 %collective-permute-done.32 = bf16[2,224,512]{2,1,0:T(8,128)(2,1)S(1)} collective-permute-done((bf16[2,224,512]{2,1,0:T(8,128)(2,1)S(1)}, bf16[2,224,512]{2,1,0:T(8,128)(2,1)S(1)}, u32[]{:S(2)}, u32[]{:S(2)}) %collective-permute-start.32) | collective-permute-done | bytes 458784 | tf_op jit(solution)/shard_map/ppermute | solution.py:139
  242.4 3.7 %collective-permute-done.33 = bf16[1,224,512]{2,1,0:T(8,128)(2,1)S(1)} collective-permute-done((bf16[1,224,512]{2,1,0:T(8,128)(2,1)S(1)}, bf16[1,224,512]{2,1,0:T(8,128)(2,1)S(1)}, u32[]{:S(2)}, u32[]{:S(2)}) %collective-permute-start.33) | collective-permute-done | bytes 229408 | tf_op jit(solution)/shard_map/ppermute | solution.py:139
  253.4 4.2 %collective-permute-done.42 = bf16[128,512]{1,0:T(8,128)(2,1)S(1)} collective-permute-done((bf16[128,512]{1,0:T(8,128)(2,1)S(1)}, bf16[128,512]{1,0:T(8,128)(2,1)S(1)}, u32[]{:S(2)}, u32[]{:S(2)}) %collective-permute-start.42) | collective-permute-done | bytes 131104 | tf_op jit(solution)/shard_map/ppermute | solution.py:139
  (154 shorter events, 86.2 us)
Async XLA Ops:
  3.2 21.3 %collective-permute-start.4 = (bf16[832,512]{1,0:T(8,128)(2,1)}, bf16[832,512]{1,0:T(8,128)(2,1)S(1)}, u32[]{:S(2)}, u32[]{:S(2)}) collective-permute-start(bf16[832,512]{1,0:T(8,128)(2,1)} %get-tuple-element.135.refs_13_.refs_6_.refs_12_.refs_20_), channel_id=1, source_target_pairs={{0,4},{4,0},{8,12},{12,8},{16,20},{20,16},{24,28},{28,24},{1,5},{5... | collective-permute-start | bytes 2555912 | tf_op jit(solution)/shard_map/ppermute | solution.py:1633
  3.8 16.6 %collective-permute-start = (bf16[512,512]{1,0:T(8,128)(2,1)}, bf16[512,512]{1,0:T(8,128)(2,1)S(1)}, u32[]{:S(2)}, u32[]{:S(2)}) collective-permute-start(bf16[512,512]{1,0:T(8,128)(2,1)} %refs_5_.3), channel_id=1, source_target_pairs={{0,1},{1,2},{2,3},{4,5},{5,6},{6,7},{8,9},{9,10},{10,11},{12,13},{... | collective-permute-start | bytes 1572872 | tf_op jit(solution)/shard_map/ppermute | solution.py:190
  8.3 16.2 %collective-permute-start.1 = (bf16[512,512]{1,0:T(8,128)(2,1)}, bf16[512,512]{1,0:T(8,128)(2,1)}, u32[]{:S(2)}, u32[]{:S(2)}) collective-permute-start(bf16[512,512]{1,0:T(8,128)(2,1)} %refs_13_.3), channel_id=1, source_target_pairs={{1,0},{2,1},{3,2},{5,4},{6,5},{7,6},{9,8},{10,9},{11,10},{13,12},{... | collective-permute-start | bytes 1572872 | tf_op jit(solution)/shard_map/ppermute | solution.py:194
  24.5 28.0 %collective-permute-start.8 = (bf16[832,512]{1,0:T(8,128)(2,1)}, bf16[832,512]{1,0:T(8,128)(2,1)S(1)}, u32[]{:S(2)}, u32[]{:S(2)}) collective-permute-start(bf16[832,512]{1,0:T(8,128)(2,1)} %get-tuple-element.135.refs_13_.refs_6_.refs_12_.refs_20_), channel_id=1, source_target_pairs={{0,16},{4,12},{8,24},{12,4},{16,0},{20,28},{24,8},{28,20},{1,17},{... | collective-permute-start | bytes 2555912 | tf_op jit(solution)/shard_map/ppermute | solution.py:1640
  26.1 26.4 %collective-permute-start.7 = (bf16[832,512]{1,0:T(8,128)(2,1)}, bf16[832,512]{1,0:T(8,128)(2,1)S(1)}, u32[]{:S(2)}, u32[]{:S(2)}) collective-permute-start(bf16[832,512]{1,0:T(8,128)(2,1)} %get-tuple-element.135.refs_13_.refs_6_.refs_12_.refs_20_), channel_id=1, source_target_pairs={{0,8},{4,20},{8,0},{12,28},{16,24},{20,4},{24,16},{28,12},{1,9},{5... | collective-permute-start | bytes 2555912 | tf_op jit(solution)/shard_map/ppermute | solution.py:1640
  27.6 21.1 %collective-permute-start.5 = (bf16[512,512]{1,0:T(8,128)(2,1)S(1)}, bf16[512,512]{1,0:T(8,128)(2,1)S(1)}, u32[]{:S(2)}, u32[]{:S(2)}) collective-permute-start(bf16[512,512]{1,0:T(8,128)(2,1)S(1)} %collective-permute-done.refs_3_.refs_6_), channel_id=1, source_target_pairs={{0,1},{1,2},{2,3},{4,5},{5,6},{6,7},{8,9},{9,10},{10,11},{12,13},{... | collective-permute-start | bytes 1572872 | tf_op jit(solution)/shard_map/ppermute | solution.py:190
  31.0 21.5 %collective-permute-start.6 = (bf16[512,512]{1,0:T(8,128)(2,1)}, bf16[512,512]{1,0:T(8,128)(2,1)}, u32[]{:S(2)}, u32[]{:S(2)}) collective-permute-start(bf16[512,512]{1,0:T(8,128)(2,1)} %refs_13_.3), channel_id=1, source_target_pairs={{0,1},{1,2},{2,3},{4,5},{5,6},{6,7},{8,9},{9,10},{10,11},{12,13},{... | collective-permute-start | bytes 1572872 | tf_op jit(solution)/shard_map/ppermute | solution.py:190
  35.3 13.3 %collective-permute-start.9 = (bf16[224,512]{1,0:T(8,128)(2,1)S(1)}, bf16[224,512]{1,0:T(8,128)(2,1)S(1)}, u32[]{:S(2)}, u32[]{:S(2)}) collective-permute-start(bf16[224,512]{1,0:T(8,128)(2,1)S(1)} %collective-permute-done.2.refs_6_.refs_12_.refs_9_), channel_id=1, source_target_pairs={{0,16},{4,12},{8,24},{12,4},{16,0},{20,28},{24,8},{28,20},{1,17},{... | collective-permute-start | bytes 688136 | tf_op jit(solution)/shard_map/ppermute | solution.py:1642
  52.6 16.1 %collective-permute-start.11 = (bf16[832,512]{1,0:T(8,128)(2,1)S(1)}, bf16[832,512]{1,0:T(8,128)(2,1)S(1)}, u32[]{:S(2)}, u32[]{:S(2)}) collective-permute-start(bf16[832,512]{1,0:T(8,128)(2,1)S(1)} %collective-permute-done.8.refs_15_.refs_8_.refs_14_.refs_22_), channel_id=1, source_target_pairs={{0,4},{4,0},{8,12},{12,8},{16,20},{20,16},{24,28},{28,24},{1,5},{5... | collective-permute-start | bytes 2555912 | tf_op jit(solution)/shard_map/ppermute | solution.py:1660
  53.2 36.0 %collective-permute-start.19 = (bf16[832,512]{1,0:T(8,128)(2,1)S(1)}, bf16[832,512]{1,0:T(8,128)(2,1)}, u32[]{:S(2)}, u32[]{:S(2)}) collective-permute-start(bf16[832,512]{1,0:T(8,128)(2,1)S(1)} %collective-permute-done.7.refs_14_.refs_7_.refs_13_.refs_21_), channel_id=1, source_target_pairs={{0,16},{4,12},{8,24},{12,4},{16,0},{20,28},{24,8},{28,20},{1,17},{... | collective-permute-start | bytes 2555912 | tf_op jit(solution)/shard_map/ppermute | solution.py:1645
  56.9 23.8 %collective-permute-start.16 = (bf16[512,512]{1,0:T(8,128)(2,1)}, bf16[512,512]{1,0:T(8,128)(2,1)}, u32[]{:S(2)}, u32[]{:S(2)}) collective-permute-start(bf16[512,512]{1,0:T(8,128)(2,1)} %collective-permute-done.6.refs_7_.refs_14_), channel_id=1, source_target_pairs={{0,1},{1,2},{2,3},{4,5},{5,6},{6,7},{8,9},{9,10},{10,11},{12,13},{... | collective-permute-start | bytes 1572872 | tf_op jit(solution)/shard_map/ppermute | solution.py:190
  62.0 18.6 %collective-permute-start.17 = (bf16[512,512]{1,0:T(8,128)(2,1)}, bf16[512,512]{1,0:T(8,128)(2,1)}, u32[]{:S(2)}, u32[]{:S(2)}) collective-permute-start(bf16[512,512]{1,0:T(8,128)(2,1)} %collective-permute-done.1.refs_8_.refs_15_), channel_id=1, source_target_pairs={{1,0},{2,1},{3,2},{5,4},{6,5},{7,6},{9,8},{10,9},{11,10},{13,12},{... | collective-permute-start | bytes 1572872 | tf_op jit(solution)/shard_map/ppermute | solution.py:194
  63.3 25.8 %collective-permute-start.18 = (bf16[512,512]{1,0:T(8,128)(2,1)}, bf16[512,512]{1,0:T(8,128)(2,1)S(1)}, u32[]{:S(2)}, u32[]{:S(2)}) collective-permute-start(bf16[512,512]{1,0:T(8,128)(2,1)} %refs_13_.3), channel_id=1, source_target_pairs={{0,3},{3,0},{4,7},{7,4},{8,11},{11,8},{12,15},{15,12},{16,19},{19,... | collective-permute-start | bytes 1572872 | tf_op jit(solution)/shard_map/ppermute | solution.py:1650
  131.7 16.4 %collective-permute-start.22 = (bf16[2,576,512]{2,1,0:T(8,128)(2,1)S(1)}, bf16[2,576,512]{2,1,0:T(8,128)(2,1)}, u32[]{:S(2)}, u32[]{:S(2)}) collective-permute-start(bf16[2,576,512]{2,1,0:T(8,128)(2,1)S(1)} %add_convert_fusion), channel_id=1, source_target_pairs={{0,8},{4,20},{8,0},{12,28},{16,24},{20,4},{24,16},{28,12},{1,9},{5... | collective-permute-start | bytes 3538952 | tf_op jit(solution)/shard_map/ppermute | solution.py:139
  163.2 26.7 %collective-permute-start.28 = (bf16[4,256,512]{2,1,0:T(8,128)(2,1)}, bf16[4,256,512]{2,1,0:T(8,128)(2,1)S(1)}, u32[]{:S(2)}, u32[]{:S(2)}) collective-permute-start(bf16[4,256,512]{2,1,0:T(8,128)(2,1)} %get-tuple-element.195), channel_id=1, source_target_pairs={{0,4},{4,0},{8,12},{12,8},{16,20},{20,16},{24,28},{28,24},{1,5},{5... | collective-permute-start | bytes 3145736 | tf_op jit(solution)/shard_map/ppermute | solution.py:139
  167.6 21.2 %collective-permute-start.27 = (bf16[288,512]{1,0:T(8,128)(2,1)S(1)}, bf16[288,512]{1,0:T(8,128)(2,1)}, u32[]{:S(2)}, u32[]{:S(2)}) collective-permute-start(bf16[288,512]{1,0:T(8,128)(2,1)S(1)} %select_bitcast_fusion), channel_id=1, source_target_pairs={{0,1},{1,0},{2,3},{3,2},{4,5},{5,4},{6,7},{7,6},{8,9},{9,8},{10,11... | collective-permute-start | bytes 884744 | tf_op jit(solution)/shard_map/ppermute | solution.py:139
  167.9 31.1 %collective-permute-start.25 = (bf16[2,256,512]{2,1,0:T(8,128)(2,1)}, bf16[2,256,512]{2,1,0:T(8,128)(2,1)S(1)}, u32[]{:S(2)}, u32[]{:S(2)}) collective-permute-start(bf16[2,256,512]{2,1,0:T(8,128)(2,1)} %get-tuple-element.190), channel_id=1, source_target_pairs={{0,1},{1,0},{2,3},{3,2},{4,5},{5,4},{6,7},{7,6},{8,9},{9,8},{10,11... | collective-permute-start | bytes 1572872 | tf_op jit(solution)/shard_map/ppermute | solution.py:1706
  169.6 29.4 %collective-permute-start.26 = (bf16[2,256,512]{2,1,0:T(8,128)(2,1)}, bf16[2,256,512]{2,1,0:T(8,128)(2,1)S(1)}, u32[]{:S(2)}, u32[]{:S(2)}) collective-permute-start(bf16[2,256,512]{2,1,0:T(8,128)(2,1)} %add_convert_fusion.4), channel_id=1, source_target_pairs={{0,2},{1,3},{2,0},{3,1},{4,6},{5,7},{6,4},{7,5},{8,10},{9,11},{10,... | collective-permute-start | bytes 1572872 | tf_op jit(solution)/shard_map/ppermute | solution.py:1707
  199.1 14.7 %collective-permute-start.30 = (bf16[288,512]{1,0:T(8,128)(2,1)S(1)}, bf16[288,512]{1,0:T(8,128)(2,1)}, u32[]{:S(2)}, u32[]{:S(2)}) collective-permute-start(bf16[288,512]{1,0:T(8,128)(2,1)S(1)} %fusion.1), channel_id=1, source_target_pairs={{0,2},{1,3},{2,0},{3,1},{4,6},{5,7},{6,4},{7,5},{8,10},{9,11},{10,... | collective-permute-start | bytes 884744 | tf_op jit(solution)/shard_map/ppermute | solution.py:139
  200.3 14.5 %collective-permute-start.29 = (bf16[2,256,512]{2,1,0:T(8,128)(2,1)}, bf16[2,256,512]{2,1,0:T(8,128)(2,1)}, u32[]{:S(2)}, u32[]{:S(2)}) collective-permute-start(bf16[2,256,512]{2,1,0:T(8,128)(2,1)} %add_convert_fusion.3), channel_id=1, source_target_pairs={{0,8},{4,20},{8,0},{12,28},{16,24},{20,4},{24,16},{28,12},{1,9},{5... | collective-permute-start | bytes 1572872 | tf_op jit(solution)/shard_map/ppermute | solution.py:139
  203.8 20.2 %collective-permute-start.34 = (bf16[512,512]{1,0:T(8,128)(2,1)}, bf16[512,512]{1,0:T(8,128)(2,1)S(1)}, u32[]{:S(2)}, u32[]{:S(2)}) collective-permute-start(bf16[512,512]{1,0:T(8,128)(2,1)} %slice_bitcast_fusion), channel_id=1, source_target_pairs={{1,0},{2,1},{3,2},{5,4},{6,5},{7,6},{9,8},{10,9},{11,10},{13,12},{... | collective-permute-start | bytes 1572872 | tf_op jit(solution)/shard_map/ppermute | solution.py:194
  215.9 13.8 %collective-permute-start.31 = (bf16[4,224,512]{2,1,0:T(8,128)(2,1)}, bf16[4,224,512]{2,1,0:T(8,128)(2,1)S(1)}, u32[]{:S(2)}, u32[]{:S(2)}) collective-permute-start(bf16[4,224,512]{2,1,0:T(8,128)(2,1)} %get-tuple-element.204), channel_id=1, source_target_pairs={{0,4},{4,0},{8,12},{12,8},{16,20},{20,16},{24,28},{28,24},{1,5},{5... | collective-permute-start | bytes 2752520 | tf_op jit(solution)/shard_map/ppermute | solution.py:139
  216.0 12.7 %collective-permute-start.37 = (bf16[288,512]{1,0:T(8,128)(2,1)S(1)}, bf16[288,512]{1,0:T(8,128)(2,1)S(1)}, u32[]{:S(2)}, u32[]{:S(2)}) collective-permute-start(bf16[288,512]{1,0:T(8,128)(2,1)S(1)} %add_convert_fusion.6), channel_id=1, source_target_pairs={{0,1},{1,0},{2,3},{3,2},{4,5},{5,4},{6,7},{7,6},{8,9},{9,8},{10,11... | collective-permute-start | bytes 884744 | tf_op jit(solution)/shard_map/ppermute | solution.py:139
  224.1 16.0 %collective-permute-start.35 = (bf16[512,512]{1,0:T(8,128)(2,1)S(1)}, bf16[512,512]{1,0:T(8,128)(2,1)S(1)}, u32[]{:S(2)}, u32[]{:S(2)}) collective-permute-start(bf16[512,512]{1,0:T(8,128)(2,1)S(1)} %fusion), channel_id=1, source_target_pairs={{1,0},{2,1},{3,2},{5,4},{6,5},{7,6},{9,8},{10,9},{11,10},{13,12},{... | collective-permute-start | bytes 1572872 | tf_op jit(solution)/shard_map/ppermute | solution.py:194
  (46 other events, 565.2 us)

commit v5 on v4

--- a/solution.py
+++ b/solution.py
@@ -465,7 +465,8 @@
         q_t3[i] = q.T
         return carry
 
-    lax.fori_loop(0, tiles, own_rows, 0)
+    for i in range(tiles):
+        own_rows(i, 0)
     q_copies = send_all((q_ref, q_t3), kept[:2], q_sems)
     wait_all(wk, sems.at[1])
     wait_all(wv, sems.at[2])
@@ -801,7 +802,8 @@
         q_t3[i] = q.T
         return carry
 
-    lax.fori_loop(0, rows // TILE, own_rows, 0)
+    for i in range(rows // TILE):
+        own_rows(i, 0)
     row_copies = send_all((n1, first_low, q_ref, q_t3), (n1_out, *early), row_sems)
     wait_all(wck, sems.at[2])
     wait_all(wcv, sems.at[3])
@@ -937,7 +939,7 @@
         vec_grad[row : row + 1, :] = vec_grad[row : row + 1, :] + value
 
     def chunk(i, carry):
-        r = pl.ds(pl.multiple_of(i * TILE, TILE), TILE)
+        r = pl.ds(i * rows, rows)
         first = n1[r, :] * vec[V_G1 : V_G1 + 1, :] + vec[V_S1 : V_S1 + 1, :]
         v = first + (mm(cctx[r, :], wco[...]) + vec[V_COB : V_COB + 1, :])
         normal2, inv2 = norm_stats(v)
@@ -948,12 +950,10 @@
         feed = second + vec[V_CB : V_CB + 1, :]
         wide = range(FFB)
 
-        @pl.when(i == 0)
-        def _():
+        if i == 0:
             for c in wide:
                 wait_all(w1.at[c], sems.at[1 + c])
             wait_all(w2, sems.at[5])
-
         es = [mm(low, w1[c]) + vec[V_EB + c : V_EB + c + 1, :] for c in wide]
         sgs = [jax.nn.sigmoid(e) for e in es]
         hs = [(e * sg).astype(BF) for e, sg in zip(es, sgs)]
@@ -966,7 +966,7 @@
         final = normal3 * vec[V_G3 : V_G3 + 1, :] + vec[V_S3 : V_S3 + 1, :]
         final_ref[r, :] = final.astype(BF)
         diff = final - targets[r, :].astype(F32)
-        pos = z * rows + i * TILE + lax.broadcasted_iota(jnp.int32, (TILE, 1), 0)
+        pos = z * rows + i * rows + lax.broadcasted_iota(jnp.int32, (rows, 1), 0)
         live = jnp.where((pos >= pad_start) & (pos < pad_end), 0.0, 1.0)
         g = live * diff
         loss[0:1, :] = loss[0:1, :] + col_sum(g * diff)
@@ -993,10 +993,11 @@
         add_vec(V_COB, col_sum(gc))
         gcc = mm_nt(gc, wco[...]).astype(BF)
         g_cc[r, :] = gcc
-        g_cc_t3[i] = gcc.T
+        for b in range(rows // TILE):
+            g_cc_t3[b] = gcc[b * TILE : (b + 1) * TILE, :].T
         return carry
 
-    lax.fori_loop(0, rows // TILE, chunk, 0)
+    chunk(0, 0)
     live_count = jnp.int32(rows) - jnp.maximum(
         jnp.minimum(pad_end, (z + 1) * rows) - jnp.maximum(pad_start, z * rows), 0
     )
@@ -1056,8 +1057,8 @@
         pltpu.VMEM((D, D), BF),
         pltpu.VMEM((FFB, D, D), BF),
         pltpu.VMEM((FFB * D, D), BF),
-        pltpu.VMEM((TILE, D), F32),
-        pltpu.VMEM((FFB, TILE, D), F32),
+        pltpu.VMEM((rows, D), F32),
+        pltpu.VMEM((FFB, rows, D), F32),
         pltpu.VMEM((8, D), F32),
         pltpu.VMEM((D, D), BF),
         pltpu.VMEM((FFB * D, D), BF),
@@ -1089,10 +1090,11 @@
     (q_ref, q_t3, *kept, cctx_t3, lse, g_cc, g_cc_t3) = refs[:9]
     slots = refs[9 : 9 + count]
     outs = refs[9 + count :]
-    mem_parts = outs[:4]
+    part_outs = outs[:4]
     (dq, *low_out) = outs[4:7]
     (wck, wcv, q_t, g_t, q_m, g_m, delta, bias, dk, dv, dq_t) = outs[7:18]
-    (mk3, mv3, mk_t3, k_low3, v_low3, bounds, sems, tile_sems, low_sems) = outs[18:]
+    (mk3, mv3, mk_t3, k_low3, v_low3, bounds, sems, tile_sems, low_sems) = outs[18:27]
+    mem_parts, part_sems = outs[27:31], outs[31]
     for i, w in enumerate((wck, wcv)):
         start_weight(sh, slots, (2 + i) * n, n, w, sems.at[i])
     slot_bounds(lens, order, bounds)
@@ -1184,10 +1186,14 @@
 
         return carry
 
+    copies = []
     for slot, out in enumerate(mem_parts):
         lax.fori_loop(
             0, sh.m_blocks // 4, lambda i, c, slot=slot, out=out: mem_tile(i, c, slot, out), 0
         )
+        copies += send_all([out], [part_outs[slot]], part_sems, slot)
+    for copy in copies:
+        copy.wait()
 
     def settle(t):
         for copy in low_copies(t):
@@ -1225,6 +1231,7 @@
         pltpu.SemaphoreType.DMA((3, nm)),
         pltpu.SemaphoreType.DMA((2, nm)),
     ]
+    scratch += [pltpu.VMEM((nm // 4, TILE, D), BF)] * 4 + [pltpu.SemaphoreType.DMA((4,))]
     specs = [SMEM_SPEC] * 3 + [VMEM_SPEC] * 2 + [ANY_SPEC] * 3 + [VMEM_SPEC] * 4
     specs += [ANY_SPEC] * len(slots)
     return call(
@@ -1235,7 +1242,7 @@
         outs,
         scratch,
         15,
-        out_specs=[VMEM_SPEC] * 5 + [ANY_SPEC] * 2,
+        out_specs=[ANY_SPEC] * 4 + [VMEM_SPEC] + [ANY_SPEC] * 2,
     )
 
 

time: 268 us -> 267 us (level); the launches traced: 267 us -> 270 us
  starting transfers between devices: 60 us -> 74.3 us
  waiting for transfers between devices: 96.4 us -> 90.3 us
  Pallas kernels: 86.2 us -> 81.5 us
    ppermute x18, starting transfers between devices: 21.6 us -> 36.2 us  [start(): self.got = lax.ppermute(send, self.axis, pairs)]
    ppermute x4, waiting for transfers between devices: 9.97 us -> 4.98 us  [seq_down(): return lax.ppermute(a, 'seq', [(i + 1, i) for i in range(count - 1)])]
    pallas_call x9, Pallas kernels: 86.2 us -> 81.5 us  [call(): pl.pallas_call(body, name=name, in_specs=specs, out_specs=out_specs or [V...]
  transfers between devices with their start and end apart: 44 -> 44, of which waited for: 25 -> 25; matrix products, arithmetic and copies ran while one was open for 6% -> 6% of each run, Pallas kernels for 20% -> 19%
where the time goes in v5:
time: 267 us; the launch traced here: 270 us
  waiting for transfers between devices  90.3 us (34%)
  Pallas kernels  81.5 us (31%)
  starting transfers between devices  74.3 us (28%)
  other arithmetic  19.1 us (7%)
  local copies, waits for them, and re-layouts  3.47 us (1%)
    pallas_call x9, Pallas kernels, call(): pl.pallas_call(body, name=name, in_specs=specs, out_specs=out_specs or [V...  81.5 us
    ppermute x18, waiting for transfers between devices, start(): self.got = lax.ppermute(send, self.axis, pairs)  36.3 us
    ppermute x18, starting transfers between devices, start(): self.got = lax.ppermute(send, self.axis, pairs)  36.2 us
    ppermute x4, starting transfers between devices, seq_up(): return lax.ppermute(a, 'seq', [(i, i + 1) for i in range(count - 1)])  17.5 us
    ppermute x2, waiting for transfers between devices, shards(): lax.ppermute(after(a, *hold), 'fsdp', p)  12.8 us
    ppermute x1, waiting for transfers between devices, shards(): ends = lax.ppermute(last, 'seq', [(0, split - 1), (split - 1, 0)])  8.89 us
    ppermute x1, waiting for transfers between devices, shards(): mem_got = lax.ppermute(after(mem_parts[2], g_ctx), 'seq', swap)  8.72 us
    convert_element_type x12, other arithmetic, sum_low(): return total.astype(BF)  8.47 us
  transfers between devices with their start and end apart: 44, of which 25 were waited for; matrix products, arithmetic and copies ran while one was open for 6% of the time, Pallas kernels for 19%

profile of v5, /device:TPU:0, one launch (start us, length us, event | category | flops | bytes accessed | tf_op | source)
XLA Modules:
  0.0 270.2 jit_solution(7654749103523584704)
XLA Ops:
  3.8 4.5 %collective-permute-start = (bf16[512,512]{1,0:T(8,128)(2,1)}, bf16[512,512]{1,0:T(8,128)(2,1)S(1)}, u32[]{:S(2)}, u32[]{:S(2)}) collective-permute-start(bf16[512,512]{1,0:T(8,128)(2,1)} %refs_5_.3), channel_id=1, source_target_pairs={{0,1},{1,2},{2,3},{4,5},{5,6},{6,7},{8,9},{9,10},{10,11},{12,13},{... | collective-permute-start | bytes 1572872 | tf_op jit(solution)/shard_map/ppermute | solution.py:190
  12.7 5.3 %collective-permute-done.3.refs_7_.refs_13_.refs_10_ = bf16[224,512]{1,0:T(8,128)(2,1)S(1)} collective-permute-done((bf16[224,512]{1,0:T(8,128)(2,1)}, bf16[224,512]{1,0:T(8,128)(2,1)S(1)}, u32[]{:S(2)}, u32[]{:S(2)}) %collective-permute-start.3) | collective-permute-done | bytes 229408 | tf_op jit(solution)/shard_map/ppermute | solution.py:1641
  20.4 4.1 %collective-permute-done.1.refs_8_.refs_15_ = bf16[512,512]{1,0:T(8,128)(2,1)} collective-permute-done((bf16[512,512]{1,0:T(8,128)(2,1)}, bf16[512,512]{1,0:T(8,128)(2,1)}, u32[]{:S(2)}, u32[]{:S(2)}) %collective-permute-start.1) | collective-permute-done | bytes 524320 | tf_op jit(solution)/shard_map/ppermute | solution.py:194
  31.0 4.3 %collective-permute-start.6 = (bf16[512,512]{1,0:T(8,128)(2,1)}, bf16[512,512]{1,0:T(8,128)(2,1)}, u32[]{:S(2)}, u32[]{:S(2)}) collective-permute-start(bf16[512,512]{1,0:T(8,128)(2,1)} %refs_13_.3), channel_id=1, source_target_pairs={{0,1},{1,2},{2,3},{4,5},{5,6},{6,7},{8,9},{9,10},{10,11},{12,13},{... | collective-permute-start | bytes 1572872 | tf_op jit(solution)/shard_map/ppermute | solution.py:190
  35.8 12.8 %collective-permute-done.9.refs_8_.refs_14_.refs_11_ = bf16[224,512]{1,0:T(8,128)(2,1)S(1)} collective-permute-done((bf16[224,512]{1,0:T(8,128)(2,1)S(1)}, bf16[224,512]{1,0:T(8,128)(2,1)S(1)}, u32[]{:S(2)}, u32[]{:S(2)}) %collective-permute-start.9) | collective-permute-done | bytes 229408 | tf_op jit(solution)/shard_map/ppermute | solution.py:1649
  48.7 3.8 %collective-permute-done.6.refs_7_.refs_14_ = bf16[512,512]{1,0:T(8,128)(2,1)} collective-permute-done((bf16[512,512]{1,0:T(8,128)(2,1)}, bf16[512,512]{1,0:T(8,128)(2,1)}, u32[]{:S(2)}, u32[]{:S(2)}) %collective-permute-start.6) | collective-permute-done | bytes 524320 | tf_op jit(solution)/shard_map/ppermute | solution.py:190
  56.9 5.2 %collective-permute-start.16 = (bf16[512,512]{1,0:T(8,128)(2,1)}, bf16[512,512]{1,0:T(8,128)(2,1)}, u32[]{:S(2)}, u32[]{:S(2)}) collective-permute-start(bf16[512,512]{1,0:T(8,128)(2,1)} %collective-permute-done.6.refs_7_.refs_14_), channel_id=1, source_target_pairs={{0,1},{1,2},{2,3},{4,5},{5,6},{6,7},{8,9},{9,10},{10,11},{12,13},{... | collective-permute-start | bytes 1572872 | tf_op jit(solution)/shard_map/ppermute | solution.py:190
  63.3 5.3 %collective-permute-start.18 = (bf16[512,512]{1,0:T(8,128)(2,1)}, bf16[512,512]{1,0:T(8,128)(2,1)S(1)}, u32[]{:S(2)}, u32[]{:S(2)}) collective-permute-start(bf16[512,512]{1,0:T(8,128)(2,1)} %refs_13_.3), channel_id=1, source_target_pairs={{0,3},{3,0},{4,7},{7,4},{8,11},{11,8},{12,15},{15,12},{16,19},{19,... | collective-permute-start | bytes 1572872 | tf_op jit(solution)/shard_map/ppermute | solution.py:1657
  71.3 8.9 %self_forward.1 = (bf16[512,512]{1,0:T(8,128)(2,1)}, bf16[2,512,256]{2,1,0:T(8,128)(2,1)}, bf16[6,256,512]{2,1,0:T(8,128)(2,1)}, bf16[6,256,512]{2,1,0:T(8,128)(...) custom-call(s32[1,4]{1,0:T(1,128)} %refs_0_.13, ...), custom_call_target="tpu_custom_call" | custom-call | flops 480000000 | bytes 216597 | tf_op jit(solution)/shard_map/self_forward/pallas_call | solution.py:537
  80.2 8.9 %collective-permute-done.18.refs_11_.refs_12_.refs_18_.refs_19_ = bf16[512,512]{1,0:T(8,128)(2,1)S(1)} collective-permute-done((bf16[512,512]{1,0:T(8,128)(2,1)}, bf16[512,512]{1,0:T(8,128)(2,1)S(1)}, u32[]{:S(2)}, u32[]{:S(2)}) %collective-permute-start.18) | collective-permute-done | bytes 524320 | tf_op jit(solution)/shard_map/ppermute | solution.py:1657
  92.7 11.6 %cross_forward.1 = (f32[512,512]{1,0:T(8,128)}, f32[512,1]{1,0:T(8,128)}, bf16[512,512]{1,0:T(8,128)(2,1)}, bf16[512,512]{1,0:T(8,128)(2,1)}, bf16[2,512,256]{2,...) custom-call(s32[1,4]{1,0:T(1,128)} %refs_0_.13, ...), custom_call_target="tpu_custom_call" | custom-call | flops 630000000 | bytes 442082 | tf_op jit(solution)/shard_map/cross_forward/pallas_call | solution.py:537
  104.2 14.9 %feed.1 = (bf16[512,512]{1,0:T(8,128)(2,1)}, f32[512,512]{1,0:T(8,128)}, bf16[512,512]{1,0:T(8,128)(2,1)}, bf16[2,512,256]{2,1,0:T(8,128)(2,1)}, f32[32,512]{1,0...) custom-call(s32[1,4]{1,0:T(1,128)} %refs_0_.13, s32[1,4]{1,0:T(1,128)} %refs_1_.13, ...), custom_call_target="tpu_custom_call" | custom-call | flops 510000000 | bytes 327680 | tf_op jit(solution)/shard_map/feed/pallas_call | solution.py:537
  122.4 4.4 %collective-permute-done.21 = bf16[4,576,512]{2,1,0:T(8,128)(2,1)S(1)} collective-permute-done((bf16[4,576,512]{2,1,0:T(8,128)(2,1)}, bf16[4,576,512]{2,1,0:T(8,128)(2,1)S(1)}, u32[]{:S(2)}, u32[]{:S(2)}) %collective-permute-start.21) | collective-permute-done | bytes 2359328 | tf_op jit(solution)/shard_map/ppermute | solution.py:139
  130.1 14.2 %cross_backward.1 = (bf16[2,256,512]{2,1,0:T(8,128)(2,1)}, bf16[2,256,512]{2,1,0:T(8,128)(2,1)}, bf16[2,256,512]{2,1,0:T(8,128)(2,1)}, bf16[2,256,512]{2,1,0:T(8...) custom-call(s32[1,4]{1,0:T(1,128)} %refs_0_.13, ...), custom_call_target="tpu_custom_call" | custom-call | flops 450000000 | bytes 461702 | tf_op jit(solution)/shard_map/cross_backward/pallas_call | solution.py:537
  150.8 9.2 %first_backward.1 = (bf16[4,256,512]{2,1,0:T(8,128)(2,1)}, bf16[4,256,512]{2,1,0:T(8,128)(2,1)}, f32[512,512]{1,0:T(8,128)}, bf16[512,512]{1,0:T(8,128)(2,1)}, b...) custom-call(s32[1,4]{1,0:T(1,128)} %refs_0_.13, s32[1,4]{1,0:T(1,128)} %refs_1_.13, s32[1,4]{1,0:T(1,128)} %refs_2_.8, ...), custom_call_target="tpu_custom_call" | custom-call | flops 180000000 | bytes 454861 | tf_op jit(solution)/shard_map/first_backward/pallas_call | solution.py:537
  165.8 11.5 %self_backward.1 = (bf16[2,512,512]{2,1,0:T(8,128)(2,1)}, bf16[512,512]{1,0:T(8,128)(2,1)}, bf16[6,256,512]{2,1,0:T(8,128)(2,1)}, bf16[6,256,512]{2,1,0:T(8,128)(2,1)}) custom-call(s32[1,4]{1,0:T(1,128)} %refs_0_.13, s32[1,4]{1,0:T(1,128)} %refs_1_.13, bf16[512,512]{1,0:T(8,128)(2,1)} %get-tuple-element.153.refs_2_, ...), custom_call_target="tpu_custom_call" | custom-call | flops 420000000 | bytes 288686 | tf_op jit(solution)/shard_map/self_backward/pallas_call | solution.py:537
  177.4 7.6 %collective-permute-done.27 = bf16[288,512]{1,0:T(8,128)(2,1)} collective-permute-done((bf16[288,512]{1,0:T(8,128)(2,1)S(1)}, bf16[288,512]{1,0:T(8,128)(2,1)}, u32[]{:S(2)}, u32[]{:S(2)}) %collective-permute-start.27) | collective-permute-done | bytes 294944 | tf_op jit(solution)/shard_map/ppermute | solution.py:139
  187.0 8.7 %collective-permute-done.25 = bf16[2,256,512]{2,1,0:T(8,128)(2,1)S(1)} collective-permute-done((bf16[2,256,512]{2,1,0:T(8,128)(2,1)}, bf16[2,256,512]{2,1,0:T(8,128)(2,1)S(1)}, u32[]{:S(2)}, u32[]{:S(2)}) %collective-permute-start.25) | collective-permute-done | bytes 524320 | tf_op jit(solution)/shard_map/ppermute | solution.py:1713
  198.5 5.4 %collective-permute-start.29 = (bf16[2,256,512]{2,1,0:T(8,128)(2,1)}, bf16[2,256,512]{2,1,0:T(8,128)(2,1)}, u32[]{:S(2)}, u32[]{:S(2)}) collective-permute-start(bf16[2,256,512]{2,1,0:T(8,128)(2,1)} %add_convert_fusion.3), channel_id=1, source_target_pairs={{0,8},{4,20},{8,0},{12,28},{16,24},{20,4},{24,16},{28,12},{1,9},{5... | collective-permute-start | bytes 1572872 | tf_op jit(solution)/shard_map/ppermute | solution.py:139
  206.0 6.8 %self_weights.1 = (bf16[4,224,512]{2,1,0:T(8,128)(2,1)}, bf16[4,224,512]{2,1,0:T(8,128)(2,1)}, f32[512,512]{1,0:T(8,128)}) custom-call(bf16[512,512]{1,0:T(8,128)(2,1)} %get-tuple-element.196.refs_0_, bf16[6,256,512]{2,1,0:T(8,128)(2,1)} %get-tuple-element.197.refs_1_, bf16[6,256,512]{2,1,0:T(8,128)(2,1)} %get-tuple-element.198.refs_2_, ...), custom_call_target="tpu_custom_call" | custom-call | flops 210000000 | bytes 221511 | tf_op jit(solution)/shard_map/self_weights/pallas_call | solution.py:537
  215.2 5.5 %collective-permute-start.36 = (bf16[1,256,512]{2,1,0:T(8,128)(2,1)S(1)}, bf16[1,256,512]{2,1,0:T(8,128)(2,1)S(1)}, u32[]{:S(2)}, u32[]{:S(2)}) collective-permute-start(bf16[1,256,512]{2,1,0:T(8,128)(2,1)S(1)} %add_convert_fusion.8), channel_id=1, source_target_pairs={{0,16},{4,12},{8,24},{12,4},{16,0},{20,28},{24,8},{28,20},{1,17},{... | collective-permute-start | bytes 786440 | tf_op jit(solution)/shard_map/ppermute | solution.py:139
  230.9 4.0 %collective-permute-start.32 = (bf16[2,224,512]{2,1,0:T(8,128)(2,1)S(1)}, bf16[2,224,512]{2,1,0:T(8,128)(2,1)S(1)}, u32[]{:S(2)}, u32[]{:S(2)}) collective-permute-start(bf16[2,224,512]{2,1,0:T(8,128)(2,1)S(1)} %add_convert_fusion.5), channel_id=1, source_target_pairs={{0,8},{4,20},{8,0},{12,28},{16,24},{20,4},{24,16},{28,12},{1,9},{5... | collective-permute-start | bytes 1376264 | tf_op jit(solution)/shard_map/ppermute | solution.py:139
  236.5 4.8 %collective-permute-done.32 = bf16[2,224,512]{2,1,0:T(8,128)(2,1)S(1)} collective-permute-done((bf16[2,224,512]{2,1,0:T(8,128)(2,1)S(1)}, bf16[2,224,512]{2,1,0:T(8,128)(2,1)S(1)}, u32[]{:S(2)}, u32[]{:S(2)}) %collective-permute-start.32) | collective-permute-done | bytes 458784 | tf_op jit(solution)/shard_map/ppermute | solution.py:139
  256.2 5.0 %collective-permute-done.42 = bf16[128,512]{1,0:T(8,128)(2,1)S(1)} collective-permute-done((bf16[128,512]{1,0:T(8,128)(2,1)S(1)}, bf16[128,512]{1,0:T(8,128)(2,1)S(1)}, u32[]{:S(2)}, u32[]{:S(2)}) %collective-permute-start.42) | collective-permute-done | bytes 131104 | tf_op jit(solution)/shard_map/ppermute | solution.py:139
  (154 shorter events, 92.0 us)
Async XLA Ops:
  3.2 21.3 %collective-permute-start.4 = (bf16[832,512]{1,0:T(8,128)(2,1)}, bf16[832,512]{1,0:T(8,128)(2,1)S(1)}, u32[]{:S(2)}, u32[]{:S(2)}) collective-permute-start(bf16[832,512]{1,0:T(8,128)(2,1)} %get-tuple-element.135.refs_13_.refs_6_.refs_12_.refs_20_), channel_id=1, source_target_pairs={{0,4},{4,0},{8,12},{12,8},{16,20},{20,16},{24,28},{28,24},{1,5},{5... | collective-permute-start | bytes 2555912 | tf_op jit(solution)/shard_map/ppermute | solution.py:1640
  3.8 16.6 %collective-permute-start = (bf16[512,512]{1,0:T(8,128)(2,1)}, bf16[512,512]{1,0:T(8,128)(2,1)S(1)}, u32[]{:S(2)}, u32[]{:S(2)}) collective-permute-start(bf16[512,512]{1,0:T(8,128)(2,1)} %refs_5_.3), channel_id=1, source_target_pairs={{0,1},{1,2},{2,3},{4,5},{5,6},{6,7},{8,9},{9,10},{10,11},{12,13},{... | collective-permute-start | bytes 1572872 | tf_op jit(solution)/shard_map/ppermute | solution.py:190
  8.3 16.2 %collective-permute-start.1 = (bf16[512,512]{1,0:T(8,128)(2,1)}, bf16[512,512]{1,0:T(8,128)(2,1)}, u32[]{:S(2)}, u32[]{:S(2)}) collective-permute-start(bf16[512,512]{1,0:T(8,128)(2,1)} %refs_13_.3), channel_id=1, source_target_pairs={{1,0},{2,1},{3,2},{5,4},{6,5},{7,6},{9,8},{10,9},{11,10},{13,12},{... | collective-permute-start | bytes 1572872 | tf_op jit(solution)/shard_map/ppermute | solution.py:194
  24.5 28.0 %collective-permute-start.8 = (bf16[832,512]{1,0:T(8,128)(2,1)}, bf16[832,512]{1,0:T(8,128)(2,1)S(1)}, u32[]{:S(2)}, u32[]{:S(2)}) collective-permute-start(bf16[832,512]{1,0:T(8,128)(2,1)} %get-tuple-element.135.refs_13_.refs_6_.refs_12_.refs_20_), channel_id=1, source_target_pairs={{0,16},{4,12},{8,24},{12,4},{16,0},{20,28},{24,8},{28,20},{1,17},{... | collective-permute-start | bytes 2555912 | tf_op jit(solution)/shard_map/ppermute | solution.py:1647
  26.1 26.4 %collective-permute-start.7 = (bf16[832,512]{1,0:T(8,128)(2,1)}, bf16[832,512]{1,0:T(8,128)(2,1)S(1)}, u32[]{:S(2)}, u32[]{:S(2)}) collective-permute-start(bf16[832,512]{1,0:T(8,128)(2,1)} %get-tuple-element.135.refs_13_.refs_6_.refs_12_.refs_20_), channel_id=1, source_target_pairs={{0,8},{4,20},{8,0},{12,28},{16,24},{20,4},{24,16},{28,12},{1,9},{5... | collective-permute-start | bytes 2555912 | tf_op jit(solution)/shard_map/ppermute | solution.py:1647
  27.6 21.1 %collective-permute-start.5 = (bf16[512,512]{1,0:T(8,128)(2,1)S(1)}, bf16[512,512]{1,0:T(8,128)(2,1)S(1)}, u32[]{:S(2)}, u32[]{:S(2)}) collective-permute-start(bf16[512,512]{1,0:T(8,128)(2,1)S(1)} %collective-permute-done.refs_3_.refs_6_), channel_id=1, source_target_pairs={{0,1},{1,2},{2,3},{4,5},{5,6},{6,7},{8,9},{9,10},{10,11},{12,13},{... | collective-permute-start | bytes 1572872 | tf_op jit(solution)/shard_map/ppermute | solution.py:190
  31.0 21.5 %collective-permute-start.6 = (bf16[512,512]{1,0:T(8,128)(2,1)}, bf16[512,512]{1,0:T(8,128)(2,1)}, u32[]{:S(2)}, u32[]{:S(2)}) collective-permute-start(bf16[512,512]{1,0:T(8,128)(2,1)} %refs_13_.3), channel_id=1, source_target_pairs={{0,1},{1,2},{2,3},{4,5},{5,6},{6,7},{8,9},{9,10},{10,11},{12,13},{... | collective-permute-start | bytes 1572872 | tf_op jit(solution)/shard_map/ppermute | solution.py:190
  52.6 16.1 %collective-permute-start.11 = (bf16[832,512]{1,0:T(8,128)(2,1)S(1)}, bf16[832,512]{1,0:T(8,128)(2,1)S(1)}, u32[]{:S(2)}, u32[]{:S(2)}) collective-permute-start(bf16[832,512]{1,0:T(8,128)(2,1)S(1)} %collective-permute-done.8.refs_15_.refs_8_.refs_14_.refs_22_), channel_id=1, source_target_pairs={{0,4},{4,0},{8,12},{12,8},{16,20},{20,16},{24,28},{28,24},{1,5},{5... | collective-permute-start | bytes 2555912 | tf_op jit(solution)/shard_map/ppermute | solution.py:1667
  53.2 36.0 %collective-permute-start.19 = (bf16[832,512]{1,0:T(8,128)(2,1)S(1)}, bf16[832,512]{1,0:T(8,128)(2,1)}, u32[]{:S(2)}, u32[]{:S(2)}) collective-permute-start(bf16[832,512]{1,0:T(8,128)(2,1)S(1)} %collective-permute-done.7.refs_14_.refs_7_.refs_13_.refs_21_), channel_id=1, source_target_pairs={{0,16},{4,12},{8,24},{12,4},{16,0},{20,28},{24,8},{28,20},{1,17},{... | collective-permute-start | bytes 2555912 | tf_op jit(solution)/shard_map/ppermute | solution.py:1652
  56.9 23.4 %collective-permute-start.16 = (bf16[512,512]{1,0:T(8,128)(2,1)}, bf16[512,512]{1,0:T(8,128)(2,1)}, u32[]{:S(2)}, u32[]{:S(2)}) collective-permute-start(bf16[512,512]{1,0:T(8,128)(2,1)} %collective-permute-done.6.refs_7_.refs_14_), channel_id=1, source_target_pairs={{0,1},{1,2},{2,3},{4,5},{5,6},{6,7},{8,9},{9,10},{10,11},{12,13},{... | collective-permute-start | bytes 1572872 | tf_op jit(solution)/shard_map/ppermute | solution.py:190
  62.0 18.2 %collective-permute-start.17 = (bf16[512,512]{1,0:T(8,128)(2,1)}, bf16[512,512]{1,0:T(8,128)(2,1)}, u32[]{:S(2)}, u32[]{:S(2)}) collective-permute-start(bf16[512,512]{1,0:T(8,128)(2,1)} %collective-permute-done.1.refs_8_.refs_15_), channel_id=1, source_target_pairs={{1,0},{2,1},{3,2},{5,4},{6,5},{7,6},{9,8},{10,9},{11,10},{13,12},{... | collective-permute-start | bytes 1572872 | tf_op jit(solution)/shard_map/ppermute | solution.py:194
  63.3 25.8 %collective-permute-start.18 = (bf16[512,512]{1,0:T(8,128)(2,1)}, bf16[512,512]{1,0:T(8,128)(2,1)S(1)}, u32[]{:S(2)}, u32[]{:S(2)}) collective-permute-start(bf16[512,512]{1,0:T(8,128)(2,1)} %refs_13_.3), channel_id=1, source_target_pairs={{0,3},{3,0},{4,7},{7,4},{8,11},{11,8},{12,15},{15,12},{16,19},{19,... | collective-permute-start | bytes 1572872 | tf_op jit(solution)/shard_map/ppermute | solution.py:1657
  129.2 16.4 %collective-permute-start.22 = (bf16[2,576,512]{2,1,0:T(8,128)(2,1)S(1)}, bf16[2,576,512]{2,1,0:T(8,128)(2,1)}, u32[]{:S(2)}, u32[]{:S(2)}) collective-permute-start(bf16[2,576,512]{2,1,0:T(8,128)(2,1)S(1)} %add_convert_fusion), channel_id=1, source_target_pairs={{0,8},{4,20},{8,0},{12,28},{16,24},{20,4},{24,16},{28,12},{1,9},{5... | collective-permute-start | bytes 3538952 | tf_op jit(solution)/shard_map/ppermute | solution.py:139
  144.3 15.8 %collective-permute-start.24 = (bf16[2,256,512]{2,1,0:T(8,128)(2,1)}, bf16[2,256,512]{2,1,0:T(8,128)(2,1)}, u32[]{:S(2)}, u32[]{:S(2)}) collective-permute-start(bf16[2,256,512]{2,1,0:T(8,128)(2,1)} %get-tuple-element.185), channel_id=1, source_target_pairs={{0,1},{1,0},{2,3},{3,2},{4,5},{5,4},{6,7},{7,6},{8,9},{9,8},{10,11... | collective-permute-start | bytes 1572872 | tf_op jit(solution)/shard_map/ppermute | solution.py:1698
  147.1 15.0 %collective-permute-start.23 = (bf16[1,576,512]{2,1,0:T(8,128)(2,1)S(1)}, bf16[1,576,512]{2,1,0:T(8,128)(2,1)S(1)}, u32[]{:S(2)}, u32[]{:S(2)}) collective-permute-start(bf16[1,576,512]{2,1,0:T(8,128)(2,1)S(1)} %add_convert_fusion.2), channel_id=1, source_target_pairs={{0,16},{4,12},{8,24},{12,4},{16,0},{20,28},{24,8},{28,20},{1,17},{... | collective-permute-start | bytes 1769480 | tf_op jit(solution)/shard_map/ppermute | solution.py:139
  163.7 22.4 %collective-permute-start.28 = (bf16[4,256,512]{2,1,0:T(8,128)(2,1)}, bf16[4,256,512]{2,1,0:T(8,128)(2,1)S(1)}, u32[]{:S(2)}, u32[]{:S(2)}) collective-permute-start(bf16[4,256,512]{2,1,0:T(8,128)(2,1)} %get-tuple-element.195), channel_id=1, source_target_pairs={{0,4},{4,0},{8,12},{12,8},{16,20},{20,16},{24,28},{28,24},{1,5},{5... | collective-permute-start | bytes 3145736 | tf_op jit(solution)/shard_map/ppermute | solution.py:139
  163.8 21.2 %collective-permute-start.27 = (bf16[288,512]{1,0:T(8,128)(2,1)S(1)}, bf16[288,512]{1,0:T(8,128)(2,1)}, u32[]{:S(2)}, u32[]{:S(2)}) collective-permute-start(bf16[288,512]{1,0:T(8,128)(2,1)S(1)} %select_bitcast_fusion), channel_id=1, source_target_pairs={{0,1},{1,0},{2,3},{3,2},{4,5},{5,4},{6,7},{7,6},{8,9},{9,8},{10,11... | collective-permute-start | bytes 884744 | tf_op jit(solution)/shard_map/ppermute | solution.py:139
  165.6 30.1 %collective-permute-start.25 = (bf16[2,256,512]{2,1,0:T(8,128)(2,1)}, bf16[2,256,512]{2,1,0:T(8,128)(2,1)S(1)}, u32[]{:S(2)}, u32[]{:S(2)}) collective-permute-start(bf16[2,256,512]{2,1,0:T(8,128)(2,1)} %get-tuple-element.190), channel_id=1, source_target_pairs={{0,1},{1,0},{2,3},{3,2},{4,5},{5,4},{6,7},{7,6},{8,9},{9,8},{10,11... | collective-permute-start | bytes 1572872 | tf_op jit(solution)/shard_map/ppermute | solution.py:1713
  165.8 29.9 %collective-permute-start.26 = (bf16[2,256,512]{2,1,0:T(8,128)(2,1)}, bf16[2,256,512]{2,1,0:T(8,128)(2,1)S(1)}, u32[]{:S(2)}, u32[]{:S(2)}) collective-permute-start(bf16[2,256,512]{2,1,0:T(8,128)(2,1)} %add_convert_fusion.4), channel_id=1, source_target_pairs={{0,2},{1,3},{2,0},{3,1},{4,6},{5,7},{6,4},{7,5},{8,10},{9,11},{10,... | collective-permute-start | bytes 1572872 | tf_op jit(solution)/shard_map/ppermute | solution.py:1714
  195.7 17.1 %collective-permute-start.30 = (bf16[288,512]{1,0:T(8,128)(2,1)S(1)}, bf16[288,512]{1,0:T(8,128)(2,1)}, u32[]{:S(2)}, u32[]{:S(2)}) collective-permute-start(bf16[288,512]{1,0:T(8,128)(2,1)S(1)} %fusion.1), channel_id=1, source_target_pairs={{0,2},{1,3},{2,0},{3,1},{4,6},{5,7},{6,4},{7,5},{8,10},{9,11},{10,... | collective-permute-start | bytes 884744 | tf_op jit(solution)/shard_map/ppermute | solution.py:139
  198.5 15.5 %collective-permute-start.29 = (bf16[2,256,512]{2,1,0:T(8,128)(2,1)}, bf16[2,256,512]{2,1,0:T(8,128)(2,1)}, u32[]{:S(2)}, u32[]{:S(2)}) collective-permute-start(bf16[2,256,512]{2,1,0:T(8,128)(2,1)} %add_convert_fusion.3), channel_id=1, source_target_pairs={{0,8},{4,20},{8,0},{12,28},{16,24},{20,4},{24,16},{28,12},{1,9},{5... | collective-permute-start | bytes 1572872 | tf_op jit(solution)/shard_map/ppermute | solution.py:139
  204.7 17.2 %collective-permute-start.34 = (bf16[512,512]{1,0:T(8,128)(2,1)}, bf16[512,512]{1,0:T(8,128)(2,1)S(1)}, u32[]{:S(2)}, u32[]{:S(2)}) collective-permute-start(bf16[512,512]{1,0:T(8,128)(2,1)} %slice_bitcast_fusion), channel_id=1, source_target_pairs={{1,0},{2,1},{3,2},{5,4},{6,5},{7,6},{9,8},{10,9},{11,10},{13,12},{... | collective-permute-start | bytes 1572872 | tf_op jit(solution)/shard_map/ppermute | solution.py:194
  215.1 15.7 %collective-permute-start.31 = (bf16[4,224,512]{2,1,0:T(8,128)(2,1)}, bf16[4,224,512]{2,1,0:T(8,128)(2,1)S(1)}, u32[]{:S(2)}, u32[]{:S(2)}) collective-permute-start(bf16[4,224,512]{2,1,0:T(8,128)(2,1)} %get-tuple-element.204), channel_id=1, source_target_pairs={{0,4},{4,0},{8,12},{12,8},{16,20},{20,16},{24,28},{28,24},{1,5},{5... | collective-permute-start | bytes 2752520 | tf_op jit(solution)/shard_map/ppermute | solution.py:139
  222.1 21.7 %collective-permute-start.35 = (bf16[512,512]{1,0:T(8,128)(2,1)S(1)}, bf16[512,512]{1,0:T(8,128)(2,1)S(1)}, u32[]{:S(2)}, u32[]{:S(2)}) collective-permute-start(bf16[512,512]{1,0:T(8,128)(2,1)S(1)} %fusion), channel_id=1, source_target_pairs={{1,0},{2,1},{3,2},{5,4},{6,5},{7,6},{9,8},{10,9},{11,10},{13,12},{... | collective-permute-start | bytes 1572872 | tf_op jit(solution)/shard_map/ppermute | solution.py:194
  (46 other events, 567.9 us)

commit v6 on v5

--- a/solution.py
+++ b/solution.py
@@ -457,16 +457,11 @@
     wait_all(wq, sems.at[0])
     tiles = rows // TILE
 
-    def own_rows(i, carry):
-        r = pl.ds(pl.multiple_of(i * TILE, TILE), TILE)
-        q = (mm(toks[0][r, :], wq[...]) + vec[V_SQB : V_SQB + 1, :]).astype(BF)
-        q = q * BF(HDIM**-0.5)
-        q_ref[r, :] = q
-        q_t3[i] = q.T
-        return carry
-
+    q = (mm(toks[0][...], wq[...]) + vec[V_SQB : V_SQB + 1, :]).astype(BF)
+    q = q * BF(HDIM**-0.5)
+    q_ref[...] = q
     for i in range(tiles):
-        own_rows(i, 0)
+        q_t3[i] = q[i * TILE : (i + 1) * TILE, :].T
     q_copies = send_all((q_ref, q_t3), kept[:2], q_sems)
     wait_all(wk, sems.at[1])
     wait_all(wv, sems.at[2])
@@ -476,23 +471,21 @@
 
     for k in range(halo + 1):
 
-        def window_rows(i, carry, k=k):
-            r = pl.ds(pl.multiple_of(i * TILE, TILE), TILE)
-            t = (halo - k) * tiles + i
-            x = toks[k][r, :]
-            key = mm(x, wk[...]).astype(BF)
-            val = (mm(x, wv[...]) + vec[V_SVB : V_SVB + 1, :]).astype(BF)
-            k3[t] = key
-            v3[t] = val
-            k_t3[t] = key.T
-            v_t3[t] = val.T
-            for copy in window_copies(t):
-                copy.start()
-            return carry
-
         @pl.when(z >= k)
-        def _(window_rows=window_rows):
-            lax.fori_loop(0, tiles, window_rows, 0)
+        def _(k=k):
+            x = toks[k][...]
+            keys = mm(x, wk[...]).astype(BF)
+            vals = (mm(x, wv[...]) + vec[V_SVB : V_SVB + 1, :]).astype(BF)
+            for i in range(tiles):
+                t = (halo - k) * tiles + i
+                key = keys[i * TILE : (i + 1) * TILE, :]
+                val = vals[i * TILE : (i + 1) * TILE, :]
+                k3[t] = key
+                v3[t] = val
+                k_t3[t] = key.T
+                v_t3[t] = val.T
+                for copy in window_copies(t):
+                    copy.start()
 
     def block(b, carry):
         spread_rows(q_t3.at[b], q_t)
@@ -788,22 +781,17 @@
     wait_all(wo, sems.at[0])
     wait_all(wcq, sems.at[1])
 
-    def own_rows(i, carry):
-        r = pl.ds(pl.multiple_of(i * TILE, TILE), TILE)
-        v = tok[r, :].astype(F32) + (mm(ctx[r, :], wo[...]) + vec[V_SOB : V_SOB + 1, :])
-        normal, inv = norm_stats(v)
-        n1[r, :] = normal
-        inv1[r, :] = inv
-        low = (normal * vec[V_G1 : V_G1 + 1, :] + vec[V_S1 : V_S1 + 1, :]).astype(BF)
-        first_low[r, :] = low
-        q = (mm(low, wcq[...]) + vec[V_CQB : V_CQB + 1, :]).astype(BF)
-        q = q * BF(HDIM**-0.5)
-        q_ref[r, :] = q
-        q_t3[i] = q.T
-        return carry
-
+    v = tok[...].astype(F32) + (mm(ctx[...], wo[...]) + vec[V_SOB : V_SOB + 1, :])
+    normal, inv = norm_stats(v)
+    n1[...] = normal
+    inv1[...] = inv
+    low = (normal * vec[V_G1 : V_G1 + 1, :] + vec[V_S1 : V_S1 + 1, :]).astype(BF)
+    first_low[...] = low
+    q = (mm(low, wcq[...]) + vec[V_CQB : V_CQB + 1, :]).astype(BF)
+    q = q * BF(HDIM**-0.5)
+    q_ref[...] = q
     for i in range(rows // TILE):
-        own_rows(i, 0)
+        q_t3[i] = q[i * TILE : (i + 1) * TILE, :].T
     row_copies = send_all((n1, first_low, q_ref, q_t3), (n1_out, *early), row_sems)
     wait_all(wck, sems.at[2])
     wait_all(wcv, sems.at[3])

time: 267 us -> 270 us (1.011); the launches traced: 270 us -> 267 us
  waiting for transfers between devices: 90.3 us -> 105 us
  Pallas kernels: 81.5 us -> 72.2 us
  starting transfers between devices: 74.3 us -> 65.3 us
    ppermute x18, waiting for transfers between devices: 36.3 us -> 46.3 us  [start(): self.got = lax.ppermute(send, self.axis, pairs)]
    pallas_call x9, Pallas kernels: 81.5 us -> 72.2 us  [call(): pl.pallas_call(body, name=name, in_specs=specs, out_specs=out_specs or [V...]
    ppermute x18, starting transfers between devices: 36.2 us -> 27.9 us  [start(): self.got = lax.ppermute(send, self.axis, pairs)]
    ppermute x4, waiting for transfers between devices: 4.98 us -> 10.3 us  [seq_down(): return lax.ppermute(a, 'seq', [(i + 1, i) for i in range(count - 1)])]
  transfers between devices with their start and end apart: 44 -> 44, of which waited for: 25 -> 26; matrix products, arithmetic and copies ran while one was open for 6% -> 6% of each run, Pallas kernels for 19% -> 16%
where the time goes in v6:
time: 270 us; the launch traced here: 267 us
  waiting for transfers between devices  105 us (39%)
  Pallas kernels  72.2 us (27%)
  starting transfers between devices  65.3 us (24%)
  other arithmetic  19.1 us (7%)
  local copies, waits for them, and re-layouts  3.47 us (1%)
    pallas_call x9, Pallas kernels, call(): pl.pallas_call(body, name=name, in_specs=specs, out_specs=out_specs or [V...  72.2 us
    ppermute x18, waiting for transfers between devices, start(): self.got = lax.ppermute(send, self.axis, pairs)  46.3 us
    ppermute x18, starting transfers between devices, start(): self.got = lax.ppermute(send, self.axis, pairs)  27.9 us
    ppermute x4, starting transfers between devices, seq_up(): return lax.ppermute(a, 'seq', [(i, i + 1) for i in range(count - 1)])  17.5 us
    ppermute x2, waiting for transfers between devices, shards(): lax.ppermute(after(a, *hold), 'fsdp', p)  12.8 us
    ppermute x4, waiting for transfers between devices, seq_down(): return lax.ppermute(a, 'seq', [(i + 1, i) for i in range(count - 1)])  10.3 us
    ppermute x1, waiting for transfers between devices, shards(): ends = lax.ppermute(last, 'seq', [(0, split - 1), (split - 1, 0)])  9.12 us
    convert_element_type x12, other arithmetic, sum_low(): return total.astype(BF)  8.39 us
  transfers between devices with their start and end apart: 44, of which 26 were waited for; matrix products, arithmetic and copies ran while one was open for 6% of the time, Pallas kernels for 16%

profile of v6, /device:TPU:0, one launch (start us, length us, event | category | flops | bytes accessed | tf_op | source)
XLA Modules:
  0.0 266.7 jit_solution(12055268092045981700)
XLA Ops:
  3.8 4.5 %collective-permute-start = (bf16[512,512]{1,0:T(8,128)(2,1)}, bf16[512,512]{1,0:T(8,128)(2,1)S(1)}, u32[]{:S(2)}, u32[]{:S(2)}) collective-permute-start(bf16[512,512]{1,0:T(8,128)(2,1)} %refs_5_.3), channel_id=1, source_target_pairs={{0,1},{1,2},{2,3},{4,5},{5,6},{6,7},{8,9},{9,10},{10,11},{12,13},{... | collective-permute-start | bytes 1572872 | tf_op jit(solution)/shard_map/ppermute | solution.py:190
  12.7 5.3 %collective-permute-done.3.refs_7_.refs_13_.refs_10_ = bf16[224,512]{1,0:T(8,128)(2,1)S(1)} collective-permute-done((bf16[224,512]{1,0:T(8,128)(2,1)}, bf16[224,512]{1,0:T(8,128)(2,1)S(1)}, u32[]{:S(2)}, u32[]{:S(2)}) %collective-permute-start.3) | collective-permute-done | bytes 229408 | tf_op jit(solution)/shard_map/ppermute | solution.py:1629
  20.4 4.1 %collective-permute-done.1.refs_8_.refs_15_ = bf16[512,512]{1,0:T(8,128)(2,1)} collective-permute-done((bf16[512,512]{1,0:T(8,128)(2,1)}, bf16[512,512]{1,0:T(8,128)(2,1)}, u32[]{:S(2)}, u32[]{:S(2)}) %collective-permute-start.1) | collective-permute-done | bytes 524320 | tf_op jit(solution)/shard_map/ppermute | solution.py:194
  31.0 4.3 %collective-permute-start.6 = (bf16[512,512]{1,0:T(8,128)(2,1)}, bf16[512,512]{1,0:T(8,128)(2,1)}, u32[]{:S(2)}, u32[]{:S(2)}) collective-permute-start(bf16[512,512]{1,0:T(8,128)(2,1)} %refs_13_.3), channel_id=1, source_target_pairs={{0,1},{1,2},{2,3},{4,5},{5,6},{6,7},{8,9},{9,10},{10,11},{12,13},{... | collective-permute-start | bytes 1572872 | tf_op jit(solution)/shard_map/ppermute | solution.py:190
  35.8 12.8 %collective-permute-done.9.refs_8_.refs_14_.refs_11_ = bf16[224,512]{1,0:T(8,128)(2,1)S(1)} collective-permute-done((bf16[224,512]{1,0:T(8,128)(2,1)S(1)}, bf16[224,512]{1,0:T(8,128)(2,1)S(1)}, u32[]{:S(2)}, u32[]{:S(2)}) %collective-permute-start.9) | collective-permute-done | bytes 229408 | tf_op jit(solution)/shard_map/ppermute | solution.py:1637
  48.7 3.8 %collective-permute-done.6.refs_7_.refs_14_ = bf16[512,512]{1,0:T(8,128)(2,1)} collective-permute-done((bf16[512,512]{1,0:T(8,128)(2,1)}, bf16[512,512]{1,0:T(8,128)(2,1)}, u32[]{:S(2)}, u32[]{:S(2)}) %collective-permute-start.6) | collective-permute-done | bytes 524320 | tf_op jit(solution)/shard_map/ppermute | solution.py:190
  56.9 5.2 %collective-permute-start.16 = (bf16[512,512]{1,0:T(8,128)(2,1)}, bf16[512,512]{1,0:T(8,128)(2,1)}, u32[]{:S(2)}, u32[]{:S(2)}) collective-permute-start(bf16[512,512]{1,0:T(8,128)(2,1)} %collective-permute-done.6.refs_7_.refs_14_), channel_id=1, source_target_pairs={{0,1},{1,2},{2,3},{4,5},{5,6},{6,7},{8,9},{9,10},{10,11},{12,13},{... | collective-permute-start | bytes 1572872 | tf_op jit(solution)/shard_map/ppermute | solution.py:190
  63.3 5.3 %collective-permute-start.18 = (bf16[512,512]{1,0:T(8,128)(2,1)}, bf16[512,512]{1,0:T(8,128)(2,1)S(1)}, u32[]{:S(2)}, u32[]{:S(2)}) collective-permute-start(bf16[512,512]{1,0:T(8,128)(2,1)} %refs_13_.3), channel_id=1, source_target_pairs={{0,3},{3,0},{4,7},{7,4},{8,11},{11,8},{12,15},{15,12},{16,19},{19,... | collective-permute-start | bytes 1572872 | tf_op jit(solution)/shard_map/ppermute | solution.py:1645
  71.3 8.7 %self_forward.1 = (bf16[512,512]{1,0:T(8,128)(2,1)}, bf16[2,512,256]{2,1,0:T(8,128)(2,1)}, bf16[6,256,512]{2,1,0:T(8,128)(2,1)}, bf16[6,256,512]{2,1,0:T(8,128)(...) custom-call(s32[1,4]{1,0:T(1,128)} %refs_0_.13, ...), custom_call_target="tpu_custom_call" | custom-call | flops 480000000 | bytes 216597 | tf_op jit(solution)/shard_map/self_forward/pallas_call | solution.py:530
  80.0 9.1 %collective-permute-done.18.refs_11_.refs_12_.refs_18_.refs_19_ = bf16[512,512]{1,0:T(8,128)(2,1)S(1)} collective-permute-done((bf16[512,512]{1,0:T(8,128)(2,1)}, bf16[512,512]{1,0:T(8,128)(2,1)S(1)}, u32[]{:S(2)}, u32[]{:S(2)}) %collective-permute-start.18) | collective-permute-done | bytes 524320 | tf_op jit(solution)/shard_map/ppermute | solution.py:1645
  92.7 11.3 %cross_forward.1 = (f32[512,512]{1,0:T(8,128)}, f32[512,1]{1,0:T(8,128)}, bf16[512,512]{1,0:T(8,128)(2,1)}, bf16[512,512]{1,0:T(8,128)(2,1)}, bf16[2,512,256]{2,...) custom-call(s32[1,4]{1,0:T(1,128)} %refs_0_.13, ...), custom_call_target="tpu_custom_call" | custom-call | flops 630000000 | bytes 442082 | tf_op jit(solution)/shard_map/cross_forward/pallas_call | solution.py:530
  104.0 15.0 %feed.1 = (bf16[512,512]{1,0:T(8,128)(2,1)}, f32[512,512]{1,0:T(8,128)}, bf16[512,512]{1,0:T(8,128)(2,1)}, bf16[2,512,256]{2,1,0:T(8,128)(2,1)}, f32[32,512]{1,0...) custom-call(s32[1,4]{1,0:T(1,128)} %refs_0_.13, s32[1,4]{1,0:T(1,128)} %refs_1_.13, ...), custom_call_target="tpu_custom_call" | custom-call | flops 510000000 | bytes 327680 | tf_op jit(solution)/shard_map/feed/pallas_call | solution.py:530
  122.1 4.4 %collective-permute-done.21 = bf16[4,576,512]{2,1,0:T(8,128)(2,1)S(1)} collective-permute-done((bf16[4,576,512]{2,1,0:T(8,128)(2,1)}, bf16[4,576,512]{2,1,0:T(8,128)(2,1)S(1)}, u32[]{:S(2)}, u32[]{:S(2)}) %collective-permute-start.21) | collective-permute-done | bytes 2359328 | tf_op jit(solution)/shard_map/ppermute | solution.py:139
  129.0 3.8 %collective-permute-start.22 = (bf16[2,576,512]{2,1,0:T(8,128)(2,1)S(1)}, bf16[2,576,512]{2,1,0:T(8,128)(2,1)}, u32[]{:S(2)}, u32[]{:S(2)}) collective-permute-start(bf16[2,576,512]{2,1,0:T(8,128)(2,1)S(1)} %add_convert_fusion), channel_id=1, source_target_pairs={{0,8},{4,20},{8,0},{12,28},{16,24},{20,4},{24,16},{28,12},{1,9},{5... | collective-permute-start | bytes 3538952 | tf_op jit(solution)/shard_map/ppermute | solution.py:139
  132.8 6.3 %cross_backward.1 = (bf16[2,256,512]{2,1,0:T(8,128)(2,1)}, bf16[2,256,512]{2,1,0:T(8,128)(2,1)}, bf16[2,256,512]{2,1,0:T(8,128)(2,1)}, bf16[2,256,512]{2,1,0:T(8...) custom-call(s32[1,4]{1,0:T(1,128)} %refs_0_.13, ...), custom_call_target="tpu_custom_call" | custom-call | flops 450000000 | bytes 461702 | tf_op jit(solution)/shard_map/cross_backward/pallas_call | solution.py:530
  139.2 7.9 %collective-permute-done.22 = bf16[2,576,512]{2,1,0:T(8,128)(2,1)} collective-permute-done((bf16[2,576,512]{2,1,0:T(8,128)(2,1)S(1)}, bf16[2,576,512]{2,1,0:T(8,128)(2,1)}, u32[]{:S(2)}, u32[]{:S(2)}) %collective-permute-start.22) | collective-permute-done | bytes 1179680 | tf_op jit(solution)/shard_map/ppermute | solution.py:139
  150.7 8.3 %first_backward.1 = (bf16[4,256,512]{2,1,0:T(8,128)(2,1)}, bf16[4,256,512]{2,1,0:T(8,128)(2,1)}, f32[512,512]{1,0:T(8,128)}, bf16[512,512]{1,0:T(8,128)(2,1)}, b...) custom-call(s32[1,4]{1,0:T(1,128)} %refs_0_.13, s32[1,4]{1,0:T(1,128)} %refs_1_.13, s32[1,4]{1,0:T(1,128)} %refs_2_.8, ...), custom_call_target="tpu_custom_call" | custom-call | flops 180000000 | bytes 454861 | tf_op jit(solution)/shard_map/first_backward/pallas_call | solution.py:530
  167.8 11.5 %self_backward.1 = (bf16[2,512,512]{2,1,0:T(8,128)(2,1)}, bf16[512,512]{1,0:T(8,128)(2,1)}, bf16[6,256,512]{2,1,0:T(8,128)(2,1)}, bf16[6,256,512]{2,1,0:T(8,128)(2,1)}) custom-call(s32[1,4]{1,0:T(1,128)} %refs_0_.13, s32[1,4]{1,0:T(1,128)} %refs_1_.13, bf16[512,512]{1,0:T(8,128)(2,1)} %get-tuple-element.153.refs_2_, ...), custom_call_target="tpu_custom_call" | custom-call | flops 420000000 | bytes 288686 | tf_op jit(solution)/shard_map/self_backward/pallas_call | solution.py:530
  179.4 7.4 %collective-permute-done.27 = bf16[288,512]{1,0:T(8,128)(2,1)} collective-permute-done((bf16[288,512]{1,0:T(8,128)(2,1)S(1)}, bf16[288,512]{1,0:T(8,128)(2,1)}, u32[]{:S(2)}, u32[]{:S(2)}) %collective-permute-start.27) | collective-permute-done | bytes 294944 | tf_op jit(solution)/shard_map/ppermute | solution.py:139
  188.8 8.2 %collective-permute-done.25 = bf16[2,256,512]{2,1,0:T(8,128)(2,1)S(1)} collective-permute-done((bf16[2,256,512]{2,1,0:T(8,128)(2,1)}, bf16[2,256,512]{2,1,0:T(8,128)(2,1)S(1)}, u32[]{:S(2)}, u32[]{:S(2)}) %collective-permute-start.25) | collective-permute-done | bytes 524320 | tf_op jit(solution)/shard_map/ppermute | solution.py:1701
  204.4 6.8 %self_weights.1 = (bf16[4,224,512]{2,1,0:T(8,128)(2,1)}, bf16[4,224,512]{2,1,0:T(8,128)(2,1)}, f32[512,512]{1,0:T(8,128)}) custom-call(bf16[512,512]{1,0:T(8,128)(2,1)} %get-tuple-element.196.refs_0_, bf16[6,256,512]{2,1,0:T(8,128)(2,1)} %get-tuple-element.197.refs_1_, bf16[6,256,512]{2,1,0:T(8,128)(2,1)} %get-tuple-element.198.refs_2_, ...), custom_call_target="tpu_custom_call" | custom-call | flops 210000000 | bytes 221511 | tf_op jit(solution)/shard_map/self_weights/pallas_call | solution.py:530
  217.4 5.4 %collective-permute-done.34 = bf16[512,512]{1,0:T(8,128)(2,1)S(1)} collective-permute-done((bf16[512,512]{1,0:T(8,128)(2,1)}, bf16[512,512]{1,0:T(8,128)(2,1)S(1)}, u32[]{:S(2)}, u32[]{:S(2)}) %collective-permute-start.34) | collective-permute-done | bytes 524320 | tf_op jit(solution)/shard_map/ppermute | solution.py:194
  234.0 4.8 %collective-permute-done.32 = bf16[2,224,512]{2,1,0:T(8,128)(2,1)S(1)} collective-permute-done((bf16[2,224,512]{2,1,0:T(8,128)(2,1)S(1)}, bf16[2,224,512]{2,1,0:T(8,128)(2,1)S(1)}, u32[]{:S(2)}, u32[]{:S(2)}) %collective-permute-start.32) | collective-permute-done | bytes 458784 | tf_op jit(solution)/shard_map/ppermute | solution.py:139
  240.8 4.2 %collective-permute-done.33 = bf16[1,224,512]{2,1,0:T(8,128)(2,1)S(1)} collective-permute-done((bf16[1,224,512]{2,1,0:T(8,128)(2,1)S(1)}, bf16[1,224,512]{2,1,0:T(8,128)(2,1)S(1)}, u32[]{:S(2)}, u32[]{:S(2)}) %collective-permute-start.33) | collective-permute-done | bytes 229408 | tf_op jit(solution)/shard_map/ppermute | solution.py:139
  (154 shorter events, 96.7 us)
Async XLA Ops:
  3.2 21.3 %collective-permute-start.4 = (bf16[832,512]{1,0:T(8,128)(2,1)}, bf16[832,512]{1,0:T(8,128)(2,1)S(1)}, u32[]{:S(2)}, u32[]{:S(2)}) collective-permute-start(bf16[832,512]{1,0:T(8,128)(2,1)} %get-tuple-element.135.refs_13_.refs_6_.refs_12_.refs_20_), channel_id=1, source_target_pairs={{0,4},{4,0},{8,12},{12,8},{16,20},{20,16},{24,28},{28,24},{1,5},{5... | collective-permute-start | bytes 2555912 | tf_op jit(solution)/shard_map/ppermute | solution.py:1628
  3.8 16.6 %collective-permute-start = (bf16[512,512]{1,0:T(8,128)(2,1)}, bf16[512,512]{1,0:T(8,128)(2,1)S(1)}, u32[]{:S(2)}, u32[]{:S(2)}) collective-permute-start(bf16[512,512]{1,0:T(8,128)(2,1)} %refs_5_.3), channel_id=1, source_target_pairs={{0,1},{1,2},{2,3},{4,5},{5,6},{6,7},{8,9},{9,10},{10,11},{12,13},{... | collective-permute-start | bytes 1572872 | tf_op jit(solution)/shard_map/ppermute | solution.py:190
  8.3 16.2 %collective-permute-start.1 = (bf16[512,512]{1,0:T(8,128)(2,1)}, bf16[512,512]{1,0:T(8,128)(2,1)}, u32[]{:S(2)}, u32[]{:S(2)}) collective-permute-start(bf16[512,512]{1,0:T(8,128)(2,1)} %refs_13_.3), channel_id=1, source_target_pairs={{1,0},{2,1},{3,2},{5,4},{6,5},{7,6},{9,8},{10,9},{11,10},{13,12},{... | collective-permute-start | bytes 1572872 | tf_op jit(solution)/shard_map/ppermute | solution.py:194
  24.5 28.0 %collective-permute-start.8 = (bf16[832,512]{1,0:T(8,128)(2,1)}, bf16[832,512]{1,0:T(8,128)(2,1)S(1)}, u32[]{:S(2)}, u32[]{:S(2)}) collective-permute-start(bf16[832,512]{1,0:T(8,128)(2,1)} %get-tuple-element.135.refs_13_.refs_6_.refs_12_.refs_20_), channel_id=1, source_target_pairs={{0,16},{4,12},{8,24},{12,4},{16,0},{20,28},{24,8},{28,20},{1,17},{... | collective-permute-start | bytes 2555912 | tf_op jit(solution)/shard_map/ppermute | solution.py:1635
  26.1 26.4 %collective-permute-start.7 = (bf16[832,512]{1,0:T(8,128)(2,1)}, bf16[832,512]{1,0:T(8,128)(2,1)S(1)}, u32[]{:S(2)}, u32[]{:S(2)}) collective-permute-start(bf16[832,512]{1,0:T(8,128)(2,1)} %get-tuple-element.135.refs_13_.refs_6_.refs_12_.refs_20_), channel_id=1, source_target_pairs={{0,8},{4,20},{8,0},{12,28},{16,24},{20,4},{24,16},{28,12},{1,9},{5... | collective-permute-start | bytes 2555912 | tf_op jit(solution)/shard_map/ppermute | solution.py:1635
  27.6 21.1 %collective-permute-start.5 = (bf16[512,512]{1,0:T(8,128)(2,1)S(1)}, bf16[512,512]{1,0:T(8,128)(2,1)S(1)}, u32[]{:S(2)}, u32[]{:S(2)}) collective-permute-start(bf16[512,512]{1,0:T(8,128)(2,1)S(1)} %collective-permute-done.refs_3_.refs_6_), channel_id=1, source_target_pairs={{0,1},{1,2},{2,3},{4,5},{5,6},{6,7},{8,9},{9,10},{10,11},{12,13},{... | collective-permute-start | bytes 1572872 | tf_op jit(solution)/shard_map/ppermute | solution.py:190
  31.0 21.5 %collective-permute-start.6 = (bf16[512,512]{1,0:T(8,128)(2,1)}, bf16[512,512]{1,0:T(8,128)(2,1)}, u32[]{:S(2)}, u32[]{:S(2)}) collective-permute-start(bf16[512,512]{1,0:T(8,128)(2,1)} %refs_13_.3), channel_id=1, source_target_pairs={{0,1},{1,2},{2,3},{4,5},{5,6},{6,7},{8,9},{9,10},{10,11},{12,13},{... | collective-permute-start | bytes 1572872 | tf_op jit(solution)/shard_map/ppermute | solution.py:190
  35.3 13.3 %collective-permute-start.9 = (bf16[224,512]{1,0:T(8,128)(2,1)S(1)}, bf16[224,512]{1,0:T(8,128)(2,1)S(1)}, u32[]{:S(2)}, u32[]{:S(2)}) collective-permute-start(bf16[224,512]{1,0:T(8,128)(2,1)S(1)} %collective-permute-done.2.refs_6_.refs_12_.refs_9_), channel_id=1, source_target_pairs={{0,16},{4,12},{8,24},{12,4},{16,0},{20,28},{24,8},{28,20},{1,17},{... | collective-permute-start | bytes 688136 | tf_op jit(solution)/shard_map/ppermute | solution.py:1637
  52.6 16.1 %collective-permute-start.11 = (bf16[832,512]{1,0:T(8,128)(2,1)S(1)}, bf16[832,512]{1,0:T(8,128)(2,1)S(1)}, u32[]{:S(2)}, u32[]{:S(2)}) collective-permute-start(bf16[832,512]{1,0:T(8,128)(2,1)S(1)} %collective-permute-done.8.refs_15_.refs_8_.refs_14_.refs_22_), channel_id=1, source_target_pairs={{0,4},{4,0},{8,12},{12,8},{16,20},{20,16},{24,28},{28,24},{1,5},{5... | collective-permute-start | bytes 2555912 | tf_op jit(solution)/shard_map/ppermute | solution.py:1655
  53.2 36.0 %collective-permute-start.19 = (bf16[832,512]{1,0:T(8,128)(2,1)S(1)}, bf16[832,512]{1,0:T(8,128)(2,1)}, u32[]{:S(2)}, u32[]{:S(2)}) collective-permute-start(bf16[832,512]{1,0:T(8,128)(2,1)S(1)} %collective-permute-done.7.refs_14_.refs_7_.refs_13_.refs_21_), channel_id=1, source_target_pairs={{0,16},{4,12},{8,24},{12,4},{16,0},{20,28},{24,8},{28,20},{1,17},{... | collective-permute-start | bytes 2555912 | tf_op jit(solution)/shard_map/ppermute | solution.py:1640
  56.9 23.1 %collective-permute-start.16 = (bf16[512,512]{1,0:T(8,128)(2,1)}, bf16[512,512]{1,0:T(8,128)(2,1)}, u32[]{:S(2)}, u32[]{:S(2)}) collective-permute-start(bf16[512,512]{1,0:T(8,128)(2,1)} %collective-permute-done.6.refs_7_.refs_14_), channel_id=1, source_target_pairs={{0,1},{1,2},{2,3},{4,5},{5,6},{6,7},{8,9},{9,10},{10,11},{12,13},{... | collective-permute-start | bytes 1572872 | tf_op jit(solution)/shard_map/ppermute | solution.py:190
  62.0 18.0 %collective-permute-start.17 = (bf16[512,512]{1,0:T(8,128)(2,1)}, bf16[512,512]{1,0:T(8,128)(2,1)}, u32[]{:S(2)}, u32[]{:S(2)}) collective-permute-start(bf16[512,512]{1,0:T(8,128)(2,1)} %collective-permute-done.1.refs_8_.refs_15_), channel_id=1, source_target_pairs={{1,0},{2,1},{3,2},{5,4},{6,5},{7,6},{9,8},{10,9},{11,10},{13,12},{... | collective-permute-start | bytes 1572872 | tf_op jit(solution)/shard_map/ppermute | solution.py:194
  63.3 25.8 %collective-permute-start.18 = (bf16[512,512]{1,0:T(8,128)(2,1)}, bf16[512,512]{1,0:T(8,128)(2,1)S(1)}, u32[]{:S(2)}, u32[]{:S(2)}) collective-permute-start(bf16[512,512]{1,0:T(8,128)(2,1)} %refs_13_.3), channel_id=1, source_target_pairs={{0,3},{3,0},{4,7},{7,4},{8,11},{11,8},{12,15},{15,12},{16,19},{19,... | collective-permute-start | bytes 1572872 | tf_op jit(solution)/shard_map/ppermute | solution.py:1645
  129.0 18.1 %collective-permute-start.22 = (bf16[2,576,512]{2,1,0:T(8,128)(2,1)S(1)}, bf16[2,576,512]{2,1,0:T(8,128)(2,1)}, u32[]{:S(2)}, u32[]{:S(2)}) collective-permute-start(bf16[2,576,512]{2,1,0:T(8,128)(2,1)S(1)} %add_convert_fusion), channel_id=1, source_target_pairs={{0,8},{4,20},{8,0},{12,28},{16,24},{20,4},{24,16},{28,12},{1,9},{5... | collective-permute-start | bytes 3538952 | tf_op jit(solution)/shard_map/ppermute | solution.py:139
  139.1 19.9 %collective-permute-start.24 = (bf16[2,256,512]{2,1,0:T(8,128)(2,1)}, bf16[2,256,512]{2,1,0:T(8,128)(2,1)}, u32[]{:S(2)}, u32[]{:S(2)}) collective-permute-start(bf16[2,256,512]{2,1,0:T(8,128)(2,1)} %get-tuple-element.185), channel_id=1, source_target_pairs={{0,1},{1,0},{2,3},{3,2},{4,5},{5,4},{6,7},{7,6},{8,9},{9,8},{10,11... | collective-permute-start | bytes 1572872 | tf_op jit(solution)/shard_map/ppermute | solution.py:1686
  162.6 25.2 %collective-permute-start.28 = (bf16[4,256,512]{2,1,0:T(8,128)(2,1)}, bf16[4,256,512]{2,1,0:T(8,128)(2,1)S(1)}, u32[]{:S(2)}, u32[]{:S(2)}) collective-permute-start(bf16[4,256,512]{2,1,0:T(8,128)(2,1)} %get-tuple-element.195), channel_id=1, source_target_pairs={{0,4},{4,0},{8,12},{12,8},{16,20},{20,16},{24,28},{28,24},{1,5},{5... | collective-permute-start | bytes 3145736 | tf_op jit(solution)/shard_map/ppermute | solution.py:139
  165.6 21.2 %collective-permute-start.27 = (bf16[288,512]{1,0:T(8,128)(2,1)S(1)}, bf16[288,512]{1,0:T(8,128)(2,1)}, u32[]{:S(2)}, u32[]{:S(2)}) collective-permute-start(bf16[288,512]{1,0:T(8,128)(2,1)S(1)} %select_bitcast_fusion), channel_id=1, source_target_pairs={{0,1},{1,0},{2,3},{3,2},{4,5},{5,4},{6,7},{7,6},{8,9},{9,8},{10,11... | collective-permute-start | bytes 884744 | tf_op jit(solution)/shard_map/ppermute | solution.py:139
  167.3 29.8 %collective-permute-start.25 = (bf16[2,256,512]{2,1,0:T(8,128)(2,1)}, bf16[2,256,512]{2,1,0:T(8,128)(2,1)S(1)}, u32[]{:S(2)}, u32[]{:S(2)}) collective-permute-start(bf16[2,256,512]{2,1,0:T(8,128)(2,1)} %get-tuple-element.190), channel_id=1, source_target_pairs={{0,1},{1,0},{2,3},{3,2},{4,5},{5,4},{6,7},{7,6},{8,9},{9,8},{10,11... | collective-permute-start | bytes 1572872 | tf_op jit(solution)/shard_map/ppermute | solution.py:1701
  167.6 29.4 %collective-permute-start.26 = (bf16[2,256,512]{2,1,0:T(8,128)(2,1)}, bf16[2,256,512]{2,1,0:T(8,128)(2,1)S(1)}, u32[]{:S(2)}, u32[]{:S(2)}) collective-permute-start(bf16[2,256,512]{2,1,0:T(8,128)(2,1)} %add_convert_fusion.4), channel_id=1, source_target_pairs={{0,2},{1,3},{2,0},{3,1},{4,6},{5,7},{6,4},{7,5},{8,10},{9,11},{10,... | collective-permute-start | bytes 1572872 | tf_op jit(solution)/shard_map/ppermute | solution.py:1702
  197.1 16.4 %collective-permute-start.30 = (bf16[288,512]{1,0:T(8,128)(2,1)S(1)}, bf16[288,512]{1,0:T(8,128)(2,1)}, u32[]{:S(2)}, u32[]{:S(2)}) collective-permute-start(bf16[288,512]{1,0:T(8,128)(2,1)S(1)} %fusion.1), channel_id=1, source_target_pairs={{0,2},{1,3},{2,0},{3,1},{4,6},{5,7},{6,4},{7,5},{8,10},{9,11},{10,... | collective-permute-start | bytes 884744 | tf_op jit(solution)/shard_map/ppermute | solution.py:139
  199.7 14.8 %collective-permute-start.29 = (bf16[2,256,512]{2,1,0:T(8,128)(2,1)}, bf16[2,256,512]{2,1,0:T(8,128)(2,1)}, u32[]{:S(2)}, u32[]{:S(2)}) collective-permute-start(bf16[2,256,512]{2,1,0:T(8,128)(2,1)} %add_convert_fusion.3), channel_id=1, source_target_pairs={{0,8},{4,20},{8,0},{12,28},{16,24},{20,4},{24,16},{28,12},{1,9},{5... | collective-permute-start | bytes 1572872 | tf_op jit(solution)/shard_map/ppermute | solution.py:139
  203.1 19.8 %collective-permute-start.34 = (bf16[512,512]{1,0:T(8,128)(2,1)}, bf16[512,512]{1,0:T(8,128)(2,1)S(1)}, u32[]{:S(2)}, u32[]{:S(2)}) collective-permute-start(bf16[512,512]{1,0:T(8,128)(2,1)} %slice_bitcast_fusion), channel_id=1, source_target_pairs={{1,0},{2,1},{3,2},{5,4},{6,5},{7,6},{9,8},{10,9},{11,10},{13,12},{... | collective-permute-start | bytes 1572872 | tf_op jit(solution)/shard_map/ppermute | solution.py:194
  215.6 14.6 %collective-permute-start.31 = (bf16[4,224,512]{2,1,0:T(8,128)(2,1)}, bf16[4,224,512]{2,1,0:T(8,128)(2,1)S(1)}, u32[]{:S(2)}, u32[]{:S(2)}) collective-permute-start(bf16[4,224,512]{2,1,0:T(8,128)(2,1)} %get-tuple-element.204), channel_id=1, source_target_pairs={{0,4},{4,0},{8,12},{12,8},{16,20},{20,16},{24,28},{28,24},{1,5},{5... | collective-permute-start | bytes 2752520 | tf_op jit(solution)/shard_map/ppermute | solution.py:139
  223.0 16.6 %collective-permute-start.35 = (bf16[512,512]{1,0:T(8,128)(2,1)S(1)}, bf16[512,512]{1,0:T(8,128)(2,1)S(1)}, u32[]{:S(2)}, u32[]{:S(2)}) collective-permute-start(bf16[512,512]{1,0:T(8,128)(2,1)S(1)} %fusion), channel_id=1, source_target_pairs={{1,0},{2,1},{3,2},{5,4},{6,5},{7,6},{9,8},{10,9},{11,10},{13,12},{... | collective-permute-start | bytes 1572872 | tf_op jit(solution)/shard_map/ppermute | solution.py:194
  (46 other events, 562.5 us)
